TPU v7x, 32 devices: a whole 2x2x4 slice. The times are simulated.
32 devices in a mesh: dp: 16 (over z, y, x), tensor: 2 (over core).
Axes of the slice: x: 2, y: 2, z: 4, core: 2. Of those that a mesh axis runs over, the one named last changes fastest.
Arguments:
- embedded: bfloat16 [16, 1024, 768], P('dp', 'tensor'), may hold values from -6 to 6
- lengths: int32 [16], P('dp'), may hold values from 256 to 1024, as said below
- patch_proj: bfloat16 [6144, 768], P(('dp', 'tensor')), may hold values from -0.078125 to 0.078125
- global_proj: bfloat16 [768, 6144], P(None, ('dp', 'tensor')), may hold values from -0.21875 to 0.21875
- qkv_weight: bfloat16 [2, 768, 3, 768], P(None, 'dp', None, 'tensor'), may hold values from -0.21875 to 0.21875
- out_weight: bfloat16 [2, 768, 768], P(None, 'tensor', 'dp'), may hold values from -0.875 to 0.875
- up_weight: bfloat16 [2, 768, 3072], P(None, 'dp', 'tensor'), may hold values from -0.21875 to 0.21875
- down_weight: bfloat16 [2, 3072, 768], P(None, 'tensor', 'dp'), may hold values from -0.109375 to 0.109375
- norm_gain: bfloat16 [3072], P(('dp', 'tensor')), may hold values from 0.25 to 1.75
- norm_bias: bfloat16 [3072], P(('dp', 'tensor')), may hold values from -1.5 to 1.5
- cotangent: bfloat16 [16, 1024, 768], P('dp', 'tensor'), may hold values from -6 to 6
Outputs:
- result: bfloat16 [16, 1024, 768], P('dp', 'tensor')
- grad_embedded: bfloat16 [16, 1024, 768], P('dp', 'tensor')
- grad_patch_proj: float32 [6144, 768], P(('dp', 'tensor'))
- grad_global_proj: float32 [768, 6144], P(None, ('dp', 'tensor'))
- grad_qkv_weight: float32 [2, 768, 3, 768], P(None, 'dp', None, 'tensor')
- grad_out_weight: float32 [2, 768, 768], P(None, 'tensor', 'dp')
- grad_up_weight: float32 [2, 768, 3072], P(None, 'dp', 'tensor')
- grad_down_weight: float32 [2, 3072, 768], P(None, 'tensor', 'dp')
- grad_norm_gain: float32 [3072], P(('dp', 'tensor'))
- grad_norm_bias: float32 [3072], P(('dp', 'tensor'))
Inputs may be any that keep to these rules, and one draw needn't show every extreme that they name: `lengths`: one slot has exactly 1024 valid bytes and another exactly 256.
All inputs are finite; a program needn't handle non-finite values.
Results may differ from a plain program's by a relative error of at most 0.03.
Values may be sent and summed in bfloat16 or wider, within the bound.
No kernel may reach another device: no remote copies, remote signals or barrier semaphores. Data moves between devices by JAX's collectives and lax.ppermute only.
A program may use at most 256 MiB of HBM per device.

v0:
```python
import jax
import jax.numpy as jnp
from jax import lax
from jax.sharding import PartitionSpec as P

D = 768
HD = 64
P_SIZE = 8
NORMS = 4


EPSILON = 1e-05
NEGATIVE = -1e30


def layer_norm(stream, gain_row, bias_row):
    average = jnp.mean(stream, axis=-1, keepdims=True)
    centered = stream - average
    variance = jnp.mean(centered * centered, axis=-1, keepdims=True)
    return centered * lax.rsqrt(variance + EPSILON) * gain_row + bias_row


def spread_rows(values_in):
    return lax.all_gather(values_in, "tensor", axis=0, tiled=True)


def collect_rows(partial_value):
    return lax.psum_scatter(
        partial_value.astype(jnp.bfloat16), "tensor", scatter_dimension=0, tiled=True
    ).astype(jnp.float32)


def unchanged(values_in):
    return values_in


def layer_weights(qkv_weight, out_weight, up_weight, down_weight, layer_index):
    return (
        lax.all_gather(qkv_weight[layer_index], "dp", axis=0, tiled=True),
        lax.all_gather(out_weight[layer_index], "dp", axis=1, tiled=True),
        lax.all_gather(up_weight[layer_index], "dp", axis=0, tiled=True),
        lax.all_gather(down_weight[layer_index], "dp", axis=1, tiled=True),
    )


def local_weights(qkv_weight, out_weight, up_weight, down_weight):
    sharded = layer_weights(qkv_weight, out_weight, up_weight, down_weight, 1)
    return (
        lax.all_gather(sharded[0], "tensor", axis=2, tiled=True),
        lax.all_gather(sharded[1], "tensor", axis=0, tiled=True),
        lax.all_gather(sharded[2], "tensor", axis=1, tiled=True),
        lax.all_gather(sharded[3], "tensor", axis=0, tiled=True),
    )


def shared_weights(patch_proj, global_proj, norm_gain, norm_bias):
    return (
        lax.all_gather(patch_proj, ("dp", "tensor"), axis=0, tiled=True),
        lax.all_gather(global_proj, ("dp", "tensor"), axis=1, tiled=True),
        lax.all_gather(norm_gain, ("dp", "tensor"), axis=0, tiled=True),
        lax.all_gather(norm_bias, ("dp", "tensor"), axis=0, tiled=True),
    )


def reduce_layer(gradients):
    return (
        lax.psum_scatter(gradients[0], "dp", scatter_dimension=0, tiled=True),
        lax.psum_scatter(gradients[1], "dp", scatter_dimension=1, tiled=True),
        lax.psum_scatter(gradients[2], "dp", scatter_dimension=0, tiled=True),
        lax.psum_scatter(gradients[3], "dp", scatter_dimension=1, tiled=True),
    )


def reduce_local(gradients):
    summed = (
        lax.psum_scatter(gradients[0], "dp", scatter_dimension=0, tiled=True),
        lax.psum_scatter(gradients[1], "dp", scatter_dimension=1, tiled=True),
        lax.psum_scatter(gradients[2], "dp", scatter_dimension=0, tiled=True),
        lax.psum_scatter(gradients[3], "dp", scatter_dimension=1, tiled=True),
    )
    return (
        lax.psum_scatter(
            summed[0].astype(jnp.bfloat16), "tensor", scatter_dimension=2, tiled=True
        ).astype(jnp.float32),
        lax.psum_scatter(
            summed[1].astype(jnp.bfloat16), "tensor", scatter_dimension=0, tiled=True
        ).astype(jnp.float32),
        lax.psum_scatter(
            summed[2].astype(jnp.bfloat16), "tensor", scatter_dimension=1, tiled=True
        ).astype(jnp.float32),
        lax.psum_scatter(
            summed[3].astype(jnp.bfloat16), "tensor", scatter_dimension=0, tiled=True
        ).astype(jnp.float32),
    )


def split_heads(packed, group_size):
    row_count = packed.shape[0]
    head_count = packed.shape[2] // HD
    head_shape = (row_count // group_size, group_size, head_count, HD)
    return (
        packed[:, 0].reshape(head_shape),
        packed[:, 1].reshape(head_shape),
        packed[:, 2].reshape(head_shape),
    )


def causal_scores(queries, keys_all, group_size):
    scores = jnp.einsum(
        "gihe,gjhe->ghij", queries, keys_all, preferred_element_type=jnp.float32
    ) * HD ** (-0.5)
    places = jnp.arange(group_size)
    return jnp.where(places[:, None] >= places[None, :], scores, NEGATIVE)


def attend_forward(packed, group_size):
    queries, keys_all, values_all = split_heads(packed, group_size)
    scores = causal_scores(queries, keys_all, group_size)
    row_max = jnp.max(scores, axis=-1, keepdims=True)
    shifted = jnp.exp(scores - row_max)
    row_total = jnp.sum(shifted, axis=-1, keepdims=True)
    softened = (shifted / row_total).astype(jnp.bfloat16)
    mixture = jnp.einsum(
        "ghij,gjhe->gihe", softened, values_all, preferred_element_type=jnp.float32
    )
    return (mixture.reshape(packed.shape[0], -1).astype(jnp.bfloat16), row_max + jnp.log(row_total))


def attend_backward(packed, log_total, grad_mix, group_size):
    queries, keys_all, values_all = split_heads(packed, group_size)
    scores = causal_scores(queries, keys_all, group_size)
    softened = jnp.exp(scores - log_total)
    grad_heads = grad_mix.reshape(queries.shape)
    grad_soft = jnp.einsum(
        "gihe,gjhe->ghij", grad_heads, values_all, preferred_element_type=jnp.float32
    )
    centre = jnp.sum(grad_soft * softened, axis=-1, keepdims=True)
    grad_scores = (softened * (grad_soft - centre)).astype(jnp.bfloat16)
    grad_values = jnp.einsum(
        "ghij,gihe->gjhe",
        softened.astype(jnp.bfloat16),
        grad_heads,
        preferred_element_type=jnp.float32,
    )
    grad_queries = jnp.einsum(
        "ghij,gjhe->gihe", grad_scores, keys_all, preferred_element_type=jnp.float32
    ) * HD ** (-0.5)
    grad_keys = jnp.einsum(
        "ghij,gihe->gjhe", grad_scores, queries, preferred_element_type=jnp.float32
    ) * HD ** (-0.5)
    row_count = packed.shape[0]
    stacked = jnp.stack(
        [
            grad_queries.reshape(row_count, -1),
            grad_keys.reshape(row_count, -1),
            grad_values.reshape(row_count, -1),
        ],
        axis=1,
    )
    return stacked.astype(jnp.bfloat16)


def layer_forward(stream, weights, gain_rows, bias_rows, norm_index, whole_group):
    joint_proj, output_proj, upward, downward = weights
    widen = spread_rows if whole_group else unchanged
    narrow = collect_rows if whole_group else unchanged
    normed = layer_norm(stream, gain_rows[norm_index], bias_rows[norm_index]).astype(jnp.bfloat16)
    normed_all = widen(normed)
    group_size = normed_all.shape[0] if whole_group else P_SIZE
    packed = jnp.einsum(
        "rd,dce->rce", normed_all, joint_proj, preferred_element_type=jnp.float32
    ).astype(jnp.bfloat16)
    mixture, log_total = attend_forward(packed, group_size)
    middle = stream + narrow(jnp.dot(mixture, output_proj, preferred_element_type=jnp.float32))
    second = layer_norm(middle, gain_rows[norm_index + 1], bias_rows[norm_index + 1]).astype(
        jnp.bfloat16
    )
    second_all = widen(second)
    hidden = jnp.dot(second_all, upward, preferred_element_type=jnp.float32)
    active = jax.nn.gelu(hidden).astype(jnp.bfloat16)
    outcome = middle + narrow(jnp.dot(active, downward, preferred_element_type=jnp.float32))
    return (
        outcome,
        (stream, normed_all, packed, mixture, log_total, middle, second_all, hidden, active),
    )


def layer_backward(grad_layer, saved, weights, gain_rows, bias_rows, norm_index, whole_group):
    stream, normed_all, packed, mixture, log_total, middle, second_all, hidden, active = saved
    joint_proj, output_proj, upward, downward = weights
    widen = spread_rows if whole_group else unchanged
    narrow = collect_rows if whole_group else unchanged
    group_size = normed_all.shape[0] if whole_group else P_SIZE
    grad_all = widen(grad_layer.astype(jnp.bfloat16))
    grad_down = jnp.einsum("rf,rd->fd", active, grad_all, preferred_element_type=jnp.float32)
    grad_active = jnp.einsum("rd,fd->rf", grad_all, downward, preferred_element_type=jnp.float32)
    gelu_value, gelu_pull = jax.vjp(jax.nn.gelu, hidden)
    grad_hidden = gelu_pull(grad_active)[0].astype(jnp.bfloat16)
    grad_up = jnp.einsum("rd,rf->df", second_all, grad_hidden, preferred_element_type=jnp.float32)
    grad_second = narrow(
        jnp.einsum("rf,df->rd", grad_hidden, upward, preferred_element_type=jnp.float32)
    )
    norm_value, second_pull = jax.vjp(
        layer_norm, middle, gain_rows[norm_index + 1], bias_rows[norm_index + 1]
    )
    grad_middle_norm, grad_gain_two, grad_bias_two = second_pull(grad_second)
    grad_middle = grad_layer + grad_middle_norm
    grad_branch = widen(grad_middle.astype(jnp.bfloat16))
    grad_output = jnp.einsum("re,rd->ed", mixture, grad_branch, preferred_element_type=jnp.float32)
    grad_mix = jnp.einsum(
        "rd,ed->re", grad_branch, output_proj, preferred_element_type=jnp.float32
    ).astype(jnp.bfloat16)
    grad_packed = attend_backward(packed, log_total, grad_mix, group_size)
    grad_joint = jnp.einsum(
        "rd,rce->dce", normed_all, grad_packed, preferred_element_type=jnp.float32
    )
    grad_normed = narrow(
        jnp.einsum("rce,dce->rd", grad_packed, joint_proj, preferred_element_type=jnp.float32)
    )
    first_value, first_pull = jax.vjp(
        layer_norm, stream, gain_rows[norm_index], bias_rows[norm_index]
    )
    grad_stream_norm, grad_gain_one, grad_bias_one = first_pull(grad_normed)
    grad_stream = grad_middle + grad_stream_norm
    return (
        grad_stream,
        (grad_joint, grad_output, grad_up, grad_down),
        (grad_gain_one, grad_gain_two),
        (grad_bias_one, grad_bias_two),
    )


def shards(
    embedded,
    lengths,
    patch_proj,
    global_proj,
    qkv_weight,
    out_weight,
    up_weight,
    down_weight,
    norm_gain,
    norm_bias,
    cotangent,
):
    half_rows = embedded.shape[1]
    positions = lax.axis_index("tensor") * half_rows + jnp.arange(half_rows, dtype=jnp.int32)
    keep_mask = (positions < lengths[0]).astype(jnp.float32)[:, None]
    masked = embedded[0].astype(jnp.float32) * keep_mask
    masked_low = masked.astype(jnp.bfloat16)
    patch_full, global_full, gain_full, bias_full = shared_weights(
        patch_proj, global_proj, norm_gain, norm_bias
    )
    gain_rows = gain_full.astype(jnp.float32).reshape(NORMS, D)
    bias_rows = bias_full.astype(jnp.float32).reshape(NORMS, D)
    patches = masked_low.reshape(half_rows // P_SIZE, P_SIZE * D)
    initial = jnp.dot(patches, patch_full, preferred_element_type=jnp.float32)
    first_weights = layer_weights(qkv_weight, out_weight, up_weight, down_weight, 0)
    global_out, first_saved = layer_forward(initial, first_weights, gain_rows, bias_rows, 0, True)
    global_low = global_out.astype(jnp.bfloat16)
    spread = jnp.dot(global_low, global_full, preferred_element_type=jnp.float32).reshape(
        half_rows, D
    )
    second_weights = local_weights(qkv_weight, out_weight, up_weight, down_weight)
    outcome, second_saved = layer_forward(
        masked + spread, second_weights, gain_rows, bias_rows, 2, False
    )
    grad_final = cotangent[0].astype(jnp.float32) * keep_mask
    second_weights = local_weights(qkv_weight, out_weight, up_weight, down_weight)
    grad_local, second_grads, second_gains, second_biases = layer_backward(
        grad_final, second_saved, second_weights, gain_rows, bias_rows, 2, False
    )
    second_summed = reduce_local(second_grads)
    first_weights = layer_weights(qkv_weight, out_weight, up_weight, down_weight, 0)
    patch_full, global_full, gain_full, bias_full = shared_weights(
        patch_proj, global_proj, norm_gain, norm_bias
    )
    grad_spread = grad_local.astype(jnp.bfloat16).reshape(half_rows // P_SIZE, P_SIZE * D)
    grad_global_proj = jnp.einsum(
        "pd,pe->de", global_low, grad_spread, preferred_element_type=jnp.float32
    )
    grad_global = jnp.einsum(
        "pe,de->pd", grad_spread, global_full, preferred_element_type=jnp.float32
    )
    grad_initial, first_grads, first_gains, first_biases = layer_backward(
        grad_global, first_saved, first_weights, gain_rows, bias_rows, 0, True
    )
    first_summed = reduce_layer(first_grads)
    grad_initial_low = grad_initial.astype(jnp.bfloat16)
    grad_patch_proj = jnp.einsum(
        "pe,pd->ed", patches, grad_initial_low, preferred_element_type=jnp.float32
    )
    grad_patches = jnp.einsum(
        "pd,ed->pe", grad_initial_low, patch_full, preferred_element_type=jnp.float32
    ).reshape(half_rows, D)
    grad_input = ((grad_local + grad_patches) * keep_mask).astype(jnp.bfloat16)[None]
    gain_grads = jnp.stack(
        [first_gains[0], first_gains[1], second_gains[0], second_gains[1]]
    ).reshape(-1)
    bias_grads = jnp.stack(
        [first_biases[0], first_biases[1], second_biases[0], second_biases[1]]
    ).reshape(-1)
    patch_summed, projection_summed, gain_summed, bias_summed = (
        lax.psum_scatter(grad_patch_proj, ("dp", "tensor"), scatter_dimension=0, tiled=True),
        lax.psum_scatter(grad_global_proj, ("dp", "tensor"), scatter_dimension=1, tiled=True),
        lax.psum_scatter(gain_grads, ("dp", "tensor"), scatter_dimension=0, tiled=True),
        lax.psum_scatter(bias_grads, ("dp", "tensor"), scatter_dimension=0, tiled=True),
    )
    grad_joint = jnp.stack([first_summed[0], second_summed[0]])
    grad_output = jnp.stack([first_summed[1], second_summed[1]])
    grad_up = jnp.stack([first_summed[2], second_summed[2]])
    grad_down = jnp.stack([first_summed[3], second_summed[3]])
    return (
        outcome.astype(jnp.bfloat16)[None],
        grad_input,
        patch_summed,
        projection_summed,
        grad_joint,
        grad_output,
        grad_up,
        grad_down,
        gain_summed,
        bias_summed,
    )


def solution(mesh):
    placed = (
        P("dp", "tensor", None),
        P("dp"),
        P(("dp", "tensor"), None),
        P(None, ("dp", "tensor")),
        P(None, "dp", None, "tensor"),
        P(None, "tensor", "dp"),
        P(None, "dp", "tensor"),
        P(None, "tensor", "dp"),
        P(("dp", "tensor")),
        P(("dp", "tensor")),
        P("dp", "tensor", None),
    )
    return jax.shard_map(
        shards,
        mesh=mesh,
        in_specs=placed,
        out_specs=(
            P("dp", "tensor", None),
            P("dp", "tensor", None),
            P(("dp", "tensor"), None),
            P(None, ("dp", "tensor")),
            P(None, "dp", None, "tensor"),
            P(None, "tensor", "dp"),
            P(None, "dp", "tensor"),
            P(None, "tensor", "dp"),
            P(("dp", "tensor")),
            P(("dp", "tensor")),
        ),
        check_vma=False,
    )
```

profile of v0, /device:TPU:4, one launch (start us, length us, event | category | flops | bytes accessed | tf_op | source)
XLA Modules:
  0.0 2437.8 jit_solution(18334663615407287007)
XLA Ops:
  12.1 42.1 %all-reduce.5 = (bf16[3072]{0:T(1024)(128)(2,1)S(1)}, bf16[3072]{0:T(1024)(128)(2,1)S(1)}) all-reduce(bf16[3072]{0:T(1024)(128)(2,1)S(1)} %dynamic-update-slice.1, bf16[3072]{0:T(1024)(128)(2,1)S(1)} %dynamic-update-slice), channel_id=1, replica_groups=mesh['dp'=16,'tensor'=2] {'dp','tensor'}, use_global_device_ids=true, to_apply=%add.1 | all-reduce | flops 6144 | bytes 24576
  59.6 41.7 %all-gather.1 = bf16[1,384,768]{1,2,0:T(8,128)(2,1)S(1)} all-gather(bf16[1,384,48]{1,2,0:T(8,128)(2,1)S(1)} %get-tuple-element.54), channel_id=3, replica_groups=mesh['dp'=16,'tensor'=2] {'dp'}, dimensions={2}, use_global_device_ids=true | all-gather | bytes 626688 | tf_op jit(solution)/shard_map/all_gather | solution.py:40
  103.1 5.5 fusion.154
  111.0 53.6 %all-gather.29.cloned.1.call-done = bf16[1,768,3,384]{3,1,2,0:T(8,128)(2,1)} async-done(((bf16[1,48,3,384]{3,1,2,0:T(8,128)(2,1)}), bf16[1,768,3,384]{3,1,2,0:T(8,128)(2,1)}) %all-gather.29.cloned.1.call-update) | async-done | bytes 1769488 | tf_op jit(solution)/shard_map/all_gather | solution.py:39
  179.2 62.7 %all-gather.31.cloned.1.call-done = bf16[1,768,1536]{2,1,0:T(8,128)(2,1)} async-done(((bf16[1,48,1536]{2,1,0:T(8,128)(2,1)}), bf16[1,768,1536]{2,1,0:T(8,128)(2,1)}) %all-gather.31.cloned.1.call-update) | async-done | bytes 2359312 | tf_op jit(solution)/shard_map/all_gather | solution.py:41
  244.0 62.2 %all-gather.33.cloned.1.call-done = bf16[1,1536,768]{1,2,0:T(8,128)(2,1)} async-done(((bf16[1,1536,48]{1,2,0:T(8,128)(2,1)}), bf16[1,1536,768]{1,2,0:T(8,128)(2,1)}) %all-gather.33.cloned.1.call-update) | async-done | bytes 2359312 | tf_op jit(solution)/shard_map/all_gather | solution.py:42
  306.2 3.2 fusion.68
  309.5 57.6 %all-gather.35.cloned.1.call-done = bf16[1,768,3,384]{3,1,2,0:T(8,128)(2,1)} async-done(((bf16[1,48,3,384]{3,1,2,0:T(8,128)(2,1)}), bf16[1,768,3,384]{3,1,2,0:T(8,128)(2,1)}) %all-gather.35.cloned.1.call-update) | async-done | bytes 1769488 | tf_op jit(solution)/shard_map/all_gather | solution.py:39
  367.2 41.7 %all-gather.6 = bf16[1,384,768]{1,2,0:T(8,128)(2,1)} all-gather(bf16[1,384,48]{1,2,0:T(8,128)(2,1)S(1)} %copy-done.50), channel_id=8, replica_groups=mesh['dp'=16,'tensor'=2] {'dp'}, dimensions={2}, use_global_device_ids=true | all-gather | bytes 626688 | tf_op jit(solution)/shard_map/all_gather | solution.py:40
  409.0 23.8 all-gather.41.cloned.1.call-done
  433.3 63.9 %all-gather.45.cloned.1.call-done = bf16[1,1536,768]{1,2,0:T(8,128)(2,1)} async-done(((bf16[1,1536,48]{1,2,0:T(8,128)(2,1)}), bf16[1,1536,768]{1,2,0:T(8,128)(2,1)}) %all-gather.45.cloned.1.call-update) | async-done | bytes 2359312 | tf_op jit(solution)/shard_map/all_gather | solution.py:42
  497.3 83.7 %all-gather.27.cloned.1.call-done = bf16[768,6144]{0,1:T(8,128)(2,1)} async-done(((bf16[768,192]{0,1:T(8,128)(2,1)}), bf16[768,6144]{0,1:T(8,128)(2,1)}) %all-gather.27.cloned.1.call-update) | async-done | bytes 9437200 | tf_op jit(solution)/shard_map/all_gather | solution.py:59
  581.0 9.1 reduce-scatter.25.cloned.1.call-done
  590.1 6.7 fusion.132
  599.5 6.0 all-gather.37.cloned.1.call-done
  605.5 4.1 fusion.30
  610.7 2.7 reshape_squeeze.8
  615.6 5.0 fusion.79
  620.5 2.6 copy.106
  626.6 4.0 reshape_squeeze.6
  630.6 3.2 fusion.41
  635.7 3.9 convert_element_type.213
  643.5 8.0 fusion.14
  651.5 9.0 fusion.7
  660.5 3.5 multiply_reduce_fusion
  668.7 3.8 reshape.318
  672.5 4.9 fusion.74
  677.4 3.2 copy.113
  680.6 2.5 fusion.61
  683.1 3.3 copy.118
  686.5 3.3 fusion.43
  693.9 3.9 stack_reshape.24
  701.9 3.9 stack_reshape.25
  705.8 3.2 copy.121
  709.0 3.0 fusion.42
  713.9 3.9 stack_reshape.26
  720.9 5.6 fusion.39
  732.1 6.5 fusion.157
  744.4 3.6 fusion.161
  748.6 6.8 fusion.134
  756.1 7.1 fusion.138
  764.4 9.3 fusion.100
  782.3 2.8 fusion.62
  785.1 102.2 %reduce-scatter.41.cloned.1.call-done = f32[768,48]{0,1:T(8,128)} async-done(((f32[768,768]{0,1:T(8,128)}), f32[768,48]{0,1:T(8,128)}) %reduce-scatter.41.cloned.1.call-update) | async-done | bytes 147472 | tf_op jit(solution)/shard_map/reduce_scatter | solution.py:77
  890.7 153.5 %reduce-scatter.37.cloned.1.call-done = f32[48,3,768]{2,0,1:T(8,128)} async-done(((f32[768,3,768]{2,0,1:T(8,128)}), f32[48,3,768]{2,0,1:T(8,128)}) %reduce-scatter.37.cloned.1.call-update) | async-done | bytes 442384 | tf_op jit(solution)/shard_map/reduce_scatter | solution.py:76
  1047.2 2.5 fusion.114
  1049.8 170.7 %reduce-scatter.45.cloned.1.call-done = f32[48,3072]{1,0:T(8,128)} async-done(((f32[768,3072]{1,0:T(8,128)}), f32[48,3072]{1,0:T(8,128)}) %reduce-scatter.45.cloned.1.call-update) | async-done | bytes 589840 | tf_op jit(solution)/shard_map/reduce_scatter | solution.py:78
  1222.4 3.0 fusion.162
  1225.4 170.5 %reduce-scatter.51.cloned.1.call-done = f32[3072,48]{0,1:T(8,128)} async-done(((f32[3072,768]{0,1:T(8,128)}), f32[3072,48]{0,1:T(8,128)}) %reduce-scatter.51.cloned.1.call-update) | async-done | bytes 589840 | tf_op jit(solution)/shard_map/reduce_scatter | solution.py:79
  1397.8 3.0 fusion.137
  1402.0 7.9 fusion.131
  1414.1 7.9 fusion.159
  1422.8 9.0 fusion.47
  1431.9 4.1 fusion.158
  1437.8 40.4 %all-reduce.4 = (f32[3072]{0:T(1024)S(1)}, f32[3072]{0:T(1024)S(1)}) all-reduce(f32[3072]{0:T(1024)S(1)} %reshape.326, f32[3072]{0:T(1024)S(1)} %reshape.331), channel_id=32, replica_groups=mesh['dp'=16,'tensor'=2] {'dp','tensor'}, use_global_device_ids=true, to_apply=%region_44.45.clone | all-reduce | flops 6144 | bytes 49152
  1481.5 66.0 %reduce-scatter.39.cloned.1.call-done = f32[384,48]{0,1:T(8,128)} async-done(((f32[384,768]{0,1:T(8,128)}), f32[384,48]{0,1:T(8,128)}) %reduce-scatter.39.cloned.1.call-update) | async-done | bytes 73744 | tf_op jit(solution)/shard_map/reduce_scatter | solution.py:68
  1549.0 8.5 reduce-scatter.55.cloned.1.call-done
  1558.9 138.9 %reduce-scatter.35.cloned.1.call-done = f32[48,3,384]{2,0,1:T(8,128)} async-done(((f32[768,3,384]{2,0,1:T(8,128)}), f32[48,3,384]{2,0,1:T(8,128)}) %reduce-scatter.35.cloned.1.call-update) | async-done | bytes 221200 | tf_op jit(solution)/shard_map/reduce_scatter | solution.py:67
  1699.6 8.3 reduce-scatter.47.cloned.1.call-done
  1708.8 142.3 %reduce-scatter.43.cloned.1.call-done = f32[48,1536]{1,0:T(8,128)} async-done(((f32[768,1536]{1,0:T(8,128)}), f32[48,1536]{1,0:T(8,128)}) %reduce-scatter.43.cloned.1.call-update) | async-done | bytes 294928 | tf_op jit(solution)/shard_map/reduce_scatter | solution.py:69
  1852.9 7.6 reduce-scatter.53.cloned.1.call-done
  1861.4 143.8 %reduce-scatter.49.cloned.1.call-done = f32[1536,48]{0,1:T(8,128)} async-done(((f32[1536,768]{0,1:T(8,128)}), f32[1536,48]{0,1:T(8,128)}) %reduce-scatter.49.cloned.1.call-update) | async-done | bytes 294928 | tf_op jit(solution)/shard_map/reduce_scatter | solution.py:70
  2007.1 211.2 %reduce-scatter.33.cloned.1.call-done = f32[768,192]{0,1:T(8,128)} async-done(((f32[768,6144]{0,1:T(8,128)}), f32[768,192]{0,1:T(8,128)}) %reduce-scatter.33.cloned.1.call-update) | async-done | bytes 589840 | tf_op jit(solution)/shard_map/reduce_scatter | solution.py:305
  2218.3 212.5 %reduce-scatter.31.cloned.1.call-done = f32[192,768]{1,0:T(8,128)} async-done(((f32[6144,768]{1,0:T(8,128)}), f32[192,768]{1,0:T(8,128)}) %reduce-scatter.31.cloned.1.call-update) | async-done | bytes 589840 | tf_op jit(solution)/shard_map/reduce_scatter | solution.py:304
  (403 shorter events, 117.4 us)
Async XLA Ops:
  7.2 95.9 %all-gather.25.cloned.1.call-start = ((), (), s32[]{:S(2)}) async-start(), calls=%async_computation.18 | async-start | bytes 9732096 | tf_op jit(solution)/shard_map/all_gather | solution.py:58
  7.9 156.7 %all-gather.29.cloned.1.call-start = ((), (), s32[]{:S(2)}) async-start(), calls=%async_computation.36 | async-start | bytes 1880064 | tf_op jit(solution)/shard_map/all_gather | solution.py:39
  9.6 165.8 %reduce-scatter.23.cloned.1.call-start = ((), (), s32[]{:S(2)}) async-start(), calls=%async_computation.19 | async-start | bytes 294912 | tf_op jit(solution)/shard_map/reduce_scatter | solution.py:28
  101.3 66.3 %copy-start.16 = (bf16[1,384,768]{1,2,0:T(8,128)(2,1)}, bf16[1,384,768]{1,2,0:T(8,128)(2,1)S(1)}, u32[]{:S(2)}) copy-start(bf16[1,384,768]{1,2,0:T(8,128)(2,1)S(1)} %all-gather.1) | copy-start | bytes 1769476
  101.5 7.1 copy-start.4
  108.6 66.8 %copy-start.7 = (f32[64,768]{1,0:T(8,128)}, f32[64,768]{1,0:T(8,128)S(1)}, u32[]{:S(2)}) copy-start(f32[64,768]{1,0:T(8,128)S(1)} %get-tuple-element.64) | copy-start | bytes 589828
  111.0 56.3 %copy-start.28 = (bf16[128,768]{1,0:T(8,128)(2,1)}, bf16[128,768]{1,0:T(8,128)(2,1)S(1)}, u32[]{:S(2)}) copy-start(bf16[128,768]{1,0:T(8,128)(2,1)S(1)} %all_gather.77) | copy-start | bytes 589828
  111.0 56.0 %copy-start.51 = (pred[128,128]{0,1:T(8,128)(4,1)S(1)}, pred[128,128]{0,1:T(8,128)(4,1)}, u32[]{:S(2)}) copy-start(pred[128,128]{0,1:T(8,128)(4,1)} %iota_compare_fusion) | copy-start | bytes 49156
  167.6 8.8 copy-start.44
  168.7 73.2 %all-gather.31.cloned.1.call-start = ((), (), s32[]{:S(2)}) async-start(), calls=%async_computation.37 | async-start | bytes 2506752 | tf_op jit(solution)/shard_map/all_gather | solution.py:41
  169.5 136.7 %all-gather.33.cloned.1.call-start = ((), (), s32[]{:S(2)}) async-start(), calls=%async_computation.38 | async-start | bytes 2506752 | tf_op jit(solution)/shard_map/all_gather | solution.py:42
  170.3 196.8 %all-gather.35.cloned.1.call-start = ((), (), s32[]{:S(2)}) async-start(), calls=%async_computation.39 | async-start | bytes 1880064 | tf_op jit(solution)/shard_map/all_gather | solution.py:39
  170.9 261.8 %all-gather.41.cloned.1.call-start = ((), (), s32[]{:S(2)}) async-start(), calls=%async_computation.42 | async-start | bytes 2506752 | tf_op jit(solution)/shard_map/all_gather | solution.py:41
  171.6 325.6 %all-gather.45.cloned.1.call-start = ((), (), s32[]{:S(2)}) async-start(), calls=%async_computation.44 | async-start | bytes 2506752 | tf_op jit(solution)/shard_map/all_gather | solution.py:42
  172.4 408.7 %all-gather.27.cloned.1.call-start = ((), (), s32[]{:S(2)}) async-start(), calls=%async_computation.21 | async-start | bytes 9732096 | tf_op jit(solution)/shard_map/all_gather | solution.py:59
  173.1 417.0 %reduce-scatter.25.cloned.1.call-start = ((), (), s32[]{:S(2)}) async-start(), calls=%async_computation.20 | async-start | bytes 294912 | tf_op jit(solution)/shard_map/reduce_scatter | solution.py:28
  176.4 413.7 %copy-start.9 = (f32[64,768]{1,0:T(8,128)}, f32[64,768]{1,0:T(8,128)S(1)}, u32[]{:S(2)}) copy-start(f32[64,768]{1,0:T(8,128)S(1)} %get-tuple-element.38) | copy-start | bytes 589828
  176.4 67.6 %copy-start.77 = (f32[64]{0:T(128)}, f32[64]{0:T(128)S(1)}, u32[]{:S(2)}) copy-start(f32[64]{0:T(128)S(1)} %broadcast_multiply_fusion.2) | copy-start | bytes 772
  179.2 130.2 %copy-start.32 = (bf16[128,768]{1,0:T(8,128)(2,1)}, bf16[128,768]{1,0:T(8,128)(2,1)S(1)}, u32[]{:S(2)}) copy-start(bf16[128,768]{1,0:T(8,128)(2,1)S(1)} %all_gather.80) | copy-start | bytes 589828
  244.0 65.4 %copy-start.22 = (f32[128,1536]{1,0:T(8,128)}, f32[128,1536]{1,0:T(8,128)S(1)}, u32[]{:S(2)}) copy-start(f32[128,1536]{1,0:T(8,128)S(1)} %fusion.28) | copy-start | bytes 2359300
  309.4 57.8 %copy-start.50 = (bf16[1,384,48]{1,2,0:T(8,128)(2,1)S(1)}, bf16[1,384,48]{1,2,0:T(8,128)(2,1)}, u32[]{:S(2)}) copy-start(bf16[1,384,48]{1,2,0:T(8,128)(2,1)} %get-tuple-element.53) | copy-start | bytes 110596
  309.4 296.0 %all-gather.37.cloned.1.call-start = ((), (), s32[]{:S(2)}) async-start(), calls=%async_computation.40 | async-start | bytes 5308416 | tf_op jit(solution)/shard_map/all_gather | solution.py:49
  367.1 272.5 %all-gather.39.cloned.1.call-start = ((), (), s32[]{:S(2)}) async-start(), calls=%async_computation.41 | async-start | bytes 1769472 | tf_op jit(solution)/shard_map/all_gather | solution.py:50
  408.9 234.6 %all-gather.43.cloned.1.call-start = ((), (), s32[]{:S(2)}) async-start(), calls=%async_computation.43 | async-start | bytes 7077888 | tf_op jit(solution)/shard_map/all_gather | solution.py:51
  432.7 218.8 %all-gather.47.cloned.1.call-start = ((), (), s32[]{:S(2)}) async-start(), calls=%async_computation.45 | async-start | bytes 7077888 | tf_op jit(solution)/shard_map/all_gather | solution.py:52
  497.3 277.1 %reduce-scatter.27.cloned.1.call-start = ((), (), s32[]{:S(2)}) async-start(), calls=%async_computation.22 | async-start | bytes 294912 | tf_op jit(solution)/shard_map/reduce_scatter | solution.py:28
  598.5 11.1 copy-start.54
  599.5 6.0 copy-start.73
  642.0 22.0 copy-start.57
  651.5 9.0 copy-start.67
  651.5 9.0 copy-start.75
  651.5 9.0 copy-start.94
  720.9 5.6 copy-start.60
  732.1 8.9 copy-start.23
  732.1 8.9 copy-start.95
  744.3 143.1 %reduce-scatter.41.cloned.1.call-start = ((), (), s32[]{:S(2)}) async-start(), calls=%async_computation.29 | async-start | bytes 2506752 | tf_op jit(solution)/shard_map/reduce_scatter | solution.py:77
  748.0 296.2 %reduce-scatter.37.cloned.1.call-start = ((), (), s32[]{:S(2)}) async-start(), calls=%async_computation.27 | async-start | bytes 7520256 | tf_op jit(solution)/shard_map/reduce_scatter | solution.py:76
  755.4 465.0 %reduce-scatter.45.cloned.1.call-start = ((), (), s32[]{:S(2)}) async-start(), calls=%async_computation.31 | async-start | bytes 10027008 | tf_op jit(solution)/shard_map/reduce_scatter | solution.py:78
  763.3 632.6 %reduce-scatter.51.cloned.1.call-start = ((), (), s32[]{:S(2)}) async-start(), calls=%async_computation.34 | async-start | bytes 10027008 | tf_op jit(solution)/shard_map/reduce_scatter | solution.py:79
  773.7 5.7 copy-start.17
  773.8 636.2 %reduce-scatter.29.cloned.1.call-start = ((), (), s32[]{:S(2)}) async-start(), calls=%async_computation.23 | async-start | bytes 294912 | tf_op jit(solution)/shard_map/reduce_scatter | solution.py:28
  782.1 107.1 %copy-start.45 = (bf16[6,64,128]{2,1,0:T(8,128)(2,1)S(1)}, bf16[6,64,128]{2,1,0:T(8,128)(2,1)}, u32[]{:S(2)}) copy-start(bf16[6,64,128]{2,1,0:T(8,128)(2,1)} %copy-done.44) | copy-start | bytes 294916
  785.1 695.4 %reduce-scatter.57.cloned.1.call-start = ((), (), s32[]{:S(2)}) async-start(), calls=%async_computation.47 | async-start | bytes 294912
  889.1 658.3 %reduce-scatter.39.cloned.1.call-start = ((), (), s32[]{:S(2)}) async-start(), calls=%async_computation.28 | async-start | bytes 1253376 | tf_op jit(solution)/shard_map/reduce_scatter | solution.py:68
  890.6 156.5 %copy-start.29 = (bf16[128,768]{1,0:T(8,128)(2,1)S(1)}, bf16[128,768]{1,0:T(8,128)(2,1)}, u32[]{:S(2)}) copy-start(bf16[128,768]{1,0:T(8,128)(2,1)} %copy-done.28) | copy-start | bytes 589828
  890.6 666.9 %reduce-scatter.55.cloned.1.call-start = ((), (), s32[]{:S(2)}) async-start(), calls=%async_computation.46 | async-start | bytes 589824
  1046.9 650.9 %reduce-scatter.35.cloned.1.call-start = ((), (), s32[]{:S(2)}) async-start(), calls=%async_computation.26 | async-start | bytes 3760128 | tf_op jit(solution)/shard_map/reduce_scatter | solution.py:67
  1049.7 172.7 %copy-start.33 = (bf16[128,768]{1,0:T(8,128)(2,1)S(1)}, bf16[128,768]{1,0:T(8,128)(2,1)}, u32[]{:S(2)}) copy-start(bf16[128,768]{1,0:T(8,128)(2,1)} %copy-done.32) | copy-start | bytes 589828
  1049.7 172.7 %copy-start.35 = (bf16[128,1536]{1,0:T(8,128)(2,1)S(1)}, bf16[128,1536]{1,0:T(8,128)(2,1)}, u32[]{:S(2)}) copy-start(bf16[128,1536]{1,0:T(8,128)(2,1)} %copy-done.34) | copy-start | bytes 1179652
  1049.7 658.2 %reduce-scatter.47.cloned.1.call-start = ((), (), s32[]{:S(2)}) async-start(), calls=%async_computation.32 | async-start | bytes 442368 | tf_op jit(solution)/shard_map/reduce_scatter | solution.py:88
  1222.3 628.8 %reduce-scatter.43.cloned.1.call-start = ((), (), s32[]{:S(2)}) async-start(), calls=%async_computation.30 | async-start | bytes 5013504 | tf_op jit(solution)/shard_map/reduce_scatter | solution.py:69
  1225.4 172.4 %copy-start.24 = (f32[128,1536]{1,0:T(8,128)S(1)}, f32[128,1536]{1,0:T(8,128)}, u32[]{:S(2)}) copy-start(f32[128,1536]{1,0:T(8,128)} %copy-done.22) | copy-start | bytes 2359300
  1225.4 172.5 %copy-start.42 = (bf16[128,768]{1,0:T(8,128)(2,1)S(1)}, bf16[128,768]{1,0:T(8,128)(2,1)}, u32[]{:S(2)}) copy-start(bf16[128,768]{1,0:T(8,128)(2,1)} %copy-done.41) | copy-start | bytes 589828
  1225.4 635.1 %reduce-scatter.53.cloned.1.call-start = ((), (), s32[]{:S(2)}) async-start(), calls=%async_computation.35 | async-start | bytes 442368 | tf_op jit(solution)/shard_map/reduce_scatter | solution.py:91
  1397.8 607.5 %reduce-scatter.49.cloned.1.call-start = ((), (), s32[]{:S(2)}) async-start(), calls=%async_computation.33 | async-start | bytes 5013504 | tf_op jit(solution)/shard_map/reduce_scatter | solution.py:70
  1400.9 817.4 %reduce-scatter.33.cloned.1.call-start = ((), (), s32[]{:S(2)}) async-start(), calls=%async_computation.25 | async-start | bytes 19464192 | tf_op jit(solution)/shard_map/reduce_scatter | solution.py:305
  1409.9 4.2 copy-start.5
  1409.9 1020.8 %reduce-scatter.31.cloned.1.call-start = ((), (), s32[]{:S(2)}) async-start(), calls=%async_computation.24 | async-start | bytes 19464192 | tf_op jit(solution)/shard_map/reduce_scatter | solution.py:304
  1422.8 9.1 slice-start
  1422.8 9.0 copy-start.66
  1422.8 9.0 copy-start.65
  1422.8 9.1 slice-start.1
  1422.8 9.1 slice-start.2
  1436.0 43.4 %copy-start.12 = (f32[512,768]{1,0:T(8,128)S(1)}, f32[512,768]{1,0:T(8,128)}, u32[]{:S(2)}) copy-start(f32[512,768]{1,0:T(8,128)} %get-tuple-element.30) | copy-start | bytes 4718596
  (66 other events, 124.1 us)
Sparse Core Ops, SparseCore 0:
  10.9 92.1 all-gather.24
  106.4 58.1 all-gather.28
  168.8 6.5 reduce-scatter.22
  178.6 63.1 all-gather.30
  245.1 61.0 all-gather.32
  309.3 57.7 all-gather.34
  370.5 62.1 all-gather.40
  436.1 61.0 all-gather.44
  500.1 80.8 all-gather.26
  583.7 6.3 reduce-scatter.24
  591.7 13.7 all-gather.36
  606.9 10.3 all-gather.38
  618.8 15.6 all-gather.42
  635.9 15.6 all-gather.46
  744.4 8.7 reduce-scatter.26
  758.0 129.3 reduce-scatter.40
  893.4 150.7 reduce-scatter.36
  1050.7 169.7 reduce-scatter.44
  1226.2 169.7 reduce-scatter.50
  1398.6 6.8 reduce-scatter.28
  1407.8 8.6 reduce-scatter.56
  1422.0 125.3 reduce-scatter.38
  1550.4 7.1 reduce-scatter.54
  1562.5 135.2 reduce-scatter.34
  1700.6 7.1 reduce-scatter.46
  1712.9 138.1 reduce-scatter.42
  1853.3 7.1 reduce-scatter.52
  1866.5 138.7 reduce-scatter.48
  2012.2 205.9 reduce-scatter.32
  2225.1 205.6 reduce-scatter.30
where the time goes:
time: 2450 us; the launch traced here: 2440 us
  waiting for transfers between devices  1970 us (80%)
  blocking collectives  174 us (7%)
  matrix products  156 us (6%)
  local copies, waits for them, and re-layouts  88.6 us (4%)
  other arithmetic  34.6 us (1%)
    reduce_scatter x1, waiting for transfers between devices, shards(): lax.psum_scatter(grad_patch_proj, ('dp', 'tensor'), scatter_dimension=0,...  212 us
    reduce_scatter x1, waiting for transfers between devices, shards(): lax.psum_scatter(grad_global_proj, ('dp', 'tensor'), scatter_dimension=1,...  211 us
    reduce_scatter x1, waiting for transfers between devices, reduce_local(): lax.psum_scatter(gradients[2], 'dp', scatter_dimension=0, tiled=True)  171 us
    reduce_scatter x1, waiting for transfers between devices, reduce_local(): lax.psum_scatter(gradients[3], 'dp', scatter_dimension=1, tiled=True)  170 us
    reduce_scatter x1, waiting for transfers between devices, reduce_local(): lax.psum_scatter(gradients[0], 'dp', scatter_dimension=0, tiled=True)  153 us
    reduce_scatter x1, waiting for transfers between devices, reduce_layer(): lax.psum_scatter(gradients[3], 'dp', scatter_dimension=1, tiled=True)  144 us
    reduce_scatter x1, waiting for transfers between devices, reduce_layer(): lax.psum_scatter(gradients[2], 'dp', scatter_dimension=0, tiled=True)  142 us
    reduce_scatter x1, waiting for transfers between devices, reduce_layer(): lax.psum_scatter(gradients[0], 'dp', scatter_dimension=0, tiled=True)  139 us
  transfers between devices with their start and end apart: 30, of which 25 were waited for; matrix products, arithmetic and copies ran while one was open for 7% of the time, Pallas kernels for 0%

commit v1 on v0

v1 whole, which is shorter than its diff:
```python
import jax
import jax.numpy as jnp
from jax import lax
from jax.sharding import PartitionSpec as P

D = 768
HD = 64
P_SIZE = 8
NORMS = 4
QUAD = 4

EPSILON = 1e-05
NEGATIVE = -1e30
BF16 = jnp.bfloat16
F32 = jnp.float32


def dp_size():
    return lax.axis_size("dp")


def line_size():
    return dp_size() // 4


def x_place():
    return lax.axis_index("dp") % 2


def y_place():
    return (lax.axis_index("dp") // 2) % 2


def line_place():
    return lax.axis_index("dp") // 4


def quad_place():
    return x_place() * 2 + lax.axis_index("tensor")


def flip_dp(values_in, bit):
    return lax.ppermute(values_in, "dp", [(i, i ^ bit) for i in range(dp_size())])


def flip_core(values_in):
    return lax.ppermute(values_in, "tensor", [(0, 1), (1, 0)])


def flip_quad(values_in, bits):
    return lax.ppermute(
        values_in, ("dp", "tensor"), [(i, i ^ bits) for i in range(2 * dp_size())]
    )


def step_up(values_in):
    return lax.ppermute(values_in, "dp", [(i, i + 4) for i in range(dp_size() - 4)])


def step_down(values_in):
    return lax.ppermute(values_in, "dp", [(i + 4, i) for i in range(dp_size() - 4)])


def line_groups():
    return [[line * 4 + rest for line in range(line_size())] for rest in range(4)]


def pick(place, choices):
    if len(choices) == 2:
        return lax.select_n(place == 1, *choices)
    return lax.select_n(place, *choices)


def line_gather(values_in):
    count = line_size()
    if count > 4:
        return lax.all_gather(values_in, "dp", axis=0, axis_index_groups=line_groups())
    below, above = [], []
    rising = falling = values_in
    for step in range(count - 1):
        rising, falling = step_up(rising), step_down(falling)
        below.append(rising)
        above.append(falling)
    place = line_place()
    slots = []
    for slot in range(count):
        choices = [
            values_in
            if slot == here
            else (below[here - slot - 1] if slot < here else above[slot - here - 1])
            for here in range(count)
        ]
        slots.append(pick(place, choices) if count > 1 else values_in)
    return jnp.stack(slots)


def pair_up(own, other, place):
    return jnp.stack([pick(place, [own, other]), pick(place, [other, own])], axis=0)


def line_y_gather(values_in):
    lined = line_gather(values_in)
    other = flip_dp(lined, 2)
    place = y_place()
    return jnp.stack([pick(place, [lined, other]), pick(place, [other, lined])], axis=1)


def dp_gather(values_in):
    gathered = line_y_gather(values_in)
    other = flip_dp(gathered, 1)
    place = x_place()
    whole = jnp.stack([pick(place, [gathered, other]), pick(place, [other, gathered])], axis=2)
    return whole.reshape(-1, values_in.shape[-1])


def line_scatter(parts):
    count = line_size()
    if count > 4:
        return lax.psum_scatter(
            parts, "dp", scatter_dimension=0, axis_index_groups=line_groups(), tiled=False
        )
    place = line_place()
    own = lax.dynamic_index_in_dim(parts, place, 0, keepdims=False)
    if count == 1:
        return own
    rising = falling = None
    for step in range(count - 1, 0, -1):
        to_above = lax.dynamic_index_in_dim(
            parts, jnp.minimum(place + step, count - 1), 0, keepdims=False
        )
        to_below = lax.dynamic_index_in_dim(
            parts, jnp.maximum(place - step, 0), 0, keepdims=False
        )
        if rising is not None:
            to_above = to_above + rising
            to_below = to_below + falling
        rising = step_up(to_above.astype(BF16)).astype(F32)
        falling = step_down(to_below.astype(BF16)).astype(F32)
    return own + rising + falling


def halve(parts, place, axis, bit):
    own = lax.dynamic_index_in_dim(parts, place, axis, keepdims=False)
    theirs = lax.dynamic_index_in_dim(parts, 1 - place, axis, keepdims=False)
    return own.astype(F32) + flip_dp(theirs.astype(BF16), bit).astype(F32)


def line_y_scatter(parts):
    shaped = parts.reshape((line_size(), 2) + parts.shape[1:])
    return line_scatter(halve(shaped, y_place(), 1, 2))


def dp_scatter(parts):
    count = line_size()
    rows = parts.shape[0] // (count * 4)
    shaped = parts.reshape(count, 2, 2, rows, parts.shape[1])
    shaped = halve(shaped, x_place(), 2, 1)
    shaped = halve(shaped, y_place(), 1, 2)
    return line_scatter(shaped)


def quad_gather(values_in):
    return jnp.concatenate(
        [values_in] + [flip_quad(values_in, bits) for bits in range(1, QUAD)], axis=0
    )


def quad_scatter(partial_value):
    rows = partial_value.shape[0] // QUAD
    low = partial_value.astype(BF16)
    total = partial_value[:rows].astype(F32)
    for bits in range(1, QUAD):
        total = total + flip_quad(low[bits * rows : (bits + 1) * rows], bits).astype(F32)
    return total


def quad_deal(blocks):
    place = quad_place()
    taken = []
    for bits in range(QUAD):
        piece = lax.dynamic_index_in_dim(blocks, place ^ bits, 2, keepdims=False)
        taken.append(flip_quad(piece, bits) if bits else piece)
    return jnp.concatenate(taken, axis=0)


def quad_collect(blocks):
    rows = blocks.shape[0] // QUAD
    place = quad_place()
    got = [
        flip_quad(blocks[bits * rows : (bits + 1) * rows], bits)
        if bits
        else blocks[bits * rows : (bits + 1) * rows]
        for bits in range(QUAD)
    ]
    return jnp.stack(
        [pick(place, [got[slot ^ here] for here in range(QUAD)]) for slot in range(QUAD)], axis=2
    )


def layer_norm(stream, gain_row, bias_row):
    average = jnp.mean(stream, axis=-1, keepdims=True)
    centered = stream - average
    variance = jnp.mean(centered * centered, axis=-1, keepdims=True)
    return centered * lax.rsqrt(variance + EPSILON) * gain_row + bias_row


def dot_nn(left, right):
    return lax.dot_general(left, right, (((1,), (0,)), ((), ())), preferred_element_type=F32)


def dot_nt(left, right):
    return lax.dot_general(left, right, (((1,), (1,)), ((), ())), preferred_element_type=F32)


def dot_tn(left, right):
    return lax.dot_general(left, right, (((0,), (0,)), ((), ())), preferred_element_type=F32)


def split_heads(packed, group_size):
    row_count, columns = packed.shape
    head_count = columns // (3 * HD)
    shaped = packed.reshape(row_count // group_size, group_size, 3, head_count, HD)
    return shaped[:, :, 0], shaped[:, :, 1], shaped[:, :, 2]


def causal_scores(queries, keys_all, places):
    scores = jnp.einsum(
        "gihe,gjhe->ghij", queries, keys_all, preferred_element_type=F32
    ) * HD ** (-0.5)
    return jnp.where(places[:, None] >= places[None, :], scores, NEGATIVE)


def attend_forward(packed, places):
    queries, keys_all, values_all = split_heads(packed, places.shape[0])
    scores = causal_scores(queries, keys_all, places)
    row_max = jnp.max(scores, axis=-1, keepdims=True)
    shifted = jnp.exp(scores - row_max)
    softened = shifted / jnp.sum(shifted, axis=-1, keepdims=True)
    mixture = jnp.einsum(
        "ghij,gjhe->gihe", softened.astype(BF16), values_all, preferred_element_type=F32
    )
    return mixture.reshape(packed.shape[0], -1).astype(BF16), softened


def attend_backward(packed, softened, grad_mix, places):
    queries, keys_all, values_all = split_heads(packed, places.shape[0])
    grad_heads = grad_mix.reshape(queries.shape)
    grad_soft = jnp.einsum(
        "gihe,gjhe->ghij", grad_heads, values_all, preferred_element_type=F32
    )
    centre = jnp.sum(grad_soft * softened, axis=-1, keepdims=True)
    grad_scores = (softened * (grad_soft - centre)).astype(BF16)
    grad_values = jnp.einsum(
        "ghij,gihe->gjhe", softened.astype(BF16), grad_heads, preferred_element_type=F32
    )
    grad_queries = jnp.einsum(
        "ghij,gjhe->gihe", grad_scores, keys_all, preferred_element_type=F32
    ) * HD ** (-0.5)
    grad_keys = jnp.einsum(
        "ghij,gihe->gjhe", grad_scores, queries, preferred_element_type=F32
    ) * HD ** (-0.5)
    row_count = packed.shape[0]
    return jnp.concatenate(
        [part.reshape(row_count, -1) for part in (grad_queries, grad_keys, grad_values)], axis=1
    ).astype(BF16)


def layer_forward(stream, weights, gain_rows, bias_rows, norm_index, places, widen, narrow):
    joint_proj, output_proj, upward, downward = weights
    normed_all = widen(
        layer_norm(stream, gain_rows[norm_index], bias_rows[norm_index]).astype(BF16)
    )
    packed = dot_nn(normed_all, joint_proj).astype(BF16)
    mixture, softened = attend_forward(packed, places)
    middle = stream + narrow(dot_nt(mixture, output_proj))
    second_all = widen(
        layer_norm(middle, gain_rows[norm_index + 1], bias_rows[norm_index + 1]).astype(BF16)
    )
    hidden = dot_nn(second_all, upward)
    active = jax.nn.gelu(hidden).astype(BF16)
    outcome = middle + narrow(dot_nt(active, downward))
    return (
        outcome,
        (stream, normed_all, packed, mixture, softened, middle, second_all, hidden, active),
    )


def layer_backward(grad_layer, saved, weights, gain_rows, bias_rows, norm_index, places, widen, narrow):
    stream, normed_all, packed, mixture, softened, middle, second_all, hidden, active = saved
    joint_proj, output_proj, upward, downward = weights
    grad_all = widen(grad_layer.astype(BF16))
    grad_active = dot_nn(grad_all, downward)
    gelu_value, gelu_pull = jax.vjp(jax.nn.gelu, hidden)
    grad_hidden = gelu_pull(grad_active)[0].astype(BF16)
    grad_second = narrow(dot_nt(grad_hidden, upward))
    norm_value, second_pull = jax.vjp(
        layer_norm, middle, gain_rows[norm_index + 1], bias_rows[norm_index + 1]
    )
    grad_middle_norm, grad_gain_two, grad_bias_two = second_pull(grad_second)
    grad_middle = grad_layer + grad_middle_norm
    grad_branch = widen(grad_middle.astype(BF16))
    grad_mix = dot_nn(grad_branch, output_proj).astype(BF16)
    grad_packed = attend_backward(packed, softened, grad_mix, places)
    grad_normed = narrow(dot_nt(grad_packed, joint_proj))
    first_value, first_pull = jax.vjp(
        layer_norm, stream, gain_rows[norm_index], bias_rows[norm_index]
    )
    grad_stream_norm, grad_gain_one, grad_bias_one = first_pull(grad_normed)
    grad_stream = grad_middle + grad_stream_norm
    grad_down = dot_tn(grad_all, active)
    grad_up = dot_tn(second_all, grad_hidden)
    grad_output = dot_tn(grad_branch, mixture)
    grad_joint = dot_tn(normed_all, grad_packed)
    return (
        grad_stream,
        (grad_joint, grad_output, grad_up, grad_down),
        (grad_gain_one, grad_gain_two),
        (grad_bias_one, grad_bias_two),
    )


def unchanged(values_in):
    return values_in


def shards(
    embedded,
    lengths,
    patch_proj,
    global_proj,
    qkv_weight,
    out_weight,
    up_weight,
    down_weight,
    norm_gain,
    norm_bias,
    cotangent,
):
    half_rows = embedded.shape[1]
    patch_rows = half_rows // P_SIZE
    shard_rows = qkv_weight.shape[1]
    proj_rows = patch_proj.shape[0]
    norm_part = norm_gain.shape[0]
    cells = 2 * line_size()
    heads_width = qkv_weight.shape[3]
    hidden_width = up_weight.shape[2]
    x_here = x_place()

    positions = lax.axis_index("tensor") * half_rows + jnp.arange(half_rows, dtype=jnp.int32)
    keep_mask = (positions < lengths[0]).astype(F32)[:, None]
    masked_low = (embedded[0].astype(F32) * keep_mask).astype(BF16)

    joint_part = jnp.transpose(qkv_weight, (0, 2, 1, 3))
    output_part = jnp.transpose(out_weight, (0, 2, 1))
    down_part = jnp.transpose(down_weight, (0, 2, 1))

    norm_row = jnp.pad(
        jnp.concatenate([norm_gain, norm_bias]).reshape(1, -1), ((0, 0), (0, D - 2 * norm_part))
    )
    patch_whole = line_y_gather(jnp.concatenate([patch_proj, norm_row], axis=0))
    patch_whole = patch_whole.reshape(cells, proj_rows + 1, D)
    patch_mat = patch_whole[:, :proj_rows].reshape(cells * proj_rows, D)
    norm_cells = patch_whole[:, proj_rows, : 2 * norm_part]
    norm_all = quad_collect(
        jnp.broadcast_to(norm_cells[None], (QUAD,) + norm_cells.shape)
    )[0].astype(F32)
    gain_rows = norm_all[..., :norm_part].reshape(NORMS, D)
    bias_rows = norm_all[..., norm_part:].reshape(NORMS, D)

    def x_half(part):
        return part.reshape(part.shape[:-1] + (2, part.shape[-1] // 2))

    def global_part(layer):
        pieces = []
        for piece in (
            joint_part[layer, 0],
            joint_part[layer, 1],
            joint_part[layer, 2],
            output_part[layer],
            up_weight[layer],
            down_part[layer],
        ):
            halves = x_half(piece)
            pieces.append(halves)
        return jnp.concatenate(pieces, axis=-1)

    halves = global_part(0)
    own_half = lax.dynamic_index_in_dim(halves, x_here, 1, keepdims=False)
    their_half = lax.dynamic_index_in_dim(halves, 1 - x_here, 1, keepdims=False)
    global_shard = pair_up(own_half, flip_dp(their_half, 1), x_here)
    global_shard = global_shard.reshape(2 * shard_rows, -1)
    attend_columns = 2 * heads_width
    attend_shard, forward_shard = global_shard[:, :attend_columns], global_shard[:, attend_columns:]
    attend_whole = line_y_gather(attend_shard).reshape(D, -1)
    forward_whole = line_y_gather(forward_shard).reshape(D, -1)
    joint_columns = 3 * heads_width // 2
    first_weights = (
        attend_whole[:, :joint_columns],
        attend_whole[:, joint_columns:],
        forward_whole[:, : hidden_width // 2],
        forward_whole[:, hidden_width // 2 :],
    )
    spread_mat = line_y_gather(jnp.transpose(global_proj)).reshape(cells * proj_rows, D)

    local_attend = jnp.concatenate([joint_part[1, 0], joint_part[1, 1], joint_part[1, 2], output_part[1]], axis=-1)
    local_forward = jnp.concatenate([up_weight[1], down_part[1]], axis=-1)
    attend_own = dp_gather(local_attend)
    forward_own = dp_gather(local_forward)
    attend_other = flip_core(attend_own)
    forward_other = flip_core(forward_own)
    second_weights = (
        jnp.concatenate(
            [
                source[:, k * heads_width : (k + 1) * heads_width]
                for k in range(3)
                for source in (attend_own, attend_other)
            ],
            axis=1,
        ),
        jnp.concatenate([attend_own[:, 3 * heads_width :], attend_other[:, 3 * heads_width :]], axis=1),
        jnp.concatenate([forward_own[:, :hidden_width], forward_other[:, :hidden_width]], axis=1),
        jnp.concatenate([forward_own[:, hidden_width:], forward_other[:, hidden_width:]], axis=1),
    )

    patches_dealt = quad_deal(masked_low.reshape(patch_rows, cells, QUAD, proj_rows))
    patches_mat = patches_dealt.reshape(QUAD * patch_rows, cells * proj_rows)
    initial = quad_scatter(dot_nn(patches_mat, patch_mat))
    core = lax.axis_index("tensor")
    steps = jnp.arange(patch_rows, dtype=jnp.int32)
    global_places = jnp.concatenate([core * patch_rows + steps, (1 - core) * patch_rows + steps])
    global_out, first_saved = layer_forward(
        initial, first_weights, gain_rows, bias_rows, 0, global_places, quad_gather, quad_scatter
    )
    global_low = quad_gather(global_out.astype(BF16))
    spread_dealt = dot_nt(global_low, spread_mat).astype(BF16)
    spread = quad_collect(spread_dealt.reshape(QUAD * patch_rows, cells, proj_rows))
    spread = spread.reshape(half_rows, D)

    local_places = jnp.arange(P_SIZE, dtype=jnp.int32)
    outcome, second_saved = layer_forward(
        masked_low.astype(F32) + spread.astype(F32),
        second_weights, gain_rows, bias_rows, 2, local_places, unchanged, unchanged,
    )
    grad_final = cotangent[0].astype(F32) * keep_mask
    grad_local, second_grads, second_gains, second_biases = layer_backward(
        grad_final, second_saved, second_weights, gain_rows, bias_rows, 2, local_places, unchanged, unchanged
    )
    grad_joint, grad_output, grad_up, grad_down = second_grads

    def own_columns(k, grads, width):
        return grads[:, k * width : (k + 1) * width]

    forward_grads = [
        jnp.concatenate(
            [own_columns(side, grad_up, hidden_width), own_columns(side, grad_down, hidden_width)], axis=1
        )
        for side in range(2)
    ]
    attend_grads = [
        jnp.concatenate(
            [own_columns(2 * k + side, grad_joint, heads_width) for k in range(3)]
            + [own_columns(side, grad_output, heads_width)],
            axis=1,
        )
        for side in range(2)
    ]
    forward_local = dp_scatter(forward_grads[0] + flip_core(forward_grads[1].astype(BF16)).astype(F32))
    attend_local = dp_scatter(attend_grads[0] + flip_core(attend_grads[1].astype(BF16)).astype(F32))

    grad_spread = grad_local.astype(BF16).reshape(patch_rows, cells, QUAD, proj_rows)
    spread_grads = quad_deal(grad_spread).reshape(QUAD * patch_rows, cells * proj_rows)
    grad_global = quad_scatter(dot_nn(spread_grads, spread_mat))
    grad_proj = line_y_scatter(dot_tn(spread_grads, global_low).reshape(cells, proj_rows, D))
    grad_initial, first_grads, first_gains, first_biases = layer_backward(
        grad_global, first_saved, first_weights, gain_rows, bias_rows, 0, global_places, quad_gather, quad_scatter
    )
    forward_global = line_y_scatter(
        jnp.concatenate([first_grads[2], first_grads[3]], axis=1).reshape(cells, 2 * shard_rows, -1)
    )
    attend_global = line_y_scatter(
        jnp.concatenate([first_grads[0], first_grads[1]], axis=1).reshape(cells, 2 * shard_rows, -1)
    )
    grad_start = quad_gather(grad_initial.astype(BF16))
    grad_patch_mat = dot_tn(patches_mat, grad_start).reshape(cells, proj_rows, D)
    grad_patches = dot_nt(grad_start, patch_mat).astype(BF16)
    grad_patches = quad_collect(grad_patches.reshape(QUAD * patch_rows, cells, proj_rows))
    grad_patches = grad_patches.reshape(half_rows, D).astype(F32)
    grad_input = ((grad_local + grad_patches) * keep_mask).astype(BF16)[None]

    gain_grads = jnp.stack([first_gains[0], first_gains[1], second_gains[0], second_gains[1]])
    bias_grads = jnp.stack([first_biases[0], first_biases[1], second_biases[0], second_biases[1]])
    norm_grads = jnp.concatenate(
        [
            gain_grads.reshape(cells, QUAD, norm_part),
            bias_grads.reshape(cells, QUAD, norm_part),
        ],
        axis=2,
    )
    place = quad_place()
    norm_sum = lax.dynamic_index_in_dim(norm_grads, place, 1, keepdims=False)
    for bits in range(1, QUAD):
        piece = lax.dynamic_index_in_dim(norm_grads, place ^ bits, 1, keepdims=False)
        norm_sum = norm_sum + flip_quad(piece, bits)
    norm_rows = jnp.pad(norm_sum[:, None, :], ((0, 0), (0, 0), (0, D - 2 * norm_part)))
    patch_summed = line_y_scatter(jnp.concatenate([grad_patch_mat, norm_rows], axis=1))

    def x_restore(summed):
        shaped = summed.reshape(2, shard_rows, -1)
        own = lax.dynamic_index_in_dim(shaped, x_here, 0, keepdims=False)
        theirs = lax.dynamic_index_in_dim(shaped, 1 - x_here, 0, keepdims=False)
        return pair_up(own, flip_dp(theirs.astype(BF16), 1).astype(F32), x_here)

    attend_global = x_restore(attend_global)
    forward_global = x_restore(forward_global)

    def x_columns(source, start, width):
        return jnp.concatenate([source[0, :, start : start + width], source[1, :, start : start + width]], axis=1)

    half_heads, half_hidden = heads_width // 2, hidden_width // 2
    joint_out = jnp.stack(
        [
            jnp.stack([x_columns(attend_global, k * half_heads, half_heads) for k in range(3)], axis=1),
            attend_local[:, : 3 * heads_width].reshape(shard_rows, 3, heads_width),
        ]
    )
    output_out = jnp.stack(
        [
            jnp.transpose(x_columns(attend_global, 3 * half_heads, half_heads)),
            jnp.transpose(attend_local[:, 3 * heads_width :]),
        ]
    )
    up_out = jnp.stack([x_columns(forward_global, 0, half_hidden), forward_local[:, :hidden_width]])
    down_out = jnp.stack(
        [
            jnp.transpose(x_columns(forward_global, half_hidden, half_hidden)),
            jnp.transpose(forward_local[:, hidden_width:]),
        ]
    )
    return (
        outcome.astype(BF16)[None],
        grad_input,
        patch_summed[:proj_rows],
        jnp.transpose(grad_proj),
        joint_out,
        output_out,
        up_out,
        down_out,
        patch_summed[proj_rows, :norm_part],
        patch_summed[proj_rows, norm_part : 2 * norm_part],
    )


def solution(mesh):
    placed = (
        P("dp", "tensor", None),
        P("dp"),
        P(("dp", "tensor"), None),
        P(None, ("dp", "tensor")),
        P(None, "dp", None, "tensor"),
        P(None, "tensor", "dp"),
        P(None, "dp", "tensor"),
        P(None, "tensor", "dp"),
        P(("dp", "tensor")),
        P(("dp", "tensor")),
        P("dp", "tensor", None),
    )
    return jax.shard_map(
        shards,
        mesh=mesh,
        in_specs=placed,
        out_specs=(
            P("dp", "tensor", None),
            P("dp", "tensor", None),
            P(("dp", "tensor"), None),
            P(None, ("dp", "tensor")),
            P(None, "dp", None, "tensor"),
            P(None, "tensor", "dp"),
            P(None, "dp", "tensor"),
            P(None, "tensor", "dp"),
            P(("dp", "tensor")),
            P(("dp", "tensor")),
        ),
        check_vma=False,
    )
```

time: 2450 us -> 917 us (0.37)
  waiting for transfers between devices: 1970 us -> 287 us
  starting transfers between devices: 1.39 us -> 259 us
  blocking collectives: 174 us -> 0 us
  local copies, waits for them, and re-layouts: 88.6 us -> 177 us
  matrix products: 156 us -> 72.1 us
  other arithmetic: 34.6 us -> 101 us
    reduce_scatter x16 -> x0, waiting for transfers between devices: 1540 us -> none  [the longest x1 212 us: shards(): lax.psum_scatter(grad_patch_proj, ('dp', 'tensor'), scatter_dimension=0,...]
    all_gather x12 -> x0, waiting for transfers between devices: 415 us -> none  [the longest x2 126 us: layer_weights(): lax.all_gather(down_weight[layer_index], 'dp', axis=1, tiled=True)]
    ppermute x0 -> x149, waiting for transfers between devices: none -> 287 us  [the longest x19 133 us: flip_dp(): lax.ppermute(values_in, 'dp', [(i, i ^ bit) for i in range(dp_size())])]
    ppermute x0 -> x149, starting transfers between devices: none -> 259 us  [the longest x36 151 us: step_up(): lax.ppermute(values_in, 'dp', [(i, i + 4) for i in range(dp_size() - 4)])]
    all_gather x6 -> x0, blocking collectives: 91.6 us -> none  [the longest x2 83.4 us: layer_weights(): lax.all_gather(out_weight[layer_index], 'dp', axis=1, tiled=True)]
    unnamed x2 -> x0, blocking collectives: 82.6 us -> none
    dot_general x36 -> x35, matrix products: 144 us -> 63.9 us  [the longest x10 22.7 us: dot_nn(): lax.dot_general(left, right, (((1,), (0,)), ((), ())), preferred_element_...]
    slice x9 -> x40, local copies, waits for them, and re-layouts: 5.96 us -> 38 us  [the longest x8 13.1 us: own_columns(): return grads[:, k * width:(k + 1) * width]]
  transfers between devices with their start and end apart: 30 -> 149, of which waited for: 25 -> 55; matrix products, arithmetic and copies ran while one was open for 7% -> 26% of each run, Pallas kernels for 0% -> 0%
where the time goes in v1:
time: 917 us; the launch traced here: 902 us
  waiting for transfers between devices  287 us (31%)
  starting transfers between devices  259 us (28%)
  local copies, waits for them, and re-layouts  177 us (19%)
  other arithmetic  101 us (11%)
  matrix products  72.1 us (8%)
    ppermute x36, starting transfers between devices, step_up(): lax.ppermute(values_in, 'dp', [(i, i + 4) for i in range(dp_size() - 4)])  151 us
    ppermute x19, waiting for transfers between devices, flip_dp(): lax.ppermute(values_in, 'dp', [(i, i ^ bit) for i in range(dp_size())])  133 us
    ppermute x54, waiting for transfers between devices, flip_quad(): lax.ppermute(values_in, ('dp', 'tensor'), [(i, i ^ bits) for i in range(2...  94.8 us
    ppermute x36, starting transfers between devices, step_down(): lax.ppermute(values_in, 'dp', [(i + 4, i) for i in range(dp_size() - 4)])  46.6 us
    ppermute x54, starting transfers between devices, flip_quad(): lax.ppermute(values_in, ('dp', 'tensor'), [(i, i ^ bits) for i in range(2...  37.3 us
    ppermute x36, waiting for transfers between devices, step_down(): lax.ppermute(values_in, 'dp', [(i + 4, i) for i in range(dp_size() - 4)])  34.3 us
    ppermute x36, waiting for transfers between devices, step_up(): lax.ppermute(values_in, 'dp', [(i, i + 4) for i in range(dp_size() - 4)])  25.3 us
    ppermute x19, starting transfers between devices, flip_dp(): lax.ppermute(values_in, 'dp', [(i, i ^ bit) for i in range(dp_size())])  22.9 us
  transfers between devices with their start and end apart: 149, of which 55 were waited for; matrix products, arithmetic and copies ran while one was open for 26% of the time, Pallas kernels for 0%

profile of v1, /device:TPU:4, one launch (start us, length us, event | category | flops | bytes accessed | tf_op | source)
XLA Modules:
  0.0 902.4 jit_solution(13867950067191934537)
XLA Ops:
  5.5 4.6 collective-permute-start.56
  10.8 3.6 reshape.395
  28.0 4.6 collective-permute-start.65
  34.1 5.2 collective-permute-done.1
  40.6 4.6 collective-permute-start.57
  50.6 5.2 collective-permute-start.20
  62.5 5.2 collective-permute-start.66
  69.1 4.6 collective-permute-start.21
  73.8 4.8 collective-permute-done.24
  79.9 4.6 collective-permute-start.22
  90.6 5.2 collective-permute-start.67
  96.0 3.9 collective-permute-start.3
  105.3 4.6 collective-permute-start.47
  114.1 4.6 collective-permute-start.4
  120.0 4.6 collective-permute-start.48
  130.2 4.4 collective-permute-start.34
  136.5 4.4 collective-permute-start.5
  144.2 5.2 collective-permute-start.35
  159.6 23.2 %collective-permute-done.52 = bf16[4,192,768]{2,1,0:T(8,128)(2,1)S(1)} collective-permute-done((bf16[4,192,768]{2,1,0:T(8,128)(2,1)S(1)}, bf16[4,192,768]{2,1,0:T(8,128)(2,1)S(1)}, u32[]{:S(2)}, u32[]{:S(2)}) %collective-permute-start.52) | collective-permute-done | bytes 1179680 | tf_op jit(solution)/shard_map/ppermute | solution.py:43
  184.5 23.6 %collective-permute-done.71 = bf16[4,48,3072]{2,1,0:T(8,128)(2,1)S(1)} collective-permute-done((bf16[4,48,3072]{2,1,0:T(8,128)(2,1)S(1)}, bf16[4,48,3072]{2,1,0:T(8,128)(2,1)S(1)}, u32[]{:S(2)}, u32[]{:S(2)}) %collective-permute-start.71) | collective-permute-done | bytes 1179680 | tf_op jit(solution)/shard_map/ppermute | solution.py:43
  210.3 23.3 %collective-permute-done.9 = bf16[4,193,768]{2,0,1:T(4,128)(2,1)S(1)} collective-permute-done((bf16[4,193,768]{2,0,1:T(4,128)(2,1)S(1)}, bf16[4,193,768]{2,0,1:T(4,128)(2,1)S(1)}, u32[]{:S(2)}, u32[]{:S(2)}) %collective-permute-start.9) | collective-permute-done | bytes 1185824 | tf_op jit(solution)/shard_map/ppermute | solution.py:43
  283.3 40.6 %collective-permute-done.29 = bf16[64,768]{1,0:T(8,128)(2,1)S(1)} collective-permute-done((bf16[64,768]{1,0:T(8,128)(2,1)S(1)}, bf16[64,768]{1,0:T(8,128)(2,1)S(1)}, u32[]{:S(2)}, u32[]{:S(2)}) %collective-permute-start.29) | collective-permute-done | bytes 98336 | tf_op jit(solution)/shard_map/ppermute | solution.py:51
  356.7 3.7 collective-permute-done.55
  360.4 6.2 collective-permute-done.54
  380.1 5.0 fusion.224
  393.5 3.6 convolution_convert_fusion
  397.1 8.2 reshape.367
  405.3 5.6 fusion.223
  412.9 10.7 %fusion.243 = (f32[64,12,8]{2,1,0:T(8,128)S(1)}, f32[64,12,8,8]{2,3,1,0:T(8,128)S(1)}) fusion(f32[64,12,8,8]{2,3,1,0:T(8,128)S(1)} %fusion.40, pred[8,8]{0,1:T(8,128)(4,1)S(1)} %copy-done.153), kind=kOutput, calls=%fused_computation.574 | output fusion | flops 294919 | bytes 417856 | tf_op jit(solution)/shard_map/sub | solution.py:237
  438.0 4.6 fusion.25
  442.6 7.1 fusion.8
  459.1 3.8 reshape.369
  462.9 4.9 fusion.22
  493.3 3.9 reshape.370
  500.5 4.1 reshape.371
  508.0 3.9 reshape.372
  517.0 6.1 fusion.248
  531.0 4.0 constant_dynamic-slice_fusion.4
  540.4 5.0 pad_maximum_fusion.4
  579.1 6.1 copy.298
  631.0 3.6 collective-permute-done.96
  649.2 9.3 %collective-permute-done.108 = bf16[4,192,768]{2,1,0:T(8,128)(2,1)} collective-permute-done((bf16[4,192,768]{2,1,0:T(8,128)(2,1)}, bf16[4,192,768]{2,1,0:T(8,128)(2,1)}, u32[]{:S(2)}, u32[]{:S(2)}) %collective-permute-start.108) | collective-permute-done | bytes 1179680 | tf_op jit(solution)/shard_map/ppermute | solution.py:43
  664.2 3.8 collective-permute-start.118
  668.0 15.8 %collective-permute-done.132 = bf16[4,96,1536]{2,1,0:T(8,128)(2,1)} collective-permute-done((bf16[4,96,1536]{2,1,0:T(8,128)(2,1)}, bf16[4,96,1536]{2,1,0:T(8,128)(2,1)}, u32[]{:S(2)}, u32[]{:S(2)}) %collective-permute-start.132) | collective-permute-done | bytes 1179680 | tf_op jit(solution)/shard_map/ppermute | solution.py:43
  686.9 3.9 collective-permute-done.120
  692.2 4.6 collective-permute-start.109
  705.6 4.4 collective-permute-start.133
  714.6 4.4 collective-permute-start.110
  720.3 4.2 collective-permute-done.110
  724.6 4.4 collective-permute-start.134
  735.5 4.7 collective-permute-start.102
  750.5 5.1 collective-permute-done.137
  755.6 3.6 collective-permute-start.103
  767.3 5.1 collective-permute-start.104
  775.4 7.0 collective-permute-done.106
  784.4 10.8 %maximum_add_fusion = f32[768,3072]{1,0:T(8,128)} fusion(f32[768,1536]{1,0:T(8,128)} %slice.604, f32[768,1536]{1,0:T(8,128)} %slice.603, bf16[768,3072]{1,0:T(8,128)(2,1)} %collective-permute-done.140), kind=kLoop, calls=%fused_computation.2 | loop fusion | flops 7077888 | bytes 23592960 | tf_op jit(solution)/shard_map/add | solution.py:467
  806.3 32.7 %collective-permute-done.141 = bf16[4,2,48,3072]{3,2,0,1:T(8,128)(2,1)S(1)} collective-permute-done((bf16[4,2,48,3072]{3,2,0,1:T(8,128)(2,1)S(1)}, bf16[4,2,48,3072]{3,2,0,1:T(8,128)(2,1)S(1)}, u32[]{:S(2)}, u32[]{:S(2)}) %collective-permute-start.141) | collective-permute-done | bytes 2359328 | tf_op jit(solution)/shard_map/ppermute | solution.py:43
  841.9 4.4 collective-permute-start.126
  850.4 4.4 collective-permute-start.127
  856.8 4.4 collective-permute-start.143
  861.3 3.6 collective-permute-start.128
  867.6 5.2 collective-permute-start.144
  885.8 4.8 collective-permute-start.145
  895.2 5.1 collective-permute-done.148
  (927 shorter events, 446.7 us)
Async XLA Ops:
  4.2 22.4 %collective-permute-start.59 = (bf16[48,1536]{1,0:T(8,128)(2,1)}, bf16[48,1536]{1,0:T(8,128)(2,1)S(1)}, u32[]{:S(2)}, u32[]{:S(2)}) collective-permute-start(bf16[48,1536]{1,0:T(8,128)(2,1)} %pad_maximum_fusion.45), channel_id=1, source_target_pairs={{8,0},{10,2},{12,4},{14,6},{16,8},{18,10},{20,12},{22,14},{24,16},... | collective-permute-start | bytes 442376 | tf_op jit(solution)/shard_map/ppermute | solution.py:61
  5.5 22.4 %collective-permute-start.56 = (bf16[48,1536]{1,0:T(8,128)(2,1)}, bf16[48,1536]{1,0:T(8,128)(2,1)S(1)}, u32[]{:S(2)}, u32[]{:S(2)}) collective-permute-start(bf16[48,1536]{1,0:T(8,128)(2,1)} %pad_maximum_fusion.45), channel_id=1, source_target_pairs={{0,8},{2,10},{4,12},{6,14},{8,16},{10,18},{12,20},{14,22},{16,24},... | collective-permute-start | bytes 442376 | tf_op jit(solution)/shard_map/ppermute | solution.py:57
  19.1 13.4 %collective-permute-start.2 = (bf16[64,8,192]{0,2,1:T(8,128)(2,1)}, bf16[64,8,192]{0,2,1:T(8,128)(2,1)S(1)}, u32[]{:S(2)}, u32[]{:S(2)}) collective-permute-start(bf16[64,8,192]{0,2,1:T(8,128)(2,1)} %get-tuple-element.128), channel_id=1, source_target_pairs={{0,3},{1,2},{2,1},{3,0},{4,7},{5,6},{6,5},{7,4},{8,11},{9,10},{10,... | collective-permute-start | bytes 589832 | tf_op jit(solution)/shard_map/ppermute | solution.py:51
  19.5 19.8 %collective-permute-start.1 = (bf16[64,8,192]{0,2,1:T(8,128)(2,1)}, bf16[64,8,192]{0,2,1:T(8,128)(2,1)}, u32[]{:S(2)}, u32[]{:S(2)}) collective-permute-start(bf16[64,8,192]{0,2,1:T(8,128)(2,1)} %get-tuple-element.129), channel_id=1, source_target_pairs={{0,2},{1,3},{2,0},{3,1},{4,6},{5,7},{6,4},{7,5},{8,10},{9,11},{10,... | collective-permute-start | bytes 589832 | tf_op jit(solution)/shard_map/ppermute | solution.py:51
  20.6 20.0 %collective-permute-start = (bf16[64,8,192]{0,2,1:T(8,128)(2,1)}, bf16[64,8,192]{0,2,1:T(8,128)(2,1)}, u32[]{:S(2)}, u32[]{:S(2)}) collective-permute-start(bf16[64,8,192]{0,2,1:T(8,128)(2,1)} %get-tuple-element.130), channel_id=1, source_target_pairs={{0,1},{1,0},{2,3},{3,2},{4,5},{5,4},{6,7},{7,6},{8,9},{9,8},{10,11... | collective-permute-start | bytes 589832 | tf_op jit(solution)/shard_map/ppermute | solution.py:51
  26.7 33.2 %collective-permute-start.68 = (bf16[48,3072]{1,0:T(8,128)(2,1)S(1)}, bf16[48,3072]{1,0:T(8,128)(2,1)S(1)}, u32[]{:S(2)}, u32[]{:S(2)}) collective-permute-start(bf16[48,3072]{1,0:T(8,128)(2,1)S(1)} %copy-done.81), channel_id=1, source_target_pairs={{8,0},{10,2},{12,4},{14,6},{16,8},{18,10},{20,12},{22,14},{24,16},... | collective-permute-start | bytes 884744 | tf_op jit(solution)/shard_map/ppermute | solution.py:61
  28.0 33.2 %collective-permute-start.65 = (bf16[48,3072]{1,0:T(8,128)(2,1)S(1)}, bf16[48,3072]{1,0:T(8,128)(2,1)S(1)}, u32[]{:S(2)}, u32[]{:S(2)}) collective-permute-start(bf16[48,3072]{1,0:T(8,128)(2,1)S(1)} %copy-done.81), channel_id=1, source_target_pairs={{0,8},{2,10},{4,12},{6,14},{8,16},{10,18},{12,20},{14,22},{16,24},... | collective-permute-start | bytes 884744 | tf_op jit(solution)/shard_map/ppermute | solution.py:57
  32.6 15.1 %collective-permute-start.19 = (bf16[48,2304]{1,0:T(8,128)(2,1)S(1)}, bf16[48,2304]{1,0:T(8,128)(2,1)S(1)}, u32[]{:S(2)}, u32[]{:S(2)}) collective-permute-start(bf16[48,2304]{1,0:T(8,128)(2,1)S(1)} %bitcast.693), channel_id=1, source_target_pairs={{0,2},{2,0},{4,6},{6,4},{8,10},{10,8},{12,14},{14,12},{16,18},{18,... | collective-permute-start | bytes 663560 | tf_op jit(solution)/shard_map/ppermute | solution.py:43
  49.3 13.2 %collective-permute-start.23 = (bf16[96,768]{1,0:T(8,128)(2,1)S(1)}, bf16[96,768]{1,0:T(8,128)(2,1)S(1)}, u32[]{:S(2)}, u32[]{:S(2)}) collective-permute-start(bf16[96,768]{1,0:T(8,128)(2,1)S(1)} %slice.519), channel_id=1, source_target_pairs={{8,0},{10,2},{12,4},{14,6},{16,8},{18,10},{20,12},{22,14},{24,16},... | collective-permute-start | bytes 442376 | tf_op jit(solution)/shard_map/ppermute | solution.py:61
  50.6 17.1 %collective-permute-start.20 = (bf16[96,768]{1,0:T(8,128)(2,1)S(1)}, bf16[96,768]{1,0:T(8,128)(2,1)S(1)}, u32[]{:S(2)}, u32[]{:S(2)}) collective-permute-start(bf16[96,768]{1,0:T(8,128)(2,1)S(1)} %slice.519), channel_id=1, source_target_pairs={{0,8},{2,10},{4,12},{6,14},{8,16},{10,18},{12,20},{14,22},{16,24},... | collective-permute-start | bytes 442376 | tf_op jit(solution)/shard_map/ppermute | solution.py:57
  59.9 36.1 %collective-permute-start.49 = (bf16[192,768]{1,0:T(8,128)(2,1)S(1)}, bf16[192,768]{1,0:T(8,128)(2,1)S(1)}, u32[]{:S(2)}, u32[]{:S(2)}) collective-permute-start(bf16[192,768]{1,0:T(8,128)(2,1)S(1)} %bitcast.687), channel_id=1, source_target_pairs={{8,0},{10,2},{12,4},{14,6},{16,8},{18,10},{20,12},{22,14},{24,16},... | collective-permute-start | bytes 884744 | tf_op jit(solution)/shard_map/ppermute | solution.py:61
  61.2 23.3 %collective-permute-start.69 = (bf16[48,3072]{1,0:T(8,128)(2,1)S(1)}, bf16[48,3072]{1,0:T(8,128)(2,1)S(1)}, u32[]{:S(2)}, u32[]{:S(2)}) collective-permute-start(bf16[48,3072]{1,0:T(8,128)(2,1)S(1)} %collective-permute-done.68), channel_id=1, source_target_pairs={{8,0},{10,2},{12,4},{14,6},{16,8},{18,10},{20,12},{22,14},{24,16},... | collective-permute-start | bytes 884744 | tf_op jit(solution)/shard_map/ppermute | solution.py:61
  62.5 25.5 %collective-permute-start.66 = (bf16[48,3072]{1,0:T(8,128)(2,1)S(1)}, bf16[48,3072]{1,0:T(8,128)(2,1)S(1)}, u32[]{:S(2)}, u32[]{:S(2)}) collective-permute-start(bf16[48,3072]{1,0:T(8,128)(2,1)S(1)} %collective-permute-done.65), channel_id=1, source_target_pairs={{0,8},{2,10},{4,12},{6,14},{8,16},{10,18},{12,20},{14,22},{16,24},... | collective-permute-start | bytes 884744 | tf_op jit(solution)/shard_map/ppermute | solution.py:57
  84.5 15.5 %collective-permute-start.46 = (bf16[192,768]{1,0:T(8,128)(2,1)S(1)}, bf16[192,768]{1,0:T(8,128)(2,1)S(1)}, u32[]{:S(2)}, u32[]{:S(2)}) collective-permute-start(bf16[192,768]{1,0:T(8,128)(2,1)S(1)} %bitcast.688), channel_id=1, source_target_pairs={{0,8},{2,10},{4,12},{6,14},{8,16},{10,18},{12,20},{14,22},{16,24},... | collective-permute-start | bytes 884744 | tf_op jit(solution)/shard_map/ppermute | solution.py:57
  88.0 22.3 %collective-permute-start.6 = (bf16[193,768]{1,0:T(8,128)(2,1)S(1)}, bf16[193,768]{1,0:T(8,128)(2,1)S(1)}, u32[]{:S(2)}, u32[]{:S(2)}) collective-permute-start(bf16[193,768]{1,0:T(8,128)(2,1)S(1)} %fusion.108), channel_id=1, source_target_pairs={{8,0},{10,2},{12,4},{14,6},{16,8},{18,10},{20,12},{22,14},{24,16},... | collective-permute-start | bytes 889352 | tf_op jit(solution)/shard_map/ppermute | solution.py:61
  89.3 14.7 %collective-permute-start.70 = (bf16[48,3072]{1,0:T(8,128)(2,1)S(1)}, bf16[48,3072]{1,0:T(8,128)(2,1)S(1)}, u32[]{:S(2)}, u32[]{:S(2)}) collective-permute-start(bf16[48,3072]{1,0:T(8,128)(2,1)S(1)} %collective-permute-done.69), channel_id=1, source_target_pairs={{8,0},{10,2},{12,4},{14,6},{16,8},{18,10},{20,12},{22,14},{24,16},... | collective-permute-start | bytes 884744 | tf_op jit(solution)/shard_map/ppermute | solution.py:61
  90.6 14.6 %collective-permute-start.67 = (bf16[48,3072]{1,0:T(8,128)(2,1)S(1)}, bf16[48,3072]{1,0:T(8,128)(2,1)S(1)}, u32[]{:S(2)}, u32[]{:S(2)}) collective-permute-start(bf16[48,3072]{1,0:T(8,128)(2,1)S(1)} %collective-permute-done.66), channel_id=1, source_target_pairs={{0,8},{2,10},{4,12},{6,14},{8,16},{10,18},{12,20},{14,22},{16,24},... | collective-permute-start | bytes 884744 | tf_op jit(solution)/shard_map/ppermute | solution.py:57
  96.0 16.7 %collective-permute-start.3 = (bf16[193,768]{1,0:T(8,128)(2,1)S(1)}, bf16[193,768]{1,0:T(8,128)(2,1)S(1)}, u32[]{:S(2)}, u32[]{:S(2)}) collective-permute-start(bf16[193,768]{1,0:T(8,128)(2,1)S(1)} %fusion.108), channel_id=1, source_target_pairs={{0,8},{2,10},{4,12},{6,14},{8,16},{10,18},{12,20},{14,22},{16,24},... | collective-permute-start | bytes 889352 | tf_op jit(solution)/shard_map/ppermute | solution.py:57
  100.0 14.1 %collective-permute-start.36 = (bf16[96,1536]{1,0:T(8,128)(2,1)S(1)}, bf16[96,1536]{1,0:T(8,128)(2,1)S(1)}, u32[]{:S(2)}, u32[]{:S(2)}) collective-permute-start(bf16[96,1536]{1,0:T(8,128)(2,1)S(1)} %slice.531), channel_id=1, source_target_pairs={{8,0},{10,2},{12,4},{14,6},{16,8},{18,10},{20,12},{22,14},{24,16},... | collective-permute-start | bytes 884744 | tf_op jit(solution)/shard_map/ppermute | solution.py:61
  104.0 14.7 %collective-permute-start.50 = (bf16[192,768]{1,0:T(8,128)(2,1)S(1)}, bf16[192,768]{1,0:T(8,128)(2,1)S(1)}, u32[]{:S(2)}, u32[]{:S(2)}) collective-permute-start(bf16[192,768]{1,0:T(8,128)(2,1)S(1)} %collective-permute-done.49), channel_id=1, source_target_pairs={{8,0},{10,2},{12,4},{14,6},{16,8},{18,10},{20,12},{22,14},{24,16},... | collective-permute-start | bytes 884744 | tf_op jit(solution)/shard_map/ppermute | solution.py:61
  105.3 14.7 %collective-permute-start.47 = (bf16[192,768]{1,0:T(8,128)(2,1)S(1)}, bf16[192,768]{1,0:T(8,128)(2,1)S(1)}, u32[]{:S(2)}, u32[]{:S(2)}) collective-permute-start(bf16[192,768]{1,0:T(8,128)(2,1)S(1)} %collective-permute-done.46), channel_id=1, source_target_pairs={{0,8},{2,10},{4,12},{6,14},{8,16},{10,18},{12,20},{14,22},{16,24},... | collective-permute-start | bytes 884744 | tf_op jit(solution)/shard_map/ppermute | solution.py:57
  110.3 14.4 %collective-permute-start.33 = (bf16[96,1536]{1,0:T(8,128)(2,1)S(1)}, bf16[96,1536]{1,0:T(8,128)(2,1)S(1)}, u32[]{:S(2)}, u32[]{:S(2)}) collective-permute-start(bf16[96,1536]{1,0:T(8,128)(2,1)S(1)} %slice.531), channel_id=1, source_target_pairs={{0,8},{2,10},{4,12},{6,14},{8,16},{10,18},{12,20},{14,22},{16,24},... | collective-permute-start | bytes 884744 | tf_op jit(solution)/shard_map/ppermute | solution.py:57
  114.1 16.1 %collective-permute-start.4 = (bf16[193,768]{1,0:T(8,128)(2,1)S(1)}, bf16[193,768]{1,0:T(8,128)(2,1)S(1)}, u32[]{:S(2)}, u32[]{:S(2)}) collective-permute-start(bf16[193,768]{1,0:T(8,128)(2,1)S(1)} %collective-permute-done.3), channel_id=1, source_target_pairs={{0,8},{2,10},{4,12},{6,14},{8,16},{10,18},{12,20},{14,22},{16,24},... | collective-permute-start | bytes 889352 | tf_op jit(solution)/shard_map/ppermute | solution.py:57
  118.7 15.9 %collective-permute-start.51 = (bf16[192,768]{1,0:T(8,128)(2,1)S(1)}, bf16[192,768]{1,0:T(8,128)(2,1)S(1)}, u32[]{:S(2)}, u32[]{:S(2)}) collective-permute-start(bf16[192,768]{1,0:T(8,128)(2,1)S(1)} %collective-permute-done.50), channel_id=1, source_target_pairs={{8,0},{10,2},{12,4},{14,6},{16,8},{18,10},{20,12},{22,14},{24,16},... | collective-permute-start | bytes 884744 | tf_op jit(solution)/shard_map/ppermute | solution.py:61
  120.0 16.5 %collective-permute-start.48 = (bf16[192,768]{1,0:T(8,128)(2,1)S(1)}, bf16[192,768]{1,0:T(8,128)(2,1)S(1)}, u32[]{:S(2)}, u32[]{:S(2)}) collective-permute-start(bf16[192,768]{1,0:T(8,128)(2,1)S(1)} %collective-permute-done.47), channel_id=1, source_target_pairs={{0,8},{2,10},{4,12},{6,14},{8,16},{10,18},{12,20},{14,22},{16,24},... | collective-permute-start | bytes 884744 | tf_op jit(solution)/shard_map/ppermute | solution.py:57
  124.7 26.6 %collective-permute-start.62 = (bf16[4,48,1536]{2,1,0:T(8,128)(2,1)S(1)}, bf16[4,48,1536]{2,1,0:T(8,128)(2,1)S(1)}, u32[]{:S(2)}, u32[]{:S(2)}) collective-permute-start(bf16[4,48,1536]{2,1,0:T(8,128)(2,1)S(1)} %pad_maximum_fusion.33), channel_id=1, source_target_pairs={{0,4},{2,6},{4,0},{6,2},{8,12},{10,14},{12,8},{14,10},{16,20},{18,... | collective-permute-start | bytes 1769480 | tf_op jit(solution)/shard_map/ppermute | solution.py:43
  125.3 15.9 %collective-permute-start.37 = (bf16[96,1536]{1,0:T(8,128)(2,1)S(1)}, bf16[96,1536]{1,0:T(8,128)(2,1)S(1)}, u32[]{:S(2)}, u32[]{:S(2)}) collective-permute-start(bf16[96,1536]{1,0:T(8,128)(2,1)S(1)} %collective-permute-done.36), channel_id=1, source_target_pairs={{8,0},{10,2},{12,4},{14,6},{16,8},{18,10},{20,12},{22,14},{24,16},... | collective-permute-start | bytes 884744 | tf_op jit(solution)/shard_map/ppermute | solution.py:61
  141.2 17.2 %collective-permute-start.26 = (bf16[4,96,768]{2,1,0:T(8,128)(2,1)S(1)}, bf16[4,96,768]{2,1,0:T(8,128)(2,1)S(1)}, u32[]{:S(2)}, u32[]{:S(2)}) collective-permute-start(bf16[4,96,768]{2,1,0:T(8,128)(2,1)S(1)} %pad_maximum_fusion.32), channel_id=1, source_target_pairs={{0,4},{2,6},{4,0},{6,2},{8,12},{10,14},{12,8},{14,10},{16,20},{18,... | collective-permute-start | bytes 1769480 | tf_op jit(solution)/shard_map/ppermute | solution.py:43
  149.4 33.4 %collective-permute-start.52 = (bf16[4,192,768]{2,1,0:T(8,128)(2,1)S(1)}, bf16[4,192,768]{2,1,0:T(8,128)(2,1)S(1)}, u32[]{:S(2)}, u32[]{:S(2)}) collective-permute-start(bf16[4,192,768]{2,1,0:T(8,128)(2,1)S(1)} %pad_maximum_fusion.25), channel_id=1, source_target_pairs={{0,4},{2,6},{4,0},{6,2},{8,12},{10,14},{12,8},{14,10},{16,20},{18,... | collective-permute-start | bytes 3538952 | tf_op jit(solution)/shard_map/ppermute | solution.py:43
  151.3 56.8 %collective-permute-start.71 = (bf16[4,48,3072]{2,1,0:T(8,128)(2,1)S(1)}, bf16[4,48,3072]{2,1,0:T(8,128)(2,1)S(1)}, u32[]{:S(2)}, u32[]{:S(2)}) collective-permute-start(bf16[4,48,3072]{2,1,0:T(8,128)(2,1)S(1)} %pad_maximum_fusion.28), channel_id=1, source_target_pairs={{0,4},{2,6},{4,0},{6,2},{8,12},{10,14},{12,8},{14,10},{16,20},{18,... | collective-permute-start | bytes 3538952 | tf_op jit(solution)/shard_map/ppermute | solution.py:43
  154.0 79.5 %collective-permute-start.9 = (bf16[4,193,768]{2,0,1:T(4,128)(2,1)S(1)}, bf16[4,193,768]{2,0,1:T(4,128)(2,1)S(1)}, u32[]{:S(2)}, u32[]{:S(2)}) collective-permute-start(bf16[4,193,768]{2,0,1:T(4,128)(2,1)S(1)} %copy.239), channel_id=1, source_target_pairs={{0,4},{2,6},{4,0},{6,2},{8,12},{10,14},{12,8},{14,10},{16,20},{18,... | collective-permute-start | bytes 3557384 | tf_op jit(solution)/shard_map/ppermute | solution.py:43
  154.7 183.5 %collective-permute-start.63 = (bf16[4,2,48,1536]{3,2,1,0:T(8,128)(2,1)}, bf16[4,2,48,1536]{3,2,1,0:T(8,128)(2,1)}, u32[]{:S(2)}, u32[]{:S(2)}) collective-permute-start(bf16[4,2,48,1536]{3,2,1,0:T(8,128)(2,1)} %pad_maximum_fusion.26), channel_id=1, source_target_pairs={{0,2},{2,0},{4,6},{6,4},{8,10},{10,8},{12,14},{14,12},{16,18},{18,... | collective-permute-start | bytes 3538952 | tf_op jit(solution)/shard_map/ppermute | solution.py:43
  158.4 121.3 %collective-permute-start.39 = (bf16[4,96,1536]{2,1,0:T(8,128)(2,1)}, bf16[4,96,1536]{2,1,0:T(8,128)(2,1)}, u32[]{:S(2)}, u32[]{:S(2)}) collective-permute-start(bf16[4,96,1536]{2,1,0:T(8,128)(2,1)} %pad_maximum_fusion.24), channel_id=1, source_target_pairs={{0,4},{2,6},{4,0},{6,2},{8,12},{10,14},{12,8},{14,10},{16,20},{18,... | collective-permute-start | bytes 3538952 | tf_op jit(solution)/shard_map/ppermute | solution.py:43
  250.0 18.2 %collective-permute-start.18 = (bf16[64,768]{1,0:T(8,128)(2,1)S(1)}, bf16[64,768]{1,0:T(8,128)(2,1)S(1)}, u32[]{:S(2)}, u32[]{:S(2)}) collective-permute-start(bf16[64,768]{1,0:T(8,128)(2,1)S(1)} %add_convert_fusion.5), channel_id=1, source_target_pairs={{0,3},{1,2},{2,1},{3,0},{4,7},{5,6},{6,5},{7,4},{8,11},{9,10},{10,... | collective-permute-start | bytes 294920 | tf_op jit(solution)/shard_map/ppermute | solution.py:51
  250.9 19.0 %collective-permute-start.17 = (bf16[64,768]{1,0:T(8,128)(2,1)S(1)}, bf16[64,768]{1,0:T(8,128)(2,1)S(1)}, u32[]{:S(2)}, u32[]{:S(2)}) collective-permute-start(bf16[64,768]{1,0:T(8,128)(2,1)S(1)} %add_convert_fusion.5), channel_id=1, source_target_pairs={{0,2},{1,3},{2,0},{3,1},{4,6},{5,7},{6,4},{7,5},{8,10},{9,11},{10,... | collective-permute-start | bytes 294920 | tf_op jit(solution)/shard_map/ppermute | solution.py:51
  251.9 18.1 %collective-permute-start.16 = (bf16[64,768]{1,0:T(8,128)(2,1)S(1)}, bf16[64,768]{1,0:T(8,128)(2,1)S(1)}, u32[]{:S(2)}, u32[]{:S(2)}) collective-permute-start(bf16[64,768]{1,0:T(8,128)(2,1)S(1)} %add_convert_fusion.5), channel_id=1, source_target_pairs={{0,1},{1,0},{2,3},{3,2},{4,5},{5,4},{6,7},{7,6},{8,9},{9,8},{10,11... | collective-permute-start | bytes 294920 | tf_op jit(solution)/shard_map/ppermute | solution.py:51
  268.2 107.3 %collective-permute-start.72 = (bf16[4,2,48,3072]{3,2,1,0:T(8,128)(2,1)}, bf16[4,2,48,3072]{3,2,1,0:T(8,128)(2,1)}, u32[]{:S(2)}, u32[]{:S(2)}) collective-permute-start(bf16[4,2,48,3072]{3,2,1,0:T(8,128)(2,1)} %pad_maximum_fusion.13), channel_id=1, source_target_pairs={{0,2},{2,0},{4,6},{6,4},{8,10},{10,8},{12,14},{14,12},{16,18},{18,... | collective-permute-start | bytes 7077896 | tf_op jit(solution)/shard_map/ppermute | solution.py:43
  279.3 44.6 %collective-permute-start.29 = (bf16[64,768]{1,0:T(8,128)(2,1)S(1)}, bf16[64,768]{1,0:T(8,128)(2,1)S(1)}, u32[]{:S(2)}, u32[]{:S(2)}) collective-permute-start(bf16[64,768]{1,0:T(8,128)(2,1)S(1)} %get-tuple-element.210), channel_id=1, source_target_pairs={{0,3},{1,2},{2,1},{3,0},{4,7},{5,6},{6,5},{7,4},{8,11},{9,10},{10,... | collective-permute-start | bytes 294920 | tf_op jit(solution)/shard_map/ppermute | solution.py:51
  279.7 46.6 %collective-permute-start.28 = (bf16[64,768]{1,0:T(8,128)(2,1)S(1)}, bf16[64,768]{1,0:T(8,128)(2,1)S(1)}, u32[]{:S(2)}, u32[]{:S(2)}) collective-permute-start(bf16[64,768]{1,0:T(8,128)(2,1)S(1)} %get-tuple-element.211), channel_id=1, source_target_pairs={{0,2},{1,3},{2,0},{3,1},{4,6},{5,7},{6,4},{7,5},{8,10},{9,11},{10,... | collective-permute-start | bytes 294920 | tf_op jit(solution)/shard_map/ppermute | solution.py:51
  347.0 38.1 %collective-permute-start.64 = (bf16[768,1536]{1,0:T(8,128)(2,1)}, bf16[768,1536]{1,0:T(8,128)(2,1)}, u32[]{:S(2)}, u32[]{:S(2)}) collective-permute-start(bf16[768,1536]{1,0:T(8,128)(2,1)} %bitcast.72), channel_id=1, source_target_pairs={{0,1},{1,0},{2,3},{3,2},{4,5},{5,4},{6,7},{7,6},{8,9},{9,8},{10,11... | collective-permute-start | bytes 7077896 | tf_op jit(solution)/shard_map/ppermute | solution.py:47
  353.4 13.2 %collective-permute-start.54 = (bf16[64,8,192]{2,1,0:T(8,128)(2,1)S(1)}, bf16[64,8,192]{2,1,0:T(8,128)(2,1)S(1)}, u32[]{:S(2)}, u32[]{:S(2)}) collective-permute-start(bf16[64,8,192]{2,1,0:T(8,128)(2,1)S(1)} %slice.427), channel_id=1, source_target_pairs={{0,2},{1,3},{2,0},{3,1},{4,6},{5,7},{6,4},{7,5},{8,10},{9,11},{10,... | collective-permute-start | bytes 589832 | tf_op jit(solution)/shard_map/ppermute | solution.py:51
  380.1 51.9 %collective-permute-start.73 = (bf16[768,3072]{1,0:T(8,128)(2,1)}, bf16[768,3072]{1,0:T(8,128)(2,1)}, u32[]{:S(2)}, u32[]{:S(2)}) collective-permute-start(bf16[768,3072]{1,0:T(8,128)(2,1)} %bitcast.89), channel_id=1, source_target_pairs={{0,1},{1,0},{2,3},{3,2},{4,5},{5,4},{6,7},{7,6},{8,9},{9,8},{10,11... | collective-permute-start | bytes 14155784 | tf_op jit(solution)/shard_map/ppermute | solution.py:47
  545.4 239.0 %collective-permute-start.140 = (bf16[768,3072]{1,0:T(8,128)(2,1)}, bf16[768,3072]{1,0:T(8,128)(2,1)}, u32[]{:S(2)}, u32[]{:S(2)}) collective-permute-start(bf16[768,3072]{1,0:T(8,128)(2,1)} %pad_maximum_fusion.4), channel_id=1, source_target_pairs={{0,1},{1,0},{2,3},{3,2},{4,5},{5,4},{6,7},{7,6},{8,9},{9,8},{10,11... | collective-permute-start | bytes 14155784 | tf_op jit(solution)/shard_map/ppermute | solution.py:47
  605.8 34.8 %collective-permute-start.115 = (bf16[4,96,768]{2,1,0:T(8,128)(2,1)}, bf16[4,96,768]{2,1,0:T(8,128)(2,1)}, u32[]{:S(2)}, u32[]{:S(2)}) collective-permute-start(bf16[4,96,768]{2,1,0:T(8,128)(2,1)} %fusion.80), channel_id=1, source_target_pairs={{0,4},{2,6},{4,0},{6,2},{8,12},{10,14},{12,8},{14,10},{16,20},{18,... | collective-permute-start | bytes 1769480 | tf_op jit(solution)/shard_map/ppermute | solution.py:43
  621.4 13.2 %collective-permute-start.96 = (bf16[64,8,192]{2,1,0:T(8,128)(2,1)S(1)}, bf16[64,8,192]{2,1,0:T(8,128)(2,1)S(1)}, u32[]{:S(2)}, u32[]{:S(2)}) collective-permute-start(bf16[64,8,192]{2,1,0:T(8,128)(2,1)S(1)} %slice.472), channel_id=1, source_target_pairs={{0,2},{1,3},{2,0},{3,1},{4,6},{5,7},{6,4},{7,5},{8,10},{9,11},{10,... | collective-permute-start | bytes 589832 | tf_op jit(solution)/shard_map/ppermute | solution.py:51
  629.4 116.5 %collective-permute-start.123 = (bf16[768,1536]{1,0:T(8,128)(2,1)}, bf16[768,1536]{1,0:T(8,128)(2,1)}, u32[]{:S(2)}, u32[]{:S(2)}) collective-permute-start(bf16[768,1536]{1,0:T(8,128)(2,1)} %pad_maximum_fusion.15), channel_id=1, source_target_pairs={{0,1},{1,0},{2,3},{3,2},{4,5},{5,4},{6,7},{7,6},{8,9},{9,8},{10,11... | collective-permute-start | bytes 7077896 | tf_op jit(solution)/shard_map/ppermute | solution.py:47
  629.4 29.2 %collective-permute-start.108 = (bf16[4,192,768]{2,1,0:T(8,128)(2,1)}, bf16[4,192,768]{2,1,0:T(8,128)(2,1)}, u32[]{:S(2)}, u32[]{:S(2)}) collective-permute-start(bf16[4,192,768]{2,1,0:T(8,128)(2,1)} %fusion.29), channel_id=1, source_target_pairs={{0,4},{2,6},{4,0},{6,2},{8,12},{10,14},{12,8},{14,10},{16,20},{18,... | collective-permute-start | bytes 3538952 | tf_op jit(solution)/shard_map/ppermute | solution.py:43
  634.6 49.2 %collective-permute-start.132 = (bf16[4,96,1536]{2,1,0:T(8,128)(2,1)}, bf16[4,96,1536]{2,1,0:T(8,128)(2,1)}, u32[]{:S(2)}, u32[]{:S(2)}) collective-permute-start(bf16[4,96,1536]{2,1,0:T(8,128)(2,1)} %fusion.30), channel_id=1, source_target_pairs={{0,4},{2,6},{4,0},{6,2},{8,12},{10,14},{12,8},{14,10},{16,20},{18,... | collective-permute-start | bytes 3538952 | tf_op jit(solution)/shard_map/ppermute | solution.py:43
  647.9 14.7 %collective-permute-start.119 = (bf16[96,768]{1,0:T(8,128)(2,1)S(1)}, bf16[96,768]{1,0:T(8,128)(2,1)S(1)}, u32[]{:S(2)}, u32[]{:S(2)}) collective-permute-start(bf16[96,768]{1,0:T(8,128)(2,1)S(1)} %get-tuple-element.134), channel_id=1, source_target_pairs={{8,0},{10,2},{12,4},{14,6},{16,8},{18,10},{20,12},{22,14},{24,16},... | collective-permute-start | bytes 442376 | tf_op jit(solution)/shard_map/ppermute | solution.py:61
  662.6 66.5 %collective-permute-start.101 = (bf16[4,193,768]{2,0,1:T(4,128)(2,1)S(1)}, bf16[4,193,768]{2,0,1:T(4,128)(2,1)S(1)}, u32[]{:S(2)}, u32[]{:S(2)}) collective-permute-start(bf16[4,193,768]{2,0,1:T(4,128)(2,1)S(1)} %bitcast.678), channel_id=1, source_target_pairs={{0,4},{2,6},{4,0},{6,2},{8,12},{10,14},{12,8},{14,10},{16,20},{18,... | collective-permute-start | bytes 3557384 | tf_op jit(solution)/shard_map/ppermute | solution.py:43
  664.2 28.0 %collective-permute-start.118 = (bf16[96,768]{1,0:T(8,128)(2,1)S(1)}, bf16[96,768]{1,0:T(8,128)(2,1)S(1)}, u32[]{:S(2)}, u32[]{:S(2)}) collective-permute-start(bf16[96,768]{1,0:T(8,128)(2,1)S(1)} %get-tuple-element.131), channel_id=1, source_target_pairs={{0,8},{2,10},{4,12},{6,14},{8,16},{10,18},{12,20},{14,22},{16,24},... | collective-permute-start | bytes 442376 | tf_op jit(solution)/shard_map/ppermute | solution.py:57
  697.9 21.1 %collective-permute-start.112 = (bf16[192,768]{1,0:T(8,128)(2,1)S(1)}, bf16[192,768]{1,0:T(8,128)(2,1)S(1)}, u32[]{:S(2)}, u32[]{:S(2)}) collective-permute-start(bf16[192,768]{1,0:T(8,128)(2,1)S(1)} %get-tuple-element.114), channel_id=1, source_target_pairs={{8,0},{10,2},{12,4},{14,6},{16,8},{18,10},{20,12},{22,14},{24,16},... | collective-permute-start | bytes 884744 | tf_op jit(solution)/shard_map/ppermute | solution.py:61
  729.1 30.2 %collective-permute-start.111 = (bf16[192,768]{1,0:T(8,128)(2,1)S(1)}, bf16[192,768]{1,0:T(8,128)(2,1)S(1)}, u32[]{:S(2)}, u32[]{:S(2)}) collective-permute-start(bf16[192,768]{1,0:T(8,128)(2,1)S(1)} %get-tuple-element.111), channel_id=1, source_target_pairs={{0,8},{2,10},{4,12},{6,14},{8,16},{10,18},{12,20},{14,22},{16,24},... | collective-permute-start | bytes 884744 | tf_op jit(solution)/shard_map/ppermute | solution.py:57
  742.6 21.4 %collective-permute-start.105 = (bf16[193,768]{1,0:T(8,128)(2,1)S(1)}, bf16[193,768]{1,0:T(8,128)(2,1)S(1)}, u32[]{:S(2)}, u32[]{:S(2)}) collective-permute-start(bf16[193,768]{1,0:T(8,128)(2,1)S(1)} %get-tuple-element.100), channel_id=1, source_target_pairs={{8,0},{10,2},{12,4},{14,6},{16,8},{18,10},{20,12},{22,14},{24,16},... | collective-permute-start | bytes 889352 | tf_op jit(solution)/shard_map/ppermute | solution.py:61
  745.9 16.0 %collective-permute-start.114 = (bf16[192,768]{1,0:T(8,128)(2,1)S(1)}, bf16[192,768]{1,0:T(8,128)(2,1)S(1)}, u32[]{:S(2)}, u32[]{:S(2)}) collective-permute-start(bf16[192,768]{1,0:T(8,128)(2,1)S(1)} %fusion.93), channel_id=1, source_target_pairs={{8,0},{10,2},{12,4},{14,6},{16,8},{18,10},{20,12},{22,14},{24,16},... | collective-permute-start | bytes 884744 | tf_op jit(solution)/shard_map/ppermute | solution.py:61
  764.0 37.4 %collective-permute-start.124 = (bf16[4,2,48,1536]{3,2,0,1:T(8,128)(2,1)}, bf16[4,2,48,1536]{3,2,0,1:T(8,128)(2,1)}, u32[]{:S(2)}, u32[]{:S(2)}) collective-permute-start(bf16[4,2,48,1536]{3,2,0,1:T(8,128)(2,1)} %fusion.32), channel_id=1, source_target_pairs={{0,2},{2,0},{4,6},{6,4},{8,10},{10,8},{12,14},{14,12},{16,18},{18,... | collective-permute-start | bytes 3538952 | tf_op jit(solution)/shard_map/ppermute | solution.py:43
  767.3 32.0 %collective-permute-start.104 = (bf16[193,768]{1,0:T(8,128)(2,1)}, bf16[193,768]{1,0:T(8,128)(2,1)}, u32[]{:S(2)}, u32[]{:S(2)}) collective-permute-start(bf16[193,768]{1,0:T(8,128)(2,1)} %get-tuple-element.97), channel_id=1, source_target_pairs={{0,8},{2,10},{4,12},{6,14},{8,16},{10,18},{12,20},{14,22},{16,24},... | collective-permute-start | bytes 889352 | tf_op jit(solution)/shard_map/ppermute | solution.py:57
  774.5 24.6 %collective-permute-start.139 = (bf16[48,1536]{1,0:T(8,128)(2,1)}, bf16[48,1536]{1,0:T(8,128)(2,1)S(1)}, u32[]{:S(2)}, u32[]{:S(2)}) collective-permute-start(bf16[48,1536]{1,0:T(8,128)(2,1)} %fusion.152), channel_id=1, source_target_pairs={{0,2},{2,0},{4,6},{6,4},{8,10},{10,8},{12,14},{14,12},{16,18},{18,... | collective-permute-start | bytes 442376 | tf_op jit(solution)/shard_map/ppermute | solution.py:43
  783.1 16.2 %collective-permute-start.107 = (bf16[193,768]{1,0:T(8,128)(2,1)}, bf16[193,768]{1,0:T(8,128)(2,1)}, u32[]{:S(2)}, u32[]{:S(2)}) collective-permute-start(bf16[193,768]{1,0:T(8,128)(2,1)} %fusion.75), channel_id=1, source_target_pairs={{8,0},{10,2},{12,4},{14,6},{16,8},{18,10},{20,12},{22,14},{24,16},... | collective-permute-start | bytes 889352 | tf_op jit(solution)/shard_map/ppermute | solution.py:61
  797.9 41.1 %collective-permute-start.141 = (bf16[4,2,48,3072]{3,2,0,1:T(8,128)(2,1)S(1)}, bf16[4,2,48,3072]{3,2,0,1:T(8,128)(2,1)S(1)}, u32[]{:S(2)}, u32[]{:S(2)}) collective-permute-start(bf16[4,2,48,3072]{3,2,0,1:T(8,128)(2,1)S(1)} %fusion.14), channel_id=1, source_target_pairs={{0,2},{2,0},{4,6},{6,4},{8,10},{10,8},{12,14},{14,12},{16,18},{18,... | collective-permute-start | bytes 7077896 | tf_op jit(solution)/shard_map/ppermute | solution.py:43
  804.7 37.0 %collective-permute-start.125 = (bf16[4,48,1536]{2,1,0:T(8,128)(2,1)S(1)}, bf16[4,48,1536]{2,1,0:T(8,128)(2,1)S(1)}, u32[]{:S(2)}, u32[]{:S(2)}) collective-permute-start(bf16[4,48,1536]{2,1,0:T(8,128)(2,1)S(1)} %fusion.81), channel_id=1, source_target_pairs={{0,4},{2,6},{4,0},{6,2},{8,12},{10,14},{12,8},{14,10},{16,20},{18,... | collective-permute-start | bytes 1769480 | tf_op jit(solution)/shard_map/ppermute | solution.py:43
  840.1 16.3 %collective-permute-start.142 = (bf16[4,48,3072]{2,1,0:T(8,128)(2,1)S(1)}, bf16[4,48,3072]{2,1,0:T(8,128)(2,1)S(1)}, u32[]{:S(2)}, u32[]{:S(2)}) collective-permute-start(bf16[4,48,3072]{2,1,0:T(8,128)(2,1)S(1)} %fusion.31), channel_id=1, source_target_pairs={{0,4},{2,6},{4,0},{6,2},{8,12},{10,14},{12,8},{14,10},{16,20},{18,... | collective-permute-start | bytes 3538952 | tf_op jit(solution)/shard_map/ppermute | solution.py:43
  846.8 14.3 %collective-permute-start.129 = (bf16[48,1536]{1,0:T(8,128)(2,1)S(1)}, bf16[48,1536]{1,0:T(8,128)(2,1)S(1)}, u32[]{:S(2)}, u32[]{:S(2)}) collective-permute-start(bf16[48,1536]{1,0:T(8,128)(2,1)S(1)} %get-tuple-element.138), channel_id=1, source_target_pairs={{8,0},{10,2},{12,4},{14,6},{16,8},{18,10},{20,12},{22,14},{24,16},... | collective-permute-start | bytes 442376 | tf_op jit(solution)/shard_map/ppermute | solution.py:61
  861.3 19.9 %collective-permute-start.128 = (bf16[48,1536]{1,0:T(8,128)(2,1)S(1)}, bf16[48,1536]{1,0:T(8,128)(2,1)S(1)}, u32[]{:S(2)}, u32[]{:S(2)}) collective-permute-start(bf16[48,1536]{1,0:T(8,128)(2,1)S(1)} %get-tuple-element.135), channel_id=1, source_target_pairs={{0,8},{2,10},{4,12},{6,14},{8,16},{10,18},{12,20},{14,22},{16,24},... | collective-permute-start | bytes 442376 | tf_op jit(solution)/shard_map/ppermute | solution.py:57
  (254 other events, 2149.2 us)

commit v2 on v1

--- a/solution.py
+++ b/solution.py
@@ -1,6 +1,8 @@
 import jax
 import jax.numpy as jnp
 from jax import lax
+from jax.experimental import pallas as pl
+from jax.experimental.pallas import tpu as pltpu
 from jax.sharding import PartitionSpec as P
 
 D = 768
@@ -53,12 +55,9 @@
     )
 
 
-def step_up(values_in):
-    return lax.ppermute(values_in, "dp", [(i, i + 4) for i in range(dp_size() - 4)])
-
-
-def step_down(values_in):
-    return lax.ppermute(values_in, "dp", [(i + 4, i) for i in range(dp_size() - 4)])
+def step_ring(values_in):
+    count = dp_size()
+    return lax.ppermute(values_in, "dp", [(i, (i + 4) % count) for i in range(count)])
 
 
 def line_groups():
@@ -71,46 +70,55 @@
     return lax.select_n(place, *choices)
 
 
-def line_gather(values_in):
+class Queue:
+    def __init__(self, depth):
+        self.arrived = [None] * depth
+
+    def send(self, transfer, values_in):
+        earlier = self.arrived.pop(0)
+        if earlier is not None:
+            values_in, _ = lax.optimization_barrier((values_in, earlier))
+        got = transfer(values_in)
+        self.arrived.append(got)
+        return got
+
+
+def line_gather(values_in, queue):
     count = line_size()
     if count > 4:
         return lax.all_gather(values_in, "dp", axis=0, axis_index_groups=line_groups())
-    below, above = [], []
-    rising = falling = values_in
+    got = [values_in]
     for step in range(count - 1):
-        rising, falling = step_up(rising), step_down(falling)
-        below.append(rising)
-        above.append(falling)
+        got.append(queue.send(step_ring, got[-1]))
     place = line_place()
-    slots = []
-    for slot in range(count):
-        choices = [
-            values_in
-            if slot == here
-            else (below[here - slot - 1] if slot < here else above[slot - here - 1])
-            for here in range(count)
-        ]
-        slots.append(pick(place, choices) if count > 1 else values_in)
-    return jnp.stack(slots)
+    if count == 1:
+        return values_in[None]
+    return jnp.stack(
+        [pick(place, [got[(here - slot) % count] for here in range(count)]) for slot in range(count)]
+    )
 
 
 def pair_up(own, other, place):
     return jnp.stack([pick(place, [own, other]), pick(place, [other, own])], axis=0)
 
 
-def line_y_gather(values_in):
-    lined = line_gather(values_in)
-    other = flip_dp(lined, 2)
+def line_y_gather(values_in, queues):
+    lined = line_gather(values_in, queues["line"])
+    other = queues["y"].send(lambda moved: flip_dp(moved, 2), lined)
     place = y_place()
     return jnp.stack([pick(place, [lined, other]), pick(place, [other, lined])], axis=1)
 
 
-def dp_gather(values_in):
-    gathered = line_y_gather(values_in)
-    other = flip_dp(gathered, 1)
-    place = x_place()
-    whole = jnp.stack([pick(place, [gathered, other]), pick(place, [other, gathered])], axis=2)
-    return whole.reshape(-1, values_in.shape[-1])
+def dp_gather(values_in, queues, y_first):
+    lined = line_gather(values_in, queues["line"])
+    order = (("y", 2, y_place(), 1), ("x", 1, x_place(), 2 if y_first else 1))
+    gathered = lined
+    for name, bit, place, axis in order if y_first else order[::-1]:
+        other = queues[name].send(lambda moved, bit=bit: flip_dp(moved, bit), gathered)
+        gathered = jnp.stack(
+            [pick(place, [gathered, other]), pick(place, [other, gathered])], axis=axis
+        )
+    return gathered.reshape(-1, values_in.shape[-1])
 
 
 def line_scatter(parts):
@@ -120,23 +128,14 @@
             parts, "dp", scatter_dimension=0, axis_index_groups=line_groups(), tiled=False
         )
     place = line_place()
-    own = lax.dynamic_index_in_dim(parts, place, 0, keepdims=False)
-    if count == 1:
-        return own
-    rising = falling = None
-    for step in range(count - 1, 0, -1):
-        to_above = lax.dynamic_index_in_dim(
-            parts, jnp.minimum(place + step, count - 1), 0, keepdims=False
-        )
-        to_below = lax.dynamic_index_in_dim(
-            parts, jnp.maximum(place - step, 0), 0, keepdims=False
-        )
-        if rising is not None:
-            to_above = to_above + rising
-            to_below = to_below + falling
-        rising = step_up(to_above.astype(BF16)).astype(F32)
-        falling = step_down(to_below.astype(BF16)).astype(F32)
-    return own + rising + falling
+
+    def slot(back):
+        return lax.dynamic_index_in_dim(parts, (place + count - back) % count, 0, keepdims=False)
+
+    total = slot(1 % count)
+    for back in range(2, count + 1):
+        total = slot(back % count) + step_ring(total.astype(BF16)).astype(F32)
+    return total
 
 
 def halve(parts, place, axis, bit):
@@ -319,8 +318,242 @@
     )
 
 
-def unchanged(values_in):
-    return values_in
+def norm_forward(stream, gain_row, bias_row):
+    centered = stream - jnp.mean(stream, axis=-1, keepdims=True)
+    scale = lax.rsqrt(jnp.mean(centered * centered, axis=-1, keepdims=True) + EPSILON)
+    unit = centered * scale
+    return unit * gain_row + bias_row, unit, scale
+
+
+def norm_backward(grad_out, unit, scale, gain_row):
+    grad_unit = grad_out * gain_row
+    first = jnp.mean(grad_unit, axis=-1, keepdims=True)
+    second = jnp.mean(grad_unit * unit, axis=-1, keepdims=True)
+    grad_in = scale * (grad_unit - first - unit * second)
+    grad_gain = jnp.sum(grad_out * unit, axis=0, keepdims=True)
+    grad_bias = jnp.sum(grad_out, axis=0, keepdims=True)
+    return grad_in, grad_gain, grad_bias
+
+
+GELU_A = 0.7978845608028654
+GELU_B = 0.044715
+TILE = 256
+BAND = 128
+PAIR = 2 * HD
+
+
+def local_body(
+    bound_ref, masked_ref, spread_ref, cotangent_ref, gain_ref, bias_ref,
+    attend_own_ref, attend_other_ref, forward_own_ref, forward_other_ref,
+    result_ref, grad_ref, grad_low_ref, normed_ref, second_ref, grad_out_ref, branch_ref,
+    packed_own_ref, packed_other_ref, mixture_own_ref, mixture_other_ref,
+    active_own_ref, active_other_ref, hidden_own_ref, hidden_other_ref, norms_ref,
+    probs_ref,
+):
+    rows = masked_ref.shape[0]
+    wide = mixture_own_ref.shape[1]
+    hidden_width = active_own_ref.shape[1]
+    attends = (attend_own_ref, attend_other_ref)
+    forwards = (forward_own_ref, forward_other_ref)
+    grad_packs = (packed_own_ref, packed_other_ref)
+    mixtures = (mixture_own_ref, mixture_other_ref)
+    actives = (active_own_ref, active_other_ref)
+    hiddens = (hidden_own_ref, hidden_other_ref)
+    bands = rows // BAND
+    pairs = wide // PAIR
+
+    row = pl.program_id(0) * rows + lax.broadcasted_iota(jnp.int32, (rows, 1), 0)
+    keep = (row < bound_ref[0]).astype(F32)
+    stream = masked_ref[...].astype(F32) + spread_ref[...].astype(F32)
+    gain_one, gain_two = gain_ref[2:3, :], gain_ref[3:4, :]
+    normed, unit_one, scale_one = norm_forward(stream, gain_one, bias_ref[2:3, :])
+    normed = normed.astype(BF16)
+    normed_ref[...] = normed
+    packs = [dot_nn(normed, attend[:, : 3 * wide]).astype(BF16) for attend in attends]
+
+    lanes = lax.broadcasted_iota(jnp.int32, (BAND, PAIR), 1)
+    low_head = lanes < HD
+    down_rows = lax.broadcasted_iota(jnp.int32, (2 * BAND, BAND), 0) % BAND
+    key_rows = lax.broadcasted_iota(jnp.int32, (2 * BAND, BAND), 1)
+    allowed = (down_rows // P_SIZE == key_rows // P_SIZE) & (down_rows >= key_rows)
+
+    def apart(pair_values):
+        zero = jnp.zeros_like(pair_values)
+        return jnp.concatenate(
+            [jnp.where(low_head, pair_values, zero), jnp.where(low_head, zero, pair_values)], axis=0
+        )
+
+    def joined(stacked):
+        return jnp.where(low_head, stacked[:BAND], stacked[BAND:])
+
+    def piece(values_in, band, part, pair):
+        start = part * wide + pair * PAIR
+        return values_in[band * BAND : (band + 1) * BAND, start : start + PAIR]
+
+    scale = HD ** (-0.5)
+    for side in range(2):
+        for band in range(bands):
+            for pair in range(pairs):
+                queries = apart(piece(packs[side], band, 0, pair)) * jnp.asarray(scale, BF16)
+                scores = dot_nt(queries, piece(packs[side], band, 1, pair))
+                scores = jnp.where(allowed, scores, NEGATIVE)
+                shifted = jnp.exp(scores - jnp.max(scores, axis=-1, keepdims=True))
+                probs = shifted / jnp.sum(shifted, axis=-1, keepdims=True)
+                probs_ref[(side * bands + band) * pairs + pair] = probs
+                mixed = dot_nn(probs.astype(BF16), piece(packs[side], band, 2, pair))
+                mixtures[side][
+                    band * BAND : (band + 1) * BAND, pair * PAIR : (pair + 1) * PAIR
+                ] = joined(mixed).astype(BF16)
+
+    middle = stream
+    for side in range(2):
+        middle = middle + dot_nt(mixtures[side][...], attends[side][:, 3 * wide :])
+    second, unit_two, scale_two = norm_forward(middle, gain_two, bias_ref[3:4, :])
+    second = second.astype(BF16)
+    second_ref[...] = second
+    grad_final = cotangent_ref[...].astype(F32) * keep
+    grad_out = grad_final.astype(BF16)
+    grad_out_ref[...] = grad_out
+
+    lifted = jnp.zeros_like(middle)
+    grad_second = jnp.zeros_like(middle)
+    chunk = min(768, hidden_width)
+    for side in range(2):
+        for start in range(0, hidden_width, chunk):
+            upward = forwards[side][:, start : start + chunk]
+            downward = forwards[side][:, hidden_width + start : hidden_width + start + chunk]
+            hidden = dot_nn(second, upward)
+            square = hidden * hidden
+            bent = jnp.tanh(GELU_A * hidden * (1.0 + GELU_B * square))
+            half = 0.5 * (1.0 + bent)
+            active = (hidden * half).astype(BF16)
+            slope = half + 0.5 * hidden * (1.0 - bent * bent) * GELU_A * (1.0 + 3.0 * GELU_B * square)
+            actives[side][:, start : start + chunk] = active
+            lifted = lifted + dot_nt(active, downward)
+            grad_hidden = (dot_nn(grad_out, downward) * slope).astype(BF16)
+            hiddens[side][:, start : start + chunk] = grad_hidden
+            grad_second = grad_second + dot_nt(grad_hidden, upward)
+    result_ref[...] = (middle + lifted).astype(BF16)
+
+    grad_in, gain_grad_two, bias_grad_two = norm_backward(grad_second, unit_two, scale_two, gain_two)
+    grad_middle = grad_final + grad_in
+    branch = grad_middle.astype(BF16)
+    branch_ref[...] = branch
+    grad_normed = jnp.zeros_like(middle)
+    for side in range(2):
+        grad_mix = dot_nn(branch, attends[side][:, 3 * wide :]).astype(BF16)
+        for band in range(bands):
+            for pair in range(pairs):
+                probs = probs_ref[(side * bands + band) * pairs + pair]
+                grad_pair = apart(piece(grad_mix, band, 0, pair))
+                grad_soft = dot_nt(grad_pair, piece(packs[side], band, 2, pair))
+                centre = jnp.sum(grad_soft * probs, axis=-1, keepdims=True)
+                grad_scores = (probs * (grad_soft - centre)).astype(BF16)
+                queries = apart(piece(packs[side], band, 0, pair))
+                grads = (
+                    joined(dot_nn(grad_scores, piece(packs[side], band, 1, pair))) * scale,
+                    dot_tn(grad_scores, queries) * scale,
+                    dot_tn(probs.astype(BF16), grad_pair),
+                )
+                for part in range(3):
+                    first = part * wide + pair * PAIR
+                    grad_packs[side][band * BAND : (band + 1) * BAND, first : first + PAIR] = (
+                        grads[part].astype(BF16)
+                    )
+        grad_normed = grad_normed + dot_nt(grad_packs[side][...], attends[side][:, : 3 * wide])
+    grad_in, gain_grad_one, bias_grad_one = norm_backward(grad_normed, unit_one, scale_one, gain_one)
+    grad_stream = grad_middle + grad_in
+    grad_ref[...] = grad_stream
+    grad_low_ref[...] = grad_stream.astype(BF16)
+
+    @pl.when(pl.program_id(0) == 0)
+    def _():
+        norms_ref[...] = jnp.zeros_like(norms_ref)
+
+    for place, value in enumerate((gain_grad_one, gain_grad_two, bias_grad_one, bias_grad_two)):
+        norms_ref[place : place + 1, :] += value
+
+
+def local_layer(bound, masked_low, spread, cotangent, gain_rows, bias_rows, attends, forwards):
+    rows = masked_low.shape[0]
+    wide = attends[0].shape[1] // 4
+    hidden_width = forwards[0].shape[1] // 2
+    tiled = lambda width: pl.BlockSpec((TILE, width), lambda i: (i, 0))
+    fixed = lambda array: pl.BlockSpec(
+        array.shape, lambda i: (0, 0), pipeline_mode=pl.Buffered(1)
+    )
+    widths = (
+        [(D, BF16), (D, F32)] + [(D, BF16)] * 5 + [(3 * wide, BF16)] * 2 + [(wide, BF16)] * 2
+        + [(hidden_width, BF16)] * 4
+    )
+    flops = 8 * rows * D * 2 * (4 * wide + 2 * hidden_width)
+    return pl.pallas_call(
+        local_body,
+        grid=(rows // TILE,),
+        in_specs=[pl.BlockSpec(memory_space=pltpu.SMEM)]
+        + [tiled(D)] * 3
+        + [fixed(array) for array in (gain_rows, bias_rows, *attends, *forwards)],
+        out_specs=[tiled(width) for width, _ in widths] + [pl.BlockSpec((8, D), lambda i: (0, 0))],
+        out_shape=[jax.ShapeDtypeStruct((rows, width), kind) for width, kind in widths]
+        + [jax.ShapeDtypeStruct((8, D), F32)],
+        scratch_shapes=[
+            pltpu.VMEM((2 * (TILE // BAND) * (wide // PAIR), 2 * BAND, BAND), F32)
+        ],
+        compiler_params=pltpu.CompilerParams(
+            dimension_semantics=("arbitrary",), vmem_limit_bytes=58 * 1024 * 1024
+        ),
+        cost_estimate=pl.CostEstimate(
+            flops=flops, transcendentals=rows * 2 * hidden_width, bytes_accessed=36 * 1024 * 1024
+        ),
+    )(bound, masked_low, spread, cotangent, gain_rows, bias_rows, *attends, *forwards)
+
+
+def grads_body(first_blocks, left_one_ref, right_one_ref, left_two_ref, right_two_ref, out_ref, turned_ref):
+    step = pl.program_id(0)
+
+    @pl.when(step == 0)
+    def _():
+        turned_ref[...] = left_one_ref[...].T
+
+    @pl.when(step == first_blocks)
+    def _():
+        turned_ref[...] = left_two_ref[...].T
+
+    @pl.when(step < first_blocks)
+    def _():
+        out_ref[...] = dot_nn(turned_ref[...], right_one_ref[...]).astype(BF16)
+
+    @pl.when(step >= first_blocks)
+    def _():
+        out_ref[...] = dot_nn(turned_ref[...], right_two_ref[...]).astype(BF16)
+
+
+def weight_grads(left_one, right_one, left_two, right_two):
+    rows, model = left_one.shape
+    block = 384
+    first, last = right_one.shape[1] // block, right_two.shape[1] // block
+    whole = pl.BlockSpec((rows, model), lambda j: (0, 0), pipeline_mode=pl.Buffered(1))
+    return pl.pallas_call(
+        lambda *refs: grads_body(first, *refs),
+        grid=(first + last,),
+        in_specs=[
+            whole,
+            pl.BlockSpec((rows, block), lambda j: (0, jnp.minimum(j, first - 1))),
+            whole,
+            pl.BlockSpec((rows, block), lambda j: (0, jnp.maximum(j - first, 0))),
+        ],
+        out_specs=pl.BlockSpec((model, block), lambda j: (0, j)),
+        out_shape=jax.ShapeDtypeStruct((model, (first + last) * block), BF16),
+        scratch_shapes=[pltpu.VMEM((model, rows), BF16)],
+        compiler_params=pltpu.CompilerParams(
+            dimension_semantics=("arbitrary",), vmem_limit_bytes=32 * 1024 * 1024
+        ),
+        cost_estimate=pl.CostEstimate(
+            flops=2 * rows * model * (first + last) * block,
+            transcendentals=0,
+            bytes_accessed=2 * (2 * rows * model + (rows + model) * (first + last) * block),
+        ),
+    )(left_one, right_one, left_two, right_two)
 
 
 def shards(
@@ -357,7 +590,8 @@
     norm_row = jnp.pad(
         jnp.concatenate([norm_gain, norm_bias]).reshape(1, -1), ((0, 0), (0, D - 2 * norm_part))
     )
-    patch_whole = line_y_gather(jnp.concatenate([patch_proj, norm_row], axis=0))
+    queues = {"line": Queue(2), "y": Queue(2), "x": Queue(2)}
+    patch_whole = line_y_gather(jnp.concatenate([patch_proj, norm_row], axis=0), queues)
     patch_whole = patch_whole.reshape(cells, proj_rows + 1, D)
     patch_mat = patch_whole[:, :proj_rows].reshape(cells * proj_rows, D)
     norm_cells = patch_whole[:, proj_rows, : 2 * norm_part]
@@ -391,8 +625,8 @@
     global_shard = global_shard.reshape(2 * shard_rows, -1)
     attend_columns = 2 * heads_width
     attend_shard, forward_shard = global_shard[:, :attend_columns], global_shard[:, attend_columns:]
-    attend_whole = line_y_gather(attend_shard).reshape(D, -1)
-    forward_whole = line_y_gather(forward_shard).reshape(D, -1)
+    attend_whole = line_y_gather(attend_shard, queues).reshape(D, -1)
+    forward_whole = line_y_gather(forward_shard, queues).reshape(D, -1)
     joint_columns = 3 * heads_width // 2
     first_weights = (
         attend_whole[:, :joint_columns],
@@ -400,27 +634,14 @@
         forward_whole[:, : hidden_width // 2],
         forward_whole[:, hidden_width // 2 :],
     )
-    spread_mat = line_y_gather(jnp.transpose(global_proj)).reshape(cells * proj_rows, D)
+    spread_mat = line_y_gather(jnp.transpose(global_proj), queues).reshape(cells * proj_rows, D)
 
     local_attend = jnp.concatenate([joint_part[1, 0], joint_part[1, 1], joint_part[1, 2], output_part[1]], axis=-1)
     local_forward = jnp.concatenate([up_weight[1], down_part[1]], axis=-1)
-    attend_own = dp_gather(local_attend)
-    forward_own = dp_gather(local_forward)
-    attend_other = flip_core(attend_own)
-    forward_other = flip_core(forward_own)
-    second_weights = (
-        jnp.concatenate(
-            [
-                source[:, k * heads_width : (k + 1) * heads_width]
-                for k in range(3)
-                for source in (attend_own, attend_other)
-            ],
-            axis=1,
-        ),
-        jnp.concatenate([attend_own[:, 3 * heads_width :], attend_other[:, 3 * heads_width :]], axis=1),
-        jnp.concatenate([forward_own[:, :hidden_width], forward_other[:, :hidden_width]], axis=1),
-        jnp.concatenate([forward_own[:, hidden_width:], forward_other[:, hidden_width:]], axis=1),
-    )
+    forward_own = dp_gather(local_forward, queues, False)
+    attend_own = dp_gather(local_attend, queues, True)
+    attends = (attend_own, flip_core(attend_own))
+    forwards = (forward_own, flip_core(forward_own))
 
     patches_dealt = quad_deal(masked_low.reshape(patch_rows, cells, QUAD, proj_rows))
     patches_mat = patches_dealt.reshape(QUAD * patch_rows, cells * proj_rows)
@@ -436,38 +657,20 @@
     spread = quad_collect(spread_dealt.reshape(QUAD * patch_rows, cells, proj_rows))
     spread = spread.reshape(half_rows, D)
 
-    local_places = jnp.arange(P_SIZE, dtype=jnp.int32)
-    outcome, second_saved = layer_forward(
-        masked_low.astype(F32) + spread.astype(F32),
-        second_weights, gain_rows, bias_rows, 2, local_places, unchanged, unchanged,
-    )
-    grad_final = cotangent[0].astype(F32) * keep_mask
-    grad_local, second_grads, second_gains, second_biases = layer_backward(
-        grad_final, second_saved, second_weights, gain_rows, bias_rows, 2, local_places, unchanged, unchanged
-    )
-    grad_joint, grad_output, grad_up, grad_down = second_grads
-
-    def own_columns(k, grads, width):
-        return grads[:, k * width : (k + 1) * width]
-
-    forward_grads = [
-        jnp.concatenate(
-            [own_columns(side, grad_up, hidden_width), own_columns(side, grad_down, hidden_width)], axis=1
-        )
-        for side in range(2)
-    ]
-    attend_grads = [
-        jnp.concatenate(
-            [own_columns(2 * k + side, grad_joint, heads_width) for k in range(3)]
-            + [own_columns(side, grad_output, heads_width)],
-            axis=1,
-        )
-        for side in range(2)
-    ]
-    forward_local = dp_scatter(forward_grads[0] + flip_core(forward_grads[1].astype(BF16)).astype(F32))
-    attend_local = dp_scatter(attend_grads[0] + flip_core(attend_grads[1].astype(BF16)).astype(F32))
-
-    grad_spread = grad_local.astype(BF16).reshape(patch_rows, cells, QUAD, proj_rows)
+    bound = jnp.clip(lengths - lax.axis_index("tensor") * half_rows, 0, half_rows)
+    (
+        outcome, grad_local, grad_low, normed, second, grad_out, branch, packed_own, packed_other,
+        mixture_own, mixture_other, active_own, active_other, hidden_own, hidden_other, local_norms,
+    ) = local_layer(bound, masked_low, spread, cotangent[0], gain_rows, bias_rows, attends, forwards)
+    second_gains, second_biases = (local_norms[0], local_norms[1]), (local_norms[2], local_norms[3])
+    forward_given = flip_core(weight_grads(second, hidden_other, grad_out, active_other))
+    forward_kept = weight_grads(second, hidden_own, grad_out, active_own)
+    forward_local = dp_scatter(forward_kept.astype(F32) + forward_given.astype(F32))
+    attend_given = flip_core(weight_grads(normed, packed_other, branch, mixture_other))
+    attend_kept = weight_grads(normed, packed_own, branch, mixture_own)
+    attend_local = dp_scatter(attend_kept.astype(F32) + attend_given.astype(F32))
+
+    grad_spread = grad_low.reshape(patch_rows, cells, QUAD, proj_rows)
     spread_grads = quad_deal(grad_spread).reshape(QUAD * patch_rows, cells * proj_rows)
     grad_global = quad_scatter(dot_nn(spread_grads, spread_mat))
     grad_proj = line_y_scatter(dot_tn(spread_grads, global_low).reshape(cells, proj_rows, D))
@@ -537,7 +740,7 @@
         ]
     )
     return (
-        outcome.astype(BF16)[None],
+        outcome[None],
         grad_input,
         patch_summed[:proj_rows],
         jnp.transpose(grad_proj),

time: 917 us -> 778 us (0.85)
  starting transfers between devices: 259 us -> 67.4 us
  waiting for transfers between devices: 287 us -> 418 us
  local copies, waits for them, and re-layouts: 177 us -> 115 us
  Pallas kernels: 0 us -> 59.8 us
  matrix products: 72.1 us -> 31.3 us
  other arithmetic: 101 us -> 71.3 us
    ppermute x72 -> x36, starting transfers between devices: 198 us -> 14.8 us  [step_ring(): lax.ppermute(values_in, 'dp', [(i, (i + 4) % count) for i in range(count)])]
    ppermute x72 -> x36, waiting for transfers between devices: 59.6 us -> 148 us  [step_ring(): lax.ppermute(values_in, 'dp', [(i, (i + 4) % count) for i in range(count)])]
    ppermute x19, waiting for transfers between devices: 133 us -> 202 us  [flip_dp(): lax.ppermute(values_in, 'dp', [(i, i ^ bit) for i in range(dp_size())])]
    pallas_call x0 -> x5, Pallas kernels: none -> 59.8 us  [the longest x1 38.6 us: local_layer(): pl.pallas_call(local_body, grid=(rows // TILE,), in_specs=[pl.BlockSpec(m...]
    ppermute x54, waiting for transfers between devices: 94.8 us -> 67.5 us  [flip_quad(): lax.ppermute(values_in, ('dp', 'tensor'), [(i, i ^ bits) for i in range(2...]
    slice x12 -> x4, local copies, waits for them, and re-layouts: 24.2 us -> 0.68 us  [the longest x1 0.6 us: shards(): local_norms[2]]
    dot_general x10 -> x6, matrix products: 22.7 us -> 10.6 us  [dot_nn(): lax.dot_general(left, right, (((1,), (0,)), ((), ())), preferred_element_...]
    dot_general x10 -> x6, matrix products: 16.2 us -> 5.41 us  [dot_tn(): lax.dot_general(left, right, (((0,), (0,)), ((), ())), preferred_element_...]
  transfers between devices with their start and end apart: 149 -> 113, of which waited for: 55 -> 57; matrix products, arithmetic and copies ran while one was open for 26% -> 24% of each run, Pallas kernels for 0% -> 3%
where the time goes in v2:
time: 778 us; the launch traced here: 767 us
  waiting for transfers between devices  418 us (54%)
  local copies, waits for them, and re-layouts  115 us (15%)
  other arithmetic  71.3 us (9%)
  starting transfers between devices  67.4 us (9%)
  Pallas kernels  59.8 us (8%)
  matrix products  31.3 us (4%)
    ppermute x19, waiting for transfers between devices, flip_dp(): lax.ppermute(values_in, 'dp', [(i, i ^ bit) for i in range(dp_size())])  202 us
    ppermute x36, waiting for transfers between devices, step_ring(): lax.ppermute(values_in, 'dp', [(i, (i + 4) % count) for i in range(count)])  148 us
    ppermute x54, waiting for transfers between devices, flip_quad(): lax.ppermute(values_in, ('dp', 'tensor'), [(i, i ^ bits) for i in range(2...  67.5 us
    pallas_call x1, Pallas kernels, local_layer(): pl.pallas_call(local_body, grid=(rows // TILE,), in_specs=[pl.BlockSpec(m...  38.6 us
    ppermute x54, starting transfers between devices, flip_quad(): lax.ppermute(values_in, ('dp', 'tensor'), [(i, i ^ bits) for i in range(2...  35.6 us
    unnamed x333, local copies, waits for them, and re-layouts  21.4 us
    pallas_call x4, Pallas kernels, weight_grads(): pl.pallas_call(lambda *refs: grads_body(first, *refs), grid=(first + last...  21.1 us
    ppermute x19, starting transfers between devices, flip_dp(): lax.ppermute(values_in, 'dp', [(i, i ^ bit) for i in range(dp_size())])  16.6 us
  transfers between devices with their start and end apart: 113, of which 57 were waited for; matrix products, arithmetic and copies ran while one was open for 24% of the time, Pallas kernels for 3%

profile of v2, /device:TPU:4, one launch (start us, length us, event | category | flops | bytes accessed | tf_op | source)
XLA Modules:
  0.0 766.7 jit_solution(8217301111453193687)
XLA Ops:
  21.8 9.5 %collective-permute-done.4 = bf16[193,768]{1,0:T(8,128)(2,1)} collective-permute-done((bf16[193,768]{1,0:T(8,128)(2,1)}, bf16[193,768]{1,0:T(8,128)(2,1)}, u32[]{:S(2)}, u32[]{:S(2)}) %collective-permute-start.4) | collective-permute-done | bytes 296480 | tf_op jit(solution)/shard_map/ppermute | solution.py:60
  36.3 8.3 %collective-permute-done.17 = bf16[96,768]{1,0:T(8,128)(2,1)S(1)} collective-permute-done((bf16[96,768]{1,0:T(8,128)(2,1)S(1)}, bf16[96,768]{1,0:T(8,128)(2,1)S(1)}, u32[]{:S(2)}, u32[]{:S(2)}) %collective-permute-start.17) | collective-permute-done | bytes 147488 | tf_op jit(solution)/shard_map/ppermute | solution.py:60
  45.7 5.8 collective-permute-done.18
  55.3 4.7 collective-permute-done.19
  61.1 3.3 collective-permute-done.27
  67.9 8.3 %collective-permute-done.2 = bf16[64,8,192]{0,2,1:T(8,128)(2,1)} collective-permute-done((bf16[64,8,192]{0,2,1:T(8,128)(2,1)}, bf16[64,8,192]{0,2,1:T(8,128)(2,1)}, u32[]{:S(2)}, u32[]{:S(2)}) %collective-permute-start.2) | collective-permute-done | bytes 196640 | tf_op jit(solution)/shard_map/ppermute | solution.py:53
  79.8 2.6 collective-permute-start.37
  82.4 10.3 %collective-permute-done.20 = bf16[4,96,768]{2,1,0:T(8,128)(2,1)} collective-permute-done((bf16[4,96,768]{2,1,0:T(8,128)(2,1)S(1)}, bf16[4,96,768]{2,1,0:T(8,128)(2,1)}, u32[]{:S(2)}, u32[]{:S(2)}) %collective-permute-start.20) | collective-permute-done | bytes 589856 | tf_op jit(solution)/shard_map/ppermute | solution.py:45
  100.3 3.0 fusion.162
  108.0 2.7 collective-permute-done.8
  121.3 5.6 collective-permute-done.39
  126.8 5.8 collective-permute-done.44
  136.7 6.4 collective-permute-done.45
  145.6 7.0 collective-permute-done.47
  165.0 18.2 %collective-permute-done.23 = bf16[64,768]{1,0:T(8,128)(2,1)S(1)} collective-permute-done((bf16[64,768]{1,0:T(8,128)(2,1)}, bf16[64,768]{1,0:T(8,128)(2,1)S(1)}, u32[]{:S(2)}, u32[]{:S(2)}) %collective-permute-start.23) | collective-permute-done | bytes 98336 | tf_op jit(solution)/shard_map/ppermute | solution.py:53
  183.2 3.2 collective-permute-done.22
  189.7 5.3 collective-permute-done.48
  197.6 4.7 collective-permute-done.49
  202.6 15.6 %collective-permute-done.40 = bf16[4,192,768]{2,1,0:T(8,128)(2,1)S(1)} collective-permute-done((bf16[4,192,768]{2,1,0:T(8,128)(2,1)S(1)}, bf16[4,192,768]{2,1,0:T(8,128)(2,1)S(1)}, u32[]{:S(2)}, u32[]{:S(2)}) %collective-permute-start.40) | collective-permute-done | bytes 1179680 | tf_op jit(solution)/shard_map/ppermute | solution.py:45
  221.3 58.8 %collective-permute-done.50 = bf16[4,48,1536]{2,1,0:T(8,128)(2,1)S(1)} collective-permute-done((bf16[4,48,1536]{2,1,0:T(8,128)(2,1)S(1)}, bf16[4,48,1536]{2,1,0:T(8,128)(2,1)S(1)}, u32[]{:S(2)}, u32[]{:S(2)}) %collective-permute-start.50) | collective-permute-done | bytes 589856 | tf_op jit(solution)/shard_map/ppermute | solution.py:45
  282.3 2.6 copy.289
  292.6 16.6 %collective-permute-done.51 = bf16[4,2,48,1536]{3,2,0,1:T(8,128)(2,1)S(1)} collective-permute-done((bf16[4,2,48,1536]{3,2,0,1:T(8,128)(2,1)S(1)}, bf16[4,2,48,1536]{3,2,0,1:T(8,128)(2,1)S(1)}, u32[]{:S(2)}, u32[]{:S(2)}) %collective-permute-start.51) | collective-permute-done | bytes 1179680 | tf_op jit(solution)/shard_map/ppermute | solution.py:45
  322.6 2.7 collective-permute-done.35
  330.9 4.2 collective-permute-done.43
  335.1 6.2 collective-permute-done.42
  344.9 38.6 %shard_map.186 = (bf16[512,768]{1,0:T(8,128)(2,1)}, f32[512,768]{1,0:T(8,128)}, bf16[512,768]{1,0:T(8,128)(2,1)}, bf16[512,768]{1,0:T(8,128)(2,1)}, bf16[512,768...) custom-call(s32[1]{0:T(128)S(6)} %min.6.bound_ref, ...), custom_call_target="tpu_custom_call" | custom-call | flops 28991029248 | bytes 37748736 | tf_op jit(solution)/shard_map/pallas_call | solution.py:490
  383.6 2.7 reshape.267
  386.3 4.0 constant_dynamic-slice_fusion.4
  399.7 4.2 shard_map.188
  404.2 3.3 shard_map.187
  407.6 6.6 shard_map.189
  416.5 7.0 shard_map.190
  434.7 3.6 fusion.166
  445.5 2.6 collective-permute-done.60
  465.0 6.0 copy.315
  474.6 2.8 fusion.8
  492.6 3.2 copy.310
  506.8 3.1 collective-permute-done.76
  512.2 2.5 convolution_convert_fusion
  524.2 2.6 select_maximum_fusion
  531.2 3.7 collective-permute-done.78
  537.5 2.7 copy.302
  540.2 3.4 reshape.287
  547.1 5.3 collective-permute-done.92
  553.5 5.8 collective-permute-done.87
  561.6 4.6 collective-permute-done.93
  566.3 18.3 %collective-permute-done.102 = bf16[4,96,1536]{2,1,0:T(8,128)(2,1)} collective-permute-done((bf16[4,96,1536]{2,1,0:T(8,128)(2,1)}, bf16[4,96,1536]{2,1,0:T(8,128)(2,1)}, u32[]{:S(2)}, u32[]{:S(2)}) %collective-permute-start.102) | collective-permute-done | bytes 1179680 | tf_op jit(solution)/shard_map/ppermute | solution.py:45
  586.3 5.2 collective-permute-done.94
  592.7 3.3 collective-permute-done.95
  598.3 4.7 collective-permute-done.103
  603.1 6.2 collective-permute-done.89
  609.9 5.8 collective-permute-done.104
  615.8 6.2 collective-permute-done.90
  622.8 5.7 collective-permute-done.84
  628.9 2.5 convert_add_fusion.1
  636.0 2.7 collective-permute-done.85
  638.9 4.2 convert_add_fusion
  644.4 19.3 %collective-permute-done.106 = bf16[48,1536]{1,0:T(8,128)(2,1)S(1)} collective-permute-done((bf16[48,1536]{1,0:T(8,128)(2,1)S(1)}, bf16[48,1536]{1,0:T(8,128)(2,1)S(1)}, u32[]{:S(2)}, u32[]{:S(2)}) %collective-permute-start.106) | collective-permute-done | bytes 147488 | tf_op jit(solution)/shard_map/ppermute | solution.py:45
  668.0 39.9 %collective-permute-done.108 = bf16[4,2,48,3072]{3,2,0,1:T(8,128)(2,1)S(1)} collective-permute-done((bf16[4,2,48,3072]{3,2,0,1:T(8,128)(2,1)S(1)}, bf16[4,2,48,3072]{3,2,0,1:T(8,128)(2,1)S(1)}, u32[]{:S(2)}, u32[]{:S(2)}) %collective-permute-start.108) | collective-permute-done | bytes 2359328 | tf_op jit(solution)/shard_map/ppermute | solution.py:45
  710.9 6.3 collective-permute-done.99
  717.4 13.4 %collective-permute-done.109 = bf16[4,48,3072]{2,1,0:T(8,128)(2,1)S(1)} collective-permute-done((bf16[4,48,3072]{2,1,0:T(8,128)(2,1)S(1)}, bf16[4,48,3072]{2,1,0:T(8,128)(2,1)S(1)}, u32[]{:S(2)}, u32[]{:S(2)}) %collective-permute-start.109) | collective-permute-done | bytes 1179680 | tf_op jit(solution)/shard_map/ppermute | solution.py:45
  731.2 11.3 %collective-permute-done.110 = bf16[48,3072]{1,0:T(8,128)(2,1)S(1)} collective-permute-done((bf16[48,3072]{1,0:T(8,128)(2,1)S(1)}, bf16[48,3072]{1,0:T(8,128)(2,1)S(1)}, u32[]{:S(2)}, u32[]{:S(2)}) %collective-permute-start.110) | collective-permute-done | bytes 294944 | tf_op jit(solution)/shard_map/ppermute | solution.py:60
  748.8 6.2 collective-permute-done.111
  756.8 7.8 %collective-permute-done.112 = bf16[48,3072]{1,0:T(8,128)(2,1)S(1)} collective-permute-done((bf16[48,3072]{1,0:T(8,128)(2,1)S(1)}, bf16[48,3072]{1,0:T(8,128)(2,1)S(1)}, u32[]{:S(2)}, u32[]{:S(2)}) %collective-permute-start.112) | collective-permute-done | bytes 294944 | tf_op jit(solution)/shard_map/ppermute | solution.py:60
  (770 shorter events, 253.0 us)
Async XLA Ops:
  3.2 16.9 %collective-permute-start.3 = (bf16[193,768]{1,0:T(8,128)(2,1)}, bf16[193,768]{1,0:T(8,128)(2,1)}, u32[]{:S(2)}, u32[]{:S(2)}) collective-permute-start(bf16[193,768]{1,0:T(8,128)(2,1)} %fusion.64), channel_id=1, source_target_pairs={{0,8},{2,10},{4,12},{6,14},{8,16},{10,18},{12,20},{14,22},{16,24},... | collective-permute-start | bytes 889352 | tf_op jit(solution)/shard_map/ppermute | solution.py:60
  17.2 47.3 %collective-permute-start = (bf16[64,8,192]{0,2,1:T(8,128)(2,1)}, bf16[64,8,192]{0,2,1:T(8,128)(2,1)S(1)}, u32[]{:S(2)}, u32[]{:S(2)}) collective-permute-start(bf16[64,8,192]{0,2,1:T(8,128)(2,1)} %bitcast.4), channel_id=1, source_target_pairs={{0,1},{1,0},{2,3},{3,2},{4,5},{5,4},{6,7},{7,6},{8,9},{9,8},{10,11... | collective-permute-start | bytes 589832 | tf_op jit(solution)/shard_map/ppermute | solution.py:53
  18.2 47.9 %collective-permute-start.1 = (bf16[64,8,192]{0,2,1:T(8,128)(2,1)}, bf16[64,8,192]{0,2,1:T(8,128)(2,1)}, u32[]{:S(2)}, u32[]{:S(2)}) collective-permute-start(bf16[64,8,192]{0,2,1:T(8,128)(2,1)} %bitcast.5), channel_id=1, source_target_pairs={{0,2},{1,3},{2,0},{3,1},{4,6},{5,7},{6,4},{7,5},{8,10},{9,11},{10,... | collective-permute-start | bytes 589832 | tf_op jit(solution)/shard_map/ppermute | solution.py:53
  31.3 13.3 %collective-permute-start.5 = (bf16[193,768]{1,0:T(8,128)(2,1)}, bf16[193,768]{1,0:T(8,128)(2,1)}, u32[]{:S(2)}, u32[]{:S(2)}) collective-permute-start(bf16[193,768]{1,0:T(8,128)(2,1)} %collective-permute-done.4), channel_id=1, source_target_pairs={{0,8},{2,10},{4,12},{6,14},{8,16},{10,18},{12,20},{14,22},{16,24},... | collective-permute-start | bytes 889352 | tf_op jit(solution)/shard_map/ppermute | solution.py:60
  31.3 13.3 %collective-permute-start.17 = (bf16[96,768]{1,0:T(8,128)(2,1)S(1)}, bf16[96,768]{1,0:T(8,128)(2,1)S(1)}, u32[]{:S(2)}, u32[]{:S(2)}) collective-permute-start(bf16[96,768]{1,0:T(8,128)(2,1)S(1)} %slice.394), channel_id=1, source_target_pairs={{0,8},{2,10},{4,12},{6,14},{8,16},{10,18},{12,20},{14,22},{16,24},... | collective-permute-start | bytes 442376 | tf_op jit(solution)/shard_map/ppermute | solution.py:60
  54.8 41.2 %collective-permute-start.6 = (bf16[4,193,768]{2,0,1:T(4,128)(2,1)}, bf16[4,193,768]{2,0,1:T(4,128)(2,1)}, u32[]{:S(2)}, u32[]{:S(2)}) collective-permute-start(bf16[4,193,768]{2,0,1:T(4,128)(2,1)} %copy.269), channel_id=1, source_target_pairs={{0,4},{2,6},{4,0},{6,2},{8,12},{10,14},{12,8},{14,10},{16,20},{18,... | collective-permute-start | bytes 3557384 | tf_op jit(solution)/shard_map/ppermute | solution.py:45
  60.1 32.6 %collective-permute-start.20 = (bf16[4,96,768]{2,1,0:T(8,128)(2,1)S(1)}, bf16[4,96,768]{2,1,0:T(8,128)(2,1)}, u32[]{:S(2)}, u32[]{:S(2)}) collective-permute-start(bf16[4,96,768]{2,1,0:T(8,128)(2,1)S(1)} %pad_maximum_fusion.15), channel_id=1, source_target_pairs={{0,4},{2,6},{4,0},{6,2},{8,12},{10,14},{12,8},{14,10},{16,20},{18,... | collective-permute-start | bytes 1769480 | tf_op jit(solution)/shard_map/ppermute | solution.py:45
  64.4 13.6 %collective-permute-start.28 = (bf16[96,1536]{1,0:T(8,128)(2,1)}, bf16[96,1536]{1,0:T(8,128)(2,1)}, u32[]{:S(2)}, u32[]{:S(2)}) collective-permute-start(bf16[96,1536]{1,0:T(8,128)(2,1)} %collective-permute-done.27), channel_id=1, source_target_pairs={{0,8},{2,10},{4,12},{6,14},{8,16},{10,18},{12,20},{14,22},{16,24},... | collective-permute-start | bytes 884744 | tf_op jit(solution)/shard_map/ppermute | solution.py:60
  64.5 11.7 %collective-permute-start.2 = (bf16[64,8,192]{0,2,1:T(8,128)(2,1)}, bf16[64,8,192]{0,2,1:T(8,128)(2,1)}, u32[]{:S(2)}, u32[]{:S(2)}) collective-permute-start(bf16[64,8,192]{0,2,1:T(8,128)(2,1)} %bitcast.6), channel_id=1, source_target_pairs={{0,3},{1,2},{2,1},{3,0},{4,7},{5,6},{6,5},{7,4},{8,11},{9,10},{10,... | collective-permute-start | bytes 589832 | tf_op jit(solution)/shard_map/ppermute | solution.py:53
  78.0 17.1 %collective-permute-start.29 = (bf16[96,1536]{1,0:T(8,128)(2,1)}, bf16[96,1536]{1,0:T(8,128)(2,1)S(1)}, u32[]{:S(2)}, u32[]{:S(2)}) collective-permute-start(bf16[96,1536]{1,0:T(8,128)(2,1)} %collective-permute-done.28), channel_id=1, source_target_pairs={{0,8},{2,10},{4,12},{6,14},{8,16},{10,18},{12,20},{14,22},{16,24},... | collective-permute-start | bytes 884744 | tf_op jit(solution)/shard_map/ppermute | solution.py:60
  79.8 16.0 %collective-permute-start.37 = (bf16[192,768]{1,0:T(8,128)(2,1)}, bf16[192,768]{1,0:T(8,128)(2,1)}, u32[]{:S(2)}, u32[]{:S(2)}) collective-permute-start(bf16[192,768]{1,0:T(8,128)(2,1)} %bitcast.560), channel_id=1, source_target_pairs={{0,8},{2,10},{4,12},{6,14},{8,16},{10,18},{12,20},{14,22},{16,24},... | collective-permute-start | bytes 884744 | tf_op jit(solution)/shard_map/ppermute | solution.py:60
  95.8 19.2 %collective-permute-start.38 = (bf16[192,768]{1,0:T(8,128)(2,1)}, bf16[192,768]{1,0:T(8,128)(2,1)}, u32[]{:S(2)}, u32[]{:S(2)}) collective-permute-start(bf16[192,768]{1,0:T(8,128)(2,1)} %collective-permute-done.37), channel_id=1, source_target_pairs={{0,8},{2,10},{4,12},{6,14},{8,16},{10,18},{12,20},{14,22},{16,24},... | collective-permute-start | bytes 884744 | tf_op jit(solution)/shard_map/ppermute | solution.py:60
  113.1 19.8 %collective-permute-start.15 = (bf16[64,768]{1,0:T(8,128)(2,1)S(1)}, bf16[64,768]{1,0:T(8,128)(2,1)S(1)}, u32[]{:S(2)}, u32[]{:S(2)}) collective-permute-start(bf16[64,768]{1,0:T(8,128)(2,1)S(1)} %add_convert_fusion.2), channel_id=1, source_target_pairs={{0,3},{1,2},{2,1},{3,0},{4,7},{5,6},{6,5},{7,4},{8,11},{9,10},{10,... | collective-permute-start | bytes 294920 | tf_op jit(solution)/shard_map/ppermute | solution.py:53
  113.6 19.3 %collective-permute-start.14 = (bf16[64,768]{1,0:T(8,128)(2,1)S(1)}, bf16[64,768]{1,0:T(8,128)(2,1)S(1)}, u32[]{:S(2)}, u32[]{:S(2)}) collective-permute-start(bf16[64,768]{1,0:T(8,128)(2,1)S(1)} %add_convert_fusion.2), channel_id=1, source_target_pairs={{0,2},{1,3},{2,0},{3,1},{4,6},{5,7},{6,4},{7,5},{8,10},{9,11},{10,... | collective-permute-start | bytes 294920 | tf_op jit(solution)/shard_map/ppermute | solution.py:53
  114.5 18.4 %collective-permute-start.13 = (bf16[64,768]{1,0:T(8,128)(2,1)S(1)}, bf16[64,768]{1,0:T(8,128)(2,1)S(1)}, u32[]{:S(2)}, u32[]{:S(2)}) collective-permute-start(bf16[64,768]{1,0:T(8,128)(2,1)S(1)} %add_convert_fusion.2), channel_id=1, source_target_pairs={{0,1},{1,0},{2,3},{3,2},{4,5},{5,4},{6,7},{7,6},{8,9},{9,8},{10,11... | collective-permute-start | bytes 294920 | tf_op jit(solution)/shard_map/ppermute | solution.py:53
  115.0 11.8 %collective-permute-start.39 = (bf16[192,768]{1,0:T(8,128)(2,1)}, bf16[192,768]{1,0:T(8,128)(2,1)S(1)}, u32[]{:S(2)}, u32[]{:S(2)}) collective-permute-start(bf16[192,768]{1,0:T(8,128)(2,1)} %collective-permute-done.38), channel_id=1, source_target_pairs={{0,8},{2,10},{4,12},{6,14},{8,16},{10,18},{12,20},{14,22},{16,24},... | collective-permute-start | bytes 884744 | tf_op jit(solution)/shard_map/ppermute | solution.py:60
  117.3 15.3 %collective-permute-start.44 = (bf16[48,3072]{1,0:T(8,128)(2,1)}, bf16[48,3072]{1,0:T(8,128)(2,1)}, u32[]{:S(2)}, u32[]{:S(2)}) collective-permute-start(bf16[48,3072]{1,0:T(8,128)(2,1)} %pad_maximum_fusion.27), channel_id=1, source_target_pairs={{0,8},{2,10},{4,12},{6,14},{8,16},{10,18},{12,20},{14,22},{16,24},... | collective-permute-start | bytes 884744 | tf_op jit(solution)/shard_map/ppermute | solution.py:60
  156.4 39.0 %collective-permute-start.53 = (bf16[4,48,3072]{2,1,0:T(8,128)(2,1)}, bf16[4,48,3072]{2,1,0:T(8,128)(2,1)}, u32[]{:S(2)}, u32[]{:S(2)}) collective-permute-start(bf16[4,48,3072]{2,1,0:T(8,128)(2,1)} %pad_maximum_fusion.13), channel_id=1, source_target_pairs={{0,2},{2,0},{4,6},{6,4},{8,10},{10,8},{12,14},{14,12},{16,18},{18,... | collective-permute-start | bytes 3538952 | tf_op jit(solution)/shard_map/ppermute | solution.py:45
  159.9 23.3 %collective-permute-start.23 = (bf16[64,768]{1,0:T(8,128)(2,1)}, bf16[64,768]{1,0:T(8,128)(2,1)S(1)}, u32[]{:S(2)}, u32[]{:S(2)}) collective-permute-start(bf16[64,768]{1,0:T(8,128)(2,1)} %get-tuple-element.236), channel_id=1, source_target_pairs={{0,3},{1,2},{2,1},{3,0},{4,7},{5,6},{6,5},{7,4},{8,11},{9,10},{10,... | collective-permute-start | bytes 294920 | tf_op jit(solution)/shard_map/ppermute | solution.py:53
  161.6 24.8 %collective-permute-start.22 = (bf16[64,768]{1,0:T(8,128)(2,1)S(1)}, bf16[64,768]{1,0:T(8,128)(2,1)}, u32[]{:S(2)}, u32[]{:S(2)}) collective-permute-start(bf16[64,768]{1,0:T(8,128)(2,1)S(1)} %get-tuple-element.237), channel_id=1, source_target_pairs={{0,2},{1,3},{2,0},{3,1},{4,6},{5,7},{6,4},{7,5},{8,10},{9,11},{10,... | collective-permute-start | bytes 294920 | tf_op jit(solution)/shard_map/ppermute | solution.py:53
  163.3 34.0 %collective-permute-start.30 = (bf16[4,96,1536]{2,1,0:T(8,128)(2,1)}, bf16[4,96,1536]{2,1,0:T(8,128)(2,1)}, u32[]{:S(2)}, u32[]{:S(2)}) collective-permute-start(bf16[4,96,1536]{2,1,0:T(8,128)(2,1)} %pad_maximum_fusion.10), channel_id=1, source_target_pairs={{0,4},{2,6},{4,0},{6,2},{8,12},{10,14},{12,8},{14,10},{16,20},{18,... | collective-permute-start | bytes 3538952 | tf_op jit(solution)/shard_map/ppermute | solution.py:45
  165.0 22.6 %collective-permute-start.46 = (bf16[48,1536]{1,0:T(8,128)(2,1)}, bf16[48,1536]{1,0:T(8,128)(2,1)S(1)}, u32[]{:S(2)}, u32[]{:S(2)}) collective-permute-start(bf16[48,1536]{1,0:T(8,128)(2,1)} %pad_maximum_fusion.28), channel_id=1, source_target_pairs={{0,8},{2,10},{4,12},{6,14},{8,16},{10,18},{12,20},{14,22},{16,24},... | collective-permute-start | bytes 442376 | tf_op jit(solution)/shard_map/ppermute | solution.py:60
  189.3 28.9 %collective-permute-start.40 = (bf16[4,192,768]{2,1,0:T(8,128)(2,1)S(1)}, bf16[4,192,768]{2,1,0:T(8,128)(2,1)S(1)}, u32[]{:S(2)}, u32[]{:S(2)}) collective-permute-start(bf16[4,192,768]{2,1,0:T(8,128)(2,1)S(1)} %pad_maximum_fusion.11), channel_id=1, source_target_pairs={{0,4},{2,6},{4,0},{6,2},{8,12},{10,14},{12,8},{14,10},{16,20},{18,... | collective-permute-start | bytes 3538952 | tf_op jit(solution)/shard_map/ppermute | solution.py:45
  197.3 84.2 %collective-permute-start.54 = (bf16[4,2,48,3072]{3,2,0,1:T(8,128)(2,1)S(1)}, bf16[4,2,48,3072]{3,2,0,1:T(8,128)(2,1)S(1)}, u32[]{:S(2)}, u32[]{:S(2)}) collective-permute-start(bf16[4,2,48,3072]{3,2,0,1:T(8,128)(2,1)S(1)} %pad_maximum_fusion.6), channel_id=1, source_target_pairs={{0,4},{2,6},{4,0},{6,2},{8,12},{10,14},{12,8},{14,10},{16,20},{18,... | collective-permute-start | bytes 7077896 | tf_op jit(solution)/shard_map/ppermute | solution.py:45
  218.3 61.9 %collective-permute-start.50 = (bf16[4,48,1536]{2,1,0:T(8,128)(2,1)S(1)}, bf16[4,48,1536]{2,1,0:T(8,128)(2,1)S(1)}, u32[]{:S(2)}, u32[]{:S(2)}) collective-permute-start(bf16[4,48,1536]{2,1,0:T(8,128)(2,1)S(1)} %pad_maximum_fusion.16), channel_id=1, source_target_pairs={{0,4},{2,6},{4,0},{6,2},{8,12},{10,14},{12,8},{14,10},{16,20},{18,... | collective-permute-start | bytes 1769480 | tf_op jit(solution)/shard_map/ppermute | solution.py:45
  219.4 67.4 %collective-permute-start.26 = (bf16[64,768]{1,0:T(8,128)(2,1)S(1)}, bf16[64,768]{1,0:T(8,128)(2,1)S(1)}, u32[]{:S(2)}, u32[]{:S(2)}) collective-permute-start(bf16[64,768]{1,0:T(8,128)(2,1)S(1)} %add_convert_fusion.1), channel_id=1, source_target_pairs={{0,3},{1,2},{2,1},{3,0},{4,7},{5,6},{6,5},{7,4},{8,11},{9,10},{10,... | collective-permute-start | bytes 294920 | tf_op jit(solution)/shard_map/ppermute | solution.py:53
  219.5 67.4 %collective-permute-start.25 = (bf16[64,768]{1,0:T(8,128)(2,1)S(1)}, bf16[64,768]{1,0:T(8,128)(2,1)S(1)}, u32[]{:S(2)}, u32[]{:S(2)}) collective-permute-start(bf16[64,768]{1,0:T(8,128)(2,1)S(1)} %add_convert_fusion.1), channel_id=1, source_target_pairs={{0,2},{1,3},{2,0},{3,1},{4,6},{5,7},{6,4},{7,5},{8,10},{9,11},{10,... | collective-permute-start | bytes 294920 | tf_op jit(solution)/shard_map/ppermute | solution.py:53
  221.3 65.6 %collective-permute-start.24 = (bf16[64,768]{1,0:T(8,128)(2,1)S(1)}, bf16[64,768]{1,0:T(8,128)(2,1)S(1)}, u32[]{:S(2)}, u32[]{:S(2)}) collective-permute-start(bf16[64,768]{1,0:T(8,128)(2,1)S(1)} %add_convert_fusion.1), channel_id=1, source_target_pairs={{0,1},{1,0},{2,3},{3,2},{4,5},{5,4},{6,7},{7,6},{8,9},{9,8},{10,11... | collective-permute-start | bytes 294920 | tf_op jit(solution)/shard_map/ppermute | solution.py:53
  280.4 28.9 %collective-permute-start.51 = (bf16[4,2,48,1536]{3,2,0,1:T(8,128)(2,1)S(1)}, bf16[4,2,48,1536]{3,2,0,1:T(8,128)(2,1)S(1)}, u32[]{:S(2)}, u32[]{:S(2)}) collective-permute-start(bf16[4,2,48,1536]{3,2,0,1:T(8,128)(2,1)S(1)} %pad_maximum_fusion.12), channel_id=1, source_target_pairs={{0,2},{2,0},{4,6},{6,4},{8,10},{10,8},{12,14},{14,12},{16,18},{18,... | collective-permute-start | bytes 3538952 | tf_op jit(solution)/shard_map/ppermute | solution.py:45
  284.9 60.0 %collective-permute-start.55 = (bf16[768,3072]{1,0:T(8,128)(2,1)}, bf16[768,3072]{1,0:T(8,128)(2,1)}, u32[]{:S(2)}, u32[]{:S(2)}) collective-permute-start(bf16[768,3072]{1,0:T(8,128)(2,1)} %bitcast.83.forward_own_ref), channel_id=1, source_target_pairs={{0,1},{1,0},{2,3},{3,2},{4,5},{5,4},{6,7},{7,6},{8,9},{9,8},{10,11... | collective-permute-start | bytes 14155784 | tf_op jit(solution)/shard_map/ppermute | solution.py:49
  290.5 25.7 %collective-permute-start.31 = (bf16[64,768]{1,0:T(8,128)(2,1)}, bf16[64,768]{1,0:T(8,128)(2,1)S(1)}, u32[]{:S(2)}, u32[]{:S(2)}) collective-permute-start(bf16[64,768]{1,0:T(8,128)(2,1)} %get-tuple-element.232), channel_id=1, source_target_pairs={{0,1},{1,0},{2,3},{3,2},{4,5},{5,4},{6,7},{7,6},{8,9},{9,8},{10,11... | collective-permute-start | bytes 294920 | tf_op jit(solution)/shard_map/ppermute | solution.py:53
  291.0 25.3 %collective-permute-start.33 = (bf16[64,768]{1,0:T(8,128)(2,1)}, bf16[64,768]{1,0:T(8,128)(2,1)}, u32[]{:S(2)}, u32[]{:S(2)}) collective-permute-start(bf16[64,768]{1,0:T(8,128)(2,1)} %get-tuple-element.233), channel_id=1, source_target_pairs={{0,3},{1,2},{2,1},{3,0},{4,7},{5,6},{6,5},{7,4},{8,11},{9,10},{10,... | collective-permute-start | bytes 294920 | tf_op jit(solution)/shard_map/ppermute | solution.py:53
  291.6 24.6 %collective-permute-start.32 = (bf16[64,768]{1,0:T(8,128)(2,1)}, bf16[64,768]{1,0:T(8,128)(2,1)}, u32[]{:S(2)}, u32[]{:S(2)}) collective-permute-start(bf16[64,768]{1,0:T(8,128)(2,1)} %get-tuple-element.234), channel_id=1, source_target_pairs={{0,2},{1,3},{2,0},{3,1},{4,6},{5,7},{6,4},{7,5},{8,10},{9,11},{10,... | collective-permute-start | bytes 294920 | tf_op jit(solution)/shard_map/ppermute | solution.py:53
  311.3 33.7 %collective-permute-start.52 = (bf16[768,1536]{1,0:T(8,128)(2,1)}, bf16[768,1536]{1,0:T(8,128)(2,1)}, u32[]{:S(2)}, u32[]{:S(2)}) collective-permute-start(bf16[768,1536]{1,0:T(8,128)(2,1)} %bitcast.74.attend_own_ref), channel_id=1, source_target_pairs={{0,1},{1,0},{2,3},{3,2},{4,5},{5,4},{6,7},{7,6},{8,9},{9,8},{10,11... | collective-permute-start | bytes 7077896 | tf_op jit(solution)/shard_map/ppermute | solution.py:49
  328.3 13.0 %collective-permute-start.42 = (bf16[64,8,192]{2,1,0:T(8,128)(2,1)S(1)}, bf16[64,8,192]{2,1,0:T(8,128)(2,1)S(1)}, u32[]{:S(2)}, u32[]{:S(2)}) collective-permute-start(bf16[64,8,192]{2,1,0:T(8,128)(2,1)S(1)} %slice.329), channel_id=1, source_target_pairs={{0,2},{1,3},{2,0},{3,1},{4,6},{5,7},{6,4},{7,5},{8,10},{9,11},{10,... | collective-permute-start | bytes 589832 | tf_op jit(solution)/shard_map/ppermute | solution.py:53
  396.0 30.2 %collective-permute-start.56 = (bf16[64,8,192]{2,1,0:T(8,128)(2,1)S(1)}, bf16[64,8,192]{2,1,0:T(8,128)(2,1)}, u32[]{:S(2)}, u32[]{:S(2)}) collective-permute-start(bf16[64,8,192]{2,1,0:T(8,128)(2,1)S(1)} %bitcast.563), channel_id=1, source_target_pairs={{0,1},{1,0},{2,3},{3,2},{4,5},{5,4},{6,7},{7,6},{8,9},{9,8},{10,11... | collective-permute-start | bytes 589832 | tf_op jit(solution)/shard_map/ppermute | solution.py:53
  396.1 32.9 %collective-permute-start.57 = (bf16[64,8,192]{2,1,0:T(8,128)(2,1)}, bf16[64,8,192]{2,1,0:T(8,128)(2,1)}, u32[]{:S(2)}, u32[]{:S(2)}) collective-permute-start(bf16[64,8,192]{2,1,0:T(8,128)(2,1)} %bitcast.502), channel_id=1, source_target_pairs={{0,2},{1,3},{2,0},{3,1},{4,6},{5,7},{6,4},{7,5},{8,10},{9,11},{10,... | collective-permute-start | bytes 589832 | tf_op jit(solution)/shard_map/ppermute | solution.py:53
  397.3 34.6 %collective-permute-start.58 = (bf16[64,8,192]{2,1,0:T(8,128)(2,1)}, bf16[64,8,192]{2,1,0:T(8,128)(2,1)}, u32[]{:S(2)}, u32[]{:S(2)}) collective-permute-start(bf16[64,8,192]{2,1,0:T(8,128)(2,1)} %bitcast.562), channel_id=1, source_target_pairs={{0,3},{1,2},{2,1},{3,0},{4,7},{5,6},{6,5},{7,4},{8,11},{9,10},{10,... | collective-permute-start | bytes 589832 | tf_op jit(solution)/shard_map/ppermute | solution.py:53
  403.8 225.1 %collective-permute-start.96 = (bf16[768,1536]{1,0:T(8,128)(2,1)}, bf16[768,1536]{1,0:T(8,128)(2,1)}, u32[]{:S(2)}, u32[]{:S(2)}) collective-permute-start(bf16[768,1536]{1,0:T(8,128)(2,1)} %shard_map.188), channel_id=1, source_target_pairs={{0,1},{1,0},{2,3},{3,2},{4,5},{5,4},{6,7},{7,6},{8,9},{9,8},{10,11... | collective-permute-start | bytes 7077896 | tf_op jit(solution)/shard_map/ppermute | solution.py:49
  459.1 12.0 %collective-permute-start.65 = (bf16[64,768]{1,0:T(8,128)(2,1)}, bf16[64,768]{1,0:T(8,128)(2,1)}, u32[]{:S(2)}, u32[]{:S(2)}) collective-permute-start(bf16[64,768]{1,0:T(8,128)(2,1)} %get-tuple-element.226), channel_id=1, source_target_pairs={{0,1},{1,0},{2,3},{3,2},{4,5},{5,4},{6,7},{7,6},{8,9},{9,8},{10,11... | collective-permute-start | bytes 294920 | tf_op jit(solution)/shard_map/ppermute | solution.py:53
  459.2 11.8 %collective-permute-start.67 = (bf16[64,768]{1,0:T(8,128)(2,1)}, bf16[64,768]{1,0:T(8,128)(2,1)}, u32[]{:S(2)}, u32[]{:S(2)}) collective-permute-start(bf16[64,768]{1,0:T(8,128)(2,1)} %get-tuple-element.227), channel_id=1, source_target_pairs={{0,3},{1,2},{2,1},{3,0},{4,7},{5,6},{6,5},{7,4},{8,11},{9,10},{10,... | collective-permute-start | bytes 294920 | tf_op jit(solution)/shard_map/ppermute | solution.py:53
  498.0 45.6 %collective-permute-start.91 = (bf16[4,96,768]{2,1,0:T(8,128)(2,1)}, bf16[4,96,768]{2,1,0:T(8,128)(2,1)}, u32[]{:S(2)}, u32[]{:S(2)}) collective-permute-start(bf16[4,96,768]{2,1,0:T(8,128)(2,1)} %fusion.48), channel_id=1, source_target_pairs={{0,4},{2,6},{4,0},{6,2},{8,12},{10,14},{12,8},{14,10},{16,20},{18,... | collective-permute-start | bytes 1769480 | tf_op jit(solution)/shard_map/ppermute | solution.py:45
  521.3 13.6 %collective-permute-start.78 = (bf16[64,8,192]{2,1,0:T(8,128)(2,1)}, bf16[64,8,192]{2,1,0:T(8,128)(2,1)}, u32[]{:S(2)}, u32[]{:S(2)}) collective-permute-start(bf16[64,8,192]{2,1,0:T(8,128)(2,1)} %slice.357), channel_id=1, source_target_pairs={{0,2},{1,3},{2,0},{3,1},{4,6},{5,7},{6,4},{7,5},{8,10},{9,11},{10,... | collective-permute-start | bytes 589832 | tf_op jit(solution)/shard_map/ppermute | solution.py:53
  530.1 108.8 %collective-permute-start.107 = (bf16[768,3072]{1,0:T(8,128)(2,1)}, bf16[768,3072]{1,0:T(8,128)(2,1)}, u32[]{:S(2)}, u32[]{:S(2)}) collective-permute-start(bf16[768,3072]{1,0:T(8,128)(2,1)} %copy-done.1), channel_id=1, source_target_pairs={{0,1},{1,0},{2,3},{3,2},{4,5},{5,4},{6,7},{7,6},{8,9},{9,8},{10,11... | collective-permute-start | bytes 14155784 | tf_op jit(solution)/shard_map/ppermute | solution.py:49
  530.2 29.2 %collective-permute-start.87 = (bf16[4,192,768]{2,1,0:T(8,128)(2,1)}, bf16[4,192,768]{2,1,0:T(8,128)(2,1)}, u32[]{:S(2)}, u32[]{:S(2)}) collective-permute-start(bf16[4,192,768]{2,1,0:T(8,128)(2,1)} %fusion.7), channel_id=1, source_target_pairs={{0,4},{2,6},{4,0},{6,2},{8,12},{10,14},{12,8},{14,10},{16,20},{18,... | collective-permute-start | bytes 3538952 | tf_op jit(solution)/shard_map/ppermute | solution.py:45
  534.9 49.7 %collective-permute-start.102 = (bf16[4,96,1536]{2,1,0:T(8,128)(2,1)}, bf16[4,96,1536]{2,1,0:T(8,128)(2,1)}, u32[]{:S(2)}, u32[]{:S(2)}) collective-permute-start(bf16[4,96,1536]{2,1,0:T(8,128)(2,1)} %fusion.8), channel_id=1, source_target_pairs={{0,4},{2,6},{4,0},{6,2},{8,12},{10,14},{12,8},{14,10},{16,20},{18,... | collective-permute-start | bytes 3538952 | tf_op jit(solution)/shard_map/ppermute | solution.py:45
  552.4 57.1 %collective-permute-start.83 = (bf16[4,193,768]{2,0,1:T(4,128)(2,1)S(1)}, bf16[4,193,768]{2,0,1:T(4,128)(2,1)S(1)}, u32[]{:S(2)}, u32[]{:S(2)}) collective-permute-start(bf16[4,193,768]{2,0,1:T(4,128)(2,1)S(1)} %bitcast.550), channel_id=1, source_target_pairs={{0,4},{2,6},{4,0},{6,2},{8,12},{10,14},{12,8},{14,10},{16,20},{18,... | collective-permute-start | bytes 3557384 | tf_op jit(solution)/shard_map/ppermute | solution.py:45
  566.2 25.3 %collective-permute-start.88 = (bf16[192,768]{1,0:T(8,128)(2,1)S(1)}, bf16[192,768]{1,0:T(8,128)(2,1)S(1)}, u32[]{:S(2)}, u32[]{:S(2)}) collective-permute-start(bf16[192,768]{1,0:T(8,128)(2,1)S(1)} %fusion.68), channel_id=1, source_target_pairs={{0,8},{2,10},{4,12},{6,14},{8,16},{10,18},{12,20},{14,22},{16,24},... | collective-permute-start | bytes 884744 | tf_op jit(solution)/shard_map/ppermute | solution.py:60
  591.5 11.5 %collective-permute-start.103 = (bf16[96,1536]{1,0:T(8,128)(2,1)S(1)}, bf16[96,1536]{1,0:T(8,128)(2,1)S(1)}, u32[]{:S(2)}, u32[]{:S(2)}) collective-permute-start(bf16[96,1536]{1,0:T(8,128)(2,1)S(1)} %fusion.69), channel_id=1, source_target_pairs={{0,8},{2,10},{4,12},{6,14},{8,16},{10,18},{12,20},{14,22},{16,24},... | collective-permute-start | bytes 884744 | tf_op jit(solution)/shard_map/ppermute | solution.py:60
  596.0 13.3 %collective-permute-start.89 = (bf16[192,768]{1,0:T(8,128)(2,1)S(1)}, bf16[192,768]{1,0:T(8,128)(2,1)S(1)}, u32[]{:S(2)}, u32[]{:S(2)}) collective-permute-start(bf16[192,768]{1,0:T(8,128)(2,1)S(1)} %fusion.54), channel_id=1, source_target_pairs={{0,8},{2,10},{4,12},{6,14},{8,16},{10,18},{12,20},{14,22},{16,24},... | collective-permute-start | bytes 884744 | tf_op jit(solution)/shard_map/ppermute | solution.py:60
  603.1 12.6 %collective-permute-start.104 = (bf16[96,1536]{1,0:T(8,128)(2,1)S(1)}, bf16[96,1536]{1,0:T(8,128)(2,1)S(1)}, u32[]{:S(2)}, u32[]{:S(2)}) collective-permute-start(bf16[96,1536]{1,0:T(8,128)(2,1)S(1)} %fusion.52), channel_id=1, source_target_pairs={{0,8},{2,10},{4,12},{6,14},{8,16},{10,18},{12,20},{14,22},{16,24},... | collective-permute-start | bytes 884744 | tf_op jit(solution)/shard_map/ppermute | solution.py:60
  609.4 12.6 %collective-permute-start.90 = (bf16[192,768]{1,0:T(8,128)(2,1)S(1)}, bf16[192,768]{1,0:T(8,128)(2,1)S(1)}, u32[]{:S(2)}, u32[]{:S(2)}) collective-permute-start(bf16[192,768]{1,0:T(8,128)(2,1)S(1)} %fusion.55), channel_id=1, source_target_pairs={{0,8},{2,10},{4,12},{6,14},{8,16},{10,18},{12,20},{14,22},{16,24},... | collective-permute-start | bytes 884744 | tf_op jit(solution)/shard_map/ppermute | solution.py:60
  609.8 18.7 %collective-permute-start.84 = (bf16[193,768]{1,0:T(8,128)(2,1)S(1)}, bf16[193,768]{1,0:T(8,128)(2,1)S(1)}, u32[]{:S(2)}, u32[]{:S(2)}) collective-permute-start(bf16[193,768]{1,0:T(8,128)(2,1)S(1)} %fusion.65), channel_id=1, source_target_pairs={{0,8},{2,10},{4,12},{6,14},{8,16},{10,18},{12,20},{14,22},{16,24},... | collective-permute-start | bytes 889352 | tf_op jit(solution)/shard_map/ppermute | solution.py:60
  615.7 19.2 %collective-permute-start.105 = (bf16[96,1536]{1,0:T(8,128)(2,1)S(1)}, bf16[96,1536]{1,0:T(8,128)(2,1)S(1)}, u32[]{:S(2)}, u32[]{:S(2)}) collective-permute-start(bf16[96,1536]{1,0:T(8,128)(2,1)S(1)} %fusion.53), channel_id=1, source_target_pairs={{0,8},{2,10},{4,12},{6,14},{8,16},{10,18},{12,20},{14,22},{16,24},... | collective-permute-start | bytes 884744 | tf_op jit(solution)/shard_map/ppermute | solution.py:60
  631.6 34.5 %collective-permute-start.97 = (bf16[4,2,48,1536]{3,2,0,1:T(8,128)(2,1)S(1)}, bf16[4,2,48,1536]{3,2,0,1:T(8,128)(2,1)S(1)}, u32[]{:S(2)}, u32[]{:S(2)}) collective-permute-start(bf16[4,2,48,1536]{3,2,0,1:T(8,128)(2,1)S(1)} %fusion.10), channel_id=1, source_target_pairs={{0,2},{2,0},{4,6},{6,4},{8,10},{10,8},{12,14},{14,12},{16,18},{18,... | collective-permute-start | bytes 3538952 | tf_op jit(solution)/shard_map/ppermute | solution.py:45
  635.0 28.8 %collective-permute-start.106 = (bf16[48,1536]{1,0:T(8,128)(2,1)S(1)}, bf16[48,1536]{1,0:T(8,128)(2,1)S(1)}, u32[]{:S(2)}, u32[]{:S(2)}) collective-permute-start(bf16[48,1536]{1,0:T(8,128)(2,1)S(1)} %fusion.96), channel_id=1, source_target_pairs={{0,2},{2,0},{4,6},{6,4},{8,10},{10,8},{12,14},{14,12},{16,18},{18,... | collective-permute-start | bytes 442376 | tf_op jit(solution)/shard_map/ppermute | solution.py:45
  638.8 25.1 %collective-permute-start.86 = (bf16[193,768]{1,0:T(8,128)(2,1)S(1)}, bf16[193,768]{1,0:T(8,128)(2,1)S(1)}, u32[]{:S(2)}, u32[]{:S(2)}) collective-permute-start(bf16[193,768]{1,0:T(8,128)(2,1)S(1)} %fusion.46), channel_id=1, source_target_pairs={{0,8},{2,10},{4,12},{6,14},{8,16},{10,18},{12,20},{14,22},{16,24},... | collective-permute-start | bytes 889352 | tf_op jit(solution)/shard_map/ppermute | solution.py:60
  643.4 64.5 %collective-permute-start.108 = (bf16[4,2,48,3072]{3,2,0,1:T(8,128)(2,1)S(1)}, bf16[4,2,48,3072]{3,2,0,1:T(8,128)(2,1)S(1)}, u32[]{:S(2)}, u32[]{:S(2)}) collective-permute-start(bf16[4,2,48,3072]{3,2,0,1:T(8,128)(2,1)S(1)} %fusion.1), channel_id=1, source_target_pairs={{0,2},{2,0},{4,6},{6,4},{8,10},{10,8},{12,14},{14,12},{16,18},{18,... | collective-permute-start | bytes 7077896 | tf_op jit(solution)/shard_map/ppermute | solution.py:45
  667.0 43.1 %collective-permute-start.98 = (bf16[4,48,1536]{2,1,0:T(8,128)(2,1)S(1)}, bf16[4,48,1536]{2,1,0:T(8,128)(2,1)S(1)}, u32[]{:S(2)}, u32[]{:S(2)}) collective-permute-start(bf16[4,48,1536]{2,1,0:T(8,128)(2,1)S(1)} %fusion.49), channel_id=1, source_target_pairs={{0,4},{2,6},{4,0},{6,2},{8,12},{10,14},{12,8},{14,10},{16,20},{18,... | collective-permute-start | bytes 1769480 | tf_op jit(solution)/shard_map/ppermute | solution.py:45
  709.1 21.7 %collective-permute-start.109 = (bf16[4,48,3072]{2,1,0:T(8,128)(2,1)S(1)}, bf16[4,48,3072]{2,1,0:T(8,128)(2,1)S(1)}, u32[]{:S(2)}, u32[]{:S(2)}) collective-permute-start(bf16[4,48,3072]{2,1,0:T(8,128)(2,1)S(1)} %fusion.9), channel_id=1, source_target_pairs={{0,4},{2,6},{4,0},{6,2},{8,12},{10,14},{12,8},{14,10},{16,20},{18,... | collective-permute-start | bytes 3538952 | tf_op jit(solution)/shard_map/ppermute | solution.py:45
  717.3 13.8 %collective-permute-start.100 = (bf16[48,1536]{1,0:T(8,128)(2,1)S(1)}, bf16[48,1536]{1,0:T(8,128)(2,1)S(1)}, u32[]{:S(2)}, u32[]{:S(2)}) collective-permute-start(bf16[48,1536]{1,0:T(8,128)(2,1)S(1)} %fusion.71), channel_id=1, source_target_pairs={{0,8},{2,10},{4,12},{6,14},{8,16},{10,18},{12,20},{14,22},{16,24},... | collective-permute-start | bytes 442376 | tf_op jit(solution)/shard_map/ppermute | solution.py:60
  731.0 11.5 %collective-permute-start.110 = (bf16[48,3072]{1,0:T(8,128)(2,1)S(1)}, bf16[48,3072]{1,0:T(8,128)(2,1)S(1)}, u32[]{:S(2)}, u32[]{:S(2)}) collective-permute-start(bf16[48,3072]{1,0:T(8,128)(2,1)S(1)} %fusion.70), channel_id=1, source_target_pairs={{0,8},{2,10},{4,12},{6,14},{8,16},{10,18},{12,20},{14,22},{16,24},... | collective-permute-start | bytes 884744 | tf_op jit(solution)/shard_map/ppermute | solution.py:60
  731.2 13.2 %collective-permute-start.101 = (bf16[48,1536]{1,0:T(8,128)(2,1)S(1)}, bf16[48,1536]{1,0:T(8,128)(2,1)S(1)}, u32[]{:S(2)}, u32[]{:S(2)}) collective-permute-start(bf16[48,1536]{1,0:T(8,128)(2,1)S(1)} %fusion.72), channel_id=1, source_target_pairs={{0,8},{2,10},{4,12},{6,14},{8,16},{10,18},{12,20},{14,22},{16,24},... | collective-permute-start | bytes 442376 | tf_op jit(solution)/shard_map/ppermute | solution.py:60
  743.4 11.6 %collective-permute-start.111 = (bf16[48,3072]{1,0:T(8,128)(2,1)}, bf16[48,3072]{1,0:T(8,128)(2,1)}, u32[]{:S(2)}, u32[]{:S(2)}) collective-permute-start(bf16[48,3072]{1,0:T(8,128)(2,1)} %fusion.50), channel_id=1, source_target_pairs={{0,8},{2,10},{4,12},{6,14},{8,16},{10,18},{12,20},{14,22},{16,24},... | collective-permute-start | bytes 884744 | tf_op jit(solution)/shard_map/ppermute | solution.py:60
  (208 other events, 1635.9 us)

commit v3 on v2

--- a/solution.py
+++ b/solution.py
@@ -55,9 +55,13 @@
     )
 
 
-def step_ring(values_in):
+def step_line(values_in, offset):
     count = dp_size()
-    return lax.ppermute(values_in, "dp", [(i, (i + 4) % count) for i in range(count)])
+    return lax.ppermute(values_in, "dp", [(i, (i + 4 * offset) % count) for i in range(count)])
+
+
+def after(values_in, *earlier):
+    return lax.optimization_barrier((values_in,) + earlier)[0]
 
 
 def line_groups():
@@ -70,29 +74,29 @@
     return lax.select_n(place, *choices)
 
 
-class Queue:
-    def __init__(self, depth):
-        self.arrived = [None] * depth
-
-    def send(self, transfer, values_in):
-        earlier = self.arrived.pop(0)
-        if earlier is not None:
-            values_in, _ = lax.optimization_barrier((values_in, earlier))
-        got = transfer(values_in)
-        self.arrived.append(got)
+class LineQueue:
+    def __init__(self):
+        self.arrived = [(), ()]
+
+    def step(self, values_in):
+        got = step_line(after(values_in, *self.arrived.pop(0)), 1)
+        self.arrived.append((got,))
         return got
+
+    def hold(self, *earlier):
+        self.arrived[0] = self.arrived[0] + earlier
 
 
 def line_gather(values_in, queue):
     count = line_size()
     if count > 4:
         return lax.all_gather(values_in, "dp", axis=0, axis_index_groups=line_groups())
-    got = [values_in]
-    for step in range(count - 1):
-        got.append(queue.send(step_ring, got[-1]))
-    place = line_place()
     if count == 1:
         return values_in[None]
+    got = [values_in]
+    for _ in range(1, count):
+        got.append(queue.step(got[-1]))
+    place = line_place()
     return jnp.stack(
         [pick(place, [got[(here - slot) % count] for here in range(count)]) for slot in range(count)]
     )
@@ -102,39 +106,26 @@
     return jnp.stack([pick(place, [own, other]), pick(place, [other, own])], axis=0)
 
 
-def line_y_gather(values_in, queues):
-    lined = line_gather(values_in, queues["line"])
-    other = queues["y"].send(lambda moved: flip_dp(moved, 2), lined)
+def y_gather(lined):
+    other = flip_dp(lined, 2)
     place = y_place()
     return jnp.stack([pick(place, [lined, other]), pick(place, [other, lined])], axis=1)
-
-
-def dp_gather(values_in, queues, y_first):
-    lined = line_gather(values_in, queues["line"])
-    order = (("y", 2, y_place(), 1), ("x", 1, x_place(), 2 if y_first else 1))
-    gathered = lined
-    for name, bit, place, axis in order if y_first else order[::-1]:
-        other = queues[name].send(lambda moved, bit=bit: flip_dp(moved, bit), gathered)
-        gathered = jnp.stack(
-            [pick(place, [gathered, other]), pick(place, [other, gathered])], axis=axis
-        )
-    return gathered.reshape(-1, values_in.shape[-1])
 
 
 def line_scatter(parts):
     count = line_size()
     if count > 4:
         return lax.psum_scatter(
-            parts, "dp", scatter_dimension=0, axis_index_groups=line_groups(), tiled=False
+            parts.astype(F32), "dp", scatter_dimension=0, axis_index_groups=line_groups(), tiled=False
         )
     place = line_place()
 
-    def slot(back):
-        return lax.dynamic_index_in_dim(parts, (place + count - back) % count, 0, keepdims=False)
-
-    total = slot(1 % count)
+    def slot(offset):
+        return lax.dynamic_index_in_dim(parts, (place + count + offset) % count, 0, keepdims=False)
+
+    total = slot(-1).astype(F32)
     for back in range(2, count + 1):
-        total = slot(back % count) + step_ring(total.astype(BF16)).astype(F32)
+        total = slot(-back).astype(F32) + step_line(total.astype(BF16), 1).astype(F32)
     return total
 
 
@@ -144,18 +135,12 @@
     return own.astype(F32) + flip_dp(theirs.astype(BF16), bit).astype(F32)
 
 
+def y_scatter(parts):
+    return halve(parts.reshape((line_size(), 2) + parts.shape[1:]), y_place(), 1, 2)
+
+
 def line_y_scatter(parts):
-    shaped = parts.reshape((line_size(), 2) + parts.shape[1:])
-    return line_scatter(halve(shaped, y_place(), 1, 2))
-
-
-def dp_scatter(parts):
-    count = line_size()
-    rows = parts.shape[0] // (count * 4)
-    shaped = parts.reshape(count, 2, 2, rows, parts.shape[1])
-    shaped = halve(shaped, x_place(), 2, 1)
-    shaped = halve(shaped, y_place(), 1, 2)
-    return line_scatter(shaped)
+    return line_scatter(y_scatter(parts))
 
 
 def quad_gather(values_in):
@@ -264,55 +249,62 @@
     ).astype(BF16)
 
 
-def layer_forward(stream, weights, gain_rows, bias_rows, norm_index, places, widen, narrow):
-    joint_proj, output_proj, upward, downward = weights
-    normed_all = widen(
-        layer_norm(stream, gain_rows[norm_index], bias_rows[norm_index]).astype(BF16)
-    )
+def layer_forward(stream, attend_of, forward_of, gain_rows, bias_rows, norm_index, places):
+    normed = layer_norm(stream, gain_rows[norm_index], bias_rows[norm_index]).astype(BF16)
+    normed_all = quad_gather(normed)
+    joint_proj, output_proj = attend_of()
     packed = dot_nn(normed_all, joint_proj).astype(BF16)
     mixture, softened = attend_forward(packed, places)
-    middle = stream + narrow(dot_nt(mixture, output_proj))
-    second_all = widen(
+    middle = stream + quad_scatter(dot_nt(mixture, output_proj))
+    second_all = quad_gather(
         layer_norm(middle, gain_rows[norm_index + 1], bias_rows[norm_index + 1]).astype(BF16)
     )
+    upward, downward = forward_of(normed_all)
     hidden = dot_nn(second_all, upward)
     active = jax.nn.gelu(hidden).astype(BF16)
-    outcome = middle + narrow(dot_nt(active, downward))
+    outcome = middle + quad_scatter(dot_nt(active, downward))
     return (
         outcome,
         (stream, normed_all, packed, mixture, softened, middle, second_all, hidden, active),
-    )
-
-
-def layer_backward(grad_layer, saved, weights, gain_rows, bias_rows, norm_index, places, widen, narrow):
+        (joint_proj, output_proj, upward, downward),
+    )
+
+
+def layer_backward(grad_layer, saved, weights, gain_rows, bias_rows, norm_index, places, ties):
     stream, normed_all, packed, mixture, softened, middle, second_all, hidden, active = saved
     joint_proj, output_proj, upward, downward = weights
-    grad_all = widen(grad_layer.astype(BF16))
+    grad_all = quad_gather(after(grad_layer.astype(BF16), *ties[0]))
     grad_active = dot_nn(grad_all, downward)
     gelu_value, gelu_pull = jax.vjp(jax.nn.gelu, hidden)
     grad_hidden = gelu_pull(grad_active)[0].astype(BF16)
-    grad_second = narrow(dot_nt(grad_hidden, upward))
+    grad_second = quad_scatter(after(dot_nt(grad_hidden, upward), *ties[1]))
+    forward_grads = jnp.concatenate(
+        [dot_tn(second_all, grad_hidden).astype(BF16), dot_tn(grad_all, active).astype(BF16)], axis=1
+    )
     norm_value, second_pull = jax.vjp(
         layer_norm, middle, gain_rows[norm_index + 1], bias_rows[norm_index + 1]
     )
     grad_middle_norm, grad_gain_two, grad_bias_two = second_pull(grad_second)
     grad_middle = grad_layer + grad_middle_norm
-    grad_branch = widen(grad_middle.astype(BF16))
+    grad_branch = quad_gather(after(grad_middle.astype(BF16), *ties[2]))
     grad_mix = dot_nn(grad_branch, output_proj).astype(BF16)
+    forward_half = y_scatter(forward_grads.reshape(ties[5] + (-1,)))
     grad_packed = attend_backward(packed, softened, grad_mix, places)
-    grad_normed = narrow(dot_nt(grad_packed, joint_proj))
+    grad_normed = quad_scatter(after(dot_nt(grad_packed, joint_proj), *ties[3]))
+    attend_grads = jnp.concatenate(
+        [dot_tn(normed_all, grad_packed).astype(BF16), dot_tn(grad_branch, mixture).astype(BF16)], axis=1
+    )
     first_value, first_pull = jax.vjp(
         layer_norm, stream, gain_rows[norm_index], bias_rows[norm_index]
     )
     grad_stream_norm, grad_gain_one, grad_bias_one = first_pull(grad_normed)
     grad_stream = grad_middle + grad_stream_norm
-    grad_down = dot_tn(grad_all, active)
-    grad_up = dot_tn(second_all, grad_hidden)
-    grad_output = dot_tn(grad_branch, mixture)
-    grad_joint = dot_tn(normed_all, grad_packed)
+    grad_start = quad_gather(after(grad_stream.astype(BF16), *ties[4]))
+    attend_half = y_scatter(attend_grads.reshape(ties[5] + (-1,)))
     return (
-        grad_stream,
-        (grad_joint, grad_output, grad_up, grad_down),
+        grad_start,
+        attend_half,
+        forward_half,
         (grad_gain_one, grad_gain_two),
         (grad_bias_one, grad_bias_two),
     )
@@ -344,21 +336,25 @@
 
 def local_body(
     bound_ref, masked_ref, spread_ref, cotangent_ref, gain_ref, bias_ref,
-    attend_own_ref, attend_other_ref, forward_own_ref, forward_other_ref,
+    first_ref, last_ref,
     result_ref, grad_ref, grad_low_ref, normed_ref, second_ref, grad_out_ref, branch_ref,
-    packed_own_ref, packed_other_ref, mixture_own_ref, mixture_other_ref,
-    active_own_ref, active_other_ref, hidden_own_ref, hidden_other_ref, norms_ref,
+    joint_first_ref, joint_last_ref, value_first_ref, value_last_ref,
+    mixture_first_ref, mixture_last_ref, hidden_first_ref, hidden_last_ref,
+    active_first_ref, active_last_ref, norms_ref,
     probs_ref,
 ):
     rows = masked_ref.shape[0]
-    wide = mixture_own_ref.shape[1]
-    hidden_width = active_own_ref.shape[1]
-    attends = (attend_own_ref, attend_other_ref)
-    forwards = (forward_own_ref, forward_other_ref)
-    grad_packs = (packed_own_ref, packed_other_ref)
-    mixtures = (mixture_own_ref, mixture_other_ref)
-    actives = (active_own_ref, active_other_ref)
-    hiddens = (hidden_own_ref, hidden_other_ref)
+    wide = mixture_first_ref.shape[1]
+    hidden_width = active_first_ref.shape[1]
+    grad_joints = (joint_first_ref, joint_last_ref)
+    grad_values = (value_first_ref, value_last_ref)
+    mixtures = (mixture_first_ref, mixture_last_ref)
+    actives = (active_first_ref, active_last_ref)
+    hiddens = (hidden_first_ref, hidden_last_ref)
+
+    def weight(side, start, stop):
+        return (first_ref, last_ref)[side][:, 0, :, start:stop].reshape(D, stop - start)
+
     bands = rows // BAND
     pairs = wide // PAIR
 
@@ -369,7 +365,7 @@
     normed, unit_one, scale_one = norm_forward(stream, gain_one, bias_ref[2:3, :])
     normed = normed.astype(BF16)
     normed_ref[...] = normed
-    packs = [dot_nn(normed, attend[:, : 3 * wide]).astype(BF16) for attend in attends]
+    packs = [dot_nn(normed, weight(side, 0, 3 * wide)).astype(BF16) for side in range(2)]
 
     lanes = lax.broadcasted_iota(jnp.int32, (BAND, PAIR), 1)
     low_head = lanes < HD
@@ -407,7 +403,7 @@
 
     middle = stream
     for side in range(2):
-        middle = middle + dot_nt(mixtures[side][...], attends[side][:, 3 * wide :])
+        middle = middle + dot_nt(mixtures[side][...], weight(side, 3 * wide, 4 * wide))
     second, unit_two, scale_two = norm_forward(middle, gain_two, bias_ref[3:4, :])
     second = second.astype(BF16)
     second_ref[...] = second
@@ -420,8 +416,9 @@
     chunk = min(768, hidden_width)
     for side in range(2):
         for start in range(0, hidden_width, chunk):
-            upward = forwards[side][:, start : start + chunk]
-            downward = forwards[side][:, hidden_width + start : hidden_width + start + chunk]
+            first = 4 * wide + start
+            upward = weight(side, first, first + chunk)
+            downward = weight(side, first + hidden_width, first + hidden_width + chunk)
             hidden = dot_nn(second, upward)
             square = hidden * hidden
             bent = jnp.tanh(GELU_A * hidden * (1.0 + GELU_B * square))
@@ -441,7 +438,7 @@
     branch_ref[...] = branch
     grad_normed = jnp.zeros_like(middle)
     for side in range(2):
-        grad_mix = dot_nn(branch, attends[side][:, 3 * wide :]).astype(BF16)
+        grad_mix = dot_nn(branch, weight(side, 3 * wide, 4 * wide)).astype(BF16)
         for band in range(bands):
             for pair in range(pairs):
                 probs = probs_ref[(side * bands + band) * pairs + pair]
@@ -455,12 +452,13 @@
                     dot_tn(grad_scores, queries) * scale,
                     dot_tn(probs.astype(BF16), grad_pair),
                 )
-                for part in range(3):
+                rows_here = slice(band * BAND, (band + 1) * BAND)
+                for part in range(2):
                     first = part * wide + pair * PAIR
-                    grad_packs[side][band * BAND : (band + 1) * BAND, first : first + PAIR] = (
-                        grads[part].astype(BF16)
-                    )
-        grad_normed = grad_normed + dot_nt(grad_packs[side][...], attends[side][:, : 3 * wide])
+                    grad_joints[side][rows_here, first : first + PAIR] = grads[part].astype(BF16)
+                grad_values[side][rows_here, pair * PAIR : (pair + 1) * PAIR] = grads[2].astype(BF16)
+        grad_normed = grad_normed + dot_nt(grad_joints[side][...], weight(side, 0, 2 * wide))
+        grad_normed = grad_normed + dot_nt(grad_values[side][...], weight(side, 2 * wide, 3 * wide))
     grad_in, gain_grad_one, bias_grad_one = norm_backward(grad_normed, unit_one, scale_one, gain_one)
     grad_stream = grad_middle + grad_in
     grad_ref[...] = grad_stream
@@ -474,16 +472,15 @@
         norms_ref[place : place + 1, :] += value
 
 
-def local_layer(bound, masked_low, spread, cotangent, gain_rows, bias_rows, attends, forwards):
+def local_layer(bound, masked_low, spread, cotangent, gain_rows, bias_rows, weights, wide):
     rows = masked_low.shape[0]
-    wide = attends[0].shape[1] // 4
-    hidden_width = forwards[0].shape[1] // 2
+    hidden_width = weights.shape[3] // 2 - 2 * wide
     tiled = lambda width: pl.BlockSpec((TILE, width), lambda i: (i, 0))
     fixed = lambda array: pl.BlockSpec(
         array.shape, lambda i: (0, 0), pipeline_mode=pl.Buffered(1)
     )
     widths = (
-        [(D, BF16), (D, F32)] + [(D, BF16)] * 5 + [(3 * wide, BF16)] * 2 + [(wide, BF16)] * 2
+        [(D, BF16), (D, F32)] + [(D, BF16)] * 5 + [(2 * wide, BF16)] * 2 + [(wide, BF16)] * 4
         + [(hidden_width, BF16)] * 4
     )
     flops = 8 * rows * D * 2 * (4 * wide + 2 * hidden_width)
@@ -492,7 +489,15 @@
         grid=(rows // TILE,),
         in_specs=[pl.BlockSpec(memory_space=pltpu.SMEM)]
         + [tiled(D)] * 3
-        + [fixed(array) for array in (gain_rows, bias_rows, *attends, *forwards)],
+        + [fixed(array) for array in (gain_rows, bias_rows)]
+        + [
+            pl.BlockSpec(
+                (weights.shape[0], 1) + weights.shape[2:],
+                lambda i, side=side: (0, side, 0, 0),
+                pipeline_mode=pl.Buffered(1),
+            )
+            for side in range(2)
+        ],
         out_specs=[tiled(width) for width, _ in widths] + [pl.BlockSpec((8, D), lambda i: (0, 0))],
         out_shape=[jax.ShapeDtypeStruct((rows, width), kind) for width, kind in widths]
         + [jax.ShapeDtypeStruct((8, D), F32)],
@@ -505,55 +510,79 @@
         cost_estimate=pl.CostEstimate(
             flops=flops, transcendentals=rows * 2 * hidden_width, bytes_accessed=36 * 1024 * 1024
         ),
-    )(bound, masked_low, spread, cotangent, gain_rows, bias_rows, *attends, *forwards)
-
-
-def grads_body(first_blocks, left_one_ref, right_one_ref, left_two_ref, right_two_ref, out_ref, turned_ref):
-    step = pl.program_id(0)
-
-    @pl.when(step == 0)
+    )(bound, masked_low, spread, cotangent, gain_rows, bias_rows, weights, weights)
+
+
+def grads_body(
+    normed_ref, branch_ref, second_ref, grad_out_ref,
+    joint_first_ref, joint_last_ref, value_first_ref, value_last_ref,
+    mixture_first_ref, mixture_last_ref, hidden_first_ref, hidden_last_ref,
+    active_first_ref, active_last_ref, out_ref, turned_ref, branch_turned_ref,
+):
+    block, side = pl.program_id(0), pl.program_id(1)
+    half = value_first_ref.shape[1]
+    shape = out_ref.shape[:3]
+
+    @pl.when((side == 0) & (block == 0))
     def _():
-        turned_ref[...] = left_one_ref[...].T
-
-    @pl.when(step == first_blocks)
+        turned_ref[...] = normed_ref[...].T
+        branch_turned_ref[...] = branch_ref[...].T
+
+    @pl.when((side == 0) & (block == 2))
     def _():
-        turned_ref[...] = left_two_ref[...].T
-
-    @pl.when(step < first_blocks)
+        turned_ref[...] = second_ref[...].T
+
+    @pl.when((side == 0) & (block == 4))
     def _():
-        out_ref[...] = dot_nn(turned_ref[...], right_one_ref[...]).astype(BF16)
-
-    @pl.when(step >= first_blocks)
-    def _():
-        out_ref[...] = dot_nn(turned_ref[...], right_two_ref[...]).astype(BF16)
-
-
-def weight_grads(left_one, right_one, left_two, right_two):
-    rows, model = left_one.shape
-    block = 384
-    first, last = right_one.shape[1] // block, right_two.shape[1] // block
-    whole = pl.BlockSpec((rows, model), lambda j: (0, 0), pipeline_mode=pl.Buffered(1))
+        turned_ref[...] = grad_out_ref[...].T
+
+    def give(place, chosen, left_ref, right_ref, columns):
+        @pl.when(chosen & (side == place))
+        def _():
+            product = dot_nn(left_ref[...], right_ref[...]).astype(BF16)
+            out_ref[:, :, :, columns] = product.reshape(shape + (product.shape[1],))
+
+    for place, (joint, value, mixture, hidden, active) in enumerate(
+        (
+            (joint_first_ref, value_first_ref, mixture_first_ref, hidden_first_ref, active_first_ref),
+            (joint_last_ref, value_last_ref, mixture_last_ref, hidden_last_ref, active_last_ref),
+        )
+    ):
+        give(place, block == 0, turned_ref, joint, slice(None))
+        give(place, block == 1, turned_ref, value, slice(0, half))
+        give(place, block == 1, branch_turned_ref, mixture, slice(half, 2 * half))
+        give(place, (block == 2) | (block == 3), turned_ref, hidden, slice(None))
+        give(place, block >= 4, turned_ref, active, slice(None))
+
+
+def weight_grads(lefts, joints, values, mixtures, hiddens, actives, shape):
+    rows, model = lefts[0].shape
+    block = joints[0].shape[1]
+
+    def given(array, first=None):
+        if first is None:
+            return pl.BlockSpec(array.shape, lambda b, s: (0, 0), pipeline_mode=pl.Buffered(1))
+        return pl.BlockSpec((rows, block), lambda b, s: (0, jnp.clip(b - first, 0, 1)))
+
+    arrays = (*lefts, *joints, *values, *mixtures, *hiddens, *actives)
     return pl.pallas_call(
-        lambda *refs: grads_body(first, *refs),
-        grid=(first + last,),
-        in_specs=[
-            whole,
-            pl.BlockSpec((rows, block), lambda j: (0, jnp.minimum(j, first - 1))),
-            whole,
-            pl.BlockSpec((rows, block), lambda j: (0, jnp.maximum(j - first, 0))),
-        ],
-        out_specs=pl.BlockSpec((model, block), lambda j: (0, j)),
-        out_shape=jax.ShapeDtypeStruct((model, (first + last) * block), BF16),
-        scratch_shapes=[pltpu.VMEM((model, rows), BF16)],
+        grads_body,
+        grid=(shape[3] // block, 2),
+        in_specs=[given(array) for array in (*lefts, *joints, *values, *mixtures)]
+        + [given(array, 2) for array in hiddens]
+        + [given(array, 4) for array in actives],
+        out_specs=pl.BlockSpec((shape[0], 1, shape[2], block), lambda b, s: (0, s, 0, b)),
+        out_shape=jax.ShapeDtypeStruct(shape, BF16),
+        scratch_shapes=[pltpu.VMEM((model, rows), BF16)] * 2,
         compiler_params=pltpu.CompilerParams(
-            dimension_semantics=("arbitrary",), vmem_limit_bytes=32 * 1024 * 1024
+            dimension_semantics=("arbitrary", "arbitrary"), vmem_limit_bytes=48 * 1024 * 1024
         ),
         cost_estimate=pl.CostEstimate(
-            flops=2 * rows * model * (first + last) * block,
+            flops=4 * rows * model * shape[3],
             transcendentals=0,
-            bytes_accessed=2 * (2 * rows * model + (rows + model) * (first + last) * block),
+            bytes_accessed=2 * (4 * rows * model + 2 * (rows + model) * shape[3]),
         ),
-    )(left_one, right_one, left_two, right_two)
+    )(*arrays)
 
 
 def shards(
@@ -581,7 +610,8 @@
 
     positions = lax.axis_index("tensor") * half_rows + jnp.arange(half_rows, dtype=jnp.int32)
     keep_mask = (positions < lengths[0]).astype(F32)[:, None]
-    masked_low = (embedded[0].astype(F32) * keep_mask).astype(BF16)
+    masked_low = jnp.where(keep_mask > 0, embedded[0], jnp.zeros_like(embedded[0]))
+    masked_low = lax.optimization_barrier(masked_low)
 
     joint_part = jnp.transpose(qkv_weight, (0, 2, 1, 3))
     output_part = jnp.transpose(out_weight, (0, 2, 1))
@@ -590,8 +620,17 @@
     norm_row = jnp.pad(
         jnp.concatenate([norm_gain, norm_bias]).reshape(1, -1), ((0, 0), (0, D - 2 * norm_part))
     )
-    queues = {"line": Queue(2), "y": Queue(2), "x": Queue(2)}
-    patch_whole = line_y_gather(jnp.concatenate([patch_proj, norm_row], axis=0), queues)
+    local_shard = jnp.concatenate(
+        [joint_part[1, 0], joint_part[1, 1], joint_part[1, 2], output_part[1], up_weight[1], down_part[1]],
+        axis=-1,
+    )
+    local_whole = lax.all_gather(local_shard, ("dp", "tensor"), axis=0)
+
+    patch_pieces = masked_low.reshape(patch_rows, cells, QUAD, proj_rows)
+    patches_dealt = quad_deal(patch_pieces)
+    queue = LineQueue()
+    patch_lined = line_gather(jnp.concatenate([patch_proj, norm_row], axis=0), queue)
+    patch_whole = y_gather(patch_lined)
     patch_whole = patch_whole.reshape(cells, proj_rows + 1, D)
     patch_mat = patch_whole[:, :proj_rows].reshape(cells * proj_rows, D)
     norm_cells = patch_whole[:, proj_rows, : 2 * norm_part]
@@ -600,6 +639,7 @@
     )[0].astype(F32)
     gain_rows = norm_all[..., :norm_part].reshape(NORMS, D)
     bias_rows = norm_all[..., norm_part:].reshape(NORMS, D)
+    gain_rows, bias_rows = lax.optimization_barrier((gain_rows, bias_rows))
 
     def x_half(part):
         return part.reshape(part.shape[:-1] + (2, part.shape[-1] // 2))
@@ -625,66 +665,70 @@
     global_shard = global_shard.reshape(2 * shard_rows, -1)
     attend_columns = 2 * heads_width
     attend_shard, forward_shard = global_shard[:, :attend_columns], global_shard[:, attend_columns:]
-    attend_whole = line_y_gather(attend_shard, queues).reshape(D, -1)
-    forward_whole = line_y_gather(forward_shard, queues).reshape(D, -1)
+    attend_lined = line_gather(attend_shard, queue)
+    forward_lined = line_gather(forward_shard, queue)
+    spread_lined = line_gather(jnp.transpose(global_proj), queue)
     joint_columns = 3 * heads_width // 2
-    first_weights = (
-        attend_whole[:, :joint_columns],
-        attend_whole[:, joint_columns:],
-        forward_whole[:, : hidden_width // 2],
-        forward_whole[:, hidden_width // 2 :],
-    )
-    spread_mat = line_y_gather(jnp.transpose(global_proj), queues).reshape(cells * proj_rows, D)
-
-    local_attend = jnp.concatenate([joint_part[1, 0], joint_part[1, 1], joint_part[1, 2], output_part[1]], axis=-1)
-    local_forward = jnp.concatenate([up_weight[1], down_part[1]], axis=-1)
-    forward_own = dp_gather(local_forward, queues, False)
-    attend_own = dp_gather(local_attend, queues, True)
-    attends = (attend_own, flip_core(attend_own))
-    forwards = (forward_own, flip_core(forward_own))
-
-    patches_dealt = quad_deal(masked_low.reshape(patch_rows, cells, QUAD, proj_rows))
+
     patches_mat = patches_dealt.reshape(QUAD * patch_rows, cells * proj_rows)
-    initial = quad_scatter(dot_nn(patches_mat, patch_mat))
+    start_partial = dot_nn(patches_mat, patch_mat)
+    initial = quad_scatter(start_partial)
+
+    def attend_of():
+        whole = y_gather(after(attend_lined, start_partial)).reshape(D, -1)
+        return whole[:, :joint_columns], whole[:, joint_columns:]
+
+    def forward_of(marker):
+        whole = y_gather(after(forward_lined, marker)).reshape(D, -1)
+        return whole[:, : hidden_width // 2], whole[:, hidden_width // 2 :]
+
     core = lax.axis_index("tensor")
     steps = jnp.arange(patch_rows, dtype=jnp.int32)
     global_places = jnp.concatenate([core * patch_rows + steps, (1 - core) * patch_rows + steps])
-    global_out, first_saved = layer_forward(
-        initial, first_weights, gain_rows, bias_rows, 0, global_places, quad_gather, quad_scatter
-    )
+    global_out, first_saved, first_weights = layer_forward(
+        initial, attend_of, forward_of, gain_rows, bias_rows, 0, global_places
+    )
+    spread_mat = y_gather(after(spread_lined, first_saved[6])).reshape(cells * proj_rows, D)
     global_low = quad_gather(global_out.astype(BF16))
     spread_dealt = dot_nt(global_low, spread_mat).astype(BF16)
     spread = quad_collect(spread_dealt.reshape(QUAD * patch_rows, cells, proj_rows))
     spread = spread.reshape(half_rows, D)
 
+    dp = dp_size()
+    whole_rows = shard_rows % 16 == 0
+    local_weights = local_whole.reshape(dp, 2, shard_rows, -1)
+    if not whole_rows:
+        local_weights = jnp.transpose(local_weights, (1, 0, 2, 3)).reshape(1, 2, D, -1)
     bound = jnp.clip(lengths - lax.axis_index("tensor") * half_rows, 0, half_rows)
     (
-        outcome, grad_local, grad_low, normed, second, grad_out, branch, packed_own, packed_other,
-        mixture_own, mixture_other, active_own, active_other, hidden_own, hidden_other, local_norms,
-    ) = local_layer(bound, masked_low, spread, cotangent[0], gain_rows, bias_rows, attends, forwards)
+        outcome, grad_local, grad_low, normed, second, grad_out, branch,
+        *grad_factors, local_norms,
+    ) = local_layer(bound, masked_low, spread, cotangent[0], gain_rows, bias_rows, local_weights, heads_width)
     second_gains, second_biases = (local_norms[0], local_norms[1]), (local_norms[2], local_norms[3])
-    forward_given = flip_core(weight_grads(second, hidden_other, grad_out, active_other))
-    forward_kept = weight_grads(second, hidden_own, grad_out, active_own)
-    forward_local = dp_scatter(forward_kept.astype(F32) + forward_given.astype(F32))
-    attend_given = flip_core(weight_grads(normed, packed_other, branch, mixture_other))
-    attend_kept = weight_grads(normed, packed_own, branch, mixture_own)
-    attend_local = dp_scatter(attend_kept.astype(F32) + attend_given.astype(F32))
-
     grad_spread = grad_low.reshape(patch_rows, cells, QUAD, proj_rows)
     spread_grads = quad_deal(grad_spread).reshape(QUAD * patch_rows, cells * proj_rows)
+    factor_pairs = [grad_factors[k : k + 2] for k in range(0, 10, 2)]
+    local_grads = weight_grads(
+        (normed, branch, second, grad_out), *factor_pairs, local_weights.shape
+    )
+    spread_grads = after(spread_grads, local_grads)
+    if not whole_rows:
+        local_grads = jnp.transpose(local_grads.reshape(2, dp, shard_rows, -1), (1, 0, 2, 3))
+    local_summed = lax.psum_scatter(
+        local_grads.reshape(2 * dp, shard_rows, -1), ("dp", "tensor"), scatter_dimension=0
+    ).astype(F32)
+
     grad_global = quad_scatter(dot_nn(spread_grads, spread_mat))
-    grad_proj = line_y_scatter(dot_tn(spread_grads, global_low).reshape(cells, proj_rows, D))
-    grad_initial, first_grads, first_gains, first_biases = layer_backward(
-        grad_global, first_saved, first_weights, gain_rows, bias_rows, 0, global_places, quad_gather, quad_scatter
-    )
-    forward_global = line_y_scatter(
-        jnp.concatenate([first_grads[2], first_grads[3]], axis=1).reshape(cells, 2 * shard_rows, -1)
-    )
-    attend_global = line_y_scatter(
-        jnp.concatenate([first_grads[0], first_grads[1]], axis=1).reshape(cells, 2 * shard_rows, -1)
-    )
-    grad_start = quad_gather(grad_initial.astype(BF16))
-    grad_patch_mat = dot_tn(patches_mat, grad_start).reshape(cells, proj_rows, D)
+    proj_grads = dot_tn(spread_grads, global_low).astype(BF16).reshape(cells, proj_rows, D)
+    proj_half = y_scatter(proj_grads)
+    ties = ((), (), (), (), (), (cells, 2 * shard_rows))
+    grad_start, attend_half, forward_half, first_gains, first_biases = layer_backward(
+        grad_global, first_saved, first_weights, gain_rows, bias_rows, 0, global_places, ties
+    )
+    grad_proj = line_scatter(proj_half)
+    forward_global = line_scatter(forward_half)
+    attend_global = line_scatter(attend_half)
+    grad_patch_mat = dot_tn(patches_mat, grad_start).astype(BF16).reshape(cells, proj_rows, D)
     grad_patches = dot_nt(grad_start, patch_mat).astype(BF16)
     grad_patches = quad_collect(grad_patches.reshape(QUAD * patch_rows, cells, proj_rows))
     grad_patches = grad_patches.reshape(half_rows, D).astype(F32)
@@ -704,7 +748,7 @@
     for bits in range(1, QUAD):
         piece = lax.dynamic_index_in_dim(norm_grads, place ^ bits, 1, keepdims=False)
         norm_sum = norm_sum + flip_quad(piece, bits)
-    norm_rows = jnp.pad(norm_sum[:, None, :], ((0, 0), (0, 0), (0, D - 2 * norm_part)))
+    norm_rows = jnp.pad(norm_sum[:, None, :].astype(BF16), ((0, 0), (0, 0), (0, D - 2 * norm_part)))
     patch_summed = line_y_scatter(jnp.concatenate([grad_patch_mat, norm_rows], axis=1))
 
     def x_restore(summed):
@@ -723,20 +767,20 @@
     joint_out = jnp.stack(
         [
             jnp.stack([x_columns(attend_global, k * half_heads, half_heads) for k in range(3)], axis=1),
-            attend_local[:, : 3 * heads_width].reshape(shard_rows, 3, heads_width),
+            local_summed[:, : 3 * heads_width].reshape(shard_rows, 3, heads_width),
         ]
     )
     output_out = jnp.stack(
         [
             jnp.transpose(x_columns(attend_global, 3 * half_heads, half_heads)),
-            jnp.transpose(attend_local[:, 3 * heads_width :]),
+            jnp.transpose(local_summed[:, 3 * heads_width : 4 * heads_width]),
         ]
     )
-    up_out = jnp.stack([x_columns(forward_global, 0, half_hidden), forward_local[:, :hidden_width]])
+    up_out = jnp.stack([x_columns(forward_global, 0, half_hidden), local_summed[:, 4 * heads_width : 4 * heads_width + hidden_width]])
     down_out = jnp.stack(
         [
             jnp.transpose(x_columns(forward_global, half_hidden, half_hidden)),
-            jnp.transpose(forward_local[:, hidden_width:]),
+            jnp.transpose(local_summed[:, 4 * heads_width + hidden_width :]),
         ]
     )
     return (

time: 778 us -> 572 us (0.74)
  the two profiles are of different devices: /device:TPU:4 before, /device:TPU:0 now
where the time goes in v3:
time: 572 us; the launch traced here: 562 us
  waiting for transfers between devices  229 us (40%)
  starting transfers between devices  98.4 us (17%)
  local copies, waits for them, and re-layouts  89.1 us (16%)
  Pallas kernels  64.8 us (11%)
  other arithmetic  41.4 us (7%)
  matrix products  21.5 us (4%)
  between operations  17.3 us (3%)
    ppermute x24, waiting for transfers between devices, step_line(): lax.ppermute(values_in, 'dp', [(i, (i + 4 * offset) % count) for i in ran...  148 us
    ppermute x54, waiting for transfers between devices, flip_quad(): lax.ppermute(values_in, ('dp', 'tensor'), [(i, i ^ bits) for i in range(2...  51.4 us
    pallas_call x1, Pallas kernels, local_layer(): pl.pallas_call(local_body, grid=(rows // TILE,), in_specs=[pl.BlockSpec(m...  47 us
    ppermute x24, starting transfers between devices, step_line(): lax.ppermute(values_in, 'dp', [(i, (i + 4 * offset) % count) for i in ran...  46.3 us
    ppermute x54, starting transfers between devices, flip_quad(): lax.ppermute(values_in, ('dp', 'tensor'), [(i, i ^ bits) for i in range(2...  36.4 us
    ppermute x11, waiting for transfers between devices, flip_dp(): lax.ppermute(values_in, 'dp', [(i, i ^ bit) for i in range(dp_size())])  30.1 us
    unnamed x255, local copies, waits for them, and re-layouts  21.8 us
    pallas_call x1, Pallas kernels, weight_grads(): pl.pallas_call(grads_body, grid=(shape[3] // block, 2), in_specs=[given(a...  17.8 us
  transfers between devices with their start and end apart: 91, of which 47 were waited for; matrix products, arithmetic and copies ran while one was open for 21% of the time, Pallas kernels for 3%

profile of v3, /device:TPU:0, one launch (start us, length us, event | category | flops | bytes accessed | tf_op | source)
XLA Modules:
  0.0 561.6 jit_solution(8044316515173204591)
XLA Ops:
  14.9 3.1 collective-permute-start.3
  23.0 4.3 collective-permute-done.3
  27.3 2.4 collective-permute-done.16
  29.8 15.4 %collective-permute-done.4 = bf16[193,768]{1,0:T(8,128)(2,1)S(1)} collective-permute-done((bf16[193,768]{1,0:T(8,128)(2,1)S(1)}, bf16[193,768]{1,0:T(8,128)(2,1)S(1)}, u32[]{:S(2)}, u32[]{:S(2)}) %collective-permute-start.4) | collective-permute-done | bytes 296480 | tf_op jit(solution)/shard_map/ppermute | solution.py:60
  47.3 17.3 %collective-permute-done.17 = bf16[96,768]{1,0:T(8,128)(2,1)} collective-permute-done((bf16[96,768]{1,0:T(8,128)(2,1)}, bf16[96,768]{1,0:T(8,128)(2,1)}, u32[]{:S(2)}, u32[]{:S(2)}) %collective-permute-start.17) | collective-permute-done | bytes 147488 | tf_op jit(solution)/shard_map/ppermute | solution.py:60
  64.6 4.3 fusion.126
  68.8 2.1 copy.218
  70.9 2.0 copy.219
  73.9 3.3 collective-permute-done.18
  78.0 3.6 collective-permute-start.19
  82.9 12.6 %collective-permute-done.19 = bf16[96,768]{1,0:T(8,128)(2,1)S(1)} collective-permute-done((bf16[96,768]{1,0:T(8,128)(2,1)}, bf16[96,768]{1,0:T(8,128)(2,1)S(1)}, u32[]{:S(2)}, u32[]{:S(2)}) %collective-permute-start.19) | collective-permute-done | bytes 147488 | tf_op jit(solution)/shard_map/ppermute | solution.py:60
  95.5 10.5 %collective-permute-start.28 = (bf16[96,1536]{1,0:T(8,128)(2,1)}, bf16[96,1536]{1,0:T(8,128)(2,1)}, u32[]{:S(2)}, u32[]{:S(2)}) collective-permute-start(bf16[96,1536]{1,0:T(8,128)(2,1)} %collective-permute-done.27), channel_id=1, source_target_pairs={{0,8},{2,10},{4,12},{6,14},{8,16},{10,18},{12,20},{14,22},{16,24},... | collective-permute-start | bytes 884744 | tf_op jit(solution)/shard_map/ppermute | solution.py:60
  112.1 6.3 %collective-permute-done.28 = bf16[96,1536]{1,0:T(8,128)(2,1)} collective-permute-done((bf16[96,1536]{1,0:T(8,128)(2,1)}, bf16[96,1536]{1,0:T(8,128)(2,1)}, u32[]{:S(2)}, u32[]{:S(2)}) %collective-permute-start.28) | collective-permute-done | bytes 294944 | tf_op jit(solution)/shard_map/ppermute | solution.py:60
  118.4 9.9 %collective-permute-start.29 = (bf16[96,1536]{1,0:T(8,128)(2,1)}, bf16[96,1536]{1,0:T(8,128)(2,1)S(1)}, u32[]{:S(2)}, u32[]{:S(2)}) collective-permute-start(bf16[96,1536]{1,0:T(8,128)(2,1)} %collective-permute-done.28), channel_id=1, source_target_pairs={{0,8},{2,10},{4,12},{6,14},{8,16},{10,18},{12,20},{14,22},{16,24},... | collective-permute-start | bytes 884744 | tf_op jit(solution)/shard_map/ppermute | solution.py:60
  128.3 4.4 collective-permute-start.37
  133.8 9.0 %collective-permute-done.29 = bf16[96,1536]{1,0:T(8,128)(2,1)S(1)} collective-permute-done((bf16[96,1536]{1,0:T(8,128)(2,1)}, bf16[96,1536]{1,0:T(8,128)(2,1)S(1)}, u32[]{:S(2)}, u32[]{:S(2)}) %collective-permute-start.29) | collective-permute-done | bytes 294944 | tf_op jit(solution)/shard_map/ppermute | solution.py:60
  142.9 5.3 collective-permute-done.37
  154.2 3.3 collective-permute-start.11
  157.7 3.0 fusion.149
  164.7 2.2 collective-permute-done.9
  166.9 2.4 collective-permute-done.8
  173.0 8.6 %collective-permute-done.39 = bf16[192,768]{1,0:T(8,128)(2,1)S(1)} collective-permute-done((bf16[192,768]{1,0:T(8,128)(2,1)S(1)}, bf16[192,768]{1,0:T(8,128)(2,1)S(1)}, u32[]{:S(2)}, u32[]{:S(2)}) %collective-permute-start.39) | collective-permute-done | bytes 294944 | tf_op jit(solution)/shard_map/ppermute | solution.py:60
  181.7 2.2 select_bitcast_fusion.15
  183.8 6.6 %collective-permute-done.20 = bf16[4,96,768]{2,1,0:T(8,128)(2,1)S(1)} collective-permute-done((bf16[4,96,768]{2,1,0:T(8,128)(2,1)S(1)}, bf16[4,96,768]{2,1,0:T(8,128)(2,1)S(1)}, u32[]{:S(2)}, u32[]{:S(2)}) %collective-permute-start.20) | collective-permute-done | bytes 589856 | tf_op jit(solution)/shard_map/ppermute | solution.py:45
  204.1 2.7 collective-permute-done.22
  218.4 3.0 collective-permute-done.33
  221.4 2.4 collective-permute-done.32
  225.8 3.8 collective-permute-done.40
  245.5 4.6 collective-permute-done.42
  253.0 1.9 reshape.246.spread_ref
  254.8 47.0 %shard_map.186 = (bf16[512,768]{1,0:T(8,128)(2,1)}, f32[512,768]{1,0:T(8,128)}, bf16[512,768]{1,0:T(8,128)(2,1)}, bf16[512,768]{1,0:T(8,128)(2,1)}, bf16[512,768...) custom-call(s32[1]{0:T(128)S(6)} %min.6.bound_ref, ...), custom_call_target="tpu_custom_call" | custom-call | flops 28991029248 | bytes 37748736 | tf_op jit(solution)/shard_map/pallas_call | solution.py:487
  301.9 2.7 reshape.248
  304.6 4.0 dynamic-slice_reduce_fusion
  308.6 2.0 concatenate.107
  322.2 17.8 %shard_map.187 = bf16[16,2,48,4608]{3,2,1,0:T(8,128)(2,1)} custom-call(bf16[512,768]{1,0:T(8,128)(2,1)S(1)} %copy-done, bf16[512,768]{1,0:T(8,128)(2,1)S(1)} %copy-done.3, bf16[512,768]{1,0:T(8,128)(2,1)S(1)} %copy-done.1, bf16[512,768]{1,0:T(8,128)(2,1)S(1)} %copy-done.2, bf16[512,768]{1,0:T(8,128)(2,1)S(1)} %copy-done.4, ...), custom_call_target="tpu_custom_call" | custom-call | flops 7247757312 | bytes 26738688 | tf_op jit(solution)/shard_map/pallas_call | solution.py:568
  350.6 2.7 collective-permute-done.48
  367.6 3.0 copy.260
  370.7 1.9 multiply_reduce_fusion.1
  379.6 2.4 collective-permute-done.57
  392.2 1.9 collective-permute-start.79
  394.1 2.3 collective-permute-done.60
  402.3 5.1 collective-permute-done.64
  407.4 4.4 collective-permute-done.63
  411.7 2.5 convolution_convert_fusion.2
  422.1 2.0 collective-permute-start.84
  425.4 2.0 collective-permute-start.71
  427.4 4.3 collective-permute-done.66
  433.1 2.7 copy.248
  435.8 3.5 reshape.264
  440.8 2.1 collective-permute-start.80
  443.0 2.7 fusion.28
  445.7 2.3 collective-permute-done.80
  450.9 5.7 %collective-permute-done.81 = bf16[96,768]{1,0:T(8,128)(2,1)S(1)} collective-permute-done((bf16[96,768]{1,0:T(8,128)(2,1)S(1)}, bf16[96,768]{1,0:T(8,128)(2,1)S(1)}, u32[]{:S(2)}, u32[]{:S(2)}) %collective-permute-start.81) | collective-permute-done | bytes 147488 | tf_op jit(solution)/shard_map/ppermute | solution.py:60
  456.6 7.3 %collective-permute-done.84 = bf16[4,96,1536]{2,1,0:T(8,128)(2,1)} collective-permute-done((bf16[4,96,1536]{2,1,0:T(8,128)(2,1)}, bf16[4,96,1536]{2,1,0:T(8,128)(2,1)}, u32[]{:S(2)}, u32[]{:S(2)}) %collective-permute-start.84) | collective-permute-done | bytes 1179680 | tf_op jit(solution)/shard_map/ppermute | solution.py:45
  465.6 2.1 collective-permute-start.85
  469.7 2.5 collective-permute-done.83
  473.1 6.1 %collective-permute-done.85 = bf16[96,1536]{1,0:T(8,128)(2,1)S(1)} collective-permute-done((bf16[96,1536]{1,0:T(8,128)(2,1)S(1)}, bf16[96,1536]{1,0:T(8,128)(2,1)S(1)}, u32[]{:S(2)}, u32[]{:S(2)}) %collective-permute-start.85) | collective-permute-done | bytes 294944 | tf_op jit(solution)/shard_map/ppermute | solution.py:60
  479.3 1.9 collective-permute-start.86
  481.2 10.6 %collective-permute-done.77 = bf16[192,768]{1,0:T(8,128)(2,1)S(1)} collective-permute-done((bf16[192,768]{1,0:T(8,128)(2,1)S(1)}, bf16[192,768]{1,0:T(8,128)(2,1)S(1)}, u32[]{:S(2)}, u32[]{:S(2)}) %collective-permute-start.77) | collective-permute-done | bytes 294944 | tf_op jit(solution)/shard_map/ppermute | solution.py:60
  493.4 7.6 %collective-permute-done.71 = bf16[4,193,768]{2,0,1:T(4,128)(2,1)} collective-permute-done((bf16[4,193,768]{2,0,1:T(4,128)(2,1)}, bf16[4,193,768]{2,0,1:T(4,128)(2,1)}, u32[]{:S(2)}, u32[]{:S(2)}) %collective-permute-start.71) | collective-permute-done | bytes 1185824 | tf_op jit(solution)/shard_map/ppermute | solution.py:45
  507.0 12.9 %collective-permute-done.72 = bf16[193,768]{1,0:T(8,128)(2,1)S(1)} collective-permute-done((bf16[193,768]{1,0:T(8,128)(2,1)S(1)}, bf16[193,768]{1,0:T(8,128)(2,1)S(1)}, u32[]{:S(2)}, u32[]{:S(2)}) %collective-permute-start.72) | collective-permute-done | bytes 296480 | tf_op jit(solution)/shard_map/ppermute | solution.py:60
  520.0 6.2 %collective-permute-done.87 = bf16[96,1536]{1,0:T(8,128)(2,1)S(1)} collective-permute-done((bf16[96,1536]{1,0:T(8,128)(2,1)S(1)}, bf16[96,1536]{1,0:T(8,128)(2,1)S(1)}, u32[]{:S(2)}, u32[]{:S(2)}) %collective-permute-start.87) | collective-permute-done | bytes 294944 | tf_op jit(solution)/shard_map/ppermute | solution.py:60
  527.3 11.0 %collective-permute-done.73 = bf16[193,768]{1,0:T(8,128)(2,1)S(1)} collective-permute-done((bf16[193,768]{1,0:T(8,128)(2,1)S(1)}, bf16[193,768]{1,0:T(8,128)(2,1)S(1)}, u32[]{:S(2)}, u32[]{:S(2)}) %collective-permute-start.73) | collective-permute-done | bytes 296480 | tf_op jit(solution)/shard_map/ppermute | solution.py:60
  538.6 9.9 %collective-permute-done.74 = bf16[193,768]{1,0:T(8,128)(2,1)S(1)} collective-permute-done((bf16[193,768]{1,0:T(8,128)(2,1)S(1)}, bf16[193,768]{1,0:T(8,128)(2,1)S(1)}, u32[]{:S(2)}, u32[]{:S(2)}) %collective-permute-start.74) | collective-permute-done | bytes 296480 | tf_op jit(solution)/shard_map/ppermute | solution.py:60
  (604 shorter events, 177.1 us)
Async XLA Ops:
  7.2 247.6 %all-gather.3.cloned.1.call-start = ((), (), s32[]{:S(2)}) async-start(), calls=%async_computation.2 | async-start | bytes 14598144 | tf_op jit(solution)/shard_map/all_gather | solution.py:627
  13.1 536.9 %reduce-scatter.2.cloned.1.call-start = ((), (), s32[]{:S(2)}) async-start(), calls=%async_computation.1 | async-start | bytes 14598144 | tf_op jit(solution)/shard_map/reduce_scatter | solution.py:717
  14.9 12.4 %collective-permute-start.3 = (bf16[193,768]{1,0:T(8,128)(2,1)S(1)}, bf16[193,768]{1,0:T(8,128)(2,1)S(1)}, u32[]{:S(2)}, u32[]{:S(2)}) collective-permute-start(bf16[193,768]{1,0:T(8,128)(2,1)S(1)} %fusion.56), channel_id=1, source_target_pairs={{0,8},{2,10},{4,12},{6,14},{8,16},{10,18},{12,20},{14,22},{16,24},... | collective-permute-start | bytes 889352 | tf_op jit(solution)/shard_map/ppermute | solution.py:60
  20.8 8.9 %collective-permute-start.16 = (bf16[48,2304]{1,0:T(8,128)(2,1)S(1)}, bf16[48,2304]{1,0:T(8,128)(2,1)S(1)}, u32[]{:S(2)}, u32[]{:S(2)}) collective-permute-start(bf16[48,2304]{1,0:T(8,128)(2,1)S(1)} %bitcast.489), channel_id=1, source_target_pairs={{0,2},{2,0},{4,6},{6,4},{8,10},{10,8},{12,14},{14,12},{16,18},{18,... | collective-permute-start | bytes 663560 | tf_op jit(solution)/shard_map/ppermute | solution.py:45
  27.3 17.9 %collective-permute-start.4 = (bf16[193,768]{1,0:T(8,128)(2,1)S(1)}, bf16[193,768]{1,0:T(8,128)(2,1)S(1)}, u32[]{:S(2)}, u32[]{:S(2)}) collective-permute-start(bf16[193,768]{1,0:T(8,128)(2,1)S(1)} %collective-permute-done.3), channel_id=1, source_target_pairs={{0,8},{2,10},{4,12},{6,14},{8,16},{10,18},{12,20},{14,22},{16,24},... | collective-permute-start | bytes 889352 | tf_op jit(solution)/shard_map/ppermute | solution.py:60
  45.2 19.4 %collective-permute-start.5 = (bf16[193,768]{1,0:T(8,128)(2,1)S(1)}, bf16[193,768]{1,0:T(8,128)(2,1)}, u32[]{:S(2)}, u32[]{:S(2)}) collective-permute-start(bf16[193,768]{1,0:T(8,128)(2,1)S(1)} %collective-permute-done.4), channel_id=1, source_target_pairs={{0,8},{2,10},{4,12},{6,14},{8,16},{10,18},{12,20},{14,22},{16,24},... | collective-permute-start | bytes 889352 | tf_op jit(solution)/shard_map/ppermute | solution.py:60
  45.9 18.6 %collective-permute-start.17 = (bf16[96,768]{1,0:T(8,128)(2,1)}, bf16[96,768]{1,0:T(8,128)(2,1)}, u32[]{:S(2)}, u32[]{:S(2)}) collective-permute-start(bf16[96,768]{1,0:T(8,128)(2,1)} %slice.386), channel_id=1, source_target_pairs={{0,8},{2,10},{4,12},{6,14},{8,16},{10,18},{12,20},{14,22},{16,24},... | collective-permute-start | bytes 442376 | tf_op jit(solution)/shard_map/ppermute | solution.py:60
  64.6 12.7 %collective-permute-start.18 = (bf16[96,768]{1,0:T(8,128)(2,1)}, bf16[96,768]{1,0:T(8,128)(2,1)}, u32[]{:S(2)}, u32[]{:S(2)}) collective-permute-start(bf16[96,768]{1,0:T(8,128)(2,1)} %collective-permute-done.17), channel_id=1, source_target_pairs={{0,8},{2,10},{4,12},{6,14},{8,16},{10,18},{12,20},{14,22},{16,24},... | collective-permute-start | bytes 442376 | tf_op jit(solution)/shard_map/ppermute | solution.py:60
  70.9 83.3 %collective-permute-start = (bf16[64,8,192]{0,2,1:T(8,128)(2,1)}, bf16[64,8,192]{0,2,1:T(8,128)(2,1)}, u32[]{:S(2)}, u32[]{:S(2)}) collective-permute-start(bf16[64,8,192]{0,2,1:T(8,128)(2,1)} %bitcast.4), channel_id=1, source_target_pairs={{0,1},{1,0},{2,3},{3,2},{4,5},{5,4},{6,7},{7,6},{8,9},{9,8},{10,11... | collective-permute-start | bytes 589832 | tf_op jit(solution)/shard_map/ppermute | solution.py:53
  72.9 84.6 %collective-permute-start.1 = (bf16[64,8,192]{0,2,1:T(8,128)(2,1)}, bf16[64,8,192]{0,2,1:T(8,128)(2,1)}, u32[]{:S(2)}, u32[]{:S(2)}) collective-permute-start(bf16[64,8,192]{0,2,1:T(8,128)(2,1)} %bitcast.5), channel_id=1, source_target_pairs={{0,2},{1,3},{2,0},{3,1},{4,6},{5,7},{6,4},{7,5},{8,10},{9,11},{10,... | collective-permute-start | bytes 589832 | tf_op jit(solution)/shard_map/ppermute | solution.py:53
  77.2 18.2 %collective-permute-start.27 = (bf16[96,1536]{1,0:T(8,128)(2,1)S(1)}, bf16[96,1536]{1,0:T(8,128)(2,1)}, u32[]{:S(2)}, u32[]{:S(2)}) collective-permute-start(bf16[96,1536]{1,0:T(8,128)(2,1)S(1)} %slice.396), channel_id=1, source_target_pairs={{0,8},{2,10},{4,12},{6,14},{8,16},{10,18},{12,20},{14,22},{16,24},... | collective-permute-start | bytes 884744 | tf_op jit(solution)/shard_map/ppermute | solution.py:60
  78.0 17.5 %collective-permute-start.19 = (bf16[96,768]{1,0:T(8,128)(2,1)}, bf16[96,768]{1,0:T(8,128)(2,1)S(1)}, u32[]{:S(2)}, u32[]{:S(2)}) collective-permute-start(bf16[96,768]{1,0:T(8,128)(2,1)} %collective-permute-done.18), channel_id=1, source_target_pairs={{0,8},{2,10},{4,12},{6,14},{8,16},{10,18},{12,20},{14,22},{16,24},... | collective-permute-start | bytes 442376 | tf_op jit(solution)/shard_map/ppermute | solution.py:60
  95.5 23.0 %collective-permute-start.28 = (bf16[96,1536]{1,0:T(8,128)(2,1)}, bf16[96,1536]{1,0:T(8,128)(2,1)}, u32[]{:S(2)}, u32[]{:S(2)}) collective-permute-start(bf16[96,1536]{1,0:T(8,128)(2,1)} %collective-permute-done.27), channel_id=1, source_target_pairs={{0,8},{2,10},{4,12},{6,14},{8,16},{10,18},{12,20},{14,22},{16,24},... | collective-permute-start | bytes 884744 | tf_op jit(solution)/shard_map/ppermute | solution.py:60
  107.6 43.1 %collective-permute-start.6 = (bf16[4,193,768]{2,0,1:T(4,128)(2,1)}, bf16[4,193,768]{2,0,1:T(4,128)(2,1)}, u32[]{:S(2)}, u32[]{:S(2)}) collective-permute-start(bf16[4,193,768]{2,0,1:T(4,128)(2,1)} %copy.221), channel_id=1, source_target_pairs={{0,4},{2,6},{4,0},{6,2},{8,12},{10,14},{12,8},{14,10},{16,20},{18,... | collective-permute-start | bytes 3557384 | tf_op jit(solution)/shard_map/ppermute | solution.py:45
  118.4 24.4 %collective-permute-start.29 = (bf16[96,1536]{1,0:T(8,128)(2,1)}, bf16[96,1536]{1,0:T(8,128)(2,1)S(1)}, u32[]{:S(2)}, u32[]{:S(2)}) collective-permute-start(bf16[96,1536]{1,0:T(8,128)(2,1)} %collective-permute-done.28), channel_id=1, source_target_pairs={{0,8},{2,10},{4,12},{6,14},{8,16},{10,18},{12,20},{14,22},{16,24},... | collective-permute-start | bytes 884744 | tf_op jit(solution)/shard_map/ppermute | solution.py:60
  128.3 19.8 %collective-permute-start.37 = (bf16[192,768]{1,0:T(8,128)(2,1)S(1)}, bf16[192,768]{1,0:T(8,128)(2,1)}, u32[]{:S(2)}, u32[]{:S(2)}) collective-permute-start(bf16[192,768]{1,0:T(8,128)(2,1)S(1)} %bitcast.482), channel_id=1, source_target_pairs={{0,8},{2,10},{4,12},{6,14},{8,16},{10,18},{12,20},{14,22},{16,24},... | collective-permute-start | bytes 884744 | tf_op jit(solution)/shard_map/ppermute | solution.py:60
  142.9 14.7 %collective-permute-start.2 = (bf16[64,8,192]{0,2,1:T(8,128)(2,1)S(1)}, bf16[64,8,192]{0,2,1:T(8,128)(2,1)S(1)}, u32[]{:S(2)}, u32[]{:S(2)}) collective-permute-start(bf16[64,8,192]{0,2,1:T(8,128)(2,1)S(1)} %bitcast.475), channel_id=1, source_target_pairs={{0,3},{1,2},{2,1},{3,0},{4,7},{5,6},{6,5},{7,4},{8,11},{9,10},{10,... | collective-permute-start | bytes 589832 | tf_op jit(solution)/shard_map/ppermute | solution.py:53
  148.1 22.7 %collective-permute-start.38 = (bf16[192,768]{1,0:T(8,128)(2,1)}, bf16[192,768]{1,0:T(8,128)(2,1)S(1)}, u32[]{:S(2)}, u32[]{:S(2)}) collective-permute-start(bf16[192,768]{1,0:T(8,128)(2,1)} %collective-permute-done.37), channel_id=1, source_target_pairs={{0,8},{2,10},{4,12},{6,14},{8,16},{10,18},{12,20},{14,22},{16,24},... | collective-permute-start | bytes 884744 | tf_op jit(solution)/shard_map/ppermute | solution.py:60
  150.8 58.5 %collective-permute-start.30 = (bf16[4,96,1536]{2,1,0:T(8,128)(2,1)}, bf16[4,96,1536]{2,1,0:T(8,128)(2,1)}, u32[]{:S(2)}, u32[]{:S(2)}) collective-permute-start(bf16[4,96,1536]{2,1,0:T(8,128)(2,1)} %pad_maximum_fusion.6), channel_id=1, source_target_pairs={{0,4},{2,6},{4,0},{6,2},{8,12},{10,14},{12,8},{14,10},{16,20},{18,... | collective-permute-start | bytes 3538952 | tf_op jit(solution)/shard_map/ppermute | solution.py:45
  154.2 7.2 %collective-permute-start.11 = (bf16[1,8,192]{2,1,0:T(8,128)(2,1)S(1)}, bf16[1,8,192]{2,1,0:T(8,128)(2,1)S(1)}, u32[]{:S(2)}, u32[]{:S(2)}) collective-permute-start(bf16[1,8,192]{2,1,0:T(8,128)(2,1)S(1)} %bitcast.495), channel_id=1, source_target_pairs={{0,2},{1,3},{2,0},{3,1},{4,6},{5,7},{6,4},{7,5},{8,10},{9,11},{10,... | collective-permute-start | bytes 9224 | tf_op jit(solution)/shard_map/ppermute | solution.py:53
  164.0 26.4 %collective-permute-start.20 = (bf16[4,96,768]{2,1,0:T(8,128)(2,1)S(1)}, bf16[4,96,768]{2,1,0:T(8,128)(2,1)S(1)}, u32[]{:S(2)}, u32[]{:S(2)}) collective-permute-start(bf16[4,96,768]{2,1,0:T(8,128)(2,1)S(1)} %pad_maximum_fusion.11), channel_id=1, source_target_pairs={{0,4},{2,6},{4,0},{6,2},{8,12},{10,14},{12,8},{14,10},{16,20},{18,... | collective-permute-start | bytes 1769480 | tf_op jit(solution)/shard_map/ppermute | solution.py:45
  170.8 10.8 %collective-permute-start.39 = (bf16[192,768]{1,0:T(8,128)(2,1)S(1)}, bf16[192,768]{1,0:T(8,128)(2,1)S(1)}, u32[]{:S(2)}, u32[]{:S(2)}) collective-permute-start(bf16[192,768]{1,0:T(8,128)(2,1)S(1)} %collective-permute-done.38), channel_id=1, source_target_pairs={{0,8},{2,10},{4,12},{6,14},{8,16},{10,18},{12,20},{14,22},{16,24},... | collective-permute-start | bytes 884744 | tf_op jit(solution)/shard_map/ppermute | solution.py:60
  172.0 18.7 %collective-permute-start.15 = (bf16[64,768]{1,0:T(8,128)(2,1)S(1)}, bf16[64,768]{1,0:T(8,128)(2,1)S(1)}, u32[]{:S(2)}, u32[]{:S(2)}) collective-permute-start(bf16[64,768]{1,0:T(8,128)(2,1)S(1)} %add_convert_fusion.2), channel_id=1, source_target_pairs={{0,3},{1,2},{2,1},{3,0},{4,7},{5,6},{6,5},{7,4},{8,11},{9,10},{10,... | collective-permute-start | bytes 294920 | tf_op jit(solution)/shard_map/ppermute | solution.py:53
  172.0 18.6 %collective-permute-start.14 = (bf16[64,768]{1,0:T(8,128)(2,1)S(1)}, bf16[64,768]{1,0:T(8,128)(2,1)S(1)}, u32[]{:S(2)}, u32[]{:S(2)}) collective-permute-start(bf16[64,768]{1,0:T(8,128)(2,1)S(1)} %add_convert_fusion.2), channel_id=1, source_target_pairs={{0,2},{1,3},{2,0},{3,1},{4,6},{5,7},{6,4},{7,5},{8,10},{9,11},{10,... | collective-permute-start | bytes 294920 | tf_op jit(solution)/shard_map/ppermute | solution.py:53
  181.7 9.0 %collective-permute-start.13 = (bf16[64,768]{1,0:T(8,128)(2,1)S(1)}, bf16[64,768]{1,0:T(8,128)(2,1)S(1)}, u32[]{:S(2)}, u32[]{:S(2)}) collective-permute-start(bf16[64,768]{1,0:T(8,128)(2,1)S(1)} %add_convert_fusion.2), channel_id=1, source_target_pairs={{0,1},{1,0},{2,3},{3,2},{4,5},{5,4},{6,7},{7,6},{8,9},{9,8},{10,11... | collective-permute-start | bytes 294920 | tf_op jit(solution)/shard_map/ppermute | solution.py:53
  201.8 27.7 %collective-permute-start.40 = (bf16[4,192,768]{2,1,0:T(8,128)(2,1)S(1)}, bf16[4,192,768]{2,1,0:T(8,128)(2,1)S(1)}, u32[]{:S(2)}, u32[]{:S(2)}) collective-permute-start(bf16[4,192,768]{2,1,0:T(8,128)(2,1)S(1)} %pad_maximum_fusion.7), channel_id=1, source_target_pairs={{0,4},{2,6},{4,0},{6,2},{8,12},{10,14},{12,8},{14,10},{16,20},{18,... | collective-permute-start | bytes 3538952 | tf_op jit(solution)/shard_map/ppermute | solution.py:45
  207.6 6.4 %collective-permute-start.25 = (bf16[64,768]{1,0:T(8,128)(2,1)S(1)}, bf16[64,768]{1,0:T(8,128)(2,1)S(1)}, u32[]{:S(2)}, u32[]{:S(2)}) collective-permute-start(bf16[64,768]{1,0:T(8,128)(2,1)S(1)} %add_convert_fusion.1), channel_id=1, source_target_pairs={{0,2},{1,3},{2,0},{3,1},{4,6},{5,7},{6,4},{7,5},{8,10},{9,11},{10,... | collective-permute-start | bytes 294920 | tf_op jit(solution)/shard_map/ppermute | solution.py:53
  217.4 6.4 %collective-permute-start.32 = (bf16[64,768]{1,0:T(8,128)(2,1)S(1)}, bf16[64,768]{1,0:T(8,128)(2,1)S(1)}, u32[]{:S(2)}, u32[]{:S(2)}) collective-permute-start(bf16[64,768]{1,0:T(8,128)(2,1)S(1)} %get-tuple-element.220), channel_id=1, source_target_pairs={{0,2},{1,3},{2,0},{3,1},{4,6},{5,7},{6,4},{7,5},{8,10},{9,11},{10,... | collective-permute-start | bytes 294920 | tf_op jit(solution)/shard_map/ppermute | solution.py:53
  223.9 6.1 %collective-permute-start.36 = (bf16[64,768]{1,0:T(8,128)(2,1)S(1)}, bf16[64,768]{1,0:T(8,128)(2,1)S(1)}, u32[]{:S(2)}, u32[]{:S(2)}) collective-permute-start(bf16[64,768]{1,0:T(8,128)(2,1)S(1)} %fusion.75), channel_id=1, source_target_pairs={{0,3},{1,2},{2,1},{3,0},{4,7},{5,6},{6,5},{7,4},{8,11},{9,10},{10,... | collective-permute-start | bytes 294920 | tf_op jit(solution)/shard_map/ppermute | solution.py:53
  224.5 6.7 %collective-permute-start.35 = (bf16[64,768]{1,0:T(8,128)(2,1)S(1)}, bf16[64,768]{1,0:T(8,128)(2,1)S(1)}, u32[]{:S(2)}, u32[]{:S(2)}) collective-permute-start(bf16[64,768]{1,0:T(8,128)(2,1)S(1)} %fusion.75), channel_id=1, source_target_pairs={{0,2},{1,3},{2,0},{3,1},{4,6},{5,7},{6,4},{7,5},{8,10},{9,11},{10,... | collective-permute-start | bytes 294920 | tf_op jit(solution)/shard_map/ppermute | solution.py:53
  235.5 10.0 %collective-permute-start.41 = (bf16[64,8,192]{2,1,0:T(8,128)(2,1)}, bf16[64,8,192]{2,1,0:T(8,128)(2,1)}, u32[]{:S(2)}, u32[]{:S(2)}) collective-permute-start(bf16[64,8,192]{2,1,0:T(8,128)(2,1)} %slice.321), channel_id=1, source_target_pairs={{0,1},{1,0},{2,3},{3,2},{4,5},{5,4},{6,7},{7,6},{8,9},{9,8},{10,11... | collective-permute-start | bytes 589832 | tf_op jit(solution)/shard_map/ppermute | solution.py:53
  235.6 9.9 %collective-permute-start.43 = (bf16[64,8,192]{2,1,0:T(8,128)(2,1)}, bf16[64,8,192]{2,1,0:T(8,128)(2,1)}, u32[]{:S(2)}, u32[]{:S(2)}) collective-permute-start(bf16[64,8,192]{2,1,0:T(8,128)(2,1)} %slice.325), channel_id=1, source_target_pairs={{0,3},{1,2},{2,1},{3,0},{4,7},{5,6},{6,5},{7,4},{8,11},{9,10},{10,... | collective-permute-start | bytes 589832 | tf_op jit(solution)/shard_map/ppermute | solution.py:53
  236.7 13.4 %collective-permute-start.42 = (bf16[64,8,192]{2,1,0:T(8,128)(2,1)}, bf16[64,8,192]{2,1,0:T(8,128)(2,1)}, u32[]{:S(2)}, u32[]{:S(2)}) collective-permute-start(bf16[64,8,192]{2,1,0:T(8,128)(2,1)} %slice.323), channel_id=1, source_target_pairs={{0,2},{1,3},{2,0},{3,1},{4,6},{5,7},{6,4},{7,5},{8,10},{9,11},{10,... | collective-permute-start | bytes 589832 | tf_op jit(solution)/shard_map/ppermute | solution.py:53
  316.0 25.4 %collective-permute-start.46 = (bf16[64,8,192]{2,1,0:T(8,128)(2,1)}, bf16[64,8,192]{2,1,0:T(8,128)(2,1)}, u32[]{:S(2)}, u32[]{:S(2)}) collective-permute-start(bf16[64,8,192]{2,1,0:T(8,128)(2,1)} %bitcast.434), channel_id=1, source_target_pairs={{0,3},{1,2},{2,1},{3,0},{4,7},{5,6},{6,5},{7,4},{8,11},{9,10},{10,... | collective-permute-start | bytes 589832 | tf_op jit(solution)/shard_map/ppermute | solution.py:53
  316.3 26.2 %collective-permute-start.44 = (bf16[64,8,192]{2,1,0:T(8,128)(2,1)}, bf16[64,8,192]{2,1,0:T(8,128)(2,1)}, u32[]{:S(2)}, u32[]{:S(2)}) collective-permute-start(bf16[64,8,192]{2,1,0:T(8,128)(2,1)} %bitcast.436), channel_id=1, source_target_pairs={{0,1},{1,0},{2,3},{3,2},{4,5},{5,4},{6,7},{7,6},{8,9},{9,8},{10,11... | collective-permute-start | bytes 589832 | tf_op jit(solution)/shard_map/ppermute | solution.py:53
  317.2 26.6 %collective-permute-start.45 = (bf16[64,8,192]{2,1,0:T(8,128)(2,1)}, bf16[64,8,192]{2,1,0:T(8,128)(2,1)}, u32[]{:S(2)}, u32[]{:S(2)}) collective-permute-start(bf16[64,8,192]{2,1,0:T(8,128)(2,1)} %bitcast.435), channel_id=1, source_target_pairs={{0,2},{1,3},{2,0},{3,1},{4,6},{5,7},{6,4},{7,5},{8,10},{9,11},{10,... | collective-permute-start | bytes 589832 | tf_op jit(solution)/shard_map/ppermute | solution.py:53
  354.2 6.4 %collective-permute-start.51 = (bf16[64,768]{1,0:T(8,128)(2,1)S(1)}, bf16[64,768]{1,0:T(8,128)(2,1)S(1)}, u32[]{:S(2)}, u32[]{:S(2)}) collective-permute-start(bf16[64,768]{1,0:T(8,128)(2,1)S(1)} %get-tuple-element.146), channel_id=1, source_target_pairs={{0,2},{1,3},{2,0},{3,1},{4,6},{5,7},{6,4},{7,5},{8,10},{9,11},{10,... | collective-permute-start | bytes 294920 | tf_op jit(solution)/shard_map/ppermute | solution.py:53
  356.9 91.4 %collective-permute-start.75 = (bf16[4,192,768]{2,1,0:T(8,128)(2,1)}, bf16[4,192,768]{2,1,0:T(8,128)(2,1)}, u32[]{:S(2)}, u32[]{:S(2)}) collective-permute-start(bf16[4,192,768]{2,1,0:T(8,128)(2,1)} %dynamic-slice_bitcast_fusion.2), channel_id=1, source_target_pairs={{0,4},{2,6},{4,0},{6,2},{8,12},{10,14},{12,8},{14,10},{16,20},{18,... | collective-permute-start | bytes 3538952 | tf_op jit(solution)/shard_map/ppermute | solution.py:45
  362.7 8.0 %collective-permute-start.53 = (bf16[64,768]{1,0:T(8,128)(2,1)}, bf16[64,768]{1,0:T(8,128)(2,1)}, u32[]{:S(2)}, u32[]{:S(2)}) collective-permute-start(bf16[64,768]{1,0:T(8,128)(2,1)} %get-tuple-element.212), channel_id=1, source_target_pairs={{0,1},{1,0},{2,3},{3,2},{4,5},{5,4},{6,7},{7,6},{8,9},{9,8},{10,11... | collective-permute-start | bytes 294920 | tf_op jit(solution)/shard_map/ppermute | solution.py:53
  363.2 7.5 %collective-permute-start.55 = (bf16[64,768]{1,0:T(8,128)(2,1)S(1)}, bf16[64,768]{1,0:T(8,128)(2,1)}, u32[]{:S(2)}, u32[]{:S(2)}) collective-permute-start(bf16[64,768]{1,0:T(8,128)(2,1)S(1)} %get-tuple-element.213), channel_id=1, source_target_pairs={{0,3},{1,2},{2,1},{3,0},{4,7},{5,6},{6,5},{7,4},{8,11},{9,10},{10,... | collective-permute-start | bytes 294920 | tf_op jit(solution)/shard_map/ppermute | solution.py:53
  363.9 6.7 %collective-permute-start.54 = (bf16[64,768]{1,0:T(8,128)(2,1)S(1)}, bf16[64,768]{1,0:T(8,128)(2,1)}, u32[]{:S(2)}, u32[]{:S(2)}) collective-permute-start(bf16[64,768]{1,0:T(8,128)(2,1)S(1)} %get-tuple-element.214), channel_id=1, source_target_pairs={{0,2},{1,3},{2,0},{3,1},{4,6},{5,7},{6,4},{7,5},{8,10},{9,11},{10,... | collective-permute-start | bytes 294920 | tf_op jit(solution)/shard_map/ppermute | solution.py:53
  375.8 6.3 %collective-permute-start.57 = (bf16[64,768]{1,0:T(8,128)(2,1)S(1)}, bf16[64,768]{1,0:T(8,128)(2,1)S(1)}, u32[]{:S(2)}, u32[]{:S(2)}) collective-permute-start(bf16[64,768]{1,0:T(8,128)(2,1)S(1)} %fusion.100), channel_id=1, source_target_pairs={{0,2},{1,3},{2,0},{3,1},{4,6},{5,7},{6,4},{7,5},{8,10},{9,11},{10,... | collective-permute-start | bytes 294920 | tf_op jit(solution)/shard_map/ppermute | solution.py:53
  390.4 6.0 %collective-permute-start.60 = (bf16[64,768]{1,0:T(8,128)(2,1)S(1)}, bf16[64,768]{1,0:T(8,128)(2,1)S(1)}, u32[]{:S(2)}, u32[]{:S(2)}) collective-permute-start(bf16[64,768]{1,0:T(8,128)(2,1)S(1)} %get-tuple-element.211), channel_id=1, source_target_pairs={{0,2},{1,3},{2,0},{3,1},{4,6},{5,7},{6,4},{7,5},{8,10},{9,11},{10,... | collective-permute-start | bytes 294920 | tf_op jit(solution)/shard_map/ppermute | solution.py:53
  392.2 47.1 %collective-permute-start.79 = (bf16[4,96,768]{2,1,0:T(8,128)(2,1)}, bf16[4,96,768]{2,1,0:T(8,128)(2,1)}, u32[]{:S(2)}, u32[]{:S(2)}) collective-permute-start(bf16[4,96,768]{2,1,0:T(8,128)(2,1)} %dynamic-slice_bitcast_fusion.3), channel_id=1, source_target_pairs={{0,4},{2,6},{4,0},{6,2},{8,12},{10,14},{12,8},{14,10},{16,20},{18,... | collective-permute-start | bytes 1769480 | tf_op jit(solution)/shard_map/ppermute | solution.py:45
  400.2 7.1 %collective-permute-start.64 = (bf16[64,768]{1,0:T(8,128)(2,1)S(1)}, bf16[64,768]{1,0:T(8,128)(2,1)S(1)}, u32[]{:S(2)}, u32[]{:S(2)}) collective-permute-start(bf16[64,768]{1,0:T(8,128)(2,1)S(1)} %add_convert_fusion), channel_id=1, source_target_pairs={{0,3},{1,2},{2,1},{3,0},{4,7},{5,6},{6,5},{7,4},{8,11},{9,10},{10,... | collective-permute-start | bytes 294920 | tf_op jit(solution)/shard_map/ppermute | solution.py:53
  401.2 10.6 %collective-permute-start.63 = (bf16[64,768]{1,0:T(8,128)(2,1)S(1)}, bf16[64,768]{1,0:T(8,128)(2,1)S(1)}, u32[]{:S(2)}, u32[]{:S(2)}) collective-permute-start(bf16[64,768]{1,0:T(8,128)(2,1)S(1)} %add_convert_fusion), channel_id=1, source_target_pairs={{0,2},{1,3},{2,0},{3,1},{4,6},{5,7},{6,4},{7,5},{8,10},{9,11},{10,... | collective-permute-start | bytes 294920 | tf_op jit(solution)/shard_map/ppermute | solution.py:53
  402.2 9.5 %collective-permute-start.62 = (bf16[64,768]{1,0:T(8,128)(2,1)S(1)}, bf16[64,768]{1,0:T(8,128)(2,1)S(1)}, u32[]{:S(2)}, u32[]{:S(2)}) collective-permute-start(bf16[64,768]{1,0:T(8,128)(2,1)S(1)} %add_convert_fusion), channel_id=1, source_target_pairs={{0,1},{1,0},{2,3},{3,2},{4,5},{5,4},{6,7},{7,6},{8,9},{9,8},{10,11... | collective-permute-start | bytes 294920 | tf_op jit(solution)/shard_map/ppermute | solution.py:53
  417.1 8.2 %collective-permute-start.67 = (bf16[64,8,192]{2,1,0:T(8,128)(2,1)}, bf16[64,8,192]{2,1,0:T(8,128)(2,1)S(1)}, u32[]{:S(2)}, u32[]{:S(2)}) collective-permute-start(bf16[64,8,192]{2,1,0:T(8,128)(2,1)} %slice.351), channel_id=1, source_target_pairs={{0,3},{1,2},{2,1},{3,0},{4,7},{5,6},{6,5},{7,4},{8,11},{9,10},{10,... | collective-permute-start | bytes 589832 | tf_op jit(solution)/shard_map/ppermute | solution.py:53
  418.3 13.4 %collective-permute-start.66 = (bf16[64,8,192]{2,1,0:T(8,128)(2,1)}, bf16[64,8,192]{2,1,0:T(8,128)(2,1)}, u32[]{:S(2)}, u32[]{:S(2)}) collective-permute-start(bf16[64,8,192]{2,1,0:T(8,128)(2,1)} %slice.349), channel_id=1, source_target_pairs={{0,2},{1,3},{2,0},{3,1},{4,6},{5,7},{6,4},{7,5},{8,10},{9,11},{10,... | collective-permute-start | bytes 589832 | tf_op jit(solution)/shard_map/ppermute | solution.py:53
  422.1 41.8 %collective-permute-start.84 = (bf16[4,96,1536]{2,1,0:T(8,128)(2,1)}, bf16[4,96,1536]{2,1,0:T(8,128)(2,1)}, u32[]{:S(2)}, u32[]{:S(2)}) collective-permute-start(bf16[4,96,1536]{2,1,0:T(8,128)(2,1)} %dynamic-slice_bitcast_fusion.1), channel_id=1, source_target_pairs={{0,4},{2,6},{4,0},{6,2},{8,12},{10,14},{12,8},{14,10},{16,20},{18,... | collective-permute-start | bytes 3538952 | tf_op jit(solution)/shard_map/ppermute | solution.py:45
  425.4 75.7 %collective-permute-start.71 = (bf16[4,193,768]{2,0,1:T(4,128)(2,1)}, bf16[4,193,768]{2,0,1:T(4,128)(2,1)}, u32[]{:S(2)}, u32[]{:S(2)}) collective-permute-start(bf16[4,193,768]{2,0,1:T(4,128)(2,1)} %copy.254), channel_id=1, source_target_pairs={{0,4},{2,6},{4,0},{6,2},{8,12},{10,14},{12,8},{14,10},{16,20},{18,... | collective-permute-start | bytes 3557384 | tf_op jit(solution)/shard_map/ppermute | solution.py:45
  440.8 7.2 %collective-permute-start.80 = (bf16[96,768]{1,0:T(8,128)(2,1)S(1)}, bf16[96,768]{1,0:T(8,128)(2,1)S(1)}, u32[]{:S(2)}, u32[]{:S(2)}) collective-permute-start(bf16[96,768]{1,0:T(8,128)(2,1)S(1)} %fusion.83), channel_id=1, source_target_pairs={{0,8},{2,10},{4,12},{6,14},{8,16},{10,18},{12,20},{14,22},{16,24},... | collective-permute-start | bytes 442376 | tf_op jit(solution)/shard_map/ppermute | solution.py:60
  448.0 8.5 %collective-permute-start.81 = (bf16[96,768]{1,0:T(8,128)(2,1)S(1)}, bf16[96,768]{1,0:T(8,128)(2,1)S(1)}, u32[]{:S(2)}, u32[]{:S(2)}) collective-permute-start(bf16[96,768]{1,0:T(8,128)(2,1)S(1)} %fusion.62), channel_id=1, source_target_pairs={{0,8},{2,10},{4,12},{6,14},{8,16},{10,18},{12,20},{14,22},{16,24},... | collective-permute-start | bytes 442376 | tf_op jit(solution)/shard_map/ppermute | solution.py:60
  450.1 18.5 %collective-permute-start.76 = (bf16[192,768]{1,0:T(8,128)(2,1)S(1)}, bf16[192,768]{1,0:T(8,128)(2,1)S(1)}, u32[]{:S(2)}, u32[]{:S(2)}) collective-permute-start(bf16[192,768]{1,0:T(8,128)(2,1)S(1)} %fusion.60), channel_id=1, source_target_pairs={{0,8},{2,10},{4,12},{6,14},{8,16},{10,18},{12,20},{14,22},{16,24},... | collective-permute-start | bytes 884744 | tf_op jit(solution)/shard_map/ppermute | solution.py:60
  456.6 11.1 %collective-permute-start.82 = (bf16[96,768]{1,0:T(8,128)(2,1)S(1)}, bf16[96,768]{1,0:T(8,128)(2,1)S(1)}, u32[]{:S(2)}, u32[]{:S(2)}) collective-permute-start(bf16[96,768]{1,0:T(8,128)(2,1)S(1)} %fusion.63), channel_id=1, source_target_pairs={{0,8},{2,10},{4,12},{6,14},{8,16},{10,18},{12,20},{14,22},{16,24},... | collective-permute-start | bytes 442376 | tf_op jit(solution)/shard_map/ppermute | solution.py:60
  465.6 13.6 %collective-permute-start.85 = (bf16[96,1536]{1,0:T(8,128)(2,1)S(1)}, bf16[96,1536]{1,0:T(8,128)(2,1)S(1)}, u32[]{:S(2)}, u32[]{:S(2)}) collective-permute-start(bf16[96,1536]{1,0:T(8,128)(2,1)S(1)} %fusion.61), channel_id=1, source_target_pairs={{0,8},{2,10},{4,12},{6,14},{8,16},{10,18},{12,20},{14,22},{16,24},... | collective-permute-start | bytes 884744 | tf_op jit(solution)/shard_map/ppermute | solution.py:60
  468.7 23.1 %collective-permute-start.77 = (bf16[192,768]{1,0:T(8,128)(2,1)S(1)}, bf16[192,768]{1,0:T(8,128)(2,1)S(1)}, u32[]{:S(2)}, u32[]{:S(2)}) collective-permute-start(bf16[192,768]{1,0:T(8,128)(2,1)S(1)} %fusion.50), channel_id=1, source_target_pairs={{0,8},{2,10},{4,12},{6,14},{8,16},{10,18},{12,20},{14,22},{16,24},... | collective-permute-start | bytes 884744 | tf_op jit(solution)/shard_map/ppermute | solution.py:60
  479.3 25.2 %collective-permute-start.86 = (bf16[96,1536]{1,0:T(8,128)(2,1)S(1)}, bf16[96,1536]{1,0:T(8,128)(2,1)S(1)}, u32[]{:S(2)}, u32[]{:S(2)}) collective-permute-start(bf16[96,1536]{1,0:T(8,128)(2,1)S(1)} %fusion.48), channel_id=1, source_target_pairs={{0,8},{2,10},{4,12},{6,14},{8,16},{10,18},{12,20},{14,22},{16,24},... | collective-permute-start | bytes 884744 | tf_op jit(solution)/shard_map/ppermute | solution.py:60
  491.8 14.3 %collective-permute-start.78 = (bf16[192,768]{1,0:T(8,128)(2,1)S(1)}, bf16[192,768]{1,0:T(8,128)(2,1)S(1)}, u32[]{:S(2)}, u32[]{:S(2)}) collective-permute-start(bf16[192,768]{1,0:T(8,128)(2,1)S(1)} %fusion.51), channel_id=1, source_target_pairs={{0,8},{2,10},{4,12},{6,14},{8,16},{10,18},{12,20},{14,22},{16,24},... | collective-permute-start | bytes 884744 | tf_op jit(solution)/shard_map/ppermute | solution.py:60
  502.6 17.3 %collective-permute-start.72 = (bf16[193,768]{1,0:T(8,128)(2,1)S(1)}, bf16[193,768]{1,0:T(8,128)(2,1)S(1)}, u32[]{:S(2)}, u32[]{:S(2)}) collective-permute-start(bf16[193,768]{1,0:T(8,128)(2,1)S(1)} %fusion.57), channel_id=1, source_target_pairs={{0,8},{2,10},{4,12},{6,14},{8,16},{10,18},{12,20},{14,22},{16,24},... | collective-permute-start | bytes 889352 | tf_op jit(solution)/shard_map/ppermute | solution.py:60
  504.5 21.7 %collective-permute-start.87 = (bf16[96,1536]{1,0:T(8,128)(2,1)S(1)}, bf16[96,1536]{1,0:T(8,128)(2,1)S(1)}, u32[]{:S(2)}, u32[]{:S(2)}) collective-permute-start(bf16[96,1536]{1,0:T(8,128)(2,1)S(1)} %fusion.49), channel_id=1, source_target_pairs={{0,8},{2,10},{4,12},{6,14},{8,16},{10,18},{12,20},{14,22},{16,24},... | collective-permute-start | bytes 884744 | tf_op jit(solution)/shard_map/ppermute | solution.py:60
  519.9 18.4 %collective-permute-start.73 = (bf16[193,768]{1,0:T(8,128)(2,1)S(1)}, bf16[193,768]{1,0:T(8,128)(2,1)S(1)}, u32[]{:S(2)}, u32[]{:S(2)}) collective-permute-start(bf16[193,768]{1,0:T(8,128)(2,1)S(1)} %fusion.45), channel_id=1, source_target_pairs={{0,8},{2,10},{4,12},{6,14},{8,16},{10,18},{12,20},{14,22},{16,24},... | collective-permute-start | bytes 889352 | tf_op jit(solution)/shard_map/ppermute | solution.py:60
  526.3 12.1 %collective-permute-start.88 = (bf16[48,1536]{1,0:T(8,128)(2,1)S(1)}, bf16[48,1536]{1,0:T(8,128)(2,1)S(1)}, u32[]{:S(2)}, u32[]{:S(2)}) collective-permute-start(bf16[48,1536]{1,0:T(8,128)(2,1)S(1)} %fusion.84), channel_id=1, source_target_pairs={{0,2},{2,0},{4,6},{6,4},{8,10},{10,8},{12,14},{14,12},{16,18},{18,... | collective-permute-start | bytes 442376 | tf_op jit(solution)/shard_map/ppermute | solution.py:45
  538.4 10.1 %collective-permute-start.74 = (bf16[193,768]{1,0:T(8,128)(2,1)S(1)}, bf16[193,768]{1,0:T(8,128)(2,1)S(1)}, u32[]{:S(2)}, u32[]{:S(2)}) collective-permute-start(bf16[193,768]{1,0:T(8,128)(2,1)S(1)} %fusion.46), channel_id=1, source_target_pairs={{0,8},{2,10},{4,12},{6,14},{8,16},{10,18},{12,20},{14,22},{16,24},... | collective-permute-start | bytes 889352 | tf_op jit(solution)/shard_map/ppermute | solution.py:60
  (147 other events, 904.0 us)
Sparse Core Ops, SparseCore 0:
  13.2 131.5 all-gather.2
  340.2 202.5 reduce-scatter.1

commit v4 on v3

--- a/solution.py
+++ b/solution.py
@@ -87,19 +87,33 @@
         self.arrived[0] = self.arrived[0] + earlier
 
 
-def line_gather(values_in, queue):
+def line_pass(values_in, queue, holds=()):
     count = line_size()
     if count > 4:
-        return lax.all_gather(values_in, "dp", axis=0, axis_index_groups=line_groups())
+        whole = lax.all_gather(values_in, "dp", axis=0, axis_index_groups=line_groups())
+        return [whole[slot] for slot in range(count)]
+    got = [values_in]
+    for step in range(1, count):
+        if step == count - 1 and holds:
+            queue.hold(*holds)
+        got.append(queue.step(got[-1]))
+    return got
+
+
+def line_place_blocks(got):
+    count = len(got)
     if count == 1:
-        return values_in[None]
-    got = [values_in]
-    for _ in range(1, count):
-        got.append(queue.step(got[-1]))
+        return got[0][None]
+    if count > 4:
+        return jnp.stack(got)
     place = line_place()
     return jnp.stack(
         [pick(place, [got[(here - slot) % count] for here in range(count)]) for slot in range(count)]
     )
+
+
+def line_gather(values_in, queue):
+    return line_place_blocks(line_pass(values_in, queue))
 
 
 def pair_up(own, other, place):
@@ -112,7 +126,7 @@
     return jnp.stack([pick(place, [lined, other]), pick(place, [other, lined])], axis=1)
 
 
-def line_scatter(parts):
+def line_scatter(parts, marks=None):
     count = line_size()
     if count > 4:
         return lax.psum_scatter(
@@ -125,7 +139,10 @@
 
     total = slot(-1).astype(F32)
     for back in range(2, count + 1):
-        total = slot(-back).astype(F32) + step_line(total.astype(BF16), 1).astype(F32)
+        got = step_line(total.astype(BF16), 1)
+        if marks is not None:
+            marks.append(got)
+        total = slot(-back).astype(F32) + got.astype(F32)
     return total
 
 
@@ -286,7 +303,7 @@
     )
     grad_middle_norm, grad_gain_two, grad_bias_two = second_pull(grad_second)
     grad_middle = grad_layer + grad_middle_norm
-    grad_branch = quad_gather(after(grad_middle.astype(BF16), *ties[2]))
+    grad_branch = quad_gather(after(grad_middle.astype(BF16), forward_grads, *ties[2]))
     grad_mix = dot_nn(grad_branch, output_proj).astype(BF16)
     forward_half = y_scatter(forward_grads.reshape(ties[5] + (-1,)))
     grad_packed = attend_backward(packed, softened, grad_mix, places)
@@ -334,23 +351,37 @@
 PAIR = 2 * HD
 
 
-def local_body(
-    bound_ref, masked_ref, spread_ref, cotangent_ref, gain_ref, bias_ref,
-    first_ref, last_ref,
-    result_ref, grad_ref, grad_low_ref, normed_ref, second_ref, grad_out_ref, branch_ref,
-    joint_first_ref, joint_last_ref, value_first_ref, value_last_ref,
-    mixture_first_ref, mixture_last_ref, hidden_first_ref, hidden_last_ref,
-    active_first_ref, active_last_ref, norms_ref,
-    probs_ref,
+def local_body(tiles, wide, *refs):
+    @pl.when(pl.program_id(0) < tiles)
+    def _():
+        local_rows(wide, *refs)
+
+    @pl.when(pl.program_id(0) >= tiles)
+    def _():
+        local_grads(tiles, wide, *refs)
+
+
+def local_rows(
+    wide,
+    scalars_ref, masked_ref, part_0_ref, part_1_ref, part_2_ref, part_3_ref, cotangent_ref,
+    gain_ref, bias_ref, first_ref, last_ref,
+    result_ref, grad_ref, give_0_ref, give_1_ref, give_2_ref, give_3_ref, norms_ref, weights_out_ref,
+    factors_ref, normed_all_ref, branch_all_ref, second_all_ref, grad_out_all_ref,
+    turned_ref, branch_turned_ref, probs_ref, stream_ref,
 ):
     rows = masked_ref.shape[0]
-    wide = mixture_first_ref.shape[1]
-    hidden_width = active_first_ref.shape[1]
-    grad_joints = (joint_first_ref, joint_last_ref)
-    grad_values = (value_first_ref, value_last_ref)
-    mixtures = (mixture_first_ref, mixture_last_ref)
-    actives = (active_first_ref, active_last_ref)
-    hiddens = (hidden_first_ref, hidden_last_ref)
+    hidden_width = first_ref.shape[3] // 2 - 2 * wide
+    here = pl.ds(pl.multiple_of(pl.program_id(0) * rows, rows), rows)
+    normed_ref, branch_ref = normed_all_ref.at[here], branch_all_ref.at[here]
+    second_ref, grad_out_ref = second_all_ref.at[here], grad_out_all_ref.at[here]
+
+    def factor(start, width):
+        return [factors_ref.at[side, here, start : start + width] for side in range(2)]
+
+    grad_joints, grad_values = factor(0, 2 * wide), factor(2 * wide, wide)
+    mixtures = factor(3 * wide, wide)
+    hiddens = factor(4 * wide, hidden_width)
+    actives = factor(4 * wide + hidden_width, hidden_width)
 
     def weight(side, start, stop):
         return (first_ref, last_ref)[side][:, 0, :, start:stop].reshape(D, stop - start)
@@ -359,8 +390,18 @@
     pairs = wide // PAIR
 
     row = pl.program_id(0) * rows + lax.broadcasted_iota(jnp.int32, (rows, 1), 0)
-    keep = (row < bound_ref[0]).astype(F32)
-    stream = masked_ref[...].astype(F32) + spread_ref[...].astype(F32)
+    keep = (row < scalars_ref[0]).astype(F32)
+    place = scalars_ref[1]
+    part_width = D // QUAD
+    for slot in range(QUAD):
+        columns = slice(slot * part_width, (slot + 1) * part_width)
+        for bits, part_ref in enumerate((part_0_ref, part_1_ref, part_2_ref, part_3_ref)):
+
+            @pl.when((place ^ bits) == slot)
+            def _(part_ref=part_ref, columns=columns):
+                stream_ref[:, columns] = masked_ref[:, columns].astype(F32) + part_ref[...].astype(F32)
+
+    stream = stream_ref[...]
     gain_one, gain_two = gain_ref[2:3, :], gain_ref[3:4, :]
     normed, unit_one, scale_one = norm_forward(stream, gain_one, bias_ref[2:3, :])
     normed = normed.astype(BF16)
@@ -462,7 +503,14 @@
     grad_in, gain_grad_one, bias_grad_one = norm_backward(grad_normed, unit_one, scale_one, gain_one)
     grad_stream = grad_middle + grad_in
     grad_ref[...] = grad_stream
-    grad_low_ref[...] = grad_stream.astype(BF16)
+    for slot in range(QUAD):
+        columns = slice(slot * part_width, (slot + 1) * part_width)
+        for bits, give_ref in enumerate((give_0_ref, give_1_ref, give_2_ref, give_3_ref)):
+
+            @pl.when((place ^ bits) == slot)
+            def _(give_ref=give_ref, columns=columns):
+                give_ref[...] = grad_stream[:, columns].astype(BF16)
+
 
     @pl.when(pl.program_id(0) == 0)
     def _():
@@ -472,23 +520,67 @@
         norms_ref[place : place + 1, :] += value
 
 
-def local_layer(bound, masked_low, spread, cotangent, gain_rows, bias_rows, weights, wide):
+def local_grads(
+    tiles, wide,
+    scalars_ref, masked_ref, part_0_ref, part_1_ref, part_2_ref, part_3_ref, cotangent_ref,
+    gain_ref, bias_ref, first_ref, last_ref,
+    result_ref, grad_ref, give_0_ref, give_1_ref, give_2_ref, give_3_ref, norms_ref, weights_out_ref,
+    factors_ref, normed_ref, branch_ref, second_ref, grad_out_ref,
+    turned_ref, branch_turned_ref, probs_ref, stream_ref,
+):
+    step = pl.program_id(0) - tiles
+    block, side = step // 2, step % 2
+    width = weights_out_ref.shape[3]
+
+    @pl.when(step == 0)
+    def _():
+        turned_ref[...] = normed_ref[...].T
+        branch_turned_ref[...] = branch_ref[...].T
+
+    @pl.when(step == 4)
+    def _():
+        turned_ref[...] = second_ref[...].T
+
+    @pl.when(step == 8)
+    def _():
+        turned_ref[...] = grad_out_ref[...].T
+
+    def give(left_ref, right, columns):
+        product = dot_nn(left_ref[...], right).astype(BF16)
+        weights_out_ref[:, :, :, columns] = product.reshape(
+            weights_out_ref.shape[:3] + (product.shape[1],)
+        )
+
+    @pl.when(block == 1)
+    def _():
+        give(turned_ref, factors_ref[side, :, 2 * wide : 3 * wide], slice(0, wide))
+        give(branch_turned_ref, factors_ref[side, :, 3 * wide : 4 * wide], slice(wide, 2 * wide))
+
+    @pl.when(block != 1)
+    def _():
+        start = pl.multiple_of(block * width, width)
+        give(turned_ref, factors_ref[side, :, pl.ds(start, width)], slice(None))
+
+
+def local_layer(scalars, masked_low, spread_parts, cotangent, gain_rows, bias_rows, weights, wide):
     rows = masked_low.shape[0]
-    hidden_width = weights.shape[3] // 2 - 2 * wide
-    tiled = lambda width: pl.BlockSpec((TILE, width), lambda i: (i, 0))
-    fixed = lambda array: pl.BlockSpec(
-        array.shape, lambda i: (0, 0), pipeline_mode=pl.Buffered(1)
-    )
-    widths = (
-        [(D, BF16), (D, F32)] + [(D, BF16)] * 5 + [(2 * wide, BF16)] * 2 + [(wide, BF16)] * 4
-        + [(hidden_width, BF16)] * 4
-    )
-    flops = 8 * rows * D * 2 * (4 * wide + 2 * hidden_width)
+    tiles = rows // TILE
+    columns = weights.shape[3]
+    width = 2 * wide
+    assert columns == 6 * width
+    tiled = lambda size: pl.BlockSpec((TILE, size), lambda i: (jnp.minimum(i, tiles - 1), 0))
+    fixed = lambda array: pl.BlockSpec(array.shape, lambda i: (0, 0), pipeline_mode=pl.Buffered(1))
+    outs = [(D, BF16), (D, F32)] + [(D // QUAD, BF16)] * QUAD
+
+    def grads_place(i):
+        step = jnp.maximum(i - tiles, 0)
+        return (0, step % 2, 0, step // 2)
+
     return pl.pallas_call(
-        local_body,
-        grid=(rows // TILE,),
+        lambda *refs: local_body(tiles, wide, *refs),
+        grid=(tiles + 2 * (columns // width),),
         in_specs=[pl.BlockSpec(memory_space=pltpu.SMEM)]
-        + [tiled(D)] * 3
+        + [tiled(D)] + [tiled(D // QUAD)] * QUAD + [tiled(D)]
         + [fixed(array) for array in (gain_rows, bias_rows)]
         + [
             pl.BlockSpec(
@@ -498,91 +590,29 @@
             )
             for side in range(2)
         ],
-        out_specs=[tiled(width) for width, _ in widths] + [pl.BlockSpec((8, D), lambda i: (0, 0))],
-        out_shape=[jax.ShapeDtypeStruct((rows, width), kind) for width, kind in widths]
-        + [jax.ShapeDtypeStruct((8, D), F32)],
-        scratch_shapes=[
-            pltpu.VMEM((2 * (TILE // BAND) * (wide // PAIR), 2 * BAND, BAND), F32)
+        out_specs=[tiled(size) for size, _ in outs]
+        + [
+            pl.BlockSpec((8, D), lambda i: (0, 0)),
+            pl.BlockSpec((weights.shape[0], 1, weights.shape[2], width), grads_place),
+        ],
+        out_shape=[jax.ShapeDtypeStruct((rows, size), kind) for size, kind in outs]
+        + [jax.ShapeDtypeStruct((8, D), F32), jax.ShapeDtypeStruct(weights.shape, BF16)],
+        scratch_shapes=[pltpu.VMEM((2, rows, columns), BF16)]
+        + [pltpu.VMEM((rows, D), BF16)] * 4
+        + [pltpu.VMEM((D, rows), BF16)] * 2
+        + [
+            pltpu.VMEM((2 * (TILE // BAND) * (wide // PAIR), 2 * BAND, BAND), F32),
+            pltpu.VMEM((TILE, D), F32),
         ],
         compiler_params=pltpu.CompilerParams(
             dimension_semantics=("arbitrary",), vmem_limit_bytes=58 * 1024 * 1024
         ),
         cost_estimate=pl.CostEstimate(
-            flops=flops, transcendentals=rows * 2 * hidden_width, bytes_accessed=36 * 1024 * 1024
+            flops=12 * rows * D * columns,
+            transcendentals=rows * columns,
+            bytes_accessed=2 * 4 * D * columns,
         ),
-    )(bound, masked_low, spread, cotangent, gain_rows, bias_rows, weights, weights)
-
-
-def grads_body(
-    normed_ref, branch_ref, second_ref, grad_out_ref,
-    joint_first_ref, joint_last_ref, value_first_ref, value_last_ref,
-    mixture_first_ref, mixture_last_ref, hidden_first_ref, hidden_last_ref,
-    active_first_ref, active_last_ref, out_ref, turned_ref, branch_turned_ref,
-):
-    block, side = pl.program_id(0), pl.program_id(1)
-    half = value_first_ref.shape[1]
-    shape = out_ref.shape[:3]
-
-    @pl.when((side == 0) & (block == 0))
-    def _():
-        turned_ref[...] = normed_ref[...].T
-        branch_turned_ref[...] = branch_ref[...].T
-
-    @pl.when((side == 0) & (block == 2))
-    def _():
-        turned_ref[...] = second_ref[...].T
-
-    @pl.when((side == 0) & (block == 4))
-    def _():
-        turned_ref[...] = grad_out_ref[...].T
-
-    def give(place, chosen, left_ref, right_ref, columns):
-        @pl.when(chosen & (side == place))
-        def _():
-            product = dot_nn(left_ref[...], right_ref[...]).astype(BF16)
-            out_ref[:, :, :, columns] = product.reshape(shape + (product.shape[1],))
-
-    for place, (joint, value, mixture, hidden, active) in enumerate(
-        (
-            (joint_first_ref, value_first_ref, mixture_first_ref, hidden_first_ref, active_first_ref),
-            (joint_last_ref, value_last_ref, mixture_last_ref, hidden_last_ref, active_last_ref),
-        )
-    ):
-        give(place, block == 0, turned_ref, joint, slice(None))
-        give(place, block == 1, turned_ref, value, slice(0, half))
-        give(place, block == 1, branch_turned_ref, mixture, slice(half, 2 * half))
-        give(place, (block == 2) | (block == 3), turned_ref, hidden, slice(None))
-        give(place, block >= 4, turned_ref, active, slice(None))
-
-
-def weight_grads(lefts, joints, values, mixtures, hiddens, actives, shape):
-    rows, model = lefts[0].shape
-    block = joints[0].shape[1]
-
-    def given(array, first=None):
-        if first is None:
-            return pl.BlockSpec(array.shape, lambda b, s: (0, 0), pipeline_mode=pl.Buffered(1))
-        return pl.BlockSpec((rows, block), lambda b, s: (0, jnp.clip(b - first, 0, 1)))
-
-    arrays = (*lefts, *joints, *values, *mixtures, *hiddens, *actives)
-    return pl.pallas_call(
-        grads_body,
-        grid=(shape[3] // block, 2),
-        in_specs=[given(array) for array in (*lefts, *joints, *values, *mixtures)]
-        + [given(array, 2) for array in hiddens]
-        + [given(array, 4) for array in actives],
-        out_specs=pl.BlockSpec((shape[0], 1, shape[2], block), lambda b, s: (0, s, 0, b)),
-        out_shape=jax.ShapeDtypeStruct(shape, BF16),
-        scratch_shapes=[pltpu.VMEM((model, rows), BF16)] * 2,
-        compiler_params=pltpu.CompilerParams(
-            dimension_semantics=("arbitrary", "arbitrary"), vmem_limit_bytes=48 * 1024 * 1024
-        ),
-        cost_estimate=pl.CostEstimate(
-            flops=4 * rows * model * shape[3],
-            transcendentals=0,
-            bytes_accessed=2 * (4 * rows * model + 2 * (rows + model) * shape[3]),
-        ),
-    )(*arrays)
+    )(scalars, masked_low, *spread_parts, cotangent, gain_rows, bias_rows, weights, weights)
 
 
 def shards(
@@ -664,10 +694,12 @@
     global_shard = pair_up(own_half, flip_dp(their_half, 1), x_here)
     global_shard = global_shard.reshape(2 * shard_rows, -1)
     attend_columns = 2 * heads_width
-    attend_shard, forward_shard = global_shard[:, :attend_columns], global_shard[:, attend_columns:]
-    attend_lined = line_gather(attend_shard, queue)
-    forward_lined = line_gather(forward_shard, queue)
-    spread_lined = line_gather(jnp.transpose(global_proj), queue)
+    global_blocks = line_pass(global_shard, queue, (patch_whole,))
+    attend_lined = line_place_blocks([block[:, :attend_columns] for block in global_blocks])
+    forward_lined = line_place_blocks([block[:, attend_columns:] for block in global_blocks])
+    proj_part = jnp.transpose(global_proj)
+    proj_pair = pair_up(proj_part, flip_dp(proj_part, 2), y_place())
+    spread_lined = line_gather(proj_pair, queue)
     joint_columns = 3 * heads_width // 2
 
     patches_mat = patches_dealt.reshape(QUAD * patch_rows, cells * proj_rows)
@@ -688,48 +720,71 @@
     global_out, first_saved, first_weights = layer_forward(
         initial, attend_of, forward_of, gain_rows, bias_rows, 0, global_places
     )
-    spread_mat = y_gather(after(spread_lined, first_saved[6])).reshape(cells * proj_rows, D)
+    spread_mat = spread_lined.reshape(cells * proj_rows, D)
     global_low = quad_gather(global_out.astype(BF16))
     spread_dealt = dot_nt(global_low, spread_mat).astype(BF16)
-    spread = quad_collect(spread_dealt.reshape(QUAD * patch_rows, cells, proj_rows))
-    spread = spread.reshape(half_rows, D)
+    spread_blocks = spread_dealt.reshape(QUAD * patch_rows, cells, proj_rows)
+    byte_cells = cells == P_SIZE
+    if byte_cells:
+        part_place = quad_place()
+        spread_parts = [
+            spread_blocks[bits * patch_rows : (bits + 1) * patch_rows] for bits in range(QUAD)
+        ]
+        spread_parts = [
+            (flip_quad(part, bits) if bits else part).reshape(half_rows, proj_rows)
+            for bits, part in enumerate(spread_parts)
+        ]
+    else:
+        part_place = jnp.int32(0)
+        spread = quad_collect(spread_blocks).reshape(half_rows, D)
+        spread_parts = jnp.split(spread, QUAD, axis=1)
 
     dp = dp_size()
     whole_rows = shard_rows % 16 == 0
     local_weights = local_whole.reshape(dp, 2, shard_rows, -1)
     if not whole_rows:
         local_weights = jnp.transpose(local_weights, (1, 0, 2, 3)).reshape(1, 2, D, -1)
-    bound = jnp.clip(lengths - lax.axis_index("tensor") * half_rows, 0, half_rows)
-    (
-        outcome, grad_local, grad_low, normed, second, grad_out, branch,
-        *grad_factors, local_norms,
-    ) = local_layer(bound, masked_low, spread, cotangent[0], gain_rows, bias_rows, local_weights, heads_width)
+    bound = jnp.clip(lengths[0] - lax.axis_index("tensor") * half_rows, 0, half_rows)
+    scalars = jnp.stack([bound, part_place.astype(jnp.int32)])
+    local_outs = local_layer(
+        scalars, masked_low, spread_parts, cotangent[0], gain_rows, bias_rows, local_weights, heads_width
+    )
+    outcome, grad_local = local_outs[:2]
+    grad_parts = local_outs[2 : 2 + QUAD]
+    local_norms, local_grads_out = local_outs[2 + QUAD :]
     second_gains, second_biases = (local_norms[0], local_norms[1]), (local_norms[2], local_norms[3])
-    grad_spread = grad_low.reshape(patch_rows, cells, QUAD, proj_rows)
-    spread_grads = quad_deal(grad_spread).reshape(QUAD * patch_rows, cells * proj_rows)
-    factor_pairs = [grad_factors[k : k + 2] for k in range(0, 10, 2)]
-    local_grads = weight_grads(
-        (normed, branch, second, grad_out), *factor_pairs, local_weights.shape
-    )
-    spread_grads = after(spread_grads, local_grads)
+    if byte_cells:
+        spread_grads = jnp.concatenate(
+            [
+                (flip_quad(part, bits) if bits else part).reshape(patch_rows, cells, proj_rows)
+                for bits, part in enumerate(grad_parts)
+            ],
+            axis=0,
+        )
+    else:
+        grad_low = jnp.concatenate(grad_parts, axis=1)
+        spread_grads = quad_deal(grad_low.reshape(patch_rows, cells, QUAD, proj_rows))
+    spread_grads = spread_grads.reshape(QUAD * patch_rows, cells * proj_rows)
     if not whole_rows:
-        local_grads = jnp.transpose(local_grads.reshape(2, dp, shard_rows, -1), (1, 0, 2, 3))
+        local_grads_out = jnp.transpose(
+            local_grads_out.reshape(2, dp, shard_rows, -1), (1, 0, 2, 3)
+        )
     local_summed = lax.psum_scatter(
-        local_grads.reshape(2 * dp, shard_rows, -1), ("dp", "tensor"), scatter_dimension=0
+        local_grads_out.reshape(2 * dp, shard_rows, -1), ("dp", "tensor"), scatter_dimension=0
     ).astype(F32)
 
     grad_global = quad_scatter(dot_nn(spread_grads, spread_mat))
     proj_grads = dot_tn(spread_grads, global_low).astype(BF16).reshape(cells, proj_rows, D)
-    proj_half = y_scatter(proj_grads)
-    ties = ((), (), (), (), (), (cells, 2 * shard_rows))
+    marks = []
+    grad_proj = line_scatter(proj_grads.reshape(line_size(), 2, proj_rows, D), marks)
+    grad_proj = halve(grad_proj, y_place(), 0, 2)
+    ties = ((), (), tuple(marks[:1]), (), tuple(marks[1:2]), (cells, 2 * shard_rows))
     grad_start, attend_half, forward_half, first_gains, first_biases = layer_backward(
         grad_global, first_saved, first_weights, gain_rows, bias_rows, 0, global_places, ties
     )
-    grad_proj = line_scatter(proj_half)
-    forward_global = line_scatter(forward_half)
-    attend_global = line_scatter(attend_half)
+    global_summed = line_scatter(jnp.concatenate([attend_half, forward_half], axis=2))
     grad_patch_mat = dot_tn(patches_mat, grad_start).astype(BF16).reshape(cells, proj_rows, D)
-    grad_patches = dot_nt(grad_start, patch_mat).astype(BF16)
+    grad_patches = after(dot_nt(grad_start, patch_mat).astype(BF16), forward_half, *marks[2:3])
     grad_patches = quad_collect(grad_patches.reshape(QUAD * patch_rows, cells, proj_rows))
     grad_patches = grad_patches.reshape(half_rows, D).astype(F32)
     grad_input = ((grad_local + grad_patches) * keep_mask).astype(BF16)[None]
@@ -757,8 +812,9 @@
         theirs = lax.dynamic_index_in_dim(shaped, 1 - x_here, 0, keepdims=False)
         return pair_up(own, flip_dp(theirs.astype(BF16), 1).astype(F32), x_here)
 
-    attend_global = x_restore(attend_global)
-    forward_global = x_restore(forward_global)
+    global_summed = x_restore(global_summed)
+    attend_global = global_summed[..., :attend_columns]
+    forward_global = global_summed[..., attend_columns:]
 
     def x_columns(source, start, width):
         return jnp.concatenate([source[0, :, start : start + width], source[1, :, start : start + width]], axis=1)

time: 572 us -> 519 us (0.907)
  the two profiles are of different devices: /device:TPU:0 before, /device:TPU:4 now
where the time goes in v4:
time: 519 us; the launch traced here: 510 us
  waiting for transfers between devices  225 us (43%)
  local copies, waits for them, and re-layouts  78.8 us (15%)
  starting transfers between devices  70.3 us (14%)
  Pallas kernels  51.2 us (10%)
  other arithmetic  44.8 us (9%)
  matrix products  21.9 us (4%)
  between operations  17.2 us (3%)
    ppermute x18, waiting for transfers between devices, step_line(): lax.ppermute(values_in, 'dp', [(i, (i + 4 * offset) % count) for i in ran...  143 us
    ppermute x54, waiting for transfers between devices, flip_quad(): lax.ppermute(values_in, ('dp', 'tensor'), [(i, i ^ bits) for i in range(2...  67.8 us
    pallas_call x1, Pallas kernels, local_layer(): pl.pallas_call(lambda *refs: local_body(tiles, wide, *refs), grid=(tiles...  51.2 us
    ppermute x54, starting transfers between devices, flip_quad(): lax.ppermute(values_in, ('dp', 'tensor'), [(i, i ^ bits) for i in range(2...  36.9 us
    ppermute x18, starting transfers between devices, step_line(): lax.ppermute(values_in, 'dp', [(i, (i + 4 * offset) % count) for i in ran...  20 us
    ppermute x10, waiting for transfers between devices, flip_dp(): lax.ppermute(values_in, 'dp', [(i, i ^ bit) for i in range(dp_size())])  15.1 us
    unnamed x226, local copies, waits for them, and re-layouts  15 us
    ppermute x10, starting transfers between devices, flip_dp(): lax.ppermute(values_in, 'dp', [(i, i ^ bit) for i in range(dp_size())])  13.3 us
  transfers between devices with their start and end apart: 84, of which 42 were waited for; matrix products, arithmetic and copies ran while one was open for 25% of the time, Pallas kernels for 0%

profile of v4, /device:TPU:4, one launch (start us, length us, event | category | flops | bytes accessed | tf_op | source)
XLA Modules:
  0.0 509.6 jit_solution(4975438877921694122)
XLA Ops:
  14.9 1.6 collective-permute-start.3
  20.1 5.7 %collective-permute-done.3 = bf16[193,768]{1,0:T(8,128)(2,1)S(1)} collective-permute-done((bf16[193,768]{1,0:T(8,128)(2,1)S(1)}, bf16[193,768]{1,0:T(8,128)(2,1)S(1)}, u32[]{:S(2)}, u32[]{:S(2)}) %collective-permute-start.3) | collective-permute-done | bytes 296480 | tf_op jit(solution)/shard_map/ppermute | solution.py:60
  25.9 17.7 %collective-permute-done.4 = bf16[193,768]{1,0:T(8,128)(2,1)S(1)} collective-permute-done((bf16[193,768]{1,0:T(8,128)(2,1)S(1)}, bf16[193,768]{1,0:T(8,128)(2,1)S(1)}, u32[]{:S(2)}, u32[]{:S(2)}) %collective-permute-start.4) | collective-permute-done | bytes 296480 | tf_op jit(solution)/shard_map/ppermute | solution.py:60
  44.2 15.0 %collective-permute-done.5 = bf16[193,768]{1,0:T(8,128)(2,1)S(1)} collective-permute-done((bf16[193,768]{1,0:T(8,128)(2,1)S(1)}, bf16[193,768]{1,0:T(8,128)(2,1)S(1)}, u32[]{:S(2)}, u32[]{:S(2)}) %collective-permute-start.5) | collective-permute-done | bytes 296480 | tf_op jit(solution)/shard_map/ppermute | solution.py:60
  63.0 4.4 fusion.126
  67.4 2.1 copy.181
  69.5 2.0 copy.182
  72.9 2.3 collective-permute-done.17
  75.2 2.4 collective-permute-start.18
  82.5 12.6 %collective-permute-done.18 = bf16[96,2304]{1,0:T(8,128)(2,1)} collective-permute-done((bf16[96,2304]{1,0:T(8,128)(2,1)}, bf16[96,2304]{1,0:T(8,128)(2,1)}, u32[]{:S(2)}, u32[]{:S(2)}) %collective-permute-start.18) | collective-permute-done | bytes 442400 | tf_op jit(solution)/shard_map/ppermute | solution.py:60
  97.2 2.7 collective-permute-start.11
  100.1 9.8 %collective-permute-start.19 = (bf16[96,2304]{1,0:T(8,128)(2,1)}, bf16[96,2304]{1,0:T(8,128)(2,1)}, u32[]{:S(2)}, u32[]{:S(2)}) collective-permute-start(bf16[96,2304]{1,0:T(8,128)(2,1)} %collective-permute-done.18), channel_id=1, source_target_pairs={{0,8},{2,10},{4,12},{6,14},{8,16},{10,18},{12,20},{14,22},{16,24},... | collective-permute-start | bytes 1327112 | tf_op jit(solution)/shard_map/ppermute | solution.py:60
  109.9 3.0 fusion.149
  115.5 4.0 collective-permute-done.9
  119.5 2.3 collective-permute-done.8
  125.2 8.9 %collective-permute-done.35 = bf16[2,192,768]{2,1,0:T(8,128)(2,1)} collective-permute-done((bf16[2,192,768]{2,1,0:T(8,128)(2,1)}, bf16[2,192,768]{2,1,0:T(8,128)(2,1)}, u32[]{:S(2)}, u32[]{:S(2)}) %collective-permute-start.35) | collective-permute-done | bytes 589856 | tf_op jit(solution)/shard_map/ppermute | solution.py:60
  134.1 14.2 %collective-permute-done.19 = bf16[96,2304]{1,0:T(8,128)(2,1)} collective-permute-done((bf16[96,2304]{1,0:T(8,128)(2,1)}, bf16[96,2304]{1,0:T(8,128)(2,1)}, u32[]{:S(2)}, u32[]{:S(2)}) %collective-permute-start.19) | collective-permute-done | bytes 442400 | tf_op jit(solution)/shard_map/ppermute | solution.py:60
  153.0 13.1 %collective-permute-done.20 = bf16[4,96,768]{2,1,0:T(8,128)(2,1)S(1)} collective-permute-done((bf16[4,96,768]{2,1,0:T(8,128)(2,1)S(1)}, bf16[4,96,768]{2,1,0:T(8,128)(2,1)S(1)}, u32[]{:S(2)}, u32[]{:S(2)}) %collective-permute-start.20) | collective-permute-done | bytes 589856 | tf_op jit(solution)/shard_map/ppermute | solution.py:45
  170.7 1.8 fusion.150
  173.8 2.3 fusion.151
  179.0 1.9 concatenate.120
  181.5 2.7 collective-permute-done.22
  188.3 1.8 select_bitcast_fusion.3
  199.9 2.4 collective-permute-done.29
  204.6 2.9 collective-permute-done.33
  207.5 2.1 collective-permute-done.32
  211.9 1.9 slice.372
  218.7 1.8 copy.213
  220.6 1.8 copy.214
  222.4 1.8 copy.215
  226.7 3.1 collective-permute-done.40
  229.8 51.2 %shard_map.186 = (bf16[512,768]{1,0:T(8,128)(2,1)}, f32[512,768]{1,0:T(8,128)}, bf16[512,192]{1,0:T(8,128)(2,1)}, bf16[512,192]{1,0:T(8,128)(2,1)}, bf16[512,192...) custom-call(s32[2]{0:T(128)} %pad_add_fusion.refs_0_, ...), custom_call_target="tpu_custom_call" | custom-call | flops 21743271936 | bytes 28311552 | tf_op jit(solution)/shard_map/pallas_call | solution.py:579
  286.7 5.3 %collective-permute-done.42 = bf16[512,192]{1,0:T(8,128)(2,1)} collective-permute-done((bf16[512,192]{1,0:T(8,128)(2,1)}, bf16[512,192]{1,0:T(8,128)(2,1)}, u32[]{:S(2)}, u32[]{:S(2)}) %collective-permute-start.42) | collective-permute-done | bytes 196640 | tf_op jit(solution)/shard_map/ppermute | solution.py:53
  293.9 2.2 collective-permute-done.43
  297.1 2.0 fusion.153
  302.3 2.2 collective-permute-done.46
  304.6 2.4 collective-permute-done.45
  309.8 2.3 collective-permute-done.49
  312.1 2.1 collective-permute-done.48
  322.2 3.0 copy.211
  332.5 2.2 fusion.5
  334.8 2.5 collective-permute-done.55
  346.0 4.5 collective-permute-done.59
  350.5 4.5 collective-permute-done.58
  359.8 5.0 collective-permute-done.60
  371.7 1.7 copy.218
  373.4 5.1 collective-permute-start.72
  384.3 4.4 collective-permute-start.78
  388.6 14.3 %collective-permute-done.65 = bf16[2,192,768]{2,1,0:T(8,128)(2,1)S(1)} collective-permute-done((bf16[2,192,768]{2,1,0:T(8,128)(2,1)S(1)}, bf16[2,192,768]{2,1,0:T(8,128)(2,1)S(1)}, u32[]{:S(2)}, u32[]{:S(2)}) %collective-permute-start.65) | collective-permute-done | bytes 589856 | tf_op jit(solution)/shard_map/ppermute | solution.py:60
  407.8 1.9 slice.396
  409.6 1.9 slice.398
  411.5 1.9 slice.394
  413.4 1.9 slice.392
  417.4 1.8 fusion.32
  419.3 4.2 collective-permute-done.68
  423.5 9.9 %collective-permute-done.67 = bf16[64,8,192]{2,1,0:T(8,128)(2,1)S(1)} collective-permute-done((bf16[64,8,192]{2,1,0:T(8,128)(2,1)}, bf16[64,8,192]{2,1,0:T(8,128)(2,1)S(1)}, u32[]{:S(2)}, u32[]{:S(2)}) %collective-permute-start.67) | collective-permute-done | bytes 196640 | tf_op jit(solution)/shard_map/ppermute | solution.py:53
  433.8 2.7 copy.212
  436.5 3.5 reshape.281
  439.9 3.0 fusion.43
  444.3 1.8 fusion.63
  447.8 16.8 %collective-permute-done.80 = bf16[96,2304]{1,0:T(8,128)(2,1)S(1)} collective-permute-done((bf16[96,2304]{1,0:T(8,128)(2,1)S(1)}, bf16[96,2304]{1,0:T(8,128)(2,1)S(1)}, u32[]{:S(2)}, u32[]{:S(2)}) %collective-permute-start.80) | collective-permute-done | bytes 442400 | tf_op jit(solution)/shard_map/ppermute | solution.py:60
  465.8 4.3 collective-permute-done.73
  471.7 14.3 %collective-permute-done.74 = bf16[193,768]{1,0:T(8,128)(2,1)S(1)} collective-permute-done((bf16[193,768]{1,0:T(8,128)(2,1)S(1)}, bf16[193,768]{1,0:T(8,128)(2,1)S(1)}, u32[]{:S(2)}, u32[]{:S(2)}) %collective-permute-start.74) | collective-permute-done | bytes 296480 | tf_op jit(solution)/shard_map/ppermute | solution.py:60
  486.3 10.2 %collective-permute-done.75 = bf16[193,768]{1,0:T(8,128)(2,1)S(1)} collective-permute-done((bf16[193,768]{1,0:T(8,128)(2,1)S(1)}, bf16[193,768]{1,0:T(8,128)(2,1)S(1)}, u32[]{:S(2)}, u32[]{:S(2)}) %collective-permute-start.75) | collective-permute-done | bytes 296480 | tf_op jit(solution)/shard_map/ppermute | solution.py:60
  (555 shorter events, 143.2 us)
Async XLA Ops:
  7.2 222.6 %all-gather.3.cloned.1.call-start = ((), (), s32[]{:S(2)}) async-start(), calls=%async_computation.2 | async-start | bytes 14598144 | tf_op jit(solution)/shard_map/all_gather | solution.py:657
  13.1 484.9 %reduce-scatter.2.cloned.1.call-start = ((), (), s32[]{:S(2)}) async-start(), calls=%async_computation.1 | async-start | bytes 14598144 | tf_op jit(solution)/shard_map/reduce_scatter | solution.py:772
  14.9 10.9 %collective-permute-start.3 = (bf16[193,768]{1,0:T(8,128)(2,1)S(1)}, bf16[193,768]{1,0:T(8,128)(2,1)S(1)}, u32[]{:S(2)}, u32[]{:S(2)}) collective-permute-start(bf16[193,768]{1,0:T(8,128)(2,1)S(1)} %fusion.70), channel_id=1, source_target_pairs={{0,8},{2,10},{4,12},{6,14},{8,16},{10,18},{12,20},{14,22},{16,24},... | collective-permute-start | bytes 889352 | tf_op jit(solution)/shard_map/ppermute | solution.py:60
  17.4 8.4 %collective-permute-start.16 = (bf16[48,2304]{1,0:T(8,128)(2,1)S(1)}, bf16[48,2304]{1,0:T(8,128)(2,1)S(1)}, u32[]{:S(2)}, u32[]{:S(2)}) collective-permute-start(bf16[48,2304]{1,0:T(8,128)(2,1)S(1)} %dynamic-slice_bitcast_fusion.4), channel_id=1, source_target_pairs={{0,2},{2,0},{4,6},{6,4},{8,10},{10,8},{12,14},{14,12},{16,18},{18,... | collective-permute-start | bytes 663560 | tf_op jit(solution)/shard_map/ppermute | solution.py:45
  18.9 61.6 %collective-permute-start.34 = (bf16[192,768]{1,0:T(8,128)(2,1)}, bf16[192,768]{1,0:T(8,128)(2,1)}, u32[]{:S(2)}, u32[]{:S(2)}) collective-permute-start(bf16[192,768]{1,0:T(8,128)(2,1)} %bitcast.49), channel_id=1, source_target_pairs={{0,4},{2,6},{4,0},{6,2},{8,12},{10,14},{12,8},{14,10},{16,20},{18,... | collective-permute-start | bytes 884744 | tf_op jit(solution)/shard_map/ppermute | solution.py:45
  25.8 17.8 %collective-permute-start.4 = (bf16[193,768]{1,0:T(8,128)(2,1)S(1)}, bf16[193,768]{1,0:T(8,128)(2,1)S(1)}, u32[]{:S(2)}, u32[]{:S(2)}) collective-permute-start(bf16[193,768]{1,0:T(8,128)(2,1)S(1)} %collective-permute-done.3), channel_id=1, source_target_pairs={{0,8},{2,10},{4,12},{6,14},{8,16},{10,18},{12,20},{14,22},{16,24},... | collective-permute-start | bytes 889352 | tf_op jit(solution)/shard_map/ppermute | solution.py:60
  43.6 15.6 %collective-permute-start.5 = (bf16[193,768]{1,0:T(8,128)(2,1)S(1)}, bf16[193,768]{1,0:T(8,128)(2,1)S(1)}, u32[]{:S(2)}, u32[]{:S(2)}) collective-permute-start(bf16[193,768]{1,0:T(8,128)(2,1)S(1)} %collective-permute-done.4), channel_id=1, source_target_pairs={{0,8},{2,10},{4,12},{6,14},{8,16},{10,18},{12,20},{14,22},{16,24},... | collective-permute-start | bytes 889352 | tf_op jit(solution)/shard_map/ppermute | solution.py:60
  43.6 31.6 %collective-permute-start.17 = (bf16[96,2304]{1,0:T(8,128)(2,1)S(1)}, bf16[96,2304]{1,0:T(8,128)(2,1)}, u32[]{:S(2)}, u32[]{:S(2)}) collective-permute-start(bf16[96,2304]{1,0:T(8,128)(2,1)S(1)} %bitcast.439), channel_id=1, source_target_pairs={{0,8},{2,10},{4,12},{6,14},{8,16},{10,18},{12,20},{14,22},{16,24},... | collective-permute-start | bytes 1327112 | tf_op jit(solution)/shard_map/ppermute | solution.py:60
  61.2 33.9 %collective-permute-start.6 = (bf16[4,193,768]{2,0,1:T(4,128)(2,1)}, bf16[4,193,768]{2,0,1:T(4,128)(2,1)}, u32[]{:S(2)}, u32[]{:S(2)}) collective-permute-start(bf16[4,193,768]{2,0,1:T(4,128)(2,1)} %copy.184), channel_id=1, source_target_pairs={{0,4},{2,6},{4,0},{6,2},{8,12},{10,14},{12,8},{14,10},{16,20},{18,... | collective-permute-start | bytes 3557384 | tf_op jit(solution)/shard_map/ppermute | solution.py:45
  69.5 30.4 %collective-permute-start = (bf16[64,8,192]{0,2,1:T(8,128)(2,1)}, bf16[64,8,192]{0,2,1:T(8,128)(2,1)}, u32[]{:S(2)}, u32[]{:S(2)}) collective-permute-start(bf16[64,8,192]{0,2,1:T(8,128)(2,1)} %bitcast.5), channel_id=1, source_target_pairs={{0,1},{1,0},{2,3},{3,2},{4,5},{5,4},{6,7},{7,6},{8,9},{9,8},{10,11... | collective-permute-start | bytes 589832 | tf_op jit(solution)/shard_map/ppermute | solution.py:53
  71.5 28.4 %collective-permute-start.1 = (bf16[64,8,192]{0,2,1:T(8,128)(2,1)}, bf16[64,8,192]{0,2,1:T(8,128)(2,1)}, u32[]{:S(2)}, u32[]{:S(2)}) collective-permute-start(bf16[64,8,192]{0,2,1:T(8,128)(2,1)} %bitcast.6), channel_id=1, source_target_pairs={{0,2},{1,3},{2,0},{3,1},{4,6},{5,7},{6,4},{7,5},{8,10},{9,11},{10,... | collective-permute-start | bytes 589832 | tf_op jit(solution)/shard_map/ppermute | solution.py:53
  75.2 19.9 %collective-permute-start.18 = (bf16[96,2304]{1,0:T(8,128)(2,1)}, bf16[96,2304]{1,0:T(8,128)(2,1)}, u32[]{:S(2)}, u32[]{:S(2)}) collective-permute-start(bf16[96,2304]{1,0:T(8,128)(2,1)} %collective-permute-done.17), channel_id=1, source_target_pairs={{0,8},{2,10},{4,12},{6,14},{8,16},{10,18},{12,20},{14,22},{16,24},... | collective-permute-start | bytes 1327112 | tf_op jit(solution)/shard_map/ppermute | solution.py:60
  80.5 19.6 %collective-permute-start.2 = (bf16[64,8,192]{0,2,1:T(8,128)(2,1)}, bf16[64,8,192]{0,2,1:T(8,128)(2,1)S(1)}, u32[]{:S(2)}, u32[]{:S(2)}) collective-permute-start(bf16[64,8,192]{0,2,1:T(8,128)(2,1)} %bitcast.7), channel_id=1, source_target_pairs={{0,3},{1,2},{2,1},{3,0},{4,7},{5,6},{6,5},{7,4},{8,11},{9,10},{10,... | collective-permute-start | bytes 589832 | tf_op jit(solution)/shard_map/ppermute | solution.py:53
  95.1 39.0 %collective-permute-start.35 = (bf16[2,192,768]{2,1,0:T(8,128)(2,1)}, bf16[2,192,768]{2,1,0:T(8,128)(2,1)}, u32[]{:S(2)}, u32[]{:S(2)}) collective-permute-start(bf16[2,192,768]{2,1,0:T(8,128)(2,1)} %pad_maximum_fusion.9), channel_id=1, source_target_pairs={{0,8},{2,10},{4,12},{6,14},{8,16},{10,18},{12,20},{14,22},{16,24},... | collective-permute-start | bytes 1769480 | tf_op jit(solution)/shard_map/ppermute | solution.py:60
  97.2 15.7 %collective-permute-start.11 = (bf16[1,8,192]{2,1,0:T(8,128)(2,1)S(1)}, bf16[1,8,192]{2,1,0:T(8,128)(2,1)S(1)}, u32[]{:S(2)}, u32[]{:S(2)}) collective-permute-start(bf16[1,8,192]{2,1,0:T(8,128)(2,1)S(1)} %bitcast.460), channel_id=1, source_target_pairs={{0,2},{1,3},{2,0},{3,1},{4,6},{5,7},{6,4},{7,5},{8,10},{9,11},{10,... | collective-permute-start | bytes 9224 | tf_op jit(solution)/shard_map/ppermute | solution.py:53
  99.9 13.1 %collective-permute-start.12 = (bf16[1,8,192]{2,1,0:T(8,128)(2,1)S(1)}, bf16[1,8,192]{2,1,0:T(8,128)(2,1)S(1)}, u32[]{:S(2)}, u32[]{:S(2)}) collective-permute-start(bf16[1,8,192]{2,1,0:T(8,128)(2,1)S(1)} %bitcast.461), channel_id=1, source_target_pairs={{0,3},{1,2},{2,1},{3,0},{4,7},{5,6},{6,5},{7,4},{8,11},{9,10},{10,... | collective-permute-start | bytes 9224 | tf_op jit(solution)/shard_map/ppermute | solution.py:53
  99.9 13.9 %collective-permute-start.10 = (bf16[1,8,192]{2,1,0:T(8,128)(2,1)S(1)}, bf16[1,8,192]{2,1,0:T(8,128)(2,1)S(1)}, u32[]{:S(2)}, u32[]{:S(2)}) collective-permute-start(bf16[1,8,192]{2,1,0:T(8,128)(2,1)S(1)} %bitcast.462), channel_id=1, source_target_pairs={{0,1},{1,0},{2,3},{3,2},{4,5},{5,4},{6,7},{7,6},{8,9},{9,8},{10,11... | collective-permute-start | bytes 9224 | tf_op jit(solution)/shard_map/ppermute | solution.py:53
  100.1 48.2 %collective-permute-start.19 = (bf16[96,2304]{1,0:T(8,128)(2,1)}, bf16[96,2304]{1,0:T(8,128)(2,1)}, u32[]{:S(2)}, u32[]{:S(2)}) collective-permute-start(bf16[96,2304]{1,0:T(8,128)(2,1)} %collective-permute-done.18), channel_id=1, source_target_pairs={{0,8},{2,10},{4,12},{6,14},{8,16},{10,18},{12,20},{14,22},{16,24},... | collective-permute-start | bytes 1327112 | tf_op jit(solution)/shard_map/ppermute | solution.py:60
  113.0 6.5 %collective-permute-start.9 = (bf16[64,768]{1,0:T(8,128)(2,1)S(1)}, bf16[64,768]{1,0:T(8,128)(2,1)S(1)}, u32[]{:S(2)}, u32[]{:S(2)}) collective-permute-start(bf16[64,768]{1,0:T(8,128)(2,1)S(1)} %get-tuple-element.193), channel_id=1, source_target_pairs={{0,3},{1,2},{2,1},{3,0},{4,7},{5,6},{6,5},{7,4},{8,11},{9,10},{10,... | collective-permute-start | bytes 294920 | tf_op jit(solution)/shard_map/ppermute | solution.py:53
  113.8 8.0 %collective-permute-start.8 = (bf16[64,768]{1,0:T(8,128)(2,1)S(1)}, bf16[64,768]{1,0:T(8,128)(2,1)S(1)}, u32[]{:S(2)}, u32[]{:S(2)}) collective-permute-start(bf16[64,768]{1,0:T(8,128)(2,1)S(1)} %get-tuple-element.194), channel_id=1, source_target_pairs={{0,2},{1,3},{2,0},{3,1},{4,6},{5,7},{6,4},{7,5},{8,10},{9,11},{10,... | collective-permute-start | bytes 294920 | tf_op jit(solution)/shard_map/ppermute | solution.py:53
  123.3 43.8 %collective-permute-start.15 = (bf16[64,768]{1,0:T(8,128)(2,1)S(1)}, bf16[64,768]{1,0:T(8,128)(2,1)S(1)}, u32[]{:S(2)}, u32[]{:S(2)}) collective-permute-start(bf16[64,768]{1,0:T(8,128)(2,1)S(1)} %add_convert_fusion.2), channel_id=1, source_target_pairs={{0,3},{1,2},{2,1},{3,0},{4,7},{5,6},{6,5},{7,4},{8,11},{9,10},{10,... | collective-permute-start | bytes 294920 | tf_op jit(solution)/shard_map/ppermute | solution.py:53
  123.8 43.3 %collective-permute-start.14 = (bf16[64,768]{1,0:T(8,128)(2,1)S(1)}, bf16[64,768]{1,0:T(8,128)(2,1)S(1)}, u32[]{:S(2)}, u32[]{:S(2)}) collective-permute-start(bf16[64,768]{1,0:T(8,128)(2,1)S(1)} %add_convert_fusion.2), channel_id=1, source_target_pairs={{0,2},{1,3},{2,0},{3,1},{4,6},{5,7},{6,4},{7,5},{8,10},{9,11},{10,... | collective-permute-start | bytes 294920 | tf_op jit(solution)/shard_map/ppermute | solution.py:53
  125.0 42.1 %collective-permute-start.13 = (bf16[64,768]{1,0:T(8,128)(2,1)S(1)}, bf16[64,768]{1,0:T(8,128)(2,1)S(1)}, u32[]{:S(2)}, u32[]{:S(2)}) collective-permute-start(bf16[64,768]{1,0:T(8,128)(2,1)S(1)} %add_convert_fusion.2), channel_id=1, source_target_pairs={{0,1},{1,0},{2,3},{3,2},{4,5},{5,4},{6,7},{7,6},{8,9},{9,8},{10,11... | collective-permute-start | bytes 294920 | tf_op jit(solution)/shard_map/ppermute | solution.py:53
  149.8 16.3 %collective-permute-start.20 = (bf16[4,96,768]{2,1,0:T(8,128)(2,1)S(1)}, bf16[4,96,768]{2,1,0:T(8,128)(2,1)S(1)}, u32[]{:S(2)}, u32[]{:S(2)}) collective-permute-start(bf16[4,96,768]{2,1,0:T(8,128)(2,1)S(1)} %pad_maximum_fusion.8), channel_id=1, source_target_pairs={{0,4},{2,6},{4,0},{6,2},{8,12},{10,14},{12,8},{14,10},{16,20},{18,... | collective-permute-start | bytes 1769480 | tf_op jit(solution)/shard_map/ppermute | solution.py:45
  153.0 27.9 %collective-permute-start.36 = (bf16[2,192,768]{2,1,0:T(8,128)(2,1)}, bf16[2,192,768]{2,1,0:T(8,128)(2,1)}, u32[]{:S(2)}, u32[]{:S(2)}) collective-permute-start(bf16[2,192,768]{2,1,0:T(8,128)(2,1)} %collective-permute-done.35), channel_id=1, source_target_pairs={{0,8},{2,10},{4,12},{6,14},{8,16},{10,18},{12,20},{14,22},{16,24},... | collective-permute-start | bytes 1769480 | tf_op jit(solution)/shard_map/ppermute | solution.py:60
  166.1 22.2 %collective-permute-start.27 = (bf16[4,96,1536]{2,1,0:T(8,128)(2,1)}, bf16[4,96,1536]{2,1,0:T(8,128)(2,1)}, u32[]{:S(2)}, u32[]{:S(2)}) collective-permute-start(bf16[4,96,1536]{2,1,0:T(8,128)(2,1)} %pad_maximum_fusion.6), channel_id=1, source_target_pairs={{0,4},{2,6},{4,0},{6,2},{8,12},{10,14},{12,8},{14,10},{16,20},{18,... | collective-permute-start | bytes 3538952 | tf_op jit(solution)/shard_map/ppermute | solution.py:45
  178.1 6.2 %collective-permute-start.22 = (bf16[64,768]{1,0:T(8,128)(2,1)}, bf16[64,768]{1,0:T(8,128)(2,1)S(1)}, u32[]{:S(2)}, u32[]{:S(2)}) collective-permute-start(bf16[64,768]{1,0:T(8,128)(2,1)} %get-tuple-element.191), channel_id=1, source_target_pairs={{0,2},{1,3},{2,0},{3,1},{4,6},{5,7},{6,4},{7,5},{8,10},{9,11},{10,... | collective-permute-start | bytes 294920 | tf_op jit(solution)/shard_map/ppermute | solution.py:53
  180.9 17.0 %collective-permute-start.37 = (bf16[2,192,768]{2,1,0:T(8,128)(2,1)}, bf16[2,192,768]{2,1,0:T(8,128)(2,1)S(1)}, u32[]{:S(2)}, u32[]{:S(2)}) collective-permute-start(bf16[2,192,768]{2,1,0:T(8,128)(2,1)} %collective-permute-done.36), channel_id=1, source_target_pairs={{0,8},{2,10},{4,12},{6,14},{8,16},{10,18},{12,20},{14,22},{16,24},... | collective-permute-start | bytes 1769480 | tf_op jit(solution)/shard_map/ppermute | solution.py:60
  186.7 6.4 %collective-permute-start.25 = (bf16[64,768]{1,0:T(8,128)(2,1)S(1)}, bf16[64,768]{1,0:T(8,128)(2,1)S(1)}, u32[]{:S(2)}, u32[]{:S(2)}) collective-permute-start(bf16[64,768]{1,0:T(8,128)(2,1)S(1)} %add_convert_fusion.1), channel_id=1, source_target_pairs={{0,2},{1,3},{2,0},{3,1},{4,6},{5,7},{6,4},{7,5},{8,10},{9,11},{10,... | collective-permute-start | bytes 294920 | tf_op jit(solution)/shard_map/ppermute | solution.py:53
  195.9 6.4 %collective-permute-start.29 = (bf16[64,768]{1,0:T(8,128)(2,1)S(1)}, bf16[64,768]{1,0:T(8,128)(2,1)S(1)}, u32[]{:S(2)}, u32[]{:S(2)}) collective-permute-start(bf16[64,768]{1,0:T(8,128)(2,1)S(1)} %get-tuple-element.188), channel_id=1, source_target_pairs={{0,2},{1,3},{2,0},{3,1},{4,6},{5,7},{6,4},{7,5},{8,10},{9,11},{10,... | collective-permute-start | bytes 294920 | tf_op jit(solution)/shard_map/ppermute | solution.py:53
  202.9 6.7 %collective-permute-start.32 = (bf16[64,768]{1,0:T(8,128)(2,1)S(1)}, bf16[64,768]{1,0:T(8,128)(2,1)S(1)}, u32[]{:S(2)}, u32[]{:S(2)}) collective-permute-start(bf16[64,768]{1,0:T(8,128)(2,1)S(1)} %fusion.85), channel_id=1, source_target_pairs={{0,2},{1,3},{2,0},{3,1},{4,6},{5,7},{6,4},{7,5},{8,10},{9,11},{10,... | collective-permute-start | bytes 294920 | tf_op jit(solution)/shard_map/ppermute | solution.py:53
  203.9 5.7 %collective-permute-start.31 = (bf16[64,768]{1,0:T(8,128)(2,1)S(1)}, bf16[64,768]{1,0:T(8,128)(2,1)S(1)}, u32[]{:S(2)}, u32[]{:S(2)}) collective-permute-start(bf16[64,768]{1,0:T(8,128)(2,1)S(1)} %fusion.85), channel_id=1, source_target_pairs={{0,1},{1,0},{2,3},{3,2},{4,5},{5,4},{6,7},{7,6},{8,9},{9,8},{10,11... | collective-permute-start | bytes 294920 | tf_op jit(solution)/shard_map/ppermute | solution.py:53
  215.6 11.1 %collective-permute-start.38 = (bf16[64,8,192]{2,1,0:T(8,128)(2,1)}, bf16[64,8,192]{2,1,0:T(8,128)(2,1)S(1)}, u32[]{:S(2)}, u32[]{:S(2)}) collective-permute-start(bf16[64,8,192]{2,1,0:T(8,128)(2,1)} %slice.368), channel_id=1, source_target_pairs={{0,1},{1,0},{2,3},{3,2},{4,5},{5,4},{6,7},{7,6},{8,9},{9,8},{10,11... | collective-permute-start | bytes 589832 | tf_op jit(solution)/shard_map/ppermute | solution.py:53
  215.7 11.0 %collective-permute-start.39 = (bf16[64,8,192]{2,1,0:T(8,128)(2,1)}, bf16[64,8,192]{2,1,0:T(8,128)(2,1)}, u32[]{:S(2)}, u32[]{:S(2)}) collective-permute-start(bf16[64,8,192]{2,1,0:T(8,128)(2,1)} %slice.370), channel_id=1, source_target_pairs={{0,2},{1,3},{2,0},{3,1},{4,6},{5,7},{6,4},{7,5},{8,10},{9,11},{10,... | collective-permute-start | bytes 589832 | tf_op jit(solution)/shard_map/ppermute | solution.py:53
  216.8 13.0 %collective-permute-start.40 = (bf16[64,8,192]{2,1,0:T(8,128)(2,1)}, bf16[64,8,192]{2,1,0:T(8,128)(2,1)}, u32[]{:S(2)}, u32[]{:S(2)}) collective-permute-start(bf16[64,8,192]{2,1,0:T(8,128)(2,1)} %slice.372), channel_id=1, source_target_pairs={{0,3},{1,2},{2,1},{3,0},{4,7},{5,6},{6,5},{7,4},{8,11},{9,10},{10,... | collective-permute-start | bytes 589832 | tf_op jit(solution)/shard_map/ppermute | solution.py:53
  282.5 9.5 %collective-permute-start.42 = (bf16[512,192]{1,0:T(8,128)(2,1)}, bf16[512,192]{1,0:T(8,128)(2,1)}, u32[]{:S(2)}, u32[]{:S(2)}) collective-permute-start(bf16[512,192]{1,0:T(8,128)(2,1)} %get-tuple-element.47), channel_id=1, source_target_pairs={{0,2},{1,3},{2,0},{3,1},{4,6},{5,7},{6,4},{7,5},{8,10},{9,11},{10,... | collective-permute-start | bytes 589832 | tf_op jit(solution)/shard_map/ppermute | solution.py:53
  283.6 12.5 %collective-permute-start.43 = (bf16[512,192]{1,0:T(8,128)(2,1)}, bf16[512,192]{1,0:T(8,128)(2,1)S(1)}, u32[]{:S(2)}, u32[]{:S(2)}) collective-permute-start(bf16[512,192]{1,0:T(8,128)(2,1)} %get-tuple-element.48), channel_id=1, source_target_pairs={{0,3},{1,2},{2,1},{3,0},{4,7},{5,6},{6,5},{7,4},{8,11},{9,10},{10,... | collective-permute-start | bytes 589832 | tf_op jit(solution)/shard_map/ppermute | solution.py:53
  300.4 6.6 %collective-permute-start.45 = (bf16[64,768]{1,0:T(8,128)(2,1)S(1)}, bf16[64,768]{1,0:T(8,128)(2,1)S(1)}, u32[]{:S(2)}, u32[]{:S(2)}) collective-permute-start(bf16[64,768]{1,0:T(8,128)(2,1)S(1)} %get-tuple-element.185), channel_id=1, source_target_pairs={{0,2},{1,3},{2,0},{3,1},{4,6},{5,7},{6,4},{7,5},{8,10},{9,11},{10,... | collective-permute-start | bytes 294920 | tf_op jit(solution)/shard_map/ppermute | solution.py:53
  307.5 6.8 %collective-permute-start.48 = (bf16[64,768]{1,0:T(8,128)(2,1)S(1)}, bf16[64,768]{1,0:T(8,128)(2,1)S(1)}, u32[]{:S(2)}, u32[]{:S(2)}) collective-permute-start(bf16[64,768]{1,0:T(8,128)(2,1)S(1)} %get-tuple-element.112), channel_id=1, source_target_pairs={{0,2},{1,3},{2,0},{3,1},{4,6},{5,7},{6,4},{7,5},{8,10},{9,11},{10,... | collective-permute-start | bytes 294920 | tf_op jit(solution)/shard_map/ppermute | solution.py:53
  308.6 5.7 %collective-permute-start.47 = (bf16[64,768]{1,0:T(8,128)(2,1)S(1)}, bf16[64,768]{1,0:T(8,128)(2,1)S(1)}, u32[]{:S(2)}, u32[]{:S(2)}) collective-permute-start(bf16[64,768]{1,0:T(8,128)(2,1)S(1)} %get-tuple-element.112), channel_id=1, source_target_pairs={{0,1},{1,0},{2,3},{3,2},{4,5},{5,4},{6,7},{7,6},{8,9},{9,8},{10,11... | collective-permute-start | bytes 294920 | tf_op jit(solution)/shard_map/ppermute | solution.py:53
  309.8 20.8 %collective-permute-start.53 = (bf16[2,192,768]{2,1,0:T(8,128)(2,1)}, bf16[2,192,768]{2,1,0:T(8,128)(2,1)}, u32[]{:S(2)}, u32[]{:S(2)}) collective-permute-start(bf16[2,192,768]{2,1,0:T(8,128)(2,1)} %dynamic-slice_bitcast_fusion.3), channel_id=1, source_target_pairs={{0,8},{2,10},{4,12},{6,14},{8,16},{10,18},{12,20},{14,22},{16,24},... | collective-permute-start | bytes 1769480 | tf_op jit(solution)/shard_map/ppermute | solution.py:60
  317.2 10.5 %collective-permute-start.50 = (bf16[64,768]{1,0:T(8,128)(2,1)}, bf16[64,768]{1,0:T(8,128)(2,1)}, u32[]{:S(2)}, u32[]{:S(2)}) collective-permute-start(bf16[64,768]{1,0:T(8,128)(2,1)} %get-tuple-element.180), channel_id=1, source_target_pairs={{0,1},{1,0},{2,3},{3,2},{4,5},{5,4},{6,7},{7,6},{8,9},{9,8},{10,11... | collective-permute-start | bytes 294920 | tf_op jit(solution)/shard_map/ppermute | solution.py:53
  317.3 10.4 %collective-permute-start.52 = (bf16[64,768]{1,0:T(8,128)(2,1)}, bf16[64,768]{1,0:T(8,128)(2,1)}, u32[]{:S(2)}, u32[]{:S(2)}) collective-permute-start(bf16[64,768]{1,0:T(8,128)(2,1)} %get-tuple-element.181), channel_id=1, source_target_pairs={{0,3},{1,2},{2,1},{3,0},{4,7},{5,6},{6,5},{7,4},{8,11},{9,10},{10,... | collective-permute-start | bytes 294920 | tf_op jit(solution)/shard_map/ppermute | solution.py:53
  318.3 9.4 %collective-permute-start.51 = (bf16[64,768]{1,0:T(8,128)(2,1)S(1)}, bf16[64,768]{1,0:T(8,128)(2,1)}, u32[]{:S(2)}, u32[]{:S(2)}) collective-permute-start(bf16[64,768]{1,0:T(8,128)(2,1)S(1)} %get-tuple-element.182), channel_id=1, source_target_pairs={{0,2},{1,3},{2,0},{3,1},{4,6},{5,7},{6,4},{7,5},{8,10},{9,11},{10,... | collective-permute-start | bytes 294920 | tf_op jit(solution)/shard_map/ppermute | solution.py:53
  326.5 54.5 %collective-permute-start.64 = (bf16[4,96,1536]{2,1,0:T(8,128)(2,1)}, bf16[4,96,1536]{2,1,0:T(8,128)(2,1)}, u32[]{:S(2)}, u32[]{:S(2)}) collective-permute-start(bf16[4,96,1536]{2,1,0:T(8,128)(2,1)} %dynamic-slice_bitcast_fusion.1), channel_id=1, source_target_pairs={{0,4},{2,6},{4,0},{6,2},{8,12},{10,14},{12,8},{14,10},{16,20},{18,... | collective-permute-start | bytes 3538952 | tf_op jit(solution)/shard_map/ppermute | solution.py:45
  330.6 6.7 %collective-permute-start.56 = (bf16[64,768]{1,0:T(8,128)(2,1)S(1)}, bf16[64,768]{1,0:T(8,128)(2,1)S(1)}, u32[]{:S(2)}, u32[]{:S(2)}) collective-permute-start(bf16[64,768]{1,0:T(8,128)(2,1)S(1)} %fusion.101), channel_id=1, source_target_pairs={{0,3},{1,2},{2,1},{3,0},{4,7},{5,6},{6,5},{7,4},{8,11},{9,10},{10,... | collective-permute-start | bytes 294920 | tf_op jit(solution)/shard_map/ppermute | solution.py:53
  330.8 6.5 %collective-permute-start.55 = (bf16[64,768]{1,0:T(8,128)(2,1)S(1)}, bf16[64,768]{1,0:T(8,128)(2,1)S(1)}, u32[]{:S(2)}, u32[]{:S(2)}) collective-permute-start(bf16[64,768]{1,0:T(8,128)(2,1)S(1)} %fusion.101), channel_id=1, source_target_pairs={{0,2},{1,3},{2,0},{3,1},{4,6},{5,7},{6,4},{7,5},{8,10},{9,11},{10,... | collective-permute-start | bytes 294920 | tf_op jit(solution)/shard_map/ppermute | solution.py:53
  334.7 30.1 %collective-permute-start.60 = (bf16[2,192,768]{2,1,0:T(8,128)(2,1)}, bf16[2,192,768]{2,1,0:T(8,128)(2,1)}, u32[]{:S(2)}, u32[]{:S(2)}) collective-permute-start(bf16[2,192,768]{2,1,0:T(8,128)(2,1)} %fusion.5), channel_id=1, source_target_pairs={{0,8},{2,10},{4,12},{6,14},{8,16},{10,18},{12,20},{14,22},{16,24},... | collective-permute-start | bytes 1769480 | tf_op jit(solution)/shard_map/ppermute | solution.py:60
  343.4 7.1 %collective-permute-start.59 = (bf16[64,768]{1,0:T(8,128)(2,1)S(1)}, bf16[64,768]{1,0:T(8,128)(2,1)S(1)}, u32[]{:S(2)}, u32[]{:S(2)}) collective-permute-start(bf16[64,768]{1,0:T(8,128)(2,1)S(1)} %get-tuple-element.178), channel_id=1, source_target_pairs={{0,3},{1,2},{2,1},{3,0},{4,7},{5,6},{6,5},{7,4},{8,11},{9,10},{10,... | collective-permute-start | bytes 294920 | tf_op jit(solution)/shard_map/ppermute | solution.py:53
  344.1 10.9 %collective-permute-start.58 = (bf16[64,768]{1,0:T(8,128)(2,1)S(1)}, bf16[64,768]{1,0:T(8,128)(2,1)S(1)}, u32[]{:S(2)}, u32[]{:S(2)}) collective-permute-start(bf16[64,768]{1,0:T(8,128)(2,1)S(1)} %get-tuple-element.179), channel_id=1, source_target_pairs={{0,2},{1,3},{2,0},{3,1},{4,6},{5,7},{6,4},{7,5},{8,10},{9,11},{10,... | collective-permute-start | bytes 294920 | tf_op jit(solution)/shard_map/ppermute | solution.py:53
  358.8 21.3 %collective-permute-start.77 = (bf16[4,96,768]{2,1,0:T(8,128)(2,1)}, bf16[4,96,768]{2,1,0:T(8,128)(2,1)S(1)}, u32[]{:S(2)}, u32[]{:S(2)}) collective-permute-start(bf16[4,96,768]{2,1,0:T(8,128)(2,1)} %dynamic-slice_bitcast_fusion.2), channel_id=1, source_target_pairs={{0,4},{2,6},{4,0},{6,2},{8,12},{10,14},{12,8},{14,10},{16,20},{18,... | collective-permute-start | bytes 1769480 | tf_op jit(solution)/shard_map/ppermute | solution.py:45
  364.8 5.7 %collective-permute-start.63 = (bf16[64,768]{1,0:T(8,128)(2,1)S(1)}, bf16[64,768]{1,0:T(8,128)(2,1)S(1)}, u32[]{:S(2)}, u32[]{:S(2)}) collective-permute-start(bf16[64,768]{1,0:T(8,128)(2,1)S(1)} %add_convert_fusion), channel_id=1, source_target_pairs={{0,3},{1,2},{2,1},{3,0},{4,7},{5,6},{6,5},{7,4},{8,11},{9,10},{10,... | collective-permute-start | bytes 294920 | tf_op jit(solution)/shard_map/ppermute | solution.py:53
  368.1 34.9 %collective-permute-start.65 = (bf16[2,192,768]{2,1,0:T(8,128)(2,1)S(1)}, bf16[2,192,768]{2,1,0:T(8,128)(2,1)S(1)}, u32[]{:S(2)}, u32[]{:S(2)}) collective-permute-start(bf16[2,192,768]{2,1,0:T(8,128)(2,1)S(1)} %fusion.4), channel_id=1, source_target_pairs={{0,8},{2,10},{4,12},{6,14},{8,16},{10,18},{12,20},{14,22},{16,24},... | collective-permute-start | bytes 1769480 | tf_op jit(solution)/shard_map/ppermute | solution.py:60
  373.4 72.7 %collective-permute-start.72 = (bf16[4,193,768]{2,0,1:T(4,128)(2,1)}, bf16[4,193,768]{2,0,1:T(4,128)(2,1)}, u32[]{:S(2)}, u32[]{:S(2)}) collective-permute-start(bf16[4,193,768]{2,0,1:T(4,128)(2,1)} %copy.218), channel_id=1, source_target_pairs={{0,4},{2,6},{4,0},{6,2},{8,12},{10,14},{12,8},{14,10},{16,20},{18,... | collective-permute-start | bytes 3557384 | tf_op jit(solution)/shard_map/ppermute | solution.py:45
  384.3 32.1 %collective-permute-start.78 = (bf16[96,2304]{1,0:T(8,128)(2,1)}, bf16[96,2304]{1,0:T(8,128)(2,1)}, u32[]{:S(2)}, u32[]{:S(2)}) collective-permute-start(bf16[96,2304]{1,0:T(8,128)(2,1)} %fusion.66), channel_id=1, source_target_pairs={{0,8},{2,10},{4,12},{6,14},{8,16},{10,18},{12,20},{14,22},{16,24},... | collective-permute-start | bytes 1327112 | tf_op jit(solution)/shard_map/ppermute | solution.py:60
  406.0 38.2 %collective-permute-start.76 = (bf16[192,768]{1,0:T(8,128)(2,1)}, bf16[192,768]{1,0:T(8,128)(2,1)}, u32[]{:S(2)}, u32[]{:S(2)}) collective-permute-start(bf16[192,768]{1,0:T(8,128)(2,1)} %fusion.72), channel_id=1, source_target_pairs={{0,4},{2,6},{4,0},{6,2},{8,12},{10,14},{12,8},{14,10},{16,20},{18,... | collective-permute-start | bytes 884744 | tf_op jit(solution)/shard_map/ppermute | solution.py:45
  415.3 8.2 %collective-permute-start.68 = (bf16[64,8,192]{2,1,0:T(8,128)(2,1)}, bf16[64,8,192]{2,1,0:T(8,128)(2,1)S(1)}, u32[]{:S(2)}, u32[]{:S(2)}) collective-permute-start(bf16[64,8,192]{2,1,0:T(8,128)(2,1)} %slice.398), channel_id=1, source_target_pairs={{0,3},{1,2},{2,1},{3,0},{4,7},{5,6},{6,5},{7,4},{8,11},{9,10},{10,... | collective-permute-start | bytes 589832 | tf_op jit(solution)/shard_map/ppermute | solution.py:53
  416.3 17.0 %collective-permute-start.67 = (bf16[64,8,192]{2,1,0:T(8,128)(2,1)}, bf16[64,8,192]{2,1,0:T(8,128)(2,1)S(1)}, u32[]{:S(2)}, u32[]{:S(2)}) collective-permute-start(bf16[64,8,192]{2,1,0:T(8,128)(2,1)} %slice.396), channel_id=1, source_target_pairs={{0,2},{1,3},{2,0},{3,1},{4,6},{5,7},{6,4},{7,5},{8,10},{9,11},{10,... | collective-permute-start | bytes 589832 | tf_op jit(solution)/shard_map/ppermute | solution.py:53
  419.3 23.6 %collective-permute-start.79 = (bf16[96,2304]{1,0:T(8,128)(2,1)}, bf16[96,2304]{1,0:T(8,128)(2,1)}, u32[]{:S(2)}, u32[]{:S(2)}) collective-permute-start(bf16[96,2304]{1,0:T(8,128)(2,1)} %fusion.32), channel_id=1, source_target_pairs={{0,8},{2,10},{4,12},{6,14},{8,16},{10,18},{12,20},{14,22},{16,24},... | collective-permute-start | bytes 1327112 | tf_op jit(solution)/shard_map/ppermute | solution.py:60
  444.1 20.4 %collective-permute-start.80 = (bf16[96,2304]{1,0:T(8,128)(2,1)S(1)}, bf16[96,2304]{1,0:T(8,128)(2,1)S(1)}, u32[]{:S(2)}, u32[]{:S(2)}) collective-permute-start(bf16[96,2304]{1,0:T(8,128)(2,1)S(1)} %fusion.28), channel_id=1, source_target_pairs={{0,8},{2,10},{4,12},{6,14},{8,16},{10,18},{12,20},{14,22},{16,24},... | collective-permute-start | bytes 1327112 | tf_op jit(solution)/shard_map/ppermute | solution.py:60
  447.7 22.5 %collective-permute-start.73 = (bf16[193,768]{1,0:T(8,128)(2,1)S(1)}, bf16[193,768]{1,0:T(8,128)(2,1)S(1)}, u32[]{:S(2)}, u32[]{:S(2)}) collective-permute-start(bf16[193,768]{1,0:T(8,128)(2,1)S(1)} %fusion.71), channel_id=1, source_target_pairs={{0,8},{2,10},{4,12},{6,14},{8,16},{10,18},{12,20},{14,22},{16,24},... | collective-permute-start | bytes 889352 | tf_op jit(solution)/shard_map/ppermute | solution.py:60
  464.7 6.0 %collective-permute-start.81 = (bf16[48,2304]{1,0:T(8,128)(2,1)S(1)}, bf16[48,2304]{1,0:T(8,128)(2,1)S(1)}, u32[]{:S(2)}, u32[]{:S(2)}) collective-permute-start(bf16[48,2304]{1,0:T(8,128)(2,1)S(1)} %fusion.73), channel_id=1, source_target_pairs={{0,2},{2,0},{4,6},{6,4},{8,10},{10,8},{12,14},{14,12},{16,18},{18,... | collective-permute-start | bytes 663560 | tf_op jit(solution)/shard_map/ppermute | solution.py:45
  470.2 15.8 %collective-permute-start.74 = (bf16[193,768]{1,0:T(8,128)(2,1)S(1)}, bf16[193,768]{1,0:T(8,128)(2,1)S(1)}, u32[]{:S(2)}, u32[]{:S(2)}) collective-permute-start(bf16[193,768]{1,0:T(8,128)(2,1)S(1)} %fusion.60), channel_id=1, source_target_pairs={{0,8},{2,10},{4,12},{6,14},{8,16},{10,18},{12,20},{14,22},{16,24},... | collective-permute-start | bytes 889352 | tf_op jit(solution)/shard_map/ppermute | solution.py:60
  486.1 10.4 %collective-permute-start.75 = (bf16[193,768]{1,0:T(8,128)(2,1)S(1)}, bf16[193,768]{1,0:T(8,128)(2,1)S(1)}, u32[]{:S(2)}, u32[]{:S(2)}) collective-permute-start(bf16[193,768]{1,0:T(8,128)(2,1)S(1)} %fusion.61), channel_id=1, source_target_pairs={{0,8},{2,10},{4,12},{6,14},{8,16},{10,18},{12,20},{14,22},{16,24},... | collective-permute-start | bytes 889352 | tf_op jit(solution)/shard_map/ppermute | solution.py:60
  (123 other events, 912.0 us)
Sparse Core Ops, SparseCore 0:
  13.2 140.2 all-gather.2
  281.2 212.3 reduce-scatter.1

commit v5 on v4

--- a/solution.py
+++ b/solution.py
@@ -695,6 +695,7 @@
     global_shard = global_shard.reshape(2 * shard_rows, -1)
     attend_columns = 2 * heads_width
     global_blocks = line_pass(global_shard, queue, (patch_whole,))
+    queue.hold(global_blocks[-1])
     attend_lined = line_place_blocks([block[:, :attend_columns] for block in global_blocks])
     forward_lined = line_place_blocks([block[:, attend_columns:] for block in global_blocks])
     proj_part = jnp.transpose(global_proj)

time: 519 us -> 502 us (0.967)
  waiting for transfers between devices: 225 us -> 202 us
    ppermute x18, waiting for transfers between devices: 143 us -> 122 us  [step_line(): lax.ppermute(values_in, 'dp', [(i, (i + 4 * offset) % count) for i in ran...]
    unnamed x226 -> x218, local copies, waits for them, and re-layouts: 15 us -> 16.1 us
  transfers between devices with their start and end apart: 84 -> 84, of which waited for: 42 -> 36; matrix products, arithmetic and copies ran while one was open for 25% -> 27% of each run, Pallas kernels for 0% -> 0%
where the time goes in v5:
time: 502 us; the launch traced here: 493 us
  waiting for transfers between devices  202 us (40%)
  local copies, waits for them, and re-layouts  83.4 us (17%)
  starting transfers between devices  68.7 us (14%)
  Pallas kernels  51.2 us (10%)
  other arithmetic  47.1 us (9%)
  matrix products  22.7 us (5%)
  between operations  17.2 us (3%)
    ppermute x18, waiting for transfers between devices, step_line(): lax.ppermute(values_in, 'dp', [(i, (i + 4 * offset) % count) for i in ran...  122 us
    ppermute x54, waiting for transfers between devices, flip_quad(): lax.ppermute(values_in, ('dp', 'tensor'), [(i, i ^ bits) for i in range(2...  63.3 us
    pallas_call x1, Pallas kernels, local_layer(): pl.pallas_call(lambda *refs: local_body(tiles, wide, *refs), grid=(tiles...  51.2 us
    ppermute x54, starting transfers between devices, flip_quad(): lax.ppermute(values_in, ('dp', 'tensor'), [(i, i ^ bits) for i in range(2...  36.4 us
    ppermute x18, starting transfers between devices, step_line(): lax.ppermute(values_in, 'dp', [(i, (i + 4 * offset) % count) for i in ran...  22.6 us
    ppermute x10, waiting for transfers between devices, flip_dp(): lax.ppermute(values_in, 'dp', [(i, i ^ bit) for i in range(dp_size())])  16.6 us
    unnamed x218, local copies, waits for them, and re-layouts  16.1 us
  transfers between devices with their start and end apart: 84, of which 36 were waited for; matrix products, arithmetic and copies ran while one was open for 27% of the time, Pallas kernels for 0%

profile of v5, /device:TPU:4, one launch (start us, length us, event | category | flops | bytes accessed | tf_op | source)
XLA Modules:
  0.0 492.5 jit_solution(4087214928846485158)
XLA Ops:
  14.9 1.6 collective-permute-start.3
  20.8 5.0 %collective-permute-done.3 = bf16[193,768]{1,0:T(8,128)(2,1)S(1)} collective-permute-done((bf16[193,768]{1,0:T(8,128)(2,1)S(1)}, bf16[193,768]{1,0:T(8,128)(2,1)S(1)}, u32[]{:S(2)}, u32[]{:S(2)}) %collective-permute-start.3) | collective-permute-done | bytes 296480 | tf_op jit(solution)/shard_map/ppermute | solution.py:60
  26.9 16.7 %collective-permute-done.4 = bf16[193,768]{1,0:T(8,128)(2,1)} collective-permute-done((bf16[193,768]{1,0:T(8,128)(2,1)S(1)}, bf16[193,768]{1,0:T(8,128)(2,1)}, u32[]{:S(2)}, u32[]{:S(2)}) %collective-permute-start.4) | collective-permute-done | bytes 296480 | tf_op jit(solution)/shard_map/ppermute | solution.py:60
  43.7 4.2 fusion.126
  47.9 2.1 copy.181
  52.7 2.0 collective-permute-done.5
  57.8 1.7 collective-permute-start.6
  65.5 9.9 %collective-permute-done.17 = bf16[96,2304]{1,0:T(8,128)(2,1)} collective-permute-done((bf16[96,2304]{1,0:T(8,128)(2,1)S(1)}, bf16[96,2304]{1,0:T(8,128)(2,1)}, u32[]{:S(2)}, u32[]{:S(2)}) %collective-permute-start.17) | collective-permute-done | bytes 442400 | tf_op jit(solution)/shard_map/ppermute | solution.py:60
  75.4 8.9 %collective-permute-done.6 = bf16[4,193,768]{2,0,1:T(4,128)(2,1)} collective-permute-done((bf16[4,193,768]{2,0,1:T(4,128)(2,1)}, bf16[4,193,768]{2,0,1:T(4,128)(2,1)}, u32[]{:S(2)}, u32[]{:S(2)}) %collective-permute-start.6) | collective-permute-done | bytes 1185824 | tf_op jit(solution)/shard_map/ppermute | solution.py:45
  87.0 4.0 collective-permute-done.18
  93.2 3.1 fusion.149
  99.5 4.5 collective-permute-done.9
  104.0 4.9 %collective-permute-done.8 = bf16[64,768]{1,0:T(8,128)(2,1)} collective-permute-done((bf16[64,768]{1,0:T(8,128)(2,1)S(1)}, bf16[64,768]{1,0:T(8,128)(2,1)}, u32[]{:S(2)}, u32[]{:S(2)}) %collective-permute-start.8) | collective-permute-done | bytes 98336 | tf_op jit(solution)/shard_map/ppermute | solution.py:53
  112.4 5.1 %collective-permute-done.19 = bf16[96,2304]{1,0:T(8,128)(2,1)} collective-permute-done((bf16[96,2304]{1,0:T(8,128)(2,1)}, bf16[96,2304]{1,0:T(8,128)(2,1)}, u32[]{:S(2)}, u32[]{:S(2)}) %collective-permute-start.19) | collective-permute-done | bytes 442400 | tf_op jit(solution)/shard_map/ppermute | solution.py:60
  121.7 4.2 collective-permute-start.35
  126.0 7.3 %collective-permute-done.20 = bf16[4,96,768]{2,1,0:T(8,128)(2,1)S(1)} collective-permute-done((bf16[4,96,768]{2,1,0:T(8,128)(2,1)S(1)}, bf16[4,96,768]{2,1,0:T(8,128)(2,1)S(1)}, u32[]{:S(2)}, u32[]{:S(2)}) %collective-permute-start.20) | collective-permute-done | bytes 589856 | tf_op jit(solution)/shard_map/ppermute | solution.py:45
  136.2 1.7 reshape.256
  139.2 1.8 fusion.150
  141.0 1.8 fusion.8
  147.6 6.8 %collective-permute-done.35 = bf16[2,192,768]{2,1,0:T(8,128)(2,1)} collective-permute-done((bf16[2,192,768]{2,1,0:T(8,128)(2,1)}, bf16[2,192,768]{2,1,0:T(8,128)(2,1)}, u32[]{:S(2)}, u32[]{:S(2)}) %collective-permute-start.35) | collective-permute-done | bytes 589856 | tf_op jit(solution)/shard_map/ppermute | solution.py:60
  156.8 14.3 %collective-permute-done.36 = bf16[2,192,768]{2,1,0:T(8,128)(2,1)} collective-permute-done((bf16[2,192,768]{2,1,0:T(8,128)(2,1)}, bf16[2,192,768]{2,1,0:T(8,128)(2,1)}, u32[]{:S(2)}, u32[]{:S(2)}) %collective-permute-start.36) | collective-permute-done | bytes 589856 | tf_op jit(solution)/shard_map/ppermute | solution.py:60
  171.2 1.8 select_bitcast_fusion.3
  179.2 1.9 concatenate.120
  181.8 2.8 collective-permute-done.29
  187.6 1.7 select_bitcast_fusion.7
  194.0 1.9 slice.372
  200.8 1.8 copy.213
  202.7 1.8 copy.214
  204.5 1.8 copy.215
  208.8 3.1 collective-permute-done.40
  211.9 51.2 %shard_map.186 = (bf16[512,768]{1,0:T(8,128)(2,1)}, f32[512,768]{1,0:T(8,128)}, bf16[512,192]{1,0:T(8,128)(2,1)}, bf16[512,192]{1,0:T(8,128)(2,1)}, bf16[512,192...) custom-call(s32[2]{0:T(128)} %pad_add_fusion.refs_0_, ...), custom_call_target="tpu_custom_call" | custom-call | flops 21743271936 | bytes 28311552 | tf_op jit(solution)/shard_map/pallas_call | solution.py:579
  269.5 4.7 collective-permute-done.42
  276.1 2.2 collective-permute-done.43
  279.2 2.1 fusion.153
  284.5 2.2 collective-permute-done.46
  286.7 2.4 collective-permute-done.45
  291.9 2.3 collective-permute-done.49
  294.3 2.1 collective-permute-done.48
  304.4 3.0 copy.211
  314.4 2.2 fusion.5
  317.2 1.9 collective-permute-done.55
  327.9 4.5 collective-permute-done.59
  332.5 4.5 collective-permute-done.58
  340.7 1.6 collective-permute-start.77
  342.4 2.1 collective-permute-done.60
  347.8 12.6 %collective-permute-start.65 = (bf16[2,192,768]{2,1,0:T(8,128)(2,1)S(1)}, bf16[2,192,768]{2,1,0:T(8,128)(2,1)S(1)}, u32[]{:S(2)}, u32[]{:S(2)}) collective-permute-start(bf16[2,192,768]{2,1,0:T(8,128)(2,1)S(1)} %fusion.4), channel_id=1, source_target_pairs={{0,8},{2,10},{4,12},{6,14},{8,16},{10,18},{12,20},{14,22},{16,24},... | collective-permute-start | bytes 1769480 | tf_op jit(solution)/shard_map/ppermute | solution.py:60
  361.7 1.8 copy.218
  369.4 2.7 collective-permute-start.78
  372.1 13.1 %collective-permute-done.65 = bf16[2,192,768]{2,1,0:T(8,128)(2,1)S(1)} collective-permute-done((bf16[2,192,768]{2,1,0:T(8,128)(2,1)S(1)}, bf16[2,192,768]{2,1,0:T(8,128)(2,1)S(1)}, u32[]{:S(2)}, u32[]{:S(2)}) %collective-permute-start.65) | collective-permute-done | bytes 589856 | tf_op jit(solution)/shard_map/ppermute | solution.py:60
  390.6 1.9 slice.396
  392.5 1.9 slice.398
  394.4 1.9 slice.394
  396.3 1.9 slice.392
  400.3 1.8 fusion.32
  402.2 6.5 %collective-permute-done.68 = bf16[64,8,192]{2,1,0:T(8,128)(2,1)S(1)} collective-permute-done((bf16[64,8,192]{2,1,0:T(8,128)(2,1)}, bf16[64,8,192]{2,1,0:T(8,128)(2,1)S(1)}, u32[]{:S(2)}, u32[]{:S(2)}) %collective-permute-start.68) | collective-permute-done | bytes 196640 | tf_op jit(solution)/shard_map/ppermute | solution.py:53
  408.7 10.2 %collective-permute-done.67 = bf16[64,8,192]{2,1,0:T(8,128)(2,1)S(1)} collective-permute-done((bf16[64,8,192]{2,1,0:T(8,128)(2,1)}, bf16[64,8,192]{2,1,0:T(8,128)(2,1)S(1)}, u32[]{:S(2)}, u32[]{:S(2)}) %collective-permute-start.67) | collective-permute-done | bytes 196640 | tf_op jit(solution)/shard_map/ppermute | solution.py:53
  419.4 2.7 copy.212
  422.1 3.5 reshape.281
  425.5 3.0 fusion.43
  430.0 1.8 fusion.63
  433.4 13.3 %collective-permute-done.80 = bf16[96,2304]{1,0:T(8,128)(2,1)S(1)} collective-permute-done((bf16[96,2304]{1,0:T(8,128)(2,1)S(1)}, bf16[96,2304]{1,0:T(8,128)(2,1)S(1)}, u32[]{:S(2)}, u32[]{:S(2)}) %collective-permute-start.80) | collective-permute-done | bytes 442400 | tf_op jit(solution)/shard_map/ppermute | solution.py:60
  448.0 4.7 collective-permute-done.73
  454.2 15.4 %collective-permute-done.74 = bf16[193,768]{1,0:T(8,128)(2,1)S(1)} collective-permute-done((bf16[193,768]{1,0:T(8,128)(2,1)S(1)}, bf16[193,768]{1,0:T(8,128)(2,1)S(1)}, u32[]{:S(2)}, u32[]{:S(2)}) %collective-permute-start.74) | collective-permute-done | bytes 296480 | tf_op jit(solution)/shard_map/ppermute | solution.py:60
  469.8 9.6 %collective-permute-done.75 = bf16[193,768]{1,0:T(8,128)(2,1)S(1)} collective-permute-done((bf16[193,768]{1,0:T(8,128)(2,1)S(1)}, bf16[193,768]{1,0:T(8,128)(2,1)S(1)}, u32[]{:S(2)}, u32[]{:S(2)}) %collective-permute-start.75) | collective-permute-done | bytes 296480 | tf_op jit(solution)/shard_map/ppermute | solution.py:60
  (547 shorter events, 145.2 us)
Async XLA Ops:
  7.2 204.7 %all-gather.3.cloned.1.call-start = ((), (), s32[]{:S(2)}) async-start(), calls=%async_computation.2 | async-start | bytes 14598144 | tf_op jit(solution)/shard_map/all_gather | solution.py:657
  13.1 467.9 %reduce-scatter.2.cloned.1.call-start = ((), (), s32[]{:S(2)}) async-start(), calls=%async_computation.1 | async-start | bytes 14598144 | tf_op jit(solution)/shard_map/reduce_scatter | solution.py:773
  14.9 10.9 %collective-permute-start.3 = (bf16[193,768]{1,0:T(8,128)(2,1)S(1)}, bf16[193,768]{1,0:T(8,128)(2,1)S(1)}, u32[]{:S(2)}, u32[]{:S(2)}) collective-permute-start(bf16[193,768]{1,0:T(8,128)(2,1)S(1)} %fusion.70), channel_id=1, source_target_pairs={{0,8},{2,10},{4,12},{6,14},{8,16},{10,18},{12,20},{14,22},{16,24},... | collective-permute-start | bytes 889352 | tf_op jit(solution)/shard_map/ppermute | solution.py:60
  18.1 41.4 %collective-permute-start.16 = (bf16[48,2304]{1,0:T(8,128)(2,1)}, bf16[48,2304]{1,0:T(8,128)(2,1)}, u32[]{:S(2)}, u32[]{:S(2)}) collective-permute-start(bf16[48,2304]{1,0:T(8,128)(2,1)} %dynamic-slice_bitcast_fusion.4), channel_id=1, source_target_pairs={{0,2},{2,0},{4,6},{6,4},{8,10},{10,8},{12,14},{14,12},{16,18},{18,... | collective-permute-start | bytes 663560 | tf_op jit(solution)/shard_map/ppermute | solution.py:45
  19.6 43.9 %collective-permute-start.34 = (bf16[192,768]{1,0:T(8,128)(2,1)}, bf16[192,768]{1,0:T(8,128)(2,1)}, u32[]{:S(2)}, u32[]{:S(2)}) collective-permute-start(bf16[192,768]{1,0:T(8,128)(2,1)} %bitcast.49), channel_id=1, source_target_pairs={{0,4},{2,6},{4,0},{6,2},{8,12},{10,14},{12,8},{14,10},{16,20},{18,... | collective-permute-start | bytes 884744 | tf_op jit(solution)/shard_map/ppermute | solution.py:45
  25.8 17.9 %collective-permute-start.4 = (bf16[193,768]{1,0:T(8,128)(2,1)S(1)}, bf16[193,768]{1,0:T(8,128)(2,1)}, u32[]{:S(2)}, u32[]{:S(2)}) collective-permute-start(bf16[193,768]{1,0:T(8,128)(2,1)S(1)} %collective-permute-done.3), channel_id=1, source_target_pairs={{0,8},{2,10},{4,12},{6,14},{8,16},{10,18},{12,20},{14,22},{16,24},... | collective-permute-start | bytes 889352 | tf_op jit(solution)/shard_map/ppermute | solution.py:60
  43.7 11.1 %collective-permute-start.5 = (bf16[193,768]{1,0:T(8,128)(2,1)}, bf16[193,768]{1,0:T(8,128)(2,1)}, u32[]{:S(2)}, u32[]{:S(2)}) collective-permute-start(bf16[193,768]{1,0:T(8,128)(2,1)} %collective-permute-done.4), channel_id=1, source_target_pairs={{0,8},{2,10},{4,12},{6,14},{8,16},{10,18},{12,20},{14,22},{16,24},... | collective-permute-start | bytes 889352 | tf_op jit(solution)/shard_map/ppermute | solution.py:60
  50.1 41.0 %collective-permute-start = (bf16[64,8,192]{0,2,1:T(8,128)(2,1)}, bf16[64,8,192]{0,2,1:T(8,128)(2,1)}, u32[]{:S(2)}, u32[]{:S(2)}) collective-permute-start(bf16[64,8,192]{0,2,1:T(8,128)(2,1)} %bitcast.5), channel_id=1, source_target_pairs={{0,1},{1,0},{2,3},{3,2},{4,5},{5,4},{6,7},{7,6},{8,9},{9,8},{10,11... | collective-permute-start | bytes 589832 | tf_op jit(solution)/shard_map/ppermute | solution.py:53
  51.2 41.5 %collective-permute-start.1 = (bf16[64,8,192]{0,2,1:T(8,128)(2,1)}, bf16[64,8,192]{0,2,1:T(8,128)(2,1)}, u32[]{:S(2)}, u32[]{:S(2)}) collective-permute-start(bf16[64,8,192]{0,2,1:T(8,128)(2,1)} %bitcast.6), channel_id=1, source_target_pairs={{0,2},{1,3},{2,0},{3,1},{4,6},{5,7},{6,4},{7,5},{8,10},{9,11},{10,... | collective-permute-start | bytes 589832 | tf_op jit(solution)/shard_map/ppermute | solution.py:53
  57.8 26.5 %collective-permute-start.6 = (bf16[4,193,768]{2,0,1:T(4,128)(2,1)}, bf16[4,193,768]{2,0,1:T(4,128)(2,1)}, u32[]{:S(2)}, u32[]{:S(2)}) collective-permute-start(bf16[4,193,768]{2,0,1:T(4,128)(2,1)} %copy.184), channel_id=1, source_target_pairs={{0,4},{2,6},{4,0},{6,2},{8,12},{10,14},{12,8},{14,10},{16,20},{18,... | collective-permute-start | bytes 3557384 | tf_op jit(solution)/shard_map/ppermute | solution.py:45
  60.6 14.8 %collective-permute-start.17 = (bf16[96,2304]{1,0:T(8,128)(2,1)S(1)}, bf16[96,2304]{1,0:T(8,128)(2,1)}, u32[]{:S(2)}, u32[]{:S(2)}) collective-permute-start(bf16[96,2304]{1,0:T(8,128)(2,1)S(1)} %bitcast.439), channel_id=1, source_target_pairs={{0,8},{2,10},{4,12},{6,14},{8,16},{10,18},{12,20},{14,22},{16,24},... | collective-permute-start | bytes 1327112 | tf_op jit(solution)/shard_map/ppermute | solution.py:60
  63.5 29.6 %collective-permute-start.2 = (bf16[64,8,192]{0,2,1:T(8,128)(2,1)}, bf16[64,8,192]{0,2,1:T(8,128)(2,1)S(1)}, u32[]{:S(2)}, u32[]{:S(2)}) collective-permute-start(bf16[64,8,192]{0,2,1:T(8,128)(2,1)} %bitcast.7), channel_id=1, source_target_pairs={{0,3},{1,2},{2,1},{3,0},{4,7},{5,6},{6,5},{7,4},{8,11},{9,10},{10,... | collective-permute-start | bytes 589832 | tf_op jit(solution)/shard_map/ppermute | solution.py:53
  75.4 15.6 %collective-permute-start.18 = (bf16[96,2304]{1,0:T(8,128)(2,1)}, bf16[96,2304]{1,0:T(8,128)(2,1)}, u32[]{:S(2)}, u32[]{:S(2)}) collective-permute-start(bf16[96,2304]{1,0:T(8,128)(2,1)} %collective-permute-done.17), channel_id=1, source_target_pairs={{0,8},{2,10},{4,12},{6,14},{8,16},{10,18},{12,20},{14,22},{16,24},... | collective-permute-start | bytes 1327112 | tf_op jit(solution)/shard_map/ppermute | solution.py:60
  86.4 10.6 %collective-permute-start.11 = (bf16[1,8,192]{2,1,0:T(8,128)(2,1)S(1)}, bf16[1,8,192]{2,1,0:T(8,128)(2,1)S(1)}, u32[]{:S(2)}, u32[]{:S(2)}) collective-permute-start(bf16[1,8,192]{2,1,0:T(8,128)(2,1)S(1)} %bitcast.460), channel_id=1, source_target_pairs={{0,2},{1,3},{2,0},{3,1},{4,6},{5,7},{6,4},{7,5},{8,10},{9,11},{10,... | collective-permute-start | bytes 9224 | tf_op jit(solution)/shard_map/ppermute | solution.py:53
  91.0 6.6 %collective-permute-start.12 = (bf16[1,8,192]{2,1,0:T(8,128)(2,1)S(1)}, bf16[1,8,192]{2,1,0:T(8,128)(2,1)S(1)}, u32[]{:S(2)}, u32[]{:S(2)}) collective-permute-start(bf16[1,8,192]{2,1,0:T(8,128)(2,1)S(1)} %bitcast.461), channel_id=1, source_target_pairs={{0,3},{1,2},{2,1},{3,0},{4,7},{5,6},{6,5},{7,4},{8,11},{9,10},{10,... | collective-permute-start | bytes 9224 | tf_op jit(solution)/shard_map/ppermute | solution.py:53
  91.1 8.1 %collective-permute-start.10 = (bf16[1,8,192]{2,1,0:T(8,128)(2,1)S(1)}, bf16[1,8,192]{2,1,0:T(8,128)(2,1)S(1)}, u32[]{:S(2)}, u32[]{:S(2)}) collective-permute-start(bf16[1,8,192]{2,1,0:T(8,128)(2,1)S(1)} %bitcast.462), channel_id=1, source_target_pairs={{0,1},{1,0},{2,3},{3,2},{4,5},{5,4},{6,7},{7,6},{8,9},{9,8},{10,11... | collective-permute-start | bytes 9224 | tf_op jit(solution)/shard_map/ppermute | solution.py:53
  92.7 24.8 %collective-permute-start.19 = (bf16[96,2304]{1,0:T(8,128)(2,1)}, bf16[96,2304]{1,0:T(8,128)(2,1)}, u32[]{:S(2)}, u32[]{:S(2)}) collective-permute-start(bf16[96,2304]{1,0:T(8,128)(2,1)} %collective-permute-done.18), channel_id=1, source_target_pairs={{0,8},{2,10},{4,12},{6,14},{8,16},{10,18},{12,20},{14,22},{16,24},... | collective-permute-start | bytes 1327112 | tf_op jit(solution)/shard_map/ppermute | solution.py:60
  97.0 7.0 %collective-permute-start.9 = (bf16[64,768]{1,0:T(8,128)(2,1)S(1)}, bf16[64,768]{1,0:T(8,128)(2,1)S(1)}, u32[]{:S(2)}, u32[]{:S(2)}) collective-permute-start(bf16[64,768]{1,0:T(8,128)(2,1)S(1)} %get-tuple-element.193), channel_id=1, source_target_pairs={{0,3},{1,2},{2,1},{3,0},{4,7},{5,6},{6,5},{7,4},{8,11},{9,10},{10,... | collective-permute-start | bytes 294920 | tf_op jit(solution)/shard_map/ppermute | solution.py:53
  97.6 11.3 %collective-permute-start.8 = (bf16[64,768]{1,0:T(8,128)(2,1)S(1)}, bf16[64,768]{1,0:T(8,128)(2,1)}, u32[]{:S(2)}, u32[]{:S(2)}) collective-permute-start(bf16[64,768]{1,0:T(8,128)(2,1)S(1)} %get-tuple-element.194), channel_id=1, source_target_pairs={{0,2},{1,3},{2,0},{3,1},{4,6},{5,7},{6,4},{7,5},{8,10},{9,11},{10,... | collective-permute-start | bytes 294920 | tf_op jit(solution)/shard_map/ppermute | solution.py:53
  110.4 23.5 %collective-permute-start.15 = (bf16[64,768]{1,0:T(8,128)(2,1)S(1)}, bf16[64,768]{1,0:T(8,128)(2,1)S(1)}, u32[]{:S(2)}, u32[]{:S(2)}) collective-permute-start(bf16[64,768]{1,0:T(8,128)(2,1)S(1)} %add_convert_fusion.2), channel_id=1, source_target_pairs={{0,3},{1,2},{2,1},{3,0},{4,7},{5,6},{6,5},{7,4},{8,11},{9,10},{10,... | collective-permute-start | bytes 294920 | tf_op jit(solution)/shard_map/ppermute | solution.py:53
  110.5 23.4 %collective-permute-start.14 = (bf16[64,768]{1,0:T(8,128)(2,1)S(1)}, bf16[64,768]{1,0:T(8,128)(2,1)S(1)}, u32[]{:S(2)}, u32[]{:S(2)}) collective-permute-start(bf16[64,768]{1,0:T(8,128)(2,1)S(1)} %add_convert_fusion.2), channel_id=1, source_target_pairs={{0,2},{1,3},{2,0},{3,1},{4,6},{5,7},{6,4},{7,5},{8,10},{9,11},{10,... | collective-permute-start | bytes 294920 | tf_op jit(solution)/shard_map/ppermute | solution.py:53
  111.6 22.3 %collective-permute-start.13 = (bf16[64,768]{1,0:T(8,128)(2,1)S(1)}, bf16[64,768]{1,0:T(8,128)(2,1)S(1)}, u32[]{:S(2)}, u32[]{:S(2)}) collective-permute-start(bf16[64,768]{1,0:T(8,128)(2,1)S(1)} %add_convert_fusion.2), channel_id=1, source_target_pairs={{0,1},{1,0},{2,3},{3,2},{4,5},{5,4},{6,7},{7,6},{8,9},{9,8},{10,11... | collective-permute-start | bytes 294920 | tf_op jit(solution)/shard_map/ppermute | solution.py:53
  118.7 14.5 %collective-permute-start.20 = (bf16[4,96,768]{2,1,0:T(8,128)(2,1)S(1)}, bf16[4,96,768]{2,1,0:T(8,128)(2,1)S(1)}, u32[]{:S(2)}, u32[]{:S(2)}) collective-permute-start(bf16[4,96,768]{2,1,0:T(8,128)(2,1)S(1)} %pad_maximum_fusion.8), channel_id=1, source_target_pairs={{0,4},{2,6},{4,0},{6,2},{8,12},{10,14},{12,8},{14,10},{16,20},{18,... | collective-permute-start | bytes 1769480 | tf_op jit(solution)/shard_map/ppermute | solution.py:45
  121.7 32.6 %collective-permute-start.35 = (bf16[2,192,768]{2,1,0:T(8,128)(2,1)}, bf16[2,192,768]{2,1,0:T(8,128)(2,1)}, u32[]{:S(2)}, u32[]{:S(2)}) collective-permute-start(bf16[2,192,768]{2,1,0:T(8,128)(2,1)} %pad_maximum_fusion.9), channel_id=1, source_target_pairs={{0,8},{2,10},{4,12},{6,14},{8,16},{10,18},{12,20},{14,22},{16,24},... | collective-permute-start | bytes 1769480 | tf_op jit(solution)/shard_map/ppermute | solution.py:60
  133.2 37.9 %collective-permute-start.27 = (bf16[4,96,1536]{2,1,0:T(8,128)(2,1)}, bf16[4,96,1536]{2,1,0:T(8,128)(2,1)}, u32[]{:S(2)}, u32[]{:S(2)}) collective-permute-start(bf16[4,96,1536]{2,1,0:T(8,128)(2,1)} %pad_maximum_fusion.6), channel_id=1, source_target_pairs={{0,4},{2,6},{4,0},{6,2},{8,12},{10,14},{12,8},{14,10},{16,20},{18,... | collective-permute-start | bytes 3538952 | tf_op jit(solution)/shard_map/ppermute | solution.py:45
  145.4 9.0 %collective-permute-start.21 = (bf16[64,768]{1,0:T(8,128)(2,1)S(1)}, bf16[64,768]{1,0:T(8,128)(2,1)S(1)}, u32[]{:S(2)}, u32[]{:S(2)}) collective-permute-start(bf16[64,768]{1,0:T(8,128)(2,1)S(1)} %get-tuple-element.189), channel_id=1, source_target_pairs={{0,1},{1,0},{2,3},{3,2},{4,5},{5,4},{6,7},{7,6},{8,9},{9,8},{10,11... | collective-permute-start | bytes 294920 | tf_op jit(solution)/shard_map/ppermute | solution.py:53
  145.4 8.9 %collective-permute-start.23 = (bf16[64,768]{1,0:T(8,128)(2,1)S(1)}, bf16[64,768]{1,0:T(8,128)(2,1)S(1)}, u32[]{:S(2)}, u32[]{:S(2)}) collective-permute-start(bf16[64,768]{1,0:T(8,128)(2,1)S(1)} %get-tuple-element.190), channel_id=1, source_target_pairs={{0,3},{1,2},{2,1},{3,0},{4,7},{5,6},{6,5},{7,4},{8,11},{9,10},{10,... | collective-permute-start | bytes 294920 | tf_op jit(solution)/shard_map/ppermute | solution.py:53
  146.5 7.8 %collective-permute-start.22 = (bf16[64,768]{1,0:T(8,128)(2,1)S(1)}, bf16[64,768]{1,0:T(8,128)(2,1)S(1)}, u32[]{:S(2)}, u32[]{:S(2)}) collective-permute-start(bf16[64,768]{1,0:T(8,128)(2,1)S(1)} %get-tuple-element.191), channel_id=1, source_target_pairs={{0,2},{1,3},{2,0},{3,1},{4,6},{5,7},{6,4},{7,5},{8,10},{9,11},{10,... | collective-permute-start | bytes 294920 | tf_op jit(solution)/shard_map/ppermute | solution.py:53
  154.3 16.8 %collective-permute-start.36 = (bf16[2,192,768]{2,1,0:T(8,128)(2,1)}, bf16[2,192,768]{2,1,0:T(8,128)(2,1)}, u32[]{:S(2)}, u32[]{:S(2)}) collective-permute-start(bf16[2,192,768]{2,1,0:T(8,128)(2,1)} %collective-permute-done.35), channel_id=1, source_target_pairs={{0,8},{2,10},{4,12},{6,14},{8,16},{10,18},{12,20},{14,22},{16,24},... | collective-permute-start | bytes 1769480 | tf_op jit(solution)/shard_map/ppermute | solution.py:60
  154.9 18.5 %collective-permute-start.26 = (bf16[64,768]{1,0:T(8,128)(2,1)S(1)}, bf16[64,768]{1,0:T(8,128)(2,1)S(1)}, u32[]{:S(2)}, u32[]{:S(2)}) collective-permute-start(bf16[64,768]{1,0:T(8,128)(2,1)S(1)} %add_convert_fusion.1), channel_id=1, source_target_pairs={{0,3},{1,2},{2,1},{3,0},{4,7},{5,6},{6,5},{7,4},{8,11},{9,10},{10,... | collective-permute-start | bytes 294920 | tf_op jit(solution)/shard_map/ppermute | solution.py:53
  155.0 18.4 %collective-permute-start.25 = (bf16[64,768]{1,0:T(8,128)(2,1)S(1)}, bf16[64,768]{1,0:T(8,128)(2,1)S(1)}, u32[]{:S(2)}, u32[]{:S(2)}) collective-permute-start(bf16[64,768]{1,0:T(8,128)(2,1)S(1)} %add_convert_fusion.1), channel_id=1, source_target_pairs={{0,2},{1,3},{2,0},{3,1},{4,6},{5,7},{6,4},{7,5},{8,10},{9,11},{10,... | collective-permute-start | bytes 294920 | tf_op jit(solution)/shard_map/ppermute | solution.py:53
  156.0 17.4 %collective-permute-start.24 = (bf16[64,768]{1,0:T(8,128)(2,1)S(1)}, bf16[64,768]{1,0:T(8,128)(2,1)S(1)}, u32[]{:S(2)}, u32[]{:S(2)}) collective-permute-start(bf16[64,768]{1,0:T(8,128)(2,1)S(1)} %add_convert_fusion.1), channel_id=1, source_target_pairs={{0,1},{1,0},{2,3},{3,2},{4,5},{5,4},{6,7},{7,6},{8,9},{9,8},{10,11... | collective-permute-start | bytes 294920 | tf_op jit(solution)/shard_map/ppermute | solution.py:53
  171.1 16.5 %collective-permute-start.37 = (bf16[2,192,768]{2,1,0:T(8,128)(2,1)}, bf16[2,192,768]{2,1,0:T(8,128)(2,1)}, u32[]{:S(2)}, u32[]{:S(2)}) collective-permute-start(bf16[2,192,768]{2,1,0:T(8,128)(2,1)} %collective-permute-done.36), channel_id=1, source_target_pairs={{0,8},{2,10},{4,12},{6,14},{8,16},{10,18},{12,20},{14,22},{16,24},... | collective-permute-start | bytes 1769480 | tf_op jit(solution)/shard_map/ppermute | solution.py:60
  177.7 6.8 %collective-permute-start.29 = (bf16[64,768]{1,0:T(8,128)(2,1)}, bf16[64,768]{1,0:T(8,128)(2,1)}, u32[]{:S(2)}, u32[]{:S(2)}) collective-permute-start(bf16[64,768]{1,0:T(8,128)(2,1)} %get-tuple-element.188), channel_id=1, source_target_pairs={{0,2},{1,3},{2,0},{3,1},{4,6},{5,7},{6,4},{7,5},{8,10},{9,11},{10,... | collective-permute-start | bytes 294920 | tf_op jit(solution)/shard_map/ppermute | solution.py:53
  185.8 6.6 %collective-permute-start.32 = (bf16[64,768]{1,0:T(8,128)(2,1)S(1)}, bf16[64,768]{1,0:T(8,128)(2,1)S(1)}, u32[]{:S(2)}, u32[]{:S(2)}) collective-permute-start(bf16[64,768]{1,0:T(8,128)(2,1)S(1)} %fusion.85), channel_id=1, source_target_pairs={{0,2},{1,3},{2,0},{3,1},{4,6},{5,7},{6,4},{7,5},{8,10},{9,11},{10,... | collective-permute-start | bytes 294920 | tf_op jit(solution)/shard_map/ppermute | solution.py:53
  197.7 11.1 %collective-permute-start.38 = (bf16[64,8,192]{2,1,0:T(8,128)(2,1)}, bf16[64,8,192]{2,1,0:T(8,128)(2,1)S(1)}, u32[]{:S(2)}, u32[]{:S(2)}) collective-permute-start(bf16[64,8,192]{2,1,0:T(8,128)(2,1)} %slice.368), channel_id=1, source_target_pairs={{0,1},{1,0},{2,3},{3,2},{4,5},{5,4},{6,7},{7,6},{8,9},{9,8},{10,11... | collective-permute-start | bytes 589832 | tf_op jit(solution)/shard_map/ppermute | solution.py:53
  197.8 11.0 %collective-permute-start.39 = (bf16[64,8,192]{2,1,0:T(8,128)(2,1)}, bf16[64,8,192]{2,1,0:T(8,128)(2,1)}, u32[]{:S(2)}, u32[]{:S(2)}) collective-permute-start(bf16[64,8,192]{2,1,0:T(8,128)(2,1)} %slice.370), channel_id=1, source_target_pairs={{0,2},{1,3},{2,0},{3,1},{4,6},{5,7},{6,4},{7,5},{8,10},{9,11},{10,... | collective-permute-start | bytes 589832 | tf_op jit(solution)/shard_map/ppermute | solution.py:53
  199.0 12.9 %collective-permute-start.40 = (bf16[64,8,192]{2,1,0:T(8,128)(2,1)}, bf16[64,8,192]{2,1,0:T(8,128)(2,1)}, u32[]{:S(2)}, u32[]{:S(2)}) collective-permute-start(bf16[64,8,192]{2,1,0:T(8,128)(2,1)} %slice.372), channel_id=1, source_target_pairs={{0,3},{1,2},{2,1},{3,0},{4,7},{5,6},{6,5},{7,4},{8,11},{9,10},{10,... | collective-permute-start | bytes 589832 | tf_op jit(solution)/shard_map/ppermute | solution.py:53
  264.7 9.5 %collective-permute-start.42 = (bf16[512,192]{1,0:T(8,128)(2,1)}, bf16[512,192]{1,0:T(8,128)(2,1)}, u32[]{:S(2)}, u32[]{:S(2)}) collective-permute-start(bf16[512,192]{1,0:T(8,128)(2,1)} %get-tuple-element.47), channel_id=1, source_target_pairs={{0,2},{1,3},{2,0},{3,1},{4,6},{5,7},{6,4},{7,5},{8,10},{9,11},{10,... | collective-permute-start | bytes 589832 | tf_op jit(solution)/shard_map/ppermute | solution.py:53
  265.9 12.4 %collective-permute-start.43 = (bf16[512,192]{1,0:T(8,128)(2,1)}, bf16[512,192]{1,0:T(8,128)(2,1)S(1)}, u32[]{:S(2)}, u32[]{:S(2)}) collective-permute-start(bf16[512,192]{1,0:T(8,128)(2,1)} %get-tuple-element.48), channel_id=1, source_target_pairs={{0,3},{1,2},{2,1},{3,0},{4,7},{5,6},{6,5},{7,4},{8,11},{9,10},{10,... | collective-permute-start | bytes 589832 | tf_op jit(solution)/shard_map/ppermute | solution.py:53
  289.9 6.5 %collective-permute-start.48 = (bf16[64,768]{1,0:T(8,128)(2,1)S(1)}, bf16[64,768]{1,0:T(8,128)(2,1)S(1)}, u32[]{:S(2)}, u32[]{:S(2)}) collective-permute-start(bf16[64,768]{1,0:T(8,128)(2,1)S(1)} %get-tuple-element.112), channel_id=1, source_target_pairs={{0,2},{1,3},{2,0},{3,1},{4,6},{5,7},{6,4},{7,5},{8,10},{9,11},{10,... | collective-permute-start | bytes 294920 | tf_op jit(solution)/shard_map/ppermute | solution.py:53
  291.9 20.6 %collective-permute-start.53 = (bf16[2,192,768]{2,1,0:T(8,128)(2,1)}, bf16[2,192,768]{2,1,0:T(8,128)(2,1)}, u32[]{:S(2)}, u32[]{:S(2)}) collective-permute-start(bf16[2,192,768]{2,1,0:T(8,128)(2,1)} %dynamic-slice_bitcast_fusion.3), channel_id=1, source_target_pairs={{0,8},{2,10},{4,12},{6,14},{8,16},{10,18},{12,20},{14,22},{16,24},... | collective-permute-start | bytes 1769480 | tf_op jit(solution)/shard_map/ppermute | solution.py:60
  299.4 9.7 %collective-permute-start.50 = (bf16[64,768]{1,0:T(8,128)(2,1)}, bf16[64,768]{1,0:T(8,128)(2,1)}, u32[]{:S(2)}, u32[]{:S(2)}) collective-permute-start(bf16[64,768]{1,0:T(8,128)(2,1)} %get-tuple-element.180), channel_id=1, source_target_pairs={{0,1},{1,0},{2,3},{3,2},{4,5},{5,4},{6,7},{7,6},{8,9},{9,8},{10,11... | collective-permute-start | bytes 294920 | tf_op jit(solution)/shard_map/ppermute | solution.py:53
  299.4 9.6 %collective-permute-start.52 = (bf16[64,768]{1,0:T(8,128)(2,1)}, bf16[64,768]{1,0:T(8,128)(2,1)}, u32[]{:S(2)}, u32[]{:S(2)}) collective-permute-start(bf16[64,768]{1,0:T(8,128)(2,1)} %get-tuple-element.181), channel_id=1, source_target_pairs={{0,3},{1,2},{2,1},{3,0},{4,7},{5,6},{6,5},{7,4},{8,11},{9,10},{10,... | collective-permute-start | bytes 294920 | tf_op jit(solution)/shard_map/ppermute | solution.py:53
  300.7 8.4 %collective-permute-start.51 = (bf16[64,768]{1,0:T(8,128)(2,1)S(1)}, bf16[64,768]{1,0:T(8,128)(2,1)}, u32[]{:S(2)}, u32[]{:S(2)}) collective-permute-start(bf16[64,768]{1,0:T(8,128)(2,1)S(1)} %get-tuple-element.182), channel_id=1, source_target_pairs={{0,2},{1,3},{2,0},{3,1},{4,6},{5,7},{6,4},{7,5},{8,10},{9,11},{10,... | collective-permute-start | bytes 294920 | tf_op jit(solution)/shard_map/ppermute | solution.py:53
  308.6 57.4 %collective-permute-start.64 = (bf16[4,96,1536]{2,1,0:T(8,128)(2,1)}, bf16[4,96,1536]{2,1,0:T(8,128)(2,1)}, u32[]{:S(2)}, u32[]{:S(2)}) collective-permute-start(bf16[4,96,1536]{2,1,0:T(8,128)(2,1)} %dynamic-slice_bitcast_fusion.1), channel_id=1, source_target_pairs={{0,4},{2,6},{4,0},{6,2},{8,12},{10,14},{12,8},{14,10},{16,20},{18,... | collective-permute-start | bytes 3538952 | tf_op jit(solution)/shard_map/ppermute | solution.py:45
  312.5 6.7 %collective-permute-start.56 = (bf16[64,768]{1,0:T(8,128)(2,1)S(1)}, bf16[64,768]{1,0:T(8,128)(2,1)S(1)}, u32[]{:S(2)}, u32[]{:S(2)}) collective-permute-start(bf16[64,768]{1,0:T(8,128)(2,1)S(1)} %fusion.101), channel_id=1, source_target_pairs={{0,3},{1,2},{2,1},{3,0},{4,7},{5,6},{6,5},{7,4},{8,11},{9,10},{10,... | collective-permute-start | bytes 294920 | tf_op jit(solution)/shard_map/ppermute | solution.py:53
  316.6 27.9 %collective-permute-start.60 = (bf16[2,192,768]{2,1,0:T(8,128)(2,1)}, bf16[2,192,768]{2,1,0:T(8,128)(2,1)}, u32[]{:S(2)}, u32[]{:S(2)}) collective-permute-start(bf16[2,192,768]{2,1,0:T(8,128)(2,1)} %fusion.5), channel_id=1, source_target_pairs={{0,8},{2,10},{4,12},{6,14},{8,16},{10,18},{12,20},{14,22},{16,24},... | collective-permute-start | bytes 1769480 | tf_op jit(solution)/shard_map/ppermute | solution.py:60
  325.4 7.1 %collective-permute-start.59 = (bf16[64,768]{1,0:T(8,128)(2,1)S(1)}, bf16[64,768]{1,0:T(8,128)(2,1)S(1)}, u32[]{:S(2)}, u32[]{:S(2)}) collective-permute-start(bf16[64,768]{1,0:T(8,128)(2,1)S(1)} %get-tuple-element.178), channel_id=1, source_target_pairs={{0,3},{1,2},{2,1},{3,0},{4,7},{5,6},{6,5},{7,4},{8,11},{9,10},{10,... | collective-permute-start | bytes 294920 | tf_op jit(solution)/shard_map/ppermute | solution.py:53
  326.2 10.7 %collective-permute-start.58 = (bf16[64,768]{1,0:T(8,128)(2,1)S(1)}, bf16[64,768]{1,0:T(8,128)(2,1)S(1)}, u32[]{:S(2)}, u32[]{:S(2)}) collective-permute-start(bf16[64,768]{1,0:T(8,128)(2,1)S(1)} %get-tuple-element.179), channel_id=1, source_target_pairs={{0,2},{1,3},{2,0},{3,1},{4,6},{5,7},{6,4},{7,5},{8,10},{9,11},{10,... | collective-permute-start | bytes 294920 | tf_op jit(solution)/shard_map/ppermute | solution.py:53
  340.7 23.0 %collective-permute-start.77 = (bf16[4,96,768]{2,1,0:T(8,128)(2,1)}, bf16[4,96,768]{2,1,0:T(8,128)(2,1)S(1)}, u32[]{:S(2)}, u32[]{:S(2)}) collective-permute-start(bf16[4,96,768]{2,1,0:T(8,128)(2,1)} %dynamic-slice_bitcast_fusion.2), channel_id=1, source_target_pairs={{0,4},{2,6},{4,0},{6,2},{8,12},{10,14},{12,8},{14,10},{16,20},{18,... | collective-permute-start | bytes 1769480 | tf_op jit(solution)/shard_map/ppermute | solution.py:45
  344.5 15.9 %collective-permute-start.63 = (bf16[64,768]{1,0:T(8,128)(2,1)S(1)}, bf16[64,768]{1,0:T(8,128)(2,1)S(1)}, u32[]{:S(2)}, u32[]{:S(2)}) collective-permute-start(bf16[64,768]{1,0:T(8,128)(2,1)S(1)} %add_convert_fusion), channel_id=1, source_target_pairs={{0,3},{1,2},{2,1},{3,0},{4,7},{5,6},{6,5},{7,4},{8,11},{9,10},{10,... | collective-permute-start | bytes 294920 | tf_op jit(solution)/shard_map/ppermute | solution.py:53
  344.5 15.9 %collective-permute-start.62 = (bf16[64,768]{1,0:T(8,128)(2,1)S(1)}, bf16[64,768]{1,0:T(8,128)(2,1)S(1)}, u32[]{:S(2)}, u32[]{:S(2)}) collective-permute-start(bf16[64,768]{1,0:T(8,128)(2,1)S(1)} %add_convert_fusion), channel_id=1, source_target_pairs={{0,2},{1,3},{2,0},{3,1},{4,6},{5,7},{6,4},{7,5},{8,10},{9,11},{10,... | collective-permute-start | bytes 294920 | tf_op jit(solution)/shard_map/ppermute | solution.py:53
  347.8 37.4 %collective-permute-start.65 = (bf16[2,192,768]{2,1,0:T(8,128)(2,1)S(1)}, bf16[2,192,768]{2,1,0:T(8,128)(2,1)S(1)}, u32[]{:S(2)}, u32[]{:S(2)}) collective-permute-start(bf16[2,192,768]{2,1,0:T(8,128)(2,1)S(1)} %fusion.4), channel_id=1, source_target_pairs={{0,8},{2,10},{4,12},{6,14},{8,16},{10,18},{12,20},{14,22},{16,24},... | collective-permute-start | bytes 1769480 | tf_op jit(solution)/shard_map/ppermute | solution.py:60
  363.5 68.4 %collective-permute-start.72 = (bf16[4,193,768]{2,0,1:T(4,128)(2,1)}, bf16[4,193,768]{2,0,1:T(4,128)(2,1)}, u32[]{:S(2)}, u32[]{:S(2)}) collective-permute-start(bf16[4,193,768]{2,0,1:T(4,128)(2,1)} %copy.218), channel_id=1, source_target_pairs={{0,4},{2,6},{4,0},{6,2},{8,12},{10,14},{12,8},{14,10},{16,20},{18,... | collective-permute-start | bytes 3557384 | tf_op jit(solution)/shard_map/ppermute | solution.py:45
  369.4 30.1 %collective-permute-start.78 = (bf16[96,2304]{1,0:T(8,128)(2,1)}, bf16[96,2304]{1,0:T(8,128)(2,1)}, u32[]{:S(2)}, u32[]{:S(2)}) collective-permute-start(bf16[96,2304]{1,0:T(8,128)(2,1)} %fusion.66), channel_id=1, source_target_pairs={{0,8},{2,10},{4,12},{6,14},{8,16},{10,18},{12,20},{14,22},{16,24},... | collective-permute-start | bytes 1327112 | tf_op jit(solution)/shard_map/ppermute | solution.py:60
  388.1 41.8 %collective-permute-start.76 = (bf16[192,768]{1,0:T(8,128)(2,1)}, bf16[192,768]{1,0:T(8,128)(2,1)}, u32[]{:S(2)}, u32[]{:S(2)}) collective-permute-start(bf16[192,768]{1,0:T(8,128)(2,1)} %fusion.72), channel_id=1, source_target_pairs={{0,4},{2,6},{4,0},{6,2},{8,12},{10,14},{12,8},{14,10},{16,20},{18,... | collective-permute-start | bytes 884744 | tf_op jit(solution)/shard_map/ppermute | solution.py:45
  398.2 10.5 %collective-permute-start.68 = (bf16[64,8,192]{2,1,0:T(8,128)(2,1)}, bf16[64,8,192]{2,1,0:T(8,128)(2,1)S(1)}, u32[]{:S(2)}, u32[]{:S(2)}) collective-permute-start(bf16[64,8,192]{2,1,0:T(8,128)(2,1)} %slice.398), channel_id=1, source_target_pairs={{0,3},{1,2},{2,1},{3,0},{4,7},{5,6},{6,5},{7,4},{8,11},{9,10},{10,... | collective-permute-start | bytes 589832 | tf_op jit(solution)/shard_map/ppermute | solution.py:53
  399.5 19.4 %collective-permute-start.67 = (bf16[64,8,192]{2,1,0:T(8,128)(2,1)}, bf16[64,8,192]{2,1,0:T(8,128)(2,1)S(1)}, u32[]{:S(2)}, u32[]{:S(2)}) collective-permute-start(bf16[64,8,192]{2,1,0:T(8,128)(2,1)} %slice.396), channel_id=1, source_target_pairs={{0,2},{1,3},{2,0},{3,1},{4,6},{5,7},{6,4},{7,5},{8,10},{9,11},{10,... | collective-permute-start | bytes 589832 | tf_op jit(solution)/shard_map/ppermute | solution.py:53
  402.1 26.4 %collective-permute-start.79 = (bf16[96,2304]{1,0:T(8,128)(2,1)}, bf16[96,2304]{1,0:T(8,128)(2,1)}, u32[]{:S(2)}, u32[]{:S(2)}) collective-permute-start(bf16[96,2304]{1,0:T(8,128)(2,1)} %fusion.32), channel_id=1, source_target_pairs={{0,8},{2,10},{4,12},{6,14},{8,16},{10,18},{12,20},{14,22},{16,24},... | collective-permute-start | bytes 1327112 | tf_op jit(solution)/shard_map/ppermute | solution.py:60
  429.8 16.9 %collective-permute-start.80 = (bf16[96,2304]{1,0:T(8,128)(2,1)S(1)}, bf16[96,2304]{1,0:T(8,128)(2,1)S(1)}, u32[]{:S(2)}, u32[]{:S(2)}) collective-permute-start(bf16[96,2304]{1,0:T(8,128)(2,1)S(1)} %fusion.28), channel_id=1, source_target_pairs={{0,8},{2,10},{4,12},{6,14},{8,16},{10,18},{12,20},{14,22},{16,24},... | collective-permute-start | bytes 1327112 | tf_op jit(solution)/shard_map/ppermute | solution.py:60
  433.4 19.4 %collective-permute-start.73 = (bf16[193,768]{1,0:T(8,128)(2,1)S(1)}, bf16[193,768]{1,0:T(8,128)(2,1)S(1)}, u32[]{:S(2)}, u32[]{:S(2)}) collective-permute-start(bf16[193,768]{1,0:T(8,128)(2,1)S(1)} %fusion.71), channel_id=1, source_target_pairs={{0,8},{2,10},{4,12},{6,14},{8,16},{10,18},{12,20},{14,22},{16,24},... | collective-permute-start | bytes 889352 | tf_op jit(solution)/shard_map/ppermute | solution.py:60
  452.8 16.8 %collective-permute-start.74 = (bf16[193,768]{1,0:T(8,128)(2,1)S(1)}, bf16[193,768]{1,0:T(8,128)(2,1)S(1)}, u32[]{:S(2)}, u32[]{:S(2)}) collective-permute-start(bf16[193,768]{1,0:T(8,128)(2,1)S(1)} %fusion.60), channel_id=1, source_target_pairs={{0,8},{2,10},{4,12},{6,14},{8,16},{10,18},{12,20},{14,22},{16,24},... | collective-permute-start | bytes 889352 | tf_op jit(solution)/shard_map/ppermute | solution.py:60
  469.7 9.8 %collective-permute-start.75 = (bf16[193,768]{1,0:T(8,128)(2,1)S(1)}, bf16[193,768]{1,0:T(8,128)(2,1)S(1)}, u32[]{:S(2)}, u32[]{:S(2)}) collective-permute-start(bf16[193,768]{1,0:T(8,128)(2,1)S(1)} %fusion.61), channel_id=1, source_target_pairs={{0,8},{2,10},{4,12},{6,14},{8,16},{10,18},{12,20},{14,22},{16,24},... | collective-permute-start | bytes 889352 | tf_op jit(solution)/shard_map/ppermute | solution.py:60
  (119 other events, 789.9 us)
Sparse Core Ops, SparseCore 0:
  13.2 140.0 all-gather.2
  263.3 212.1 reduce-scatter.1

commit v6 on v5

--- a/solution.py
+++ b/solution.py
@@ -537,11 +537,11 @@
         turned_ref[...] = normed_ref[...].T
         branch_turned_ref[...] = branch_ref[...].T
 
-    @pl.when(step == 4)
+    @pl.when(step == 2)
     def _():
         turned_ref[...] = second_ref[...].T
 
-    @pl.when(step == 8)
+    @pl.when(step == 4)
     def _():
         turned_ref[...] = grad_out_ref[...].T
 
@@ -551,12 +551,12 @@
             weights_out_ref.shape[:3] + (product.shape[1],)
         )
 
-    @pl.when(block == 1)
+    @pl.when(block == 0)
     def _():
-        give(turned_ref, factors_ref[side, :, 2 * wide : 3 * wide], slice(0, wide))
-        give(branch_turned_ref, factors_ref[side, :, 3 * wide : 4 * wide], slice(wide, 2 * wide))
-
-    @pl.when(block != 1)
+        give(turned_ref, factors_ref[side, :, : 3 * wide], slice(0, 3 * wide))
+        give(branch_turned_ref, factors_ref[side, :, 3 * wide : 4 * wide], slice(3 * wide, 4 * wide))
+
+    @pl.when(block != 0)
     def _():
         start = pl.multiple_of(block * width, width)
         give(turned_ref, factors_ref[side, :, pl.ds(start, width)], slice(None))
@@ -566,8 +566,8 @@
     rows = masked_low.shape[0]
     tiles = rows // TILE
     columns = weights.shape[3]
-    width = 2 * wide
-    assert columns == 6 * width
+    width = 4 * wide
+    assert columns == 3 * width
     tiled = lambda size: pl.BlockSpec((TILE, size), lambda i: (jnp.minimum(i, tiles - 1), 0))
     fixed = lambda array: pl.BlockSpec(array.shape, lambda i: (0, 0), pipeline_mode=pl.Buffered(1))
     outs = [(D, BF16), (D, F32)] + [(D // QUAD, BF16)] * QUAD
@@ -785,11 +785,6 @@
     )
     global_summed = line_scatter(jnp.concatenate([attend_half, forward_half], axis=2))
     grad_patch_mat = dot_tn(patches_mat, grad_start).astype(BF16).reshape(cells, proj_rows, D)
-    grad_patches = after(dot_nt(grad_start, patch_mat).astype(BF16), forward_half, *marks[2:3])
-    grad_patches = quad_collect(grad_patches.reshape(QUAD * patch_rows, cells, proj_rows))
-    grad_patches = grad_patches.reshape(half_rows, D).astype(F32)
-    grad_input = ((grad_local + grad_patches) * keep_mask).astype(BF16)[None]
-
     gain_grads = jnp.stack([first_gains[0], first_gains[1], second_gains[0], second_gains[1]])
     bias_grads = jnp.stack([first_biases[0], first_biases[1], second_biases[0], second_biases[1]])
     norm_grads = jnp.concatenate(
@@ -805,7 +800,15 @@
         piece = lax.dynamic_index_in_dim(norm_grads, place ^ bits, 1, keepdims=False)
         norm_sum = norm_sum + flip_quad(piece, bits)
     norm_rows = jnp.pad(norm_sum[:, None, :].astype(BF16), ((0, 0), (0, 0), (0, D - 2 * norm_part)))
-    patch_summed = line_y_scatter(jnp.concatenate([grad_patch_mat, norm_rows], axis=1))
+    patch_marks = []
+    patch_terms = jnp.concatenate([grad_patch_mat, norm_rows], axis=1)
+    patch_half = y_scatter(patch_terms)
+    patch_summed = line_scatter(patch_half, patch_marks)
+    grad_patches = after(dot_nt(grad_start, patch_mat).astype(BF16), forward_half, patch_terms)
+    grad_patches = quad_collect(grad_patches.reshape(QUAD * patch_rows, cells, proj_rows))
+    grad_patches = grad_patches.reshape(half_rows, D).astype(F32)
+    grad_patches = after(grad_patches, *patch_marks[:1])
+    grad_input = ((grad_local + grad_patches) * keep_mask).astype(BF16)[None]
 
     def x_restore(summed):
         shaped = summed.reshape(2, shard_rows, -1)

time: 502 us -> 499 us (level)
    ppermute x10, waiting for transfers between devices: 16.6 us -> 26.2 us  [flip_dp(): lax.ppermute(values_in, 'dp', [(i, i ^ bit) for i in range(dp_size())])]
    ppermute x54, waiting for transfers between devices: 63.3 us -> 55.1 us  [flip_quad(): lax.ppermute(values_in, ('dp', 'tensor'), [(i, i ^ bits) for i in range(2...]
    unnamed x218 -> x214, local copies, waits for them, and re-layouts: 16.1 us -> 16 us
  transfers between devices with their start and end apart: 84 -> 84, of which waited for: 36 -> 37; matrix products, arithmetic and copies ran while one was open for 27% -> 28% of each run, Pallas kernels for 0% -> 0%
where the time goes in v6:
time: 499 us; the launch traced here: 490 us
  waiting for transfers between devices  199 us (40%)
  local copies, waits for them, and re-layouts  84.6 us (17%)
  starting transfers between devices  70.4 us (14%)
  Pallas kernels  49.3 us (10%)
  other arithmetic  46.1 us (9%)
  matrix products  22.8 us (5%)
  between operations  17.2 us (3%)
    ppermute x18, waiting for transfers between devices, step_line(): lax.ppermute(values_in, 'dp', [(i, (i + 4 * offset) % count) for i in ran...  118 us
    ppermute x54, waiting for transfers between devices, flip_quad(): lax.ppermute(values_in, ('dp', 'tensor'), [(i, i ^ bits) for i in range(2...  55.1 us
    pallas_call x1, Pallas kernels, local_layer(): pl.pallas_call(lambda *refs: local_body(tiles, wide, *refs), grid=(tiles...  49.3 us
    ppermute x54, starting transfers between devices, flip_quad(): lax.ppermute(values_in, ('dp', 'tensor'), [(i, i ^ bits) for i in range(2...  36.4 us
    ppermute x10, waiting for transfers between devices, flip_dp(): lax.ppermute(values_in, 'dp', [(i, i ^ bit) for i in range(dp_size())])  26.2 us
    ppermute x18, starting transfers between devices, step_line(): lax.ppermute(values_in, 'dp', [(i, (i + 4 * offset) % count) for i in ran...  24.7 us
    unnamed x214, local copies, waits for them, and re-layouts  16 us
  transfers between devices with their start and end apart: 84, of which 37 were waited for; matrix products, arithmetic and copies ran while one was open for 28% of the time, Pallas kernels for 0%

profile of v6, /device:TPU:4, one launch (start us, length us, event | category | flops | bytes accessed | tf_op | source)
XLA Modules:
  0.0 489.6 jit_solution(10914337728202406577)
XLA Ops:
  14.9 1.6 collective-permute-start.3
  20.8 5.0 %collective-permute-done.3 = bf16[193,768]{1,0:T(8,128)(2,1)S(1)} collective-permute-done((bf16[193,768]{1,0:T(8,128)(2,1)S(1)}, bf16[193,768]{1,0:T(8,128)(2,1)S(1)}, u32[]{:S(2)}, u32[]{:S(2)}) %collective-permute-start.3) | collective-permute-done | bytes 296480 | tf_op jit(solution)/shard_map/ppermute | solution.py:60
  26.9 16.7 %collective-permute-done.4 = bf16[193,768]{1,0:T(8,128)(2,1)} collective-permute-done((bf16[193,768]{1,0:T(8,128)(2,1)S(1)}, bf16[193,768]{1,0:T(8,128)(2,1)}, u32[]{:S(2)}, u32[]{:S(2)}) %collective-permute-start.4) | collective-permute-done | bytes 296480 | tf_op jit(solution)/shard_map/ppermute | solution.py:60
  43.7 4.2 fusion.126
  47.9 2.1 copy.181
  52.7 2.0 collective-permute-done.5
  57.9 1.7 collective-permute-start.6
  65.6 9.9 %collective-permute-done.17 = bf16[96,2304]{1,0:T(8,128)(2,1)} collective-permute-done((bf16[96,2304]{1,0:T(8,128)(2,1)S(1)}, bf16[96,2304]{1,0:T(8,128)(2,1)}, u32[]{:S(2)}, u32[]{:S(2)}) %collective-permute-start.17) | collective-permute-done | bytes 442400 | tf_op jit(solution)/shard_map/ppermute | solution.py:60
  75.4 9.0 %collective-permute-done.6 = bf16[4,193,768]{2,0,1:T(4,128)(2,1)} collective-permute-done((bf16[4,193,768]{2,0,1:T(4,128)(2,1)}, bf16[4,193,768]{2,0,1:T(4,128)(2,1)}, u32[]{:S(2)}, u32[]{:S(2)}) %collective-permute-start.6) | collective-permute-done | bytes 1185824 | tf_op jit(solution)/shard_map/ppermute | solution.py:45
  87.0 4.0 collective-permute-done.18
  91.0 1.6 collective-permute-start.10
  93.2 3.1 fusion.149
  99.5 4.5 collective-permute-done.9
  104.0 4.9 %collective-permute-done.8 = bf16[64,768]{1,0:T(8,128)(2,1)} collective-permute-done((bf16[64,768]{1,0:T(8,128)(2,1)S(1)}, bf16[64,768]{1,0:T(8,128)(2,1)}, u32[]{:S(2)}, u32[]{:S(2)}) %collective-permute-start.8) | collective-permute-done | bytes 98336 | tf_op jit(solution)/shard_map/ppermute | solution.py:53
  112.4 5.1 %collective-permute-done.19 = bf16[96,2304]{1,0:T(8,128)(2,1)} collective-permute-done((bf16[96,2304]{1,0:T(8,128)(2,1)}, bf16[96,2304]{1,0:T(8,128)(2,1)}, u32[]{:S(2)}, u32[]{:S(2)}) %collective-permute-start.19) | collective-permute-done | bytes 442400 | tf_op jit(solution)/shard_map/ppermute | solution.py:60
  121.7 4.3 collective-permute-start.35
  126.0 7.2 %collective-permute-done.20 = bf16[4,96,768]{2,1,0:T(8,128)(2,1)S(1)} collective-permute-done((bf16[4,96,768]{2,1,0:T(8,128)(2,1)S(1)}, bf16[4,96,768]{2,1,0:T(8,128)(2,1)S(1)}, u32[]{:S(2)}, u32[]{:S(2)}) %collective-permute-start.20) | collective-permute-done | bytes 589856 | tf_op jit(solution)/shard_map/ppermute | solution.py:45
  136.2 1.7 reshape.256
  139.2 1.8 fusion.150
  141.0 1.8 fusion.8
  147.6 6.8 %collective-permute-done.35 = bf16[2,192,768]{2,1,0:T(8,128)(2,1)} collective-permute-done((bf16[2,192,768]{2,1,0:T(8,128)(2,1)}, bf16[2,192,768]{2,1,0:T(8,128)(2,1)}, u32[]{:S(2)}, u32[]{:S(2)}) %collective-permute-start.35) | collective-permute-done | bytes 589856 | tf_op jit(solution)/shard_map/ppermute | solution.py:60
  156.8 14.3 %collective-permute-done.36 = bf16[2,192,768]{2,1,0:T(8,128)(2,1)} collective-permute-done((bf16[2,192,768]{2,1,0:T(8,128)(2,1)}, bf16[2,192,768]{2,1,0:T(8,128)(2,1)}, u32[]{:S(2)}, u32[]{:S(2)}) %collective-permute-start.36) | collective-permute-done | bytes 589856 | tf_op jit(solution)/shard_map/ppermute | solution.py:60
  171.2 1.8 select_bitcast_fusion.3
  179.2 1.9 concatenate.120
  181.9 2.8 collective-permute-done.29
  187.7 1.7 select_bitcast_fusion.7
  194.0 1.9 slice.372
  200.8 1.8 copy.213
  202.6 1.8 copy.214
  204.4 1.8 copy.215
  208.7 3.2 collective-permute-done.40
  212.0 49.3 %shard_map.186 = (bf16[512,768]{1,0:T(8,128)(2,1)}, f32[512,768]{1,0:T(8,128)}, bf16[512,192]{1,0:T(8,128)(2,1)}, bf16[512,192]{1,0:T(8,128)(2,1)}, bf16[512,192...) custom-call(s32[2]{0:T(128)} %pad_add_fusion.refs_0_, ...), custom_call_target="tpu_custom_call" | custom-call | flops 21743271936 | bytes 28311552 | tf_op jit(solution)/shard_map/pallas_call | solution.py:579
  267.6 4.7 collective-permute-done.42
  274.2 2.2 collective-permute-done.43
  277.4 2.1 fusion.153
  282.6 2.2 collective-permute-done.46
  284.9 2.4 collective-permute-done.45
  290.1 2.3 collective-permute-done.49
  292.4 2.1 collective-permute-done.48
  302.5 3.0 copy.211
  312.7 2.2 fusion.5
  315.3 2.2 collective-permute-done.55
  326.2 4.5 collective-permute-done.59
  330.7 4.5 collective-permute-done.58
  340.6 2.3 collective-permute-done.60
  344.8 2.2 fusion.4
  347.0 12.6 %collective-permute-start.75 = (bf16[2,192,768]{2,1,0:T(8,128)(2,1)}, bf16[2,192,768]{2,1,0:T(8,128)(2,1)}, u32[]{:S(2)}, u32[]{:S(2)}) collective-permute-start(bf16[2,192,768]{2,1,0:T(8,128)(2,1)} %fusion.4), channel_id=1, source_target_pairs={{0,8},{2,10},{4,12},{6,14},{8,16},{10,18},{12,20},{14,22},{16,24},... | collective-permute-start | bytes 1769480 | tf_op jit(solution)/shard_map/ppermute | solution.py:60
  362.6 1.6 copy_dynamic-update-slice_fusion
  367.7 1.9 slice.396
  369.6 1.9 slice.398
  371.5 1.9 slice.394
  376.3 2.3 collective-permute-start.78
  382.2 1.9 slice.392
  386.9 6.8 %collective-permute-done.66 = bf16[64,8,192]{2,1,0:T(8,128)(2,1)} collective-permute-done((bf16[64,8,192]{2,1,0:T(8,128)(2,1)}, bf16[64,8,192]{2,1,0:T(8,128)(2,1)}, u32[]{:S(2)}, u32[]{:S(2)}) %collective-permute-start.66) | collective-permute-done | bytes 196640 | tf_op jit(solution)/shard_map/ppermute | solution.py:53
  395.0 1.9 fusion.32
  397.1 2.7 copy.212
  399.9 3.6 reshape.280
  406.1 13.6 %collective-permute-done.79 = bf16[96,2304]{1,0:T(8,128)(2,1)} collective-permute-done((bf16[96,2304]{1,0:T(8,128)(2,1)}, bf16[96,2304]{1,0:T(8,128)(2,1)}, u32[]{:S(2)}, u32[]{:S(2)}) %collective-permute-start.79) | collective-permute-done | bytes 442400 | tf_op jit(solution)/shard_map/ppermute | solution.py:60
  421.0 9.7 %collective-permute-done.76 = bf16[192,768]{1,0:T(8,128)(2,1)S(1)} collective-permute-done((bf16[192,768]{1,0:T(8,128)(2,1)S(1)}, bf16[192,768]{1,0:T(8,128)(2,1)S(1)}, u32[]{:S(2)}, u32[]{:S(2)}) %collective-permute-start.76) | collective-permute-done | bytes 294944 | tf_op jit(solution)/shard_map/ppermute | solution.py:45
  433.1 2.8 collective-permute-start.72
  435.8 3.7 collective-permute-done.80
  439.7 8.5 %collective-permute-done.72 = bf16[193,768]{1,0:T(8,128)(2,1)S(1)} collective-permute-done((bf16[193,768]{1,0:T(8,128)(2,1)S(1)}, bf16[193,768]{1,0:T(8,128)(2,1)S(1)}, u32[]{:S(2)}, u32[]{:S(2)}) %collective-permute-start.72) | collective-permute-done | bytes 296480 | tf_op jit(solution)/shard_map/ppermute | solution.py:60
  450.5 15.7 %collective-permute-done.73 = bf16[193,768]{1,0:T(8,128)(2,1)S(1)} collective-permute-done((bf16[193,768]{1,0:T(8,128)(2,1)S(1)}, bf16[193,768]{1,0:T(8,128)(2,1)S(1)}, u32[]{:S(2)}, u32[]{:S(2)}) %collective-permute-start.73) | collective-permute-done | bytes 296480 | tf_op jit(solution)/shard_map/ppermute | solution.py:60
  466.5 10.0 %collective-permute-done.74 = bf16[193,768]{1,0:T(8,128)(2,1)S(1)} collective-permute-done((bf16[193,768]{1,0:T(8,128)(2,1)S(1)}, bf16[193,768]{1,0:T(8,128)(2,1)S(1)}, u32[]{:S(2)}, u32[]{:S(2)}) %collective-permute-start.74) | collective-permute-done | bytes 296480 | tf_op jit(solution)/shard_map/ppermute | solution.py:60
  (543 shorter events, 148.9 us)
Async XLA Ops:
  7.2 204.8 %all-gather.3.cloned.1.call-start = ((), (), s32[]{:S(2)}) async-start(), calls=%async_computation.2 | async-start | bytes 14598144 | tf_op jit(solution)/shard_map/all_gather | solution.py:657
  13.1 464.9 %reduce-scatter.2.cloned.1.call-start = ((), (), s32[]{:S(2)}) async-start(), calls=%async_computation.1 | async-start | bytes 14598144 | tf_op jit(solution)/shard_map/reduce_scatter | solution.py:773
  14.9 10.9 %collective-permute-start.3 = (bf16[193,768]{1,0:T(8,128)(2,1)S(1)}, bf16[193,768]{1,0:T(8,128)(2,1)S(1)}, u32[]{:S(2)}, u32[]{:S(2)}) collective-permute-start(bf16[193,768]{1,0:T(8,128)(2,1)S(1)} %fusion.70), channel_id=1, source_target_pairs={{0,8},{2,10},{4,12},{6,14},{8,16},{10,18},{12,20},{14,22},{16,24},... | collective-permute-start | bytes 889352 | tf_op jit(solution)/shard_map/ppermute | solution.py:60
  18.1 41.4 %collective-permute-start.16 = (bf16[48,2304]{1,0:T(8,128)(2,1)}, bf16[48,2304]{1,0:T(8,128)(2,1)}, u32[]{:S(2)}, u32[]{:S(2)}) collective-permute-start(bf16[48,2304]{1,0:T(8,128)(2,1)} %dynamic-slice_bitcast_fusion.4), channel_id=1, source_target_pairs={{0,2},{2,0},{4,6},{6,4},{8,10},{10,8},{12,14},{14,12},{16,18},{18,... | collective-permute-start | bytes 663560 | tf_op jit(solution)/shard_map/ppermute | solution.py:45
  19.6 44.0 %collective-permute-start.34 = (bf16[192,768]{1,0:T(8,128)(2,1)}, bf16[192,768]{1,0:T(8,128)(2,1)}, u32[]{:S(2)}, u32[]{:S(2)}) collective-permute-start(bf16[192,768]{1,0:T(8,128)(2,1)} %bitcast.49), channel_id=1, source_target_pairs={{0,4},{2,6},{4,0},{6,2},{8,12},{10,14},{12,8},{14,10},{16,20},{18,... | collective-permute-start | bytes 884744 | tf_op jit(solution)/shard_map/ppermute | solution.py:45
  25.8 17.9 %collective-permute-start.4 = (bf16[193,768]{1,0:T(8,128)(2,1)S(1)}, bf16[193,768]{1,0:T(8,128)(2,1)}, u32[]{:S(2)}, u32[]{:S(2)}) collective-permute-start(bf16[193,768]{1,0:T(8,128)(2,1)S(1)} %collective-permute-done.3), channel_id=1, source_target_pairs={{0,8},{2,10},{4,12},{6,14},{8,16},{10,18},{12,20},{14,22},{16,24},... | collective-permute-start | bytes 889352 | tf_op jit(solution)/shard_map/ppermute | solution.py:60
  43.7 11.1 %collective-permute-start.5 = (bf16[193,768]{1,0:T(8,128)(2,1)}, bf16[193,768]{1,0:T(8,128)(2,1)}, u32[]{:S(2)}, u32[]{:S(2)}) collective-permute-start(bf16[193,768]{1,0:T(8,128)(2,1)} %collective-permute-done.4), channel_id=1, source_target_pairs={{0,8},{2,10},{4,12},{6,14},{8,16},{10,18},{12,20},{14,22},{16,24},... | collective-permute-start | bytes 889352 | tf_op jit(solution)/shard_map/ppermute | solution.py:60
  50.0 41.0 %collective-permute-start = (bf16[64,8,192]{0,2,1:T(8,128)(2,1)}, bf16[64,8,192]{0,2,1:T(8,128)(2,1)}, u32[]{:S(2)}, u32[]{:S(2)}) collective-permute-start(bf16[64,8,192]{0,2,1:T(8,128)(2,1)} %bitcast.5), channel_id=1, source_target_pairs={{0,1},{1,0},{2,3},{3,2},{4,5},{5,4},{6,7},{7,6},{8,9},{9,8},{10,11... | collective-permute-start | bytes 589832 | tf_op jit(solution)/shard_map/ppermute | solution.py:53
  51.1 41.5 %collective-permute-start.1 = (bf16[64,8,192]{0,2,1:T(8,128)(2,1)}, bf16[64,8,192]{0,2,1:T(8,128)(2,1)}, u32[]{:S(2)}, u32[]{:S(2)}) collective-permute-start(bf16[64,8,192]{0,2,1:T(8,128)(2,1)} %bitcast.6), channel_id=1, source_target_pairs={{0,2},{1,3},{2,0},{3,1},{4,6},{5,7},{6,4},{7,5},{8,10},{9,11},{10,... | collective-permute-start | bytes 589832 | tf_op jit(solution)/shard_map/ppermute | solution.py:53
  57.9 26.5 %collective-permute-start.6 = (bf16[4,193,768]{2,0,1:T(4,128)(2,1)}, bf16[4,193,768]{2,0,1:T(4,128)(2,1)}, u32[]{:S(2)}, u32[]{:S(2)}) collective-permute-start(bf16[4,193,768]{2,0,1:T(4,128)(2,1)} %copy.184), channel_id=1, source_target_pairs={{0,4},{2,6},{4,0},{6,2},{8,12},{10,14},{12,8},{14,10},{16,20},{18,... | collective-permute-start | bytes 3557384 | tf_op jit(solution)/shard_map/ppermute | solution.py:45
  60.6 14.8 %collective-permute-start.17 = (bf16[96,2304]{1,0:T(8,128)(2,1)S(1)}, bf16[96,2304]{1,0:T(8,128)(2,1)}, u32[]{:S(2)}, u32[]{:S(2)}) collective-permute-start(bf16[96,2304]{1,0:T(8,128)(2,1)S(1)} %bitcast.439), channel_id=1, source_target_pairs={{0,8},{2,10},{4,12},{6,14},{8,16},{10,18},{12,20},{14,22},{16,24},... | collective-permute-start | bytes 1327112 | tf_op jit(solution)/shard_map/ppermute | solution.py:60
  63.6 29.5 %collective-permute-start.2 = (bf16[64,8,192]{0,2,1:T(8,128)(2,1)}, bf16[64,8,192]{0,2,1:T(8,128)(2,1)S(1)}, u32[]{:S(2)}, u32[]{:S(2)}) collective-permute-start(bf16[64,8,192]{0,2,1:T(8,128)(2,1)} %bitcast.7), channel_id=1, source_target_pairs={{0,3},{1,2},{2,1},{3,0},{4,7},{5,6},{6,5},{7,4},{8,11},{9,10},{10,... | collective-permute-start | bytes 589832 | tf_op jit(solution)/shard_map/ppermute | solution.py:53
  75.4 15.6 %collective-permute-start.18 = (bf16[96,2304]{1,0:T(8,128)(2,1)}, bf16[96,2304]{1,0:T(8,128)(2,1)}, u32[]{:S(2)}, u32[]{:S(2)}) collective-permute-start(bf16[96,2304]{1,0:T(8,128)(2,1)} %collective-permute-done.17), channel_id=1, source_target_pairs={{0,8},{2,10},{4,12},{6,14},{8,16},{10,18},{12,20},{14,22},{16,24},... | collective-permute-start | bytes 1327112 | tf_op jit(solution)/shard_map/ppermute | solution.py:60
  86.4 10.6 %collective-permute-start.11 = (bf16[1,8,192]{2,1,0:T(8,128)(2,1)S(1)}, bf16[1,8,192]{2,1,0:T(8,128)(2,1)S(1)}, u32[]{:S(2)}, u32[]{:S(2)}) collective-permute-start(bf16[1,8,192]{2,1,0:T(8,128)(2,1)S(1)} %bitcast.460), channel_id=1, source_target_pairs={{0,2},{1,3},{2,0},{3,1},{4,6},{5,7},{6,4},{7,5},{8,10},{9,11},{10,... | collective-permute-start | bytes 9224 | tf_op jit(solution)/shard_map/ppermute | solution.py:53
  91.0 8.1 %collective-permute-start.10 = (bf16[1,8,192]{2,1,0:T(8,128)(2,1)S(1)}, bf16[1,8,192]{2,1,0:T(8,128)(2,1)S(1)}, u32[]{:S(2)}, u32[]{:S(2)}) collective-permute-start(bf16[1,8,192]{2,1,0:T(8,128)(2,1)S(1)} %bitcast.462), channel_id=1, source_target_pairs={{0,1},{1,0},{2,3},{3,2},{4,5},{5,4},{6,7},{7,6},{8,9},{9,8},{10,11... | collective-permute-start | bytes 9224 | tf_op jit(solution)/shard_map/ppermute | solution.py:53
  92.7 24.8 %collective-permute-start.19 = (bf16[96,2304]{1,0:T(8,128)(2,1)}, bf16[96,2304]{1,0:T(8,128)(2,1)}, u32[]{:S(2)}, u32[]{:S(2)}) collective-permute-start(bf16[96,2304]{1,0:T(8,128)(2,1)} %collective-permute-done.18), channel_id=1, source_target_pairs={{0,8},{2,10},{4,12},{6,14},{8,16},{10,18},{12,20},{14,22},{16,24},... | collective-permute-start | bytes 1327112 | tf_op jit(solution)/shard_map/ppermute | solution.py:60
  97.0 7.0 %collective-permute-start.9 = (bf16[64,768]{1,0:T(8,128)(2,1)S(1)}, bf16[64,768]{1,0:T(8,128)(2,1)S(1)}, u32[]{:S(2)}, u32[]{:S(2)}) collective-permute-start(bf16[64,768]{1,0:T(8,128)(2,1)S(1)} %get-tuple-element.195), channel_id=1, source_target_pairs={{0,3},{1,2},{2,1},{3,0},{4,7},{5,6},{6,5},{7,4},{8,11},{9,10},{10,... | collective-permute-start | bytes 294920 | tf_op jit(solution)/shard_map/ppermute | solution.py:53
  97.6 11.3 %collective-permute-start.8 = (bf16[64,768]{1,0:T(8,128)(2,1)S(1)}, bf16[64,768]{1,0:T(8,128)(2,1)}, u32[]{:S(2)}, u32[]{:S(2)}) collective-permute-start(bf16[64,768]{1,0:T(8,128)(2,1)S(1)} %get-tuple-element.196), channel_id=1, source_target_pairs={{0,2},{1,3},{2,0},{3,1},{4,6},{5,7},{6,4},{7,5},{8,10},{9,11},{10,... | collective-permute-start | bytes 294920 | tf_op jit(solution)/shard_map/ppermute | solution.py:53
  110.4 23.5 %collective-permute-start.15 = (bf16[64,768]{1,0:T(8,128)(2,1)S(1)}, bf16[64,768]{1,0:T(8,128)(2,1)S(1)}, u32[]{:S(2)}, u32[]{:S(2)}) collective-permute-start(bf16[64,768]{1,0:T(8,128)(2,1)S(1)} %add_convert_fusion.2), channel_id=1, source_target_pairs={{0,3},{1,2},{2,1},{3,0},{4,7},{5,6},{6,5},{7,4},{8,11},{9,10},{10,... | collective-permute-start | bytes 294920 | tf_op jit(solution)/shard_map/ppermute | solution.py:53
  110.5 23.4 %collective-permute-start.14 = (bf16[64,768]{1,0:T(8,128)(2,1)S(1)}, bf16[64,768]{1,0:T(8,128)(2,1)S(1)}, u32[]{:S(2)}, u32[]{:S(2)}) collective-permute-start(bf16[64,768]{1,0:T(8,128)(2,1)S(1)} %add_convert_fusion.2), channel_id=1, source_target_pairs={{0,2},{1,3},{2,0},{3,1},{4,6},{5,7},{6,4},{7,5},{8,10},{9,11},{10,... | collective-permute-start | bytes 294920 | tf_op jit(solution)/shard_map/ppermute | solution.py:53
  111.6 22.3 %collective-permute-start.13 = (bf16[64,768]{1,0:T(8,128)(2,1)S(1)}, bf16[64,768]{1,0:T(8,128)(2,1)S(1)}, u32[]{:S(2)}, u32[]{:S(2)}) collective-permute-start(bf16[64,768]{1,0:T(8,128)(2,1)S(1)} %add_convert_fusion.2), channel_id=1, source_target_pairs={{0,1},{1,0},{2,3},{3,2},{4,5},{5,4},{6,7},{7,6},{8,9},{9,8},{10,11... | collective-permute-start | bytes 294920 | tf_op jit(solution)/shard_map/ppermute | solution.py:53
  118.7 14.5 %collective-permute-start.20 = (bf16[4,96,768]{2,1,0:T(8,128)(2,1)S(1)}, bf16[4,96,768]{2,1,0:T(8,128)(2,1)S(1)}, u32[]{:S(2)}, u32[]{:S(2)}) collective-permute-start(bf16[4,96,768]{2,1,0:T(8,128)(2,1)S(1)} %pad_maximum_fusion.8), channel_id=1, source_target_pairs={{0,4},{2,6},{4,0},{6,2},{8,12},{10,14},{12,8},{14,10},{16,20},{18,... | collective-permute-start | bytes 1769480 | tf_op jit(solution)/shard_map/ppermute | solution.py:45
  121.7 32.7 %collective-permute-start.35 = (bf16[2,192,768]{2,1,0:T(8,128)(2,1)}, bf16[2,192,768]{2,1,0:T(8,128)(2,1)}, u32[]{:S(2)}, u32[]{:S(2)}) collective-permute-start(bf16[2,192,768]{2,1,0:T(8,128)(2,1)} %pad_maximum_fusion.9), channel_id=1, source_target_pairs={{0,8},{2,10},{4,12},{6,14},{8,16},{10,18},{12,20},{14,22},{16,24},... | collective-permute-start | bytes 1769480 | tf_op jit(solution)/shard_map/ppermute | solution.py:60
  133.2 38.0 %collective-permute-start.27 = (bf16[4,96,1536]{2,1,0:T(8,128)(2,1)}, bf16[4,96,1536]{2,1,0:T(8,128)(2,1)}, u32[]{:S(2)}, u32[]{:S(2)}) collective-permute-start(bf16[4,96,1536]{2,1,0:T(8,128)(2,1)} %pad_maximum_fusion.6), channel_id=1, source_target_pairs={{0,4},{2,6},{4,0},{6,2},{8,12},{10,14},{12,8},{14,10},{16,20},{18,... | collective-permute-start | bytes 3538952 | tf_op jit(solution)/shard_map/ppermute | solution.py:45
  145.4 9.0 %collective-permute-start.21 = (bf16[64,768]{1,0:T(8,128)(2,1)S(1)}, bf16[64,768]{1,0:T(8,128)(2,1)S(1)}, u32[]{:S(2)}, u32[]{:S(2)}) collective-permute-start(bf16[64,768]{1,0:T(8,128)(2,1)S(1)} %get-tuple-element.191), channel_id=1, source_target_pairs={{0,1},{1,0},{2,3},{3,2},{4,5},{5,4},{6,7},{7,6},{8,9},{9,8},{10,11... | collective-permute-start | bytes 294920 | tf_op jit(solution)/shard_map/ppermute | solution.py:53
  145.4 8.9 %collective-permute-start.23 = (bf16[64,768]{1,0:T(8,128)(2,1)S(1)}, bf16[64,768]{1,0:T(8,128)(2,1)S(1)}, u32[]{:S(2)}, u32[]{:S(2)}) collective-permute-start(bf16[64,768]{1,0:T(8,128)(2,1)S(1)} %get-tuple-element.192), channel_id=1, source_target_pairs={{0,3},{1,2},{2,1},{3,0},{4,7},{5,6},{6,5},{7,4},{8,11},{9,10},{10,... | collective-permute-start | bytes 294920 | tf_op jit(solution)/shard_map/ppermute | solution.py:53
  146.6 7.8 %collective-permute-start.22 = (bf16[64,768]{1,0:T(8,128)(2,1)S(1)}, bf16[64,768]{1,0:T(8,128)(2,1)S(1)}, u32[]{:S(2)}, u32[]{:S(2)}) collective-permute-start(bf16[64,768]{1,0:T(8,128)(2,1)S(1)} %get-tuple-element.193), channel_id=1, source_target_pairs={{0,2},{1,3},{2,0},{3,1},{4,6},{5,7},{6,4},{7,5},{8,10},{9,11},{10,... | collective-permute-start | bytes 294920 | tf_op jit(solution)/shard_map/ppermute | solution.py:53
  154.4 16.8 %collective-permute-start.36 = (bf16[2,192,768]{2,1,0:T(8,128)(2,1)}, bf16[2,192,768]{2,1,0:T(8,128)(2,1)}, u32[]{:S(2)}, u32[]{:S(2)}) collective-permute-start(bf16[2,192,768]{2,1,0:T(8,128)(2,1)} %collective-permute-done.35), channel_id=1, source_target_pairs={{0,8},{2,10},{4,12},{6,14},{8,16},{10,18},{12,20},{14,22},{16,24},... | collective-permute-start | bytes 1769480 | tf_op jit(solution)/shard_map/ppermute | solution.py:60
  154.9 18.5 %collective-permute-start.26 = (bf16[64,768]{1,0:T(8,128)(2,1)S(1)}, bf16[64,768]{1,0:T(8,128)(2,1)S(1)}, u32[]{:S(2)}, u32[]{:S(2)}) collective-permute-start(bf16[64,768]{1,0:T(8,128)(2,1)S(1)} %add_convert_fusion.1), channel_id=1, source_target_pairs={{0,3},{1,2},{2,1},{3,0},{4,7},{5,6},{6,5},{7,4},{8,11},{9,10},{10,... | collective-permute-start | bytes 294920 | tf_op jit(solution)/shard_map/ppermute | solution.py:53
  155.0 18.4 %collective-permute-start.25 = (bf16[64,768]{1,0:T(8,128)(2,1)S(1)}, bf16[64,768]{1,0:T(8,128)(2,1)S(1)}, u32[]{:S(2)}, u32[]{:S(2)}) collective-permute-start(bf16[64,768]{1,0:T(8,128)(2,1)S(1)} %add_convert_fusion.1), channel_id=1, source_target_pairs={{0,2},{1,3},{2,0},{3,1},{4,6},{5,7},{6,4},{7,5},{8,10},{9,11},{10,... | collective-permute-start | bytes 294920 | tf_op jit(solution)/shard_map/ppermute | solution.py:53
  156.1 17.4 %collective-permute-start.24 = (bf16[64,768]{1,0:T(8,128)(2,1)S(1)}, bf16[64,768]{1,0:T(8,128)(2,1)S(1)}, u32[]{:S(2)}, u32[]{:S(2)}) collective-permute-start(bf16[64,768]{1,0:T(8,128)(2,1)S(1)} %add_convert_fusion.1), channel_id=1, source_target_pairs={{0,1},{1,0},{2,3},{3,2},{4,5},{5,4},{6,7},{7,6},{8,9},{9,8},{10,11... | collective-permute-start | bytes 294920 | tf_op jit(solution)/shard_map/ppermute | solution.py:53
  171.2 16.5 %collective-permute-start.37 = (bf16[2,192,768]{2,1,0:T(8,128)(2,1)}, bf16[2,192,768]{2,1,0:T(8,128)(2,1)}, u32[]{:S(2)}, u32[]{:S(2)}) collective-permute-start(bf16[2,192,768]{2,1,0:T(8,128)(2,1)} %collective-permute-done.36), channel_id=1, source_target_pairs={{0,8},{2,10},{4,12},{6,14},{8,16},{10,18},{12,20},{14,22},{16,24},... | collective-permute-start | bytes 1769480 | tf_op jit(solution)/shard_map/ppermute | solution.py:60
  177.8 6.8 %collective-permute-start.29 = (bf16[64,768]{1,0:T(8,128)(2,1)}, bf16[64,768]{1,0:T(8,128)(2,1)}, u32[]{:S(2)}, u32[]{:S(2)}) collective-permute-start(bf16[64,768]{1,0:T(8,128)(2,1)} %get-tuple-element.190), channel_id=1, source_target_pairs={{0,2},{1,3},{2,0},{3,1},{4,6},{5,7},{6,4},{7,5},{8,10},{9,11},{10,... | collective-permute-start | bytes 294920 | tf_op jit(solution)/shard_map/ppermute | solution.py:53
  185.8 6.6 %collective-permute-start.32 = (bf16[64,768]{1,0:T(8,128)(2,1)S(1)}, bf16[64,768]{1,0:T(8,128)(2,1)S(1)}, u32[]{:S(2)}, u32[]{:S(2)}) collective-permute-start(bf16[64,768]{1,0:T(8,128)(2,1)S(1)} %fusion.85), channel_id=1, source_target_pairs={{0,2},{1,3},{2,0},{3,1},{4,6},{5,7},{6,4},{7,5},{8,10},{9,11},{10,... | collective-permute-start | bytes 294920 | tf_op jit(solution)/shard_map/ppermute | solution.py:53
  197.7 11.0 %collective-permute-start.38 = (bf16[64,8,192]{2,1,0:T(8,128)(2,1)}, bf16[64,8,192]{2,1,0:T(8,128)(2,1)S(1)}, u32[]{:S(2)}, u32[]{:S(2)}) collective-permute-start(bf16[64,8,192]{2,1,0:T(8,128)(2,1)} %slice.368), channel_id=1, source_target_pairs={{0,1},{1,0},{2,3},{3,2},{4,5},{5,4},{6,7},{7,6},{8,9},{9,8},{10,11... | collective-permute-start | bytes 589832 | tf_op jit(solution)/shard_map/ppermute | solution.py:53
  197.9 10.9 %collective-permute-start.39 = (bf16[64,8,192]{2,1,0:T(8,128)(2,1)}, bf16[64,8,192]{2,1,0:T(8,128)(2,1)}, u32[]{:S(2)}, u32[]{:S(2)}) collective-permute-start(bf16[64,8,192]{2,1,0:T(8,128)(2,1)} %slice.370), channel_id=1, source_target_pairs={{0,2},{1,3},{2,0},{3,1},{4,6},{5,7},{6,4},{7,5},{8,10},{9,11},{10,... | collective-permute-start | bytes 589832 | tf_op jit(solution)/shard_map/ppermute | solution.py:53
  199.0 12.9 %collective-permute-start.40 = (bf16[64,8,192]{2,1,0:T(8,128)(2,1)}, bf16[64,8,192]{2,1,0:T(8,128)(2,1)}, u32[]{:S(2)}, u32[]{:S(2)}) collective-permute-start(bf16[64,8,192]{2,1,0:T(8,128)(2,1)} %slice.372), channel_id=1, source_target_pairs={{0,3},{1,2},{2,1},{3,0},{4,7},{5,6},{6,5},{7,4},{8,11},{9,10},{10,... | collective-permute-start | bytes 589832 | tf_op jit(solution)/shard_map/ppermute | solution.py:53
  262.8 9.5 %collective-permute-start.42 = (bf16[512,192]{1,0:T(8,128)(2,1)}, bf16[512,192]{1,0:T(8,128)(2,1)}, u32[]{:S(2)}, u32[]{:S(2)}) collective-permute-start(bf16[512,192]{1,0:T(8,128)(2,1)} %get-tuple-element.48), channel_id=1, source_target_pairs={{0,2},{1,3},{2,0},{3,1},{4,6},{5,7},{6,4},{7,5},{8,10},{9,11},{10,... | collective-permute-start | bytes 589832 | tf_op jit(solution)/shard_map/ppermute | solution.py:53
  264.0 12.4 %collective-permute-start.43 = (bf16[512,192]{1,0:T(8,128)(2,1)}, bf16[512,192]{1,0:T(8,128)(2,1)S(1)}, u32[]{:S(2)}, u32[]{:S(2)}) collective-permute-start(bf16[512,192]{1,0:T(8,128)(2,1)} %get-tuple-element.49), channel_id=1, source_target_pairs={{0,3},{1,2},{2,1},{3,0},{4,7},{5,6},{6,5},{7,4},{8,11},{9,10},{10,... | collective-permute-start | bytes 589832 | tf_op jit(solution)/shard_map/ppermute | solution.py:53
  290.1 20.7 %collective-permute-start.53 = (bf16[2,192,768]{2,1,0:T(8,128)(2,1)}, bf16[2,192,768]{2,1,0:T(8,128)(2,1)}, u32[]{:S(2)}, u32[]{:S(2)}) collective-permute-start(bf16[2,192,768]{2,1,0:T(8,128)(2,1)} %dynamic-slice_bitcast_fusion.3), channel_id=1, source_target_pairs={{0,8},{2,10},{4,12},{6,14},{8,16},{10,18},{12,20},{14,22},{16,24},... | collective-permute-start | bytes 1769480 | tf_op jit(solution)/shard_map/ppermute | solution.py:60
  297.5 9.8 %collective-permute-start.50 = (bf16[64,768]{1,0:T(8,128)(2,1)}, bf16[64,768]{1,0:T(8,128)(2,1)}, u32[]{:S(2)}, u32[]{:S(2)}) collective-permute-start(bf16[64,768]{1,0:T(8,128)(2,1)} %get-tuple-element.182), channel_id=1, source_target_pairs={{0,1},{1,0},{2,3},{3,2},{4,5},{5,4},{6,7},{7,6},{8,9},{9,8},{10,11... | collective-permute-start | bytes 294920 | tf_op jit(solution)/shard_map/ppermute | solution.py:53
  297.6 9.8 %collective-permute-start.52 = (bf16[64,768]{1,0:T(8,128)(2,1)}, bf16[64,768]{1,0:T(8,128)(2,1)}, u32[]{:S(2)}, u32[]{:S(2)}) collective-permute-start(bf16[64,768]{1,0:T(8,128)(2,1)} %get-tuple-element.183), channel_id=1, source_target_pairs={{0,3},{1,2},{2,1},{3,0},{4,7},{5,6},{6,5},{7,4},{8,11},{9,10},{10,... | collective-permute-start | bytes 294920 | tf_op jit(solution)/shard_map/ppermute | solution.py:53
  298.8 8.5 %collective-permute-start.51 = (bf16[64,768]{1,0:T(8,128)(2,1)S(1)}, bf16[64,768]{1,0:T(8,128)(2,1)}, u32[]{:S(2)}, u32[]{:S(2)}) collective-permute-start(bf16[64,768]{1,0:T(8,128)(2,1)S(1)} %get-tuple-element.184), channel_id=1, source_target_pairs={{0,2},{1,3},{2,0},{3,1},{4,6},{5,7},{6,4},{7,5},{8,10},{9,11},{10,... | collective-permute-start | bytes 294920 | tf_op jit(solution)/shard_map/ppermute | solution.py:53
  306.8 57.4 %collective-permute-start.64 = (bf16[4,96,1536]{2,1,0:T(8,128)(2,1)}, bf16[4,96,1536]{2,1,0:T(8,128)(2,1)}, u32[]{:S(2)}, u32[]{:S(2)}) collective-permute-start(bf16[4,96,1536]{2,1,0:T(8,128)(2,1)} %dynamic-slice_bitcast_fusion.1), channel_id=1, source_target_pairs={{0,4},{2,6},{4,0},{6,2},{8,12},{10,14},{12,8},{14,10},{16,20},{18,... | collective-permute-start | bytes 3538952 | tf_op jit(solution)/shard_map/ppermute | solution.py:45
  310.8 6.7 %collective-permute-start.56 = (bf16[64,768]{1,0:T(8,128)(2,1)S(1)}, bf16[64,768]{1,0:T(8,128)(2,1)S(1)}, u32[]{:S(2)}, u32[]{:S(2)}) collective-permute-start(bf16[64,768]{1,0:T(8,128)(2,1)S(1)} %fusion.101), channel_id=1, source_target_pairs={{0,3},{1,2},{2,1},{3,0},{4,7},{5,6},{6,5},{7,4},{8,11},{9,10},{10,... | collective-permute-start | bytes 294920 | tf_op jit(solution)/shard_map/ppermute | solution.py:53
  314.9 28.0 %collective-permute-start.60 = (bf16[2,192,768]{2,1,0:T(8,128)(2,1)}, bf16[2,192,768]{2,1,0:T(8,128)(2,1)}, u32[]{:S(2)}, u32[]{:S(2)}) collective-permute-start(bf16[2,192,768]{2,1,0:T(8,128)(2,1)} %fusion.5), channel_id=1, source_target_pairs={{0,8},{2,10},{4,12},{6,14},{8,16},{10,18},{12,20},{14,22},{16,24},... | collective-permute-start | bytes 1769480 | tf_op jit(solution)/shard_map/ppermute | solution.py:60
  323.7 7.1 %collective-permute-start.59 = (bf16[64,768]{1,0:T(8,128)(2,1)S(1)}, bf16[64,768]{1,0:T(8,128)(2,1)S(1)}, u32[]{:S(2)}, u32[]{:S(2)}) collective-permute-start(bf16[64,768]{1,0:T(8,128)(2,1)S(1)} %get-tuple-element.180), channel_id=1, source_target_pairs={{0,3},{1,2},{2,1},{3,0},{4,7},{5,6},{6,5},{7,4},{8,11},{9,10},{10,... | collective-permute-start | bytes 294920 | tf_op jit(solution)/shard_map/ppermute | solution.py:53
  324.4 10.8 %collective-permute-start.58 = (bf16[64,768]{1,0:T(8,128)(2,1)S(1)}, bf16[64,768]{1,0:T(8,128)(2,1)S(1)}, u32[]{:S(2)}, u32[]{:S(2)}) collective-permute-start(bf16[64,768]{1,0:T(8,128)(2,1)S(1)} %get-tuple-element.181), channel_id=1, source_target_pairs={{0,2},{1,3},{2,0},{3,1},{4,6},{5,7},{6,4},{7,5},{8,10},{9,11},{10,... | collective-permute-start | bytes 294920 | tf_op jit(solution)/shard_map/ppermute | solution.py:53
  339.0 21.0 %collective-permute-start.77 = (bf16[4,96,768]{2,1,0:T(8,128)(2,1)}, bf16[4,96,768]{2,1,0:T(8,128)(2,1)S(1)}, u32[]{:S(2)}, u32[]{:S(2)}) collective-permute-start(bf16[4,96,768]{2,1,0:T(8,128)(2,1)} %dynamic-slice_bitcast_fusion.2), channel_id=1, source_target_pairs={{0,4},{2,6},{4,0},{6,2},{8,12},{10,14},{12,8},{14,10},{16,20},{18,... | collective-permute-start | bytes 1769480 | tf_op jit(solution)/shard_map/ppermute | solution.py:45
  342.9 16.8 %collective-permute-start.63 = (bf16[64,768]{1,0:T(8,128)(2,1)S(1)}, bf16[64,768]{1,0:T(8,128)(2,1)S(1)}, u32[]{:S(2)}, u32[]{:S(2)}) collective-permute-start(bf16[64,768]{1,0:T(8,128)(2,1)S(1)} %add_convert_fusion), channel_id=1, source_target_pairs={{0,3},{1,2},{2,1},{3,0},{4,7},{5,6},{6,5},{7,4},{8,11},{9,10},{10,... | collective-permute-start | bytes 294920 | tf_op jit(solution)/shard_map/ppermute | solution.py:53
  342.9 16.7 %collective-permute-start.62 = (bf16[64,768]{1,0:T(8,128)(2,1)S(1)}, bf16[64,768]{1,0:T(8,128)(2,1)S(1)}, u32[]{:S(2)}, u32[]{:S(2)}) collective-permute-start(bf16[64,768]{1,0:T(8,128)(2,1)S(1)} %add_convert_fusion), channel_id=1, source_target_pairs={{0,2},{1,3},{2,0},{3,1},{4,6},{5,7},{6,4},{7,5},{8,10},{9,11},{10,... | collective-permute-start | bytes 294920 | tf_op jit(solution)/shard_map/ppermute | solution.py:53
  347.0 56.5 %collective-permute-start.75 = (bf16[2,192,768]{2,1,0:T(8,128)(2,1)}, bf16[2,192,768]{2,1,0:T(8,128)(2,1)}, u32[]{:S(2)}, u32[]{:S(2)}) collective-permute-start(bf16[2,192,768]{2,1,0:T(8,128)(2,1)} %fusion.4), channel_id=1, source_target_pairs={{0,8},{2,10},{4,12},{6,14},{8,16},{10,18},{12,20},{14,22},{16,24},... | collective-permute-start | bytes 1769480 | tf_op jit(solution)/shard_map/ppermute | solution.py:60
  373.3 10.8 %collective-permute-start.65 = (bf16[64,8,192]{2,1,0:T(8,128)(2,1)}, bf16[64,8,192]{2,1,0:T(8,128)(2,1)}, u32[]{:S(2)}, u32[]{:S(2)}) collective-permute-start(bf16[64,8,192]{2,1,0:T(8,128)(2,1)} %slice.394), channel_id=1, source_target_pairs={{0,1},{1,0},{2,3},{3,2},{4,5},{5,4},{6,7},{7,6},{8,9},{9,8},{10,11... | collective-permute-start | bytes 589832 | tf_op jit(solution)/shard_map/ppermute | solution.py:53
  373.3 13.5 %collective-permute-start.67 = (bf16[64,8,192]{2,1,0:T(8,128)(2,1)}, bf16[64,8,192]{2,1,0:T(8,128)(2,1)}, u32[]{:S(2)}, u32[]{:S(2)}) collective-permute-start(bf16[64,8,192]{2,1,0:T(8,128)(2,1)} %slice.398), channel_id=1, source_target_pairs={{0,3},{1,2},{2,1},{3,0},{4,7},{5,6},{6,5},{7,4},{8,11},{9,10},{10,... | collective-permute-start | bytes 589832 | tf_op jit(solution)/shard_map/ppermute | solution.py:53
  374.6 19.0 %collective-permute-start.66 = (bf16[64,8,192]{2,1,0:T(8,128)(2,1)}, bf16[64,8,192]{2,1,0:T(8,128)(2,1)}, u32[]{:S(2)}, u32[]{:S(2)}) collective-permute-start(bf16[64,8,192]{2,1,0:T(8,128)(2,1)} %slice.396), channel_id=1, source_target_pairs={{0,2},{1,3},{2,0},{3,1},{4,6},{5,7},{6,4},{7,5},{8,10},{9,11},{10,... | collective-permute-start | bytes 589832 | tf_op jit(solution)/shard_map/ppermute | solution.py:53
  376.3 18.7 %collective-permute-start.78 = (bf16[96,2304]{1,0:T(8,128)(2,1)}, bf16[96,2304]{1,0:T(8,128)(2,1)}, u32[]{:S(2)}, u32[]{:S(2)}) collective-permute-start(bf16[96,2304]{1,0:T(8,128)(2,1)} %fusion.66), channel_id=1, source_target_pairs={{0,8},{2,10},{4,12},{6,14},{8,16},{10,18},{12,20},{14,22},{16,24},... | collective-permute-start | bytes 1327112 | tf_op jit(solution)/shard_map/ppermute | solution.py:60
  384.1 47.4 %collective-permute-start.71 = (bf16[4,193,768]{2,0,1:T(4,128)(2,1)}, bf16[4,193,768]{2,0,1:T(4,128)(2,1)}, u32[]{:S(2)}, u32[]{:S(2)}) collective-permute-start(bf16[4,193,768]{2,0,1:T(4,128)(2,1)} %copy.218), channel_id=1, source_target_pairs={{0,4},{2,6},{4,0},{6,2},{8,12},{10,14},{12,8},{14,10},{16,20},{18,... | collective-permute-start | bytes 3557384 | tf_op jit(solution)/shard_map/ppermute | solution.py:45
  396.8 22.9 %collective-permute-start.79 = (bf16[96,2304]{1,0:T(8,128)(2,1)}, bf16[96,2304]{1,0:T(8,128)(2,1)}, u32[]{:S(2)}, u32[]{:S(2)}) collective-permute-start(bf16[96,2304]{1,0:T(8,128)(2,1)} %fusion.32), channel_id=1, source_target_pairs={{0,8},{2,10},{4,12},{6,14},{8,16},{10,18},{12,20},{14,22},{16,24},... | collective-permute-start | bytes 1327112 | tf_op jit(solution)/shard_map/ppermute | solution.py:60
  404.9 25.8 %collective-permute-start.76 = (bf16[192,768]{1,0:T(8,128)(2,1)S(1)}, bf16[192,768]{1,0:T(8,128)(2,1)S(1)}, u32[]{:S(2)}, u32[]{:S(2)}) collective-permute-start(bf16[192,768]{1,0:T(8,128)(2,1)S(1)} %fusion.72), channel_id=1, source_target_pairs={{0,4},{2,6},{4,0},{6,2},{8,12},{10,14},{12,8},{14,10},{16,20},{18,... | collective-permute-start | bytes 884744 | tf_op jit(solution)/shard_map/ppermute | solution.py:45
  420.9 18.6 %collective-permute-start.80 = (bf16[96,2304]{1,0:T(8,128)(2,1)S(1)}, bf16[96,2304]{1,0:T(8,128)(2,1)S(1)}, u32[]{:S(2)}, u32[]{:S(2)}) collective-permute-start(bf16[96,2304]{1,0:T(8,128)(2,1)S(1)} %fusion.28), channel_id=1, source_target_pairs={{0,8},{2,10},{4,12},{6,14},{8,16},{10,18},{12,20},{14,22},{16,24},... | collective-permute-start | bytes 1327112 | tf_op jit(solution)/shard_map/ppermute | solution.py:60
  433.1 15.2 %collective-permute-start.72 = (bf16[193,768]{1,0:T(8,128)(2,1)S(1)}, bf16[193,768]{1,0:T(8,128)(2,1)S(1)}, u32[]{:S(2)}, u32[]{:S(2)}) collective-permute-start(bf16[193,768]{1,0:T(8,128)(2,1)S(1)} %fusion.71), channel_id=1, source_target_pairs={{0,8},{2,10},{4,12},{6,14},{8,16},{10,18},{12,20},{14,22},{16,24},... | collective-permute-start | bytes 889352 | tf_op jit(solution)/shard_map/ppermute | solution.py:60
  439.7 9.9 %collective-permute-start.81 = (bf16[48,2304]{1,0:T(8,128)(2,1)S(1)}, bf16[48,2304]{1,0:T(8,128)(2,1)S(1)}, u32[]{:S(2)}, u32[]{:S(2)}) collective-permute-start(bf16[48,2304]{1,0:T(8,128)(2,1)S(1)} %fusion.73), channel_id=1, source_target_pairs={{0,2},{2,0},{4,6},{6,4},{8,10},{10,8},{12,14},{14,12},{16,18},{18,... | collective-permute-start | bytes 663560 | tf_op jit(solution)/shard_map/ppermute | solution.py:45
  448.3 17.9 %collective-permute-start.73 = (bf16[193,768]{1,0:T(8,128)(2,1)S(1)}, bf16[193,768]{1,0:T(8,128)(2,1)S(1)}, u32[]{:S(2)}, u32[]{:S(2)}) collective-permute-start(bf16[193,768]{1,0:T(8,128)(2,1)S(1)} %fusion.60), channel_id=1, source_target_pairs={{0,8},{2,10},{4,12},{6,14},{8,16},{10,18},{12,20},{14,22},{16,24},... | collective-permute-start | bytes 889352 | tf_op jit(solution)/shard_map/ppermute | solution.py:60
  466.3 10.2 %collective-permute-start.74 = (bf16[193,768]{1,0:T(8,128)(2,1)S(1)}, bf16[193,768]{1,0:T(8,128)(2,1)S(1)}, u32[]{:S(2)}, u32[]{:S(2)}) collective-permute-start(bf16[193,768]{1,0:T(8,128)(2,1)S(1)} %fusion.61), channel_id=1, source_target_pairs={{0,8},{2,10},{4,12},{6,14},{8,16},{10,18},{12,20},{14,22},{16,24},... | collective-permute-start | bytes 889352 | tf_op jit(solution)/shard_map/ppermute | solution.py:60
  (117 other events, 771.9 us)
Sparse Core Ops, SparseCore 0:
  13.2 140.1 all-gather.2
  261.5 207.1 reduce-scatter.1

commit v7 on v6

--- a/solution.py
+++ b/solution.py
@@ -364,13 +364,13 @@
 def local_rows(
     wide,
     scalars_ref, masked_ref, part_0_ref, part_1_ref, part_2_ref, part_3_ref, cotangent_ref,
-    gain_ref, bias_ref, first_ref, last_ref,
+    gain_ref, bias_ref, weights_ref,
     result_ref, grad_ref, give_0_ref, give_1_ref, give_2_ref, give_3_ref, norms_ref, weights_out_ref,
     factors_ref, normed_all_ref, branch_all_ref, second_all_ref, grad_out_all_ref,
-    turned_ref, branch_turned_ref, probs_ref, stream_ref,
+    turned_ref, branch_turned_ref, probs_ref, stream_ref, held_ref, sems,
 ):
     rows = masked_ref.shape[0]
-    hidden_width = first_ref.shape[3] // 2 - 2 * wide
+    hidden_width = weights_ref.shape[3] // 2 - 2 * wide
     here = pl.ds(pl.multiple_of(pl.program_id(0) * rows, rows), rows)
     normed_ref, branch_ref = normed_all_ref.at[here], branch_all_ref.at[here]
     second_ref, grad_out_ref = second_all_ref.at[here], grad_out_all_ref.at[here]
@@ -383,8 +383,28 @@
     hiddens = factor(4 * wide, hidden_width)
     actives = factor(4 * wide + hidden_width, hidden_width)
 
+    bounds = (0, 4 * wide, 4 * wide + hidden_width, 4 * wide + 2 * hidden_width)
+    opening = pl.program_id(0) == 0
+
+    def copy(side, part):
+        columns = slice(bounds[part], bounds[part + 1])
+        return pltpu.make_async_copy(
+            weights_ref.at[:, side, :, columns], held_ref.at[side, :, :, columns], sems.at[side, part]
+        )
+
+    @pl.when(opening)
+    def _():
+        for side, part in ((0, 0), (1, 0), (0, 1), (0, 2), (1, 1), (1, 2)):
+            copy(side, part).start()
+
+    def arrive(*places):
+        @pl.when(opening)
+        def _():
+            for side, part in places:
+                copy(side, part).wait()
+
     def weight(side, start, stop):
-        return (first_ref, last_ref)[side][:, 0, :, start:stop].reshape(D, stop - start)
+        return held_ref[side, :, :, start:stop].reshape(D, stop - start)
 
     bands = rows // BAND
     pairs = wide // PAIR
@@ -406,6 +426,7 @@
     normed, unit_one, scale_one = norm_forward(stream, gain_one, bias_ref[2:3, :])
     normed = normed.astype(BF16)
     normed_ref[...] = normed
+    arrive((0, 0), (1, 0))
     packs = [dot_nn(normed, weight(side, 0, 3 * wide)).astype(BF16) for side in range(2)]
 
     lanes = lax.broadcasted_iota(jnp.int32, (BAND, PAIR), 1)
@@ -456,6 +477,7 @@
     grad_second = jnp.zeros_like(middle)
     chunk = min(768, hidden_width)
     for side in range(2):
+        arrive((side, 1), (side, 2))
         for start in range(0, hidden_width, chunk):
             first = 4 * wide + start
             upward = weight(side, first, first + chunk)
@@ -523,10 +545,10 @@
 def local_grads(
     tiles, wide,
     scalars_ref, masked_ref, part_0_ref, part_1_ref, part_2_ref, part_3_ref, cotangent_ref,
-    gain_ref, bias_ref, first_ref, last_ref,
+    gain_ref, bias_ref, weights_ref,
     result_ref, grad_ref, give_0_ref, give_1_ref, give_2_ref, give_3_ref, norms_ref, weights_out_ref,
     factors_ref, normed_ref, branch_ref, second_ref, grad_out_ref,
-    turned_ref, branch_turned_ref, probs_ref, stream_ref,
+    turned_ref, branch_turned_ref, probs_ref, stream_ref, held_ref, sems,
 ):
     step = pl.program_id(0) - tiles
     block, side = step // 2, step % 2
@@ -582,14 +604,7 @@
         in_specs=[pl.BlockSpec(memory_space=pltpu.SMEM)]
         + [tiled(D)] + [tiled(D // QUAD)] * QUAD + [tiled(D)]
         + [fixed(array) for array in (gain_rows, bias_rows)]
-        + [
-            pl.BlockSpec(
-                (weights.shape[0], 1) + weights.shape[2:],
-                lambda i, side=side: (0, side, 0, 0),
-                pipeline_mode=pl.Buffered(1),
-            )
-            for side in range(2)
-        ],
+        + [pl.BlockSpec(memory_space=pl.ANY)],
         out_specs=[tiled(size) for size, _ in outs]
         + [
             pl.BlockSpec((8, D), lambda i: (0, 0)),
@@ -603,6 +618,8 @@
         + [
             pltpu.VMEM((2 * (TILE // BAND) * (wide // PAIR), 2 * BAND, BAND), F32),
             pltpu.VMEM((TILE, D), F32),
+            pltpu.VMEM((2, weights.shape[0]) + weights.shape[2:], BF16),
+            pltpu.SemaphoreType.DMA((2, 3)),
         ],
         compiler_params=pltpu.CompilerParams(
             dimension_semantics=("arbitrary",), vmem_limit_bytes=58 * 1024 * 1024
@@ -612,7 +629,7 @@
             transcendentals=rows * columns,
             bytes_accessed=2 * 4 * D * columns,
         ),
-    )(scalars, masked_low, *spread_parts, cotangent, gain_rows, bias_rows, weights, weights)
+    )(scalars, masked_low, *spread_parts, cotangent, gain_rows, bias_rows, weights)
 
 
 def shards(

time: 499 us -> 497 us (level)
  no operation moved by 1% of the time
where the time goes in v7:
time: 497 us; the launch traced here: 488 us
  waiting for transfers between devices  199 us (40%)
  local copies, waits for them, and re-layouts  84.6 us (17%)
  starting transfers between devices  70.5 us (14%)
  Pallas kernels  48.1 us (10%)
  other arithmetic  46.1 us (9%)
  matrix products  22.7 us (5%)
  between operations  17.2 us (3%)
    ppermute x18, waiting for transfers between devices, step_line(): lax.ppermute(values_in, 'dp', [(i, (i + 4 * offset) % count) for i in ran...  117 us
    ppermute x54, waiting for transfers between devices, flip_quad(): lax.ppermute(values_in, ('dp', 'tensor'), [(i, i ^ bits) for i in range(2...  55 us
    pallas_call x1, Pallas kernels, local_layer(): pl.pallas_call(lambda *refs: local_body(tiles, wide, *refs), grid=(tiles...  48.1 us
    ppermute x54, starting transfers between devices, flip_quad(): lax.ppermute(values_in, ('dp', 'tensor'), [(i, i ^ bits) for i in range(2...  36.4 us
    ppermute x10, waiting for transfers between devices, flip_dp(): lax.ppermute(values_in, 'dp', [(i, i ^ bit) for i in range(dp_size())])  26.4 us
    ppermute x18, starting transfers between devices, step_line(): lax.ppermute(values_in, 'dp', [(i, (i + 4 * offset) % count) for i in ran...  24.7 us
    unnamed x214, local copies, waits for them, and re-layouts  16 us
  transfers between devices with their start and end apart: 84, of which 37 were waited for; matrix products, arithmetic and copies ran while one was open for 28% of the time, Pallas kernels for 0%

profile of v7, /device:TPU:4, one launch (start us, length us, event | category | flops | bytes accessed | tf_op | source)
XLA Modules:
  0.0 488.0 jit_solution(13368864799664212455)
XLA Ops:
  14.9 1.6 collective-permute-start.3
  20.8 5.0 %collective-permute-done.3 = bf16[193,768]{1,0:T(8,128)(2,1)S(1)} collective-permute-done((bf16[193,768]{1,0:T(8,128)(2,1)S(1)}, bf16[193,768]{1,0:T(8,128)(2,1)S(1)}, u32[]{:S(2)}, u32[]{:S(2)}) %collective-permute-start.3) | collective-permute-done | bytes 296480 | tf_op jit(solution)/shard_map/ppermute | solution.py:60
  26.9 16.7 %collective-permute-done.4 = bf16[193,768]{1,0:T(8,128)(2,1)} collective-permute-done((bf16[193,768]{1,0:T(8,128)(2,1)S(1)}, bf16[193,768]{1,0:T(8,128)(2,1)}, u32[]{:S(2)}, u32[]{:S(2)}) %collective-permute-start.4) | collective-permute-done | bytes 296480 | tf_op jit(solution)/shard_map/ppermute | solution.py:60
  43.7 4.2 fusion.126
  47.9 2.1 copy.181
  52.7 2.0 collective-permute-done.5
  57.9 1.7 collective-permute-start.6
  65.6 9.9 %collective-permute-done.17 = bf16[96,2304]{1,0:T(8,128)(2,1)} collective-permute-done((bf16[96,2304]{1,0:T(8,128)(2,1)S(1)}, bf16[96,2304]{1,0:T(8,128)(2,1)}, u32[]{:S(2)}, u32[]{:S(2)}) %collective-permute-start.17) | collective-permute-done | bytes 442400 | tf_op jit(solution)/shard_map/ppermute | solution.py:60
  75.4 9.0 %collective-permute-done.6 = bf16[4,193,768]{2,0,1:T(4,128)(2,1)} collective-permute-done((bf16[4,193,768]{2,0,1:T(4,128)(2,1)}, bf16[4,193,768]{2,0,1:T(4,128)(2,1)}, u32[]{:S(2)}, u32[]{:S(2)}) %collective-permute-start.6) | collective-permute-done | bytes 1185824 | tf_op jit(solution)/shard_map/ppermute | solution.py:45
  87.0 4.0 collective-permute-done.18
  91.0 1.6 collective-permute-start.10
  93.2 3.1 fusion.149
  99.5 4.5 collective-permute-done.9
  104.0 4.9 %collective-permute-done.8 = bf16[64,768]{1,0:T(8,128)(2,1)} collective-permute-done((bf16[64,768]{1,0:T(8,128)(2,1)S(1)}, bf16[64,768]{1,0:T(8,128)(2,1)}, u32[]{:S(2)}, u32[]{:S(2)}) %collective-permute-start.8) | collective-permute-done | bytes 98336 | tf_op jit(solution)/shard_map/ppermute | solution.py:53
  112.4 5.1 %collective-permute-done.19 = bf16[96,2304]{1,0:T(8,128)(2,1)} collective-permute-done((bf16[96,2304]{1,0:T(8,128)(2,1)}, bf16[96,2304]{1,0:T(8,128)(2,1)}, u32[]{:S(2)}, u32[]{:S(2)}) %collective-permute-start.19) | collective-permute-done | bytes 442400 | tf_op jit(solution)/shard_map/ppermute | solution.py:60
  121.7 4.3 collective-permute-start.35
  126.0 7.2 %collective-permute-done.20 = bf16[4,96,768]{2,1,0:T(8,128)(2,1)S(1)} collective-permute-done((bf16[4,96,768]{2,1,0:T(8,128)(2,1)S(1)}, bf16[4,96,768]{2,1,0:T(8,128)(2,1)S(1)}, u32[]{:S(2)}, u32[]{:S(2)}) %collective-permute-start.20) | collective-permute-done | bytes 589856 | tf_op jit(solution)/shard_map/ppermute | solution.py:45
  136.2 1.7 reshape.256
  139.2 1.8 fusion.150
  141.0 1.8 fusion.8
  147.6 6.8 %collective-permute-done.35 = bf16[2,192,768]{2,1,0:T(8,128)(2,1)} collective-permute-done((bf16[2,192,768]{2,1,0:T(8,128)(2,1)}, bf16[2,192,768]{2,1,0:T(8,128)(2,1)}, u32[]{:S(2)}, u32[]{:S(2)}) %collective-permute-start.35) | collective-permute-done | bytes 589856 | tf_op jit(solution)/shard_map/ppermute | solution.py:60
  156.8 14.3 %collective-permute-done.36 = bf16[2,192,768]{2,1,0:T(8,128)(2,1)} collective-permute-done((bf16[2,192,768]{2,1,0:T(8,128)(2,1)}, bf16[2,192,768]{2,1,0:T(8,128)(2,1)}, u32[]{:S(2)}, u32[]{:S(2)}) %collective-permute-start.36) | collective-permute-done | bytes 589856 | tf_op jit(solution)/shard_map/ppermute | solution.py:60
  171.2 1.8 select_bitcast_fusion.3
  179.2 1.9 concatenate.120
  181.9 2.8 collective-permute-done.29
  187.7 1.7 select_bitcast_fusion.7
  194.0 1.9 slice.372
  200.8 1.8 copy.213
  202.6 1.8 copy.214
  204.4 1.8 copy.215
  208.7 3.2 collective-permute-done.40
  212.0 48.1 %shard_map.186 = (bf16[512,768]{1,0:T(8,128)(2,1)}, f32[512,768]{1,0:T(8,128)}, bf16[512,192]{1,0:T(8,128)(2,1)}, bf16[512,192]{1,0:T(8,128)(2,1)}, bf16[512,192...) custom-call(s32[2]{0:T(128)} %pad_add_fusion.refs_0_, ...), custom_call_target="tpu_custom_call" | custom-call | flops 21743271936 | bytes 28311552 | tf_op jit(solution)/shard_map/pallas_call | solution.py:601
  266.4 4.7 collective-permute-done.42
  273.0 2.2 collective-permute-done.43
  276.1 2.1 fusion.153
  281.4 2.2 collective-permute-done.46
  283.6 2.4 collective-permute-done.45
  288.9 2.3 collective-permute-done.49
  291.2 2.1 collective-permute-done.48
  301.3 2.9 copy.211
  311.5 2.2 fusion.5
  314.1 2.1 collective-permute-done.55
  325.0 4.5 collective-permute-done.59
  329.5 4.5 collective-permute-done.58
  339.4 2.3 collective-permute-done.60
  343.6 2.2 fusion.4
  345.8 12.6 %collective-permute-start.75 = (bf16[2,192,768]{2,1,0:T(8,128)(2,1)}, bf16[2,192,768]{2,1,0:T(8,128)(2,1)}, u32[]{:S(2)}, u32[]{:S(2)}) collective-permute-start(bf16[2,192,768]{2,1,0:T(8,128)(2,1)} %fusion.4), channel_id=1, source_target_pairs={{0,8},{2,10},{4,12},{6,14},{8,16},{10,18},{12,20},{14,22},{16,24},... | collective-permute-start | bytes 1769480 | tf_op jit(solution)/shard_map/ppermute | solution.py:60
  361.4 1.6 copy_dynamic-update-slice_fusion
  366.5 1.9 slice.396
  368.4 1.9 slice.398
  370.2 1.9 slice.394
  375.1 2.3 collective-permute-start.78
  381.0 1.9 slice.392
  385.5 6.8 %collective-permute-done.66 = bf16[64,8,192]{2,1,0:T(8,128)(2,1)} collective-permute-done((bf16[64,8,192]{2,1,0:T(8,128)(2,1)}, bf16[64,8,192]{2,1,0:T(8,128)(2,1)}, u32[]{:S(2)}, u32[]{:S(2)}) %collective-permute-start.66) | collective-permute-done | bytes 196640 | tf_op jit(solution)/shard_map/ppermute | solution.py:53
  393.7 1.9 fusion.32
  395.9 2.7 copy.212
  398.6 3.6 reshape.280
  404.9 13.5 %collective-permute-done.79 = bf16[96,2304]{1,0:T(8,128)(2,1)} collective-permute-done((bf16[96,2304]{1,0:T(8,128)(2,1)}, bf16[96,2304]{1,0:T(8,128)(2,1)}, u32[]{:S(2)}, u32[]{:S(2)}) %collective-permute-start.79) | collective-permute-done | bytes 442400 | tf_op jit(solution)/shard_map/ppermute | solution.py:60
  419.6 9.8 %collective-permute-done.76 = bf16[192,768]{1,0:T(8,128)(2,1)S(1)} collective-permute-done((bf16[192,768]{1,0:T(8,128)(2,1)S(1)}, bf16[192,768]{1,0:T(8,128)(2,1)S(1)}, u32[]{:S(2)}, u32[]{:S(2)}) %collective-permute-start.76) | collective-permute-done | bytes 294944 | tf_op jit(solution)/shard_map/ppermute | solution.py:45
  431.9 2.7 collective-permute-start.72
  434.6 3.4 collective-permute-done.80
  438.2 8.7 %collective-permute-done.72 = bf16[193,768]{1,0:T(8,128)(2,1)S(1)} collective-permute-done((bf16[193,768]{1,0:T(8,128)(2,1)S(1)}, bf16[193,768]{1,0:T(8,128)(2,1)S(1)}, u32[]{:S(2)}, u32[]{:S(2)}) %collective-permute-start.72) | collective-permute-done | bytes 296480 | tf_op jit(solution)/shard_map/ppermute | solution.py:60
  449.1 15.7 %collective-permute-done.73 = bf16[193,768]{1,0:T(8,128)(2,1)S(1)} collective-permute-done((bf16[193,768]{1,0:T(8,128)(2,1)S(1)}, bf16[193,768]{1,0:T(8,128)(2,1)S(1)}, u32[]{:S(2)}, u32[]{:S(2)}) %collective-permute-start.73) | collective-permute-done | bytes 296480 | tf_op jit(solution)/shard_map/ppermute | solution.py:60
  465.1 9.9 %collective-permute-done.74 = bf16[193,768]{1,0:T(8,128)(2,1)S(1)} collective-permute-done((bf16[193,768]{1,0:T(8,128)(2,1)S(1)}, bf16[193,768]{1,0:T(8,128)(2,1)S(1)}, u32[]{:S(2)}, u32[]{:S(2)}) %collective-permute-start.74) | collective-permute-done | bytes 296480 | tf_op jit(solution)/shard_map/ppermute | solution.py:60
  (543 shorter events, 148.8 us)
Async XLA Ops:
  7.2 204.8 %all-gather.3.cloned.1.call-start = ((), (), s32[]{:S(2)}) async-start(), calls=%async_computation.2 | async-start | bytes 14598144 | tf_op jit(solution)/shard_map/all_gather | solution.py:674
  13.1 463.4 %reduce-scatter.2.cloned.1.call-start = ((), (), s32[]{:S(2)}) async-start(), calls=%async_computation.1 | async-start | bytes 14598144 | tf_op jit(solution)/shard_map/reduce_scatter | solution.py:790
  14.9 10.9 %collective-permute-start.3 = (bf16[193,768]{1,0:T(8,128)(2,1)S(1)}, bf16[193,768]{1,0:T(8,128)(2,1)S(1)}, u32[]{:S(2)}, u32[]{:S(2)}) collective-permute-start(bf16[193,768]{1,0:T(8,128)(2,1)S(1)} %fusion.70), channel_id=1, source_target_pairs={{0,8},{2,10},{4,12},{6,14},{8,16},{10,18},{12,20},{14,22},{16,24},... | collective-permute-start | bytes 889352 | tf_op jit(solution)/shard_map/ppermute | solution.py:60
  18.1 41.4 %collective-permute-start.16 = (bf16[48,2304]{1,0:T(8,128)(2,1)}, bf16[48,2304]{1,0:T(8,128)(2,1)}, u32[]{:S(2)}, u32[]{:S(2)}) collective-permute-start(bf16[48,2304]{1,0:T(8,128)(2,1)} %dynamic-slice_bitcast_fusion.4), channel_id=1, source_target_pairs={{0,2},{2,0},{4,6},{6,4},{8,10},{10,8},{12,14},{14,12},{16,18},{18,... | collective-permute-start | bytes 663560 | tf_op jit(solution)/shard_map/ppermute | solution.py:45
  19.6 44.0 %collective-permute-start.34 = (bf16[192,768]{1,0:T(8,128)(2,1)}, bf16[192,768]{1,0:T(8,128)(2,1)}, u32[]{:S(2)}, u32[]{:S(2)}) collective-permute-start(bf16[192,768]{1,0:T(8,128)(2,1)} %bitcast.49), channel_id=1, source_target_pairs={{0,4},{2,6},{4,0},{6,2},{8,12},{10,14},{12,8},{14,10},{16,20},{18,... | collective-permute-start | bytes 884744 | tf_op jit(solution)/shard_map/ppermute | solution.py:45
  25.8 17.9 %collective-permute-start.4 = (bf16[193,768]{1,0:T(8,128)(2,1)S(1)}, bf16[193,768]{1,0:T(8,128)(2,1)}, u32[]{:S(2)}, u32[]{:S(2)}) collective-permute-start(bf16[193,768]{1,0:T(8,128)(2,1)S(1)} %collective-permute-done.3), channel_id=1, source_target_pairs={{0,8},{2,10},{4,12},{6,14},{8,16},{10,18},{12,20},{14,22},{16,24},... | collective-permute-start | bytes 889352 | tf_op jit(solution)/shard_map/ppermute | solution.py:60
  43.7 11.1 %collective-permute-start.5 = (bf16[193,768]{1,0:T(8,128)(2,1)}, bf16[193,768]{1,0:T(8,128)(2,1)}, u32[]{:S(2)}, u32[]{:S(2)}) collective-permute-start(bf16[193,768]{1,0:T(8,128)(2,1)} %collective-permute-done.4), channel_id=1, source_target_pairs={{0,8},{2,10},{4,12},{6,14},{8,16},{10,18},{12,20},{14,22},{16,24},... | collective-permute-start | bytes 889352 | tf_op jit(solution)/shard_map/ppermute | solution.py:60
  50.0 41.0 %collective-permute-start = (bf16[64,8,192]{0,2,1:T(8,128)(2,1)}, bf16[64,8,192]{0,2,1:T(8,128)(2,1)}, u32[]{:S(2)}, u32[]{:S(2)}) collective-permute-start(bf16[64,8,192]{0,2,1:T(8,128)(2,1)} %bitcast.5), channel_id=1, source_target_pairs={{0,1},{1,0},{2,3},{3,2},{4,5},{5,4},{6,7},{7,6},{8,9},{9,8},{10,11... | collective-permute-start | bytes 589832 | tf_op jit(solution)/shard_map/ppermute | solution.py:53
  51.1 41.5 %collective-permute-start.1 = (bf16[64,8,192]{0,2,1:T(8,128)(2,1)}, bf16[64,8,192]{0,2,1:T(8,128)(2,1)}, u32[]{:S(2)}, u32[]{:S(2)}) collective-permute-start(bf16[64,8,192]{0,2,1:T(8,128)(2,1)} %bitcast.6), channel_id=1, source_target_pairs={{0,2},{1,3},{2,0},{3,1},{4,6},{5,7},{6,4},{7,5},{8,10},{9,11},{10,... | collective-permute-start | bytes 589832 | tf_op jit(solution)/shard_map/ppermute | solution.py:53
  57.9 26.5 %collective-permute-start.6 = (bf16[4,193,768]{2,0,1:T(4,128)(2,1)}, bf16[4,193,768]{2,0,1:T(4,128)(2,1)}, u32[]{:S(2)}, u32[]{:S(2)}) collective-permute-start(bf16[4,193,768]{2,0,1:T(4,128)(2,1)} %copy.184), channel_id=1, source_target_pairs={{0,4},{2,6},{4,0},{6,2},{8,12},{10,14},{12,8},{14,10},{16,20},{18,... | collective-permute-start | bytes 3557384 | tf_op jit(solution)/shard_map/ppermute | solution.py:45
  60.6 14.8 %collective-permute-start.17 = (bf16[96,2304]{1,0:T(8,128)(2,1)S(1)}, bf16[96,2304]{1,0:T(8,128)(2,1)}, u32[]{:S(2)}, u32[]{:S(2)}) collective-permute-start(bf16[96,2304]{1,0:T(8,128)(2,1)S(1)} %bitcast.439), channel_id=1, source_target_pairs={{0,8},{2,10},{4,12},{6,14},{8,16},{10,18},{12,20},{14,22},{16,24},... | collective-permute-start | bytes 1327112 | tf_op jit(solution)/shard_map/ppermute | solution.py:60
  63.6 29.5 %collective-permute-start.2 = (bf16[64,8,192]{0,2,1:T(8,128)(2,1)}, bf16[64,8,192]{0,2,1:T(8,128)(2,1)S(1)}, u32[]{:S(2)}, u32[]{:S(2)}) collective-permute-start(bf16[64,8,192]{0,2,1:T(8,128)(2,1)} %bitcast.7), channel_id=1, source_target_pairs={{0,3},{1,2},{2,1},{3,0},{4,7},{5,6},{6,5},{7,4},{8,11},{9,10},{10,... | collective-permute-start | bytes 589832 | tf_op jit(solution)/shard_map/ppermute | solution.py:53
  75.4 15.6 %collective-permute-start.18 = (bf16[96,2304]{1,0:T(8,128)(2,1)}, bf16[96,2304]{1,0:T(8,128)(2,1)}, u32[]{:S(2)}, u32[]{:S(2)}) collective-permute-start(bf16[96,2304]{1,0:T(8,128)(2,1)} %collective-permute-done.17), channel_id=1, source_target_pairs={{0,8},{2,10},{4,12},{6,14},{8,16},{10,18},{12,20},{14,22},{16,24},... | collective-permute-start | bytes 1327112 | tf_op jit(solution)/shard_map/ppermute | solution.py:60
  86.4 10.6 %collective-permute-start.11 = (bf16[1,8,192]{2,1,0:T(8,128)(2,1)S(1)}, bf16[1,8,192]{2,1,0:T(8,128)(2,1)S(1)}, u32[]{:S(2)}, u32[]{:S(2)}) collective-permute-start(bf16[1,8,192]{2,1,0:T(8,128)(2,1)S(1)} %bitcast.460), channel_id=1, source_target_pairs={{0,2},{1,3},{2,0},{3,1},{4,6},{5,7},{6,4},{7,5},{8,10},{9,11},{10,... | collective-permute-start | bytes 9224 | tf_op jit(solution)/shard_map/ppermute | solution.py:53
  91.0 8.1 %collective-permute-start.10 = (bf16[1,8,192]{2,1,0:T(8,128)(2,1)S(1)}, bf16[1,8,192]{2,1,0:T(8,128)(2,1)S(1)}, u32[]{:S(2)}, u32[]{:S(2)}) collective-permute-start(bf16[1,8,192]{2,1,0:T(8,128)(2,1)S(1)} %bitcast.462), channel_id=1, source_target_pairs={{0,1},{1,0},{2,3},{3,2},{4,5},{5,4},{6,7},{7,6},{8,9},{9,8},{10,11... | collective-permute-start | bytes 9224 | tf_op jit(solution)/shard_map/ppermute | solution.py:53
  92.7 24.8 %collective-permute-start.19 = (bf16[96,2304]{1,0:T(8,128)(2,1)}, bf16[96,2304]{1,0:T(8,128)(2,1)}, u32[]{:S(2)}, u32[]{:S(2)}) collective-permute-start(bf16[96,2304]{1,0:T(8,128)(2,1)} %collective-permute-done.18), channel_id=1, source_target_pairs={{0,8},{2,10},{4,12},{6,14},{8,16},{10,18},{12,20},{14,22},{16,24},... | collective-permute-start | bytes 1327112 | tf_op jit(solution)/shard_map/ppermute | solution.py:60
  97.0 7.0 %collective-permute-start.9 = (bf16[64,768]{1,0:T(8,128)(2,1)S(1)}, bf16[64,768]{1,0:T(8,128)(2,1)S(1)}, u32[]{:S(2)}, u32[]{:S(2)}) collective-permute-start(bf16[64,768]{1,0:T(8,128)(2,1)S(1)} %get-tuple-element.195), channel_id=1, source_target_pairs={{0,3},{1,2},{2,1},{3,0},{4,7},{5,6},{6,5},{7,4},{8,11},{9,10},{10,... | collective-permute-start | bytes 294920 | tf_op jit(solution)/shard_map/ppermute | solution.py:53
  97.6 11.3 %collective-permute-start.8 = (bf16[64,768]{1,0:T(8,128)(2,1)S(1)}, bf16[64,768]{1,0:T(8,128)(2,1)}, u32[]{:S(2)}, u32[]{:S(2)}) collective-permute-start(bf16[64,768]{1,0:T(8,128)(2,1)S(1)} %get-tuple-element.196), channel_id=1, source_target_pairs={{0,2},{1,3},{2,0},{3,1},{4,6},{5,7},{6,4},{7,5},{8,10},{9,11},{10,... | collective-permute-start | bytes 294920 | tf_op jit(solution)/shard_map/ppermute | solution.py:53
  110.4 23.5 %collective-permute-start.15 = (bf16[64,768]{1,0:T(8,128)(2,1)S(1)}, bf16[64,768]{1,0:T(8,128)(2,1)S(1)}, u32[]{:S(2)}, u32[]{:S(2)}) collective-permute-start(bf16[64,768]{1,0:T(8,128)(2,1)S(1)} %add_convert_fusion.2), channel_id=1, source_target_pairs={{0,3},{1,2},{2,1},{3,0},{4,7},{5,6},{6,5},{7,4},{8,11},{9,10},{10,... | collective-permute-start | bytes 294920 | tf_op jit(solution)/shard_map/ppermute | solution.py:53
  110.5 23.4 %collective-permute-start.14 = (bf16[64,768]{1,0:T(8,128)(2,1)S(1)}, bf16[64,768]{1,0:T(8,128)(2,1)S(1)}, u32[]{:S(2)}, u32[]{:S(2)}) collective-permute-start(bf16[64,768]{1,0:T(8,128)(2,1)S(1)} %add_convert_fusion.2), channel_id=1, source_target_pairs={{0,2},{1,3},{2,0},{3,1},{4,6},{5,7},{6,4},{7,5},{8,10},{9,11},{10,... | collective-permute-start | bytes 294920 | tf_op jit(solution)/shard_map/ppermute | solution.py:53
  111.6 22.3 %collective-permute-start.13 = (bf16[64,768]{1,0:T(8,128)(2,1)S(1)}, bf16[64,768]{1,0:T(8,128)(2,1)S(1)}, u32[]{:S(2)}, u32[]{:S(2)}) collective-permute-start(bf16[64,768]{1,0:T(8,128)(2,1)S(1)} %add_convert_fusion.2), channel_id=1, source_target_pairs={{0,1},{1,0},{2,3},{3,2},{4,5},{5,4},{6,7},{7,6},{8,9},{9,8},{10,11... | collective-permute-start | bytes 294920 | tf_op jit(solution)/shard_map/ppermute | solution.py:53
  118.7 14.5 %collective-permute-start.20 = (bf16[4,96,768]{2,1,0:T(8,128)(2,1)S(1)}, bf16[4,96,768]{2,1,0:T(8,128)(2,1)S(1)}, u32[]{:S(2)}, u32[]{:S(2)}) collective-permute-start(bf16[4,96,768]{2,1,0:T(8,128)(2,1)S(1)} %pad_maximum_fusion.8), channel_id=1, source_target_pairs={{0,4},{2,6},{4,0},{6,2},{8,12},{10,14},{12,8},{14,10},{16,20},{18,... | collective-permute-start | bytes 1769480 | tf_op jit(solution)/shard_map/ppermute | solution.py:45
  121.7 32.7 %collective-permute-start.35 = (bf16[2,192,768]{2,1,0:T(8,128)(2,1)}, bf16[2,192,768]{2,1,0:T(8,128)(2,1)}, u32[]{:S(2)}, u32[]{:S(2)}) collective-permute-start(bf16[2,192,768]{2,1,0:T(8,128)(2,1)} %pad_maximum_fusion.9), channel_id=1, source_target_pairs={{0,8},{2,10},{4,12},{6,14},{8,16},{10,18},{12,20},{14,22},{16,24},... | collective-permute-start | bytes 1769480 | tf_op jit(solution)/shard_map/ppermute | solution.py:60
  133.2 38.0 %collective-permute-start.27 = (bf16[4,96,1536]{2,1,0:T(8,128)(2,1)}, bf16[4,96,1536]{2,1,0:T(8,128)(2,1)}, u32[]{:S(2)}, u32[]{:S(2)}) collective-permute-start(bf16[4,96,1536]{2,1,0:T(8,128)(2,1)} %pad_maximum_fusion.6), channel_id=1, source_target_pairs={{0,4},{2,6},{4,0},{6,2},{8,12},{10,14},{12,8},{14,10},{16,20},{18,... | collective-permute-start | bytes 3538952 | tf_op jit(solution)/shard_map/ppermute | solution.py:45
  145.4 9.0 %collective-permute-start.21 = (bf16[64,768]{1,0:T(8,128)(2,1)S(1)}, bf16[64,768]{1,0:T(8,128)(2,1)S(1)}, u32[]{:S(2)}, u32[]{:S(2)}) collective-permute-start(bf16[64,768]{1,0:T(8,128)(2,1)S(1)} %get-tuple-element.191), channel_id=1, source_target_pairs={{0,1},{1,0},{2,3},{3,2},{4,5},{5,4},{6,7},{7,6},{8,9},{9,8},{10,11... | collective-permute-start | bytes 294920 | tf_op jit(solution)/shard_map/ppermute | solution.py:53
  145.4 8.9 %collective-permute-start.23 = (bf16[64,768]{1,0:T(8,128)(2,1)S(1)}, bf16[64,768]{1,0:T(8,128)(2,1)S(1)}, u32[]{:S(2)}, u32[]{:S(2)}) collective-permute-start(bf16[64,768]{1,0:T(8,128)(2,1)S(1)} %get-tuple-element.192), channel_id=1, source_target_pairs={{0,3},{1,2},{2,1},{3,0},{4,7},{5,6},{6,5},{7,4},{8,11},{9,10},{10,... | collective-permute-start | bytes 294920 | tf_op jit(solution)/shard_map/ppermute | solution.py:53
  146.6 7.8 %collective-permute-start.22 = (bf16[64,768]{1,0:T(8,128)(2,1)S(1)}, bf16[64,768]{1,0:T(8,128)(2,1)S(1)}, u32[]{:S(2)}, u32[]{:S(2)}) collective-permute-start(bf16[64,768]{1,0:T(8,128)(2,1)S(1)} %get-tuple-element.193), channel_id=1, source_target_pairs={{0,2},{1,3},{2,0},{3,1},{4,6},{5,7},{6,4},{7,5},{8,10},{9,11},{10,... | collective-permute-start | bytes 294920 | tf_op jit(solution)/shard_map/ppermute | solution.py:53
  154.4 16.8 %collective-permute-start.36 = (bf16[2,192,768]{2,1,0:T(8,128)(2,1)}, bf16[2,192,768]{2,1,0:T(8,128)(2,1)}, u32[]{:S(2)}, u32[]{:S(2)}) collective-permute-start(bf16[2,192,768]{2,1,0:T(8,128)(2,1)} %collective-permute-done.35), channel_id=1, source_target_pairs={{0,8},{2,10},{4,12},{6,14},{8,16},{10,18},{12,20},{14,22},{16,24},... | collective-permute-start | bytes 1769480 | tf_op jit(solution)/shard_map/ppermute | solution.py:60
  154.9 18.5 %collective-permute-start.26 = (bf16[64,768]{1,0:T(8,128)(2,1)S(1)}, bf16[64,768]{1,0:T(8,128)(2,1)S(1)}, u32[]{:S(2)}, u32[]{:S(2)}) collective-permute-start(bf16[64,768]{1,0:T(8,128)(2,1)S(1)} %add_convert_fusion.1), channel_id=1, source_target_pairs={{0,3},{1,2},{2,1},{3,0},{4,7},{5,6},{6,5},{7,4},{8,11},{9,10},{10,... | collective-permute-start | bytes 294920 | tf_op jit(solution)/shard_map/ppermute | solution.py:53
  155.0 18.4 %collective-permute-start.25 = (bf16[64,768]{1,0:T(8,128)(2,1)S(1)}, bf16[64,768]{1,0:T(8,128)(2,1)S(1)}, u32[]{:S(2)}, u32[]{:S(2)}) collective-permute-start(bf16[64,768]{1,0:T(8,128)(2,1)S(1)} %add_convert_fusion.1), channel_id=1, source_target_pairs={{0,2},{1,3},{2,0},{3,1},{4,6},{5,7},{6,4},{7,5},{8,10},{9,11},{10,... | collective-permute-start | bytes 294920 | tf_op jit(solution)/shard_map/ppermute | solution.py:53
  156.1 17.4 %collective-permute-start.24 = (bf16[64,768]{1,0:T(8,128)(2,1)S(1)}, bf16[64,768]{1,0:T(8,128)(2,1)S(1)}, u32[]{:S(2)}, u32[]{:S(2)}) collective-permute-start(bf16[64,768]{1,0:T(8,128)(2,1)S(1)} %add_convert_fusion.1), channel_id=1, source_target_pairs={{0,1},{1,0},{2,3},{3,2},{4,5},{5,4},{6,7},{7,6},{8,9},{9,8},{10,11... | collective-permute-start | bytes 294920 | tf_op jit(solution)/shard_map/ppermute | solution.py:53
  171.2 16.5 %collective-permute-start.37 = (bf16[2,192,768]{2,1,0:T(8,128)(2,1)}, bf16[2,192,768]{2,1,0:T(8,128)(2,1)}, u32[]{:S(2)}, u32[]{:S(2)}) collective-permute-start(bf16[2,192,768]{2,1,0:T(8,128)(2,1)} %collective-permute-done.36), channel_id=1, source_target_pairs={{0,8},{2,10},{4,12},{6,14},{8,16},{10,18},{12,20},{14,22},{16,24},... | collective-permute-start | bytes 1769480 | tf_op jit(solution)/shard_map/ppermute | solution.py:60
  177.8 6.8 %collective-permute-start.29 = (bf16[64,768]{1,0:T(8,128)(2,1)}, bf16[64,768]{1,0:T(8,128)(2,1)}, u32[]{:S(2)}, u32[]{:S(2)}) collective-permute-start(bf16[64,768]{1,0:T(8,128)(2,1)} %get-tuple-element.190), channel_id=1, source_target_pairs={{0,2},{1,3},{2,0},{3,1},{4,6},{5,7},{6,4},{7,5},{8,10},{9,11},{10,... | collective-permute-start | bytes 294920 | tf_op jit(solution)/shard_map/ppermute | solution.py:53
  185.8 6.6 %collective-permute-start.32 = (bf16[64,768]{1,0:T(8,128)(2,1)S(1)}, bf16[64,768]{1,0:T(8,128)(2,1)S(1)}, u32[]{:S(2)}, u32[]{:S(2)}) collective-permute-start(bf16[64,768]{1,0:T(8,128)(2,1)S(1)} %fusion.85), channel_id=1, source_target_pairs={{0,2},{1,3},{2,0},{3,1},{4,6},{5,7},{6,4},{7,5},{8,10},{9,11},{10,... | collective-permute-start | bytes 294920 | tf_op jit(solution)/shard_map/ppermute | solution.py:53
  197.7 11.0 %collective-permute-start.38 = (bf16[64,8,192]{2,1,0:T(8,128)(2,1)}, bf16[64,8,192]{2,1,0:T(8,128)(2,1)S(1)}, u32[]{:S(2)}, u32[]{:S(2)}) collective-permute-start(bf16[64,8,192]{2,1,0:T(8,128)(2,1)} %slice.368), channel_id=1, source_target_pairs={{0,1},{1,0},{2,3},{3,2},{4,5},{5,4},{6,7},{7,6},{8,9},{9,8},{10,11... | collective-permute-start | bytes 589832 | tf_op jit(solution)/shard_map/ppermute | solution.py:53
  197.9 10.9 %collective-permute-start.39 = (bf16[64,8,192]{2,1,0:T(8,128)(2,1)}, bf16[64,8,192]{2,1,0:T(8,128)(2,1)}, u32[]{:S(2)}, u32[]{:S(2)}) collective-permute-start(bf16[64,8,192]{2,1,0:T(8,128)(2,1)} %slice.370), channel_id=1, source_target_pairs={{0,2},{1,3},{2,0},{3,1},{4,6},{5,7},{6,4},{7,5},{8,10},{9,11},{10,... | collective-permute-start | bytes 589832 | tf_op jit(solution)/shard_map/ppermute | solution.py:53
  199.0 12.9 %collective-permute-start.40 = (bf16[64,8,192]{2,1,0:T(8,128)(2,1)}, bf16[64,8,192]{2,1,0:T(8,128)(2,1)}, u32[]{:S(2)}, u32[]{:S(2)}) collective-permute-start(bf16[64,8,192]{2,1,0:T(8,128)(2,1)} %slice.372), channel_id=1, source_target_pairs={{0,3},{1,2},{2,1},{3,0},{4,7},{5,6},{6,5},{7,4},{8,11},{9,10},{10,... | collective-permute-start | bytes 589832 | tf_op jit(solution)/shard_map/ppermute | solution.py:53
  261.6 9.5 %collective-permute-start.42 = (bf16[512,192]{1,0:T(8,128)(2,1)}, bf16[512,192]{1,0:T(8,128)(2,1)}, u32[]{:S(2)}, u32[]{:S(2)}) collective-permute-start(bf16[512,192]{1,0:T(8,128)(2,1)} %get-tuple-element.48), channel_id=1, source_target_pairs={{0,2},{1,3},{2,0},{3,1},{4,6},{5,7},{6,4},{7,5},{8,10},{9,11},{10,... | collective-permute-start | bytes 589832 | tf_op jit(solution)/shard_map/ppermute | solution.py:53
  262.8 12.3 %collective-permute-start.43 = (bf16[512,192]{1,0:T(8,128)(2,1)}, bf16[512,192]{1,0:T(8,128)(2,1)S(1)}, u32[]{:S(2)}, u32[]{:S(2)}) collective-permute-start(bf16[512,192]{1,0:T(8,128)(2,1)} %get-tuple-element.49), channel_id=1, source_target_pairs={{0,3},{1,2},{2,1},{3,0},{4,7},{5,6},{6,5},{7,4},{8,11},{9,10},{10,... | collective-permute-start | bytes 589832 | tf_op jit(solution)/shard_map/ppermute | solution.py:53
  288.9 20.7 %collective-permute-start.53 = (bf16[2,192,768]{2,1,0:T(8,128)(2,1)}, bf16[2,192,768]{2,1,0:T(8,128)(2,1)}, u32[]{:S(2)}, u32[]{:S(2)}) collective-permute-start(bf16[2,192,768]{2,1,0:T(8,128)(2,1)} %dynamic-slice_bitcast_fusion.3), channel_id=1, source_target_pairs={{0,8},{2,10},{4,12},{6,14},{8,16},{10,18},{12,20},{14,22},{16,24},... | collective-permute-start | bytes 1769480 | tf_op jit(solution)/shard_map/ppermute | solution.py:60
  296.3 9.8 %collective-permute-start.50 = (bf16[64,768]{1,0:T(8,128)(2,1)}, bf16[64,768]{1,0:T(8,128)(2,1)}, u32[]{:S(2)}, u32[]{:S(2)}) collective-permute-start(bf16[64,768]{1,0:T(8,128)(2,1)} %get-tuple-element.182), channel_id=1, source_target_pairs={{0,1},{1,0},{2,3},{3,2},{4,5},{5,4},{6,7},{7,6},{8,9},{9,8},{10,11... | collective-permute-start | bytes 294920 | tf_op jit(solution)/shard_map/ppermute | solution.py:53
  296.4 9.8 %collective-permute-start.52 = (bf16[64,768]{1,0:T(8,128)(2,1)}, bf16[64,768]{1,0:T(8,128)(2,1)}, u32[]{:S(2)}, u32[]{:S(2)}) collective-permute-start(bf16[64,768]{1,0:T(8,128)(2,1)} %get-tuple-element.183), channel_id=1, source_target_pairs={{0,3},{1,2},{2,1},{3,0},{4,7},{5,6},{6,5},{7,4},{8,11},{9,10},{10,... | collective-permute-start | bytes 294920 | tf_op jit(solution)/shard_map/ppermute | solution.py:53
  297.6 8.5 %collective-permute-start.51 = (bf16[64,768]{1,0:T(8,128)(2,1)S(1)}, bf16[64,768]{1,0:T(8,128)(2,1)}, u32[]{:S(2)}, u32[]{:S(2)}) collective-permute-start(bf16[64,768]{1,0:T(8,128)(2,1)S(1)} %get-tuple-element.184), channel_id=1, source_target_pairs={{0,2},{1,3},{2,0},{3,1},{4,6},{5,7},{6,4},{7,5},{8,10},{9,11},{10,... | collective-permute-start | bytes 294920 | tf_op jit(solution)/shard_map/ppermute | solution.py:53
  305.6 57.4 %collective-permute-start.64 = (bf16[4,96,1536]{2,1,0:T(8,128)(2,1)}, bf16[4,96,1536]{2,1,0:T(8,128)(2,1)}, u32[]{:S(2)}, u32[]{:S(2)}) collective-permute-start(bf16[4,96,1536]{2,1,0:T(8,128)(2,1)} %dynamic-slice_bitcast_fusion.1), channel_id=1, source_target_pairs={{0,4},{2,6},{4,0},{6,2},{8,12},{10,14},{12,8},{14,10},{16,20},{18,... | collective-permute-start | bytes 3538952 | tf_op jit(solution)/shard_map/ppermute | solution.py:45
  309.6 6.7 %collective-permute-start.56 = (bf16[64,768]{1,0:T(8,128)(2,1)S(1)}, bf16[64,768]{1,0:T(8,128)(2,1)S(1)}, u32[]{:S(2)}, u32[]{:S(2)}) collective-permute-start(bf16[64,768]{1,0:T(8,128)(2,1)S(1)} %fusion.101), channel_id=1, source_target_pairs={{0,3},{1,2},{2,1},{3,0},{4,7},{5,6},{6,5},{7,4},{8,11},{9,10},{10,... | collective-permute-start | bytes 294920 | tf_op jit(solution)/shard_map/ppermute | solution.py:53
  313.7 28.0 %collective-permute-start.60 = (bf16[2,192,768]{2,1,0:T(8,128)(2,1)}, bf16[2,192,768]{2,1,0:T(8,128)(2,1)}, u32[]{:S(2)}, u32[]{:S(2)}) collective-permute-start(bf16[2,192,768]{2,1,0:T(8,128)(2,1)} %fusion.5), channel_id=1, source_target_pairs={{0,8},{2,10},{4,12},{6,14},{8,16},{10,18},{12,20},{14,22},{16,24},... | collective-permute-start | bytes 1769480 | tf_op jit(solution)/shard_map/ppermute | solution.py:60
  322.4 7.1 %collective-permute-start.59 = (bf16[64,768]{1,0:T(8,128)(2,1)S(1)}, bf16[64,768]{1,0:T(8,128)(2,1)S(1)}, u32[]{:S(2)}, u32[]{:S(2)}) collective-permute-start(bf16[64,768]{1,0:T(8,128)(2,1)S(1)} %get-tuple-element.180), channel_id=1, source_target_pairs={{0,3},{1,2},{2,1},{3,0},{4,7},{5,6},{6,5},{7,4},{8,11},{9,10},{10,... | collective-permute-start | bytes 294920 | tf_op jit(solution)/shard_map/ppermute | solution.py:53
  323.2 10.8 %collective-permute-start.58 = (bf16[64,768]{1,0:T(8,128)(2,1)S(1)}, bf16[64,768]{1,0:T(8,128)(2,1)S(1)}, u32[]{:S(2)}, u32[]{:S(2)}) collective-permute-start(bf16[64,768]{1,0:T(8,128)(2,1)S(1)} %get-tuple-element.181), channel_id=1, source_target_pairs={{0,2},{1,3},{2,0},{3,1},{4,6},{5,7},{6,4},{7,5},{8,10},{9,11},{10,... | collective-permute-start | bytes 294920 | tf_op jit(solution)/shard_map/ppermute | solution.py:53
  337.8 21.0 %collective-permute-start.77 = (bf16[4,96,768]{2,1,0:T(8,128)(2,1)}, bf16[4,96,768]{2,1,0:T(8,128)(2,1)S(1)}, u32[]{:S(2)}, u32[]{:S(2)}) collective-permute-start(bf16[4,96,768]{2,1,0:T(8,128)(2,1)} %dynamic-slice_bitcast_fusion.2), channel_id=1, source_target_pairs={{0,4},{2,6},{4,0},{6,2},{8,12},{10,14},{12,8},{14,10},{16,20},{18,... | collective-permute-start | bytes 1769480 | tf_op jit(solution)/shard_map/ppermute | solution.py:45
  341.7 16.8 %collective-permute-start.63 = (bf16[64,768]{1,0:T(8,128)(2,1)S(1)}, bf16[64,768]{1,0:T(8,128)(2,1)S(1)}, u32[]{:S(2)}, u32[]{:S(2)}) collective-permute-start(bf16[64,768]{1,0:T(8,128)(2,1)S(1)} %add_convert_fusion), channel_id=1, source_target_pairs={{0,3},{1,2},{2,1},{3,0},{4,7},{5,6},{6,5},{7,4},{8,11},{9,10},{10,... | collective-permute-start | bytes 294920 | tf_op jit(solution)/shard_map/ppermute | solution.py:53
  341.7 16.7 %collective-permute-start.62 = (bf16[64,768]{1,0:T(8,128)(2,1)S(1)}, bf16[64,768]{1,0:T(8,128)(2,1)S(1)}, u32[]{:S(2)}, u32[]{:S(2)}) collective-permute-start(bf16[64,768]{1,0:T(8,128)(2,1)S(1)} %add_convert_fusion), channel_id=1, source_target_pairs={{0,2},{1,3},{2,0},{3,1},{4,6},{5,7},{6,4},{7,5},{8,10},{9,11},{10,... | collective-permute-start | bytes 294920 | tf_op jit(solution)/shard_map/ppermute | solution.py:53
  345.8 56.4 %collective-permute-start.75 = (bf16[2,192,768]{2,1,0:T(8,128)(2,1)}, bf16[2,192,768]{2,1,0:T(8,128)(2,1)}, u32[]{:S(2)}, u32[]{:S(2)}) collective-permute-start(bf16[2,192,768]{2,1,0:T(8,128)(2,1)} %fusion.4), channel_id=1, source_target_pairs={{0,8},{2,10},{4,12},{6,14},{8,16},{10,18},{12,20},{14,22},{16,24},... | collective-permute-start | bytes 1769480 | tf_op jit(solution)/shard_map/ppermute | solution.py:60
  372.1 10.8 %collective-permute-start.65 = (bf16[64,8,192]{2,1,0:T(8,128)(2,1)}, bf16[64,8,192]{2,1,0:T(8,128)(2,1)}, u32[]{:S(2)}, u32[]{:S(2)}) collective-permute-start(bf16[64,8,192]{2,1,0:T(8,128)(2,1)} %slice.394), channel_id=1, source_target_pairs={{0,1},{1,0},{2,3},{3,2},{4,5},{5,4},{6,7},{7,6},{8,9},{9,8},{10,11... | collective-permute-start | bytes 589832 | tf_op jit(solution)/shard_map/ppermute | solution.py:53
  372.1 13.4 %collective-permute-start.67 = (bf16[64,8,192]{2,1,0:T(8,128)(2,1)}, bf16[64,8,192]{2,1,0:T(8,128)(2,1)}, u32[]{:S(2)}, u32[]{:S(2)}) collective-permute-start(bf16[64,8,192]{2,1,0:T(8,128)(2,1)} %slice.398), channel_id=1, source_target_pairs={{0,3},{1,2},{2,1},{3,0},{4,7},{5,6},{6,5},{7,4},{8,11},{9,10},{10,... | collective-permute-start | bytes 589832 | tf_op jit(solution)/shard_map/ppermute | solution.py:53
  373.4 19.0 %collective-permute-start.66 = (bf16[64,8,192]{2,1,0:T(8,128)(2,1)}, bf16[64,8,192]{2,1,0:T(8,128)(2,1)}, u32[]{:S(2)}, u32[]{:S(2)}) collective-permute-start(bf16[64,8,192]{2,1,0:T(8,128)(2,1)} %slice.396), channel_id=1, source_target_pairs={{0,2},{1,3},{2,0},{3,1},{4,6},{5,7},{6,4},{7,5},{8,10},{9,11},{10,... | collective-permute-start | bytes 589832 | tf_op jit(solution)/shard_map/ppermute | solution.py:53
  375.1 18.6 %collective-permute-start.78 = (bf16[96,2304]{1,0:T(8,128)(2,1)}, bf16[96,2304]{1,0:T(8,128)(2,1)}, u32[]{:S(2)}, u32[]{:S(2)}) collective-permute-start(bf16[96,2304]{1,0:T(8,128)(2,1)} %fusion.66), channel_id=1, source_target_pairs={{0,8},{2,10},{4,12},{6,14},{8,16},{10,18},{12,20},{14,22},{16,24},... | collective-permute-start | bytes 1327112 | tf_op jit(solution)/shard_map/ppermute | solution.py:60
  382.9 47.4 %collective-permute-start.71 = (bf16[4,193,768]{2,0,1:T(4,128)(2,1)}, bf16[4,193,768]{2,0,1:T(4,128)(2,1)}, u32[]{:S(2)}, u32[]{:S(2)}) collective-permute-start(bf16[4,193,768]{2,0,1:T(4,128)(2,1)} %copy.218), channel_id=1, source_target_pairs={{0,4},{2,6},{4,0},{6,2},{8,12},{10,14},{12,8},{14,10},{16,20},{18,... | collective-permute-start | bytes 3557384 | tf_op jit(solution)/shard_map/ppermute | solution.py:45
  395.5 22.8 %collective-permute-start.79 = (bf16[96,2304]{1,0:T(8,128)(2,1)}, bf16[96,2304]{1,0:T(8,128)(2,1)}, u32[]{:S(2)}, u32[]{:S(2)}) collective-permute-start(bf16[96,2304]{1,0:T(8,128)(2,1)} %fusion.32), channel_id=1, source_target_pairs={{0,8},{2,10},{4,12},{6,14},{8,16},{10,18},{12,20},{14,22},{16,24},... | collective-permute-start | bytes 1327112 | tf_op jit(solution)/shard_map/ppermute | solution.py:60
  403.6 25.8 %collective-permute-start.76 = (bf16[192,768]{1,0:T(8,128)(2,1)S(1)}, bf16[192,768]{1,0:T(8,128)(2,1)S(1)}, u32[]{:S(2)}, u32[]{:S(2)}) collective-permute-start(bf16[192,768]{1,0:T(8,128)(2,1)S(1)} %fusion.72), channel_id=1, source_target_pairs={{0,4},{2,6},{4,0},{6,2},{8,12},{10,14},{12,8},{14,10},{16,20},{18,... | collective-permute-start | bytes 884744 | tf_op jit(solution)/shard_map/ppermute | solution.py:45
  419.6 18.4 %collective-permute-start.80 = (bf16[96,2304]{1,0:T(8,128)(2,1)S(1)}, bf16[96,2304]{1,0:T(8,128)(2,1)S(1)}, u32[]{:S(2)}, u32[]{:S(2)}) collective-permute-start(bf16[96,2304]{1,0:T(8,128)(2,1)S(1)} %fusion.28), channel_id=1, source_target_pairs={{0,8},{2,10},{4,12},{6,14},{8,16},{10,18},{12,20},{14,22},{16,24},... | collective-permute-start | bytes 1327112 | tf_op jit(solution)/shard_map/ppermute | solution.py:60
  431.9 15.0 %collective-permute-start.72 = (bf16[193,768]{1,0:T(8,128)(2,1)S(1)}, bf16[193,768]{1,0:T(8,128)(2,1)S(1)}, u32[]{:S(2)}, u32[]{:S(2)}) collective-permute-start(bf16[193,768]{1,0:T(8,128)(2,1)S(1)} %fusion.71), channel_id=1, source_target_pairs={{0,8},{2,10},{4,12},{6,14},{8,16},{10,18},{12,20},{14,22},{16,24},... | collective-permute-start | bytes 889352 | tf_op jit(solution)/shard_map/ppermute | solution.py:60
  438.1 10.0 %collective-permute-start.81 = (bf16[48,2304]{1,0:T(8,128)(2,1)S(1)}, bf16[48,2304]{1,0:T(8,128)(2,1)S(1)}, u32[]{:S(2)}, u32[]{:S(2)}) collective-permute-start(bf16[48,2304]{1,0:T(8,128)(2,1)S(1)} %fusion.73), channel_id=1, source_target_pairs={{0,2},{2,0},{4,6},{6,4},{8,10},{10,8},{12,14},{14,12},{16,18},{18,... | collective-permute-start | bytes 663560 | tf_op jit(solution)/shard_map/ppermute | solution.py:45
  446.9 17.9 %collective-permute-start.73 = (bf16[193,768]{1,0:T(8,128)(2,1)S(1)}, bf16[193,768]{1,0:T(8,128)(2,1)S(1)}, u32[]{:S(2)}, u32[]{:S(2)}) collective-permute-start(bf16[193,768]{1,0:T(8,128)(2,1)S(1)} %fusion.60), channel_id=1, source_target_pairs={{0,8},{2,10},{4,12},{6,14},{8,16},{10,18},{12,20},{14,22},{16,24},... | collective-permute-start | bytes 889352 | tf_op jit(solution)/shard_map/ppermute | solution.py:60
  464.9 10.0 %collective-permute-start.74 = (bf16[193,768]{1,0:T(8,128)(2,1)S(1)}, bf16[193,768]{1,0:T(8,128)(2,1)S(1)}, u32[]{:S(2)}, u32[]{:S(2)}) collective-permute-start(bf16[193,768]{1,0:T(8,128)(2,1)S(1)} %fusion.61), channel_id=1, source_target_pairs={{0,8},{2,10},{4,12},{6,14},{8,16},{10,18},{12,20},{14,22},{16,24},... | collective-permute-start | bytes 889352 | tf_op jit(solution)/shard_map/ppermute | solution.py:60
  (117 other events, 772.4 us)
Sparse Core Ops, SparseCore 0:
  13.2 140.1 all-gather.2
  260.2 206.8 reduce-scatter.1
